TPU v7x, 512 devices: a whole 4x4x16 slice. The times are simulated.
512 devices in a mesh: rows: 64 (over y, z), cols: 8 (over x, core).
Axes of the slice: x: 4, y: 4, z: 16, core: 2. Of those that a mesh axis runs over, the one named last changes fastest.
Arguments:
- vectors: float32 [512, 131072], P(None, ('rows', 'cols')), may hold values from -80 to 80
- offsets: int32 [16, 131072], P(None, ('rows', 'cols')), may hold values from -256 to 256, as said below
- counts: int32 [131072], P(('rows', 'cols')), may hold values from 8 to 16
- labels: int32 [2, 131072], P(None, ('rows', 'cols')), may hold values from 0 to 1
- cosines: float32 [16, 131072], P(None, ('rows', 'cols')), may hold values from -1 to 1
- distances: float32 [16, 131072], P(None, ('rows', 'cols')), may hold values from 1 to 3
Outputs:
- basis: float32 [512, 131072], P('cols', 'rows')
Inputs may be any that keep to these rules, and one draw needn't show every extreme that they name: `offsets`: each offset is nonzero and at most 256 in magnitude; both -256 and 256 occur. Offsets follow a lattice: small in-row steps, steps near half of 256, and steps near 256.
All inputs are finite; a program needn't handle non-finite values.
Results may differ from a plain program's by a relative error of at most 0.00012.
Values sent between devices are 32-bit elements; how exact they have to be, the bound alone decides.
No kernel may reach another device: no remote copies, remote signals or barrier semaphores. Data moves between devices by JAX's collectives and lax.ppermute only.
A program may use at most 64 MiB of HBM per device.

v0:
```python
import jax
import jax.numpy as jnp
from jax import lax
from jax.sharding import PartitionSpec as P

REACH = 256


PI_BOND = -1.0
SIGMA_BOND = 0.178
DECAY_LENGTH = 0.319
LAYER_GAP = 2.36
SITE_MASS = 0.4
LAYER_BIAS = 0.25


def extended_2(block, sides, width):
    for axis, dim in sides:
        count = lax.axis_size(axis)
        forward = [(i, i + 1) for i in range(count - 1)]
        forward.append((count - 1, 0))
        backward = [(target, source) for source, target in forward]
        low = lax.ppermute(
            lax.slice_in_dim(block, block.shape[dim] - width, None, axis=dim), axis, forward
        )
        high = lax.ppermute(lax.slice_in_dim(block, 0, width, axis=dim), axis, backward)
        block = jnp.concatenate([low, block, high], axis=dim)
    return block


def spread(value, axis, source):
    kept = jnp.where(lax.axis_index(axis) == source, value, 0).astype(value.dtype)
    return lax.psum(kept, axis)


def hop_table(cosines, distances, counts):
    square = cosines * cosines
    bond_value = PI_BOND * jnp.exp(-(distances - 1.0) / DECAY_LENGTH) * (1.0 - square)
    bond_value = bond_value + SIGMA_BOND * jnp.exp(-(distances - LAYER_GAP) / DECAY_LENGTH) * square
    slot_index = lax.broadcasted_iota(jnp.int32, cosines.shape, 0)
    return jnp.where(slot_index < counts[None, :], bond_value, jnp.zeros_like(bond_value))


def onsite_of(labels):
    sublattice = (2 * labels[0] - 1).astype(jnp.float32)
    layer_sign = (2 * labels[1] - 1).astype(jnp.float32)
    return SITE_MASS * sublattice + LAYER_BIAS * layer_sign


def apply_local(extended, hopping, offsets, onsite):
    atom_count = hopping.shape[1]
    middle = extended[:, REACH : REACH + atom_count]
    column = jnp.arange(atom_count, dtype=jnp.int32) + REACH

    def advance(slot_index, running):
        target = column + offsets[slot_index]
        return running + hopping[slot_index][None, :] * jnp.take(extended, target, axis=1)

    return lax.fori_loop(0, hopping.shape[0], advance, onsite[None, :] * middle)


def regroup(source):
    return lax.all_to_all(source, "cols", split_axis=0, concat_axis=1, tiled=True)


def on_device(vectors, offsets, counts, labels, cosines, distances):
    highest = lax.Precision.HIGHEST
    hopping = hop_table(cosines, distances, counts)
    onsite = onsite_of(labels)
    applied = vectors
    for repeat in range(2):
        extended = extended_2(applied, ((("rows", "cols"), 1),), REACH)
        applied = apply_local(extended, hopping, offsets, onsite)
    local_block = regroup(applied)
    atom_total = local_block.shape[1] * lax.axis_size("rows")
    step_count = min(3, lax.axis_size("cols") - 1)
    column_index = lax.axis_index("cols")
    for step_index in range(step_count):
        gram_matrix = (
            lax.psum(jnp.dot(local_block, local_block.T, precision=highest), "rows") / atom_total
        )
        factor = jnp.linalg.cholesky(gram_matrix)
        candidate = jax.scipy.linalg.solve_triangular(factor, local_block, lower=True)
        leader = spread(candidate, "cols", step_index)
        coupling = lax.psum(jnp.dot(leader, local_block.T, precision=highest), "rows") / atom_total
        reduced = local_block - jnp.dot(coupling.T, leader, precision=highest)
        local_block = jnp.where(
            column_index > step_index,
            reduced,
            jnp.where(column_index == step_index, leader, local_block),
        )
    return local_block


def solution(mesh):
    placed = (
        P(None, ("rows", "cols")),
        P(None, ("rows", "cols")),
        P(("rows", "cols")),
        P(None, ("rows", "cols")),
        P(None, ("rows", "cols")),
        P(None, ("rows", "cols")),
    )
    return jax.shard_map(
        on_device, mesh=mesh, in_specs=placed, out_specs=P("cols", "rows"), check_vma=False
    )
```

profile of v0, /device:TPU:2, one launch (start us, length us, event | category | flops | bytes accessed | tf_op | source)
XLA Modules:
  0.0 2041.9 jit_solution(11783422857836279491)
XLA Ops:
  6.5 1.2 copy.18
  7.8 1.9 collective-permute-start
  9.7 3.6 collective-permute-start.1
  15.0 3.3 collective-permute-done
  18.3 1.8 collective-permute-done.1
  20.0 1.2 pad_maximum_fusion
  21.2 30.6 %while.28 = (s32[]{:T(128)}, f32[512,256]{0,1:T(8,128)S(1)}, f32[16,256]{1,0:T(8,128)S(1)}, s32[16,256]{1,0:T(8,128)}, f32[512,768]{0,1:T(8,128)S(1)}, /*index=5*/s32[]{:T(128)}) while((s32[]{:T(128)}, f32[512,256]{0,1:T(8,128)S(1)}, f32[16,256]{1,0:T(8,128)S(1)}, s32[16,256]{1,0:T(8,128)}, f32[512,768]{0,1:T(8,128)S(1)}, ...), condition=%wide.region_1.0_spmd.clone, body=%wide.region_0.2_spmd.clone.sunk | while | flops 396290 | bytes 2635341 | solution.py:59
  21.9 1.0 gather_fusion
  23.9 1.0 gather_fusion
  25.8 1.0 gather_fusion
  27.7 1.0 gather_fusion
  29.6 1.0 gather_fusion
  31.5 1.0 gather_fusion
  33.4 1.0 gather_fusion
  35.3 1.0 gather_fusion
  37.2 1.0 gather_fusion
  39.2 1.0 gather_fusion
  41.1 1.0 gather_fusion
  43.0 1.0 gather_fusion
  44.9 1.0 gather_fusion
  48.7 1.0 gather_fusion
  51.8 3.8 collective-permute-start.2
  55.6 2.1 collective-permute-start.3
  57.8 4.8 collective-permute-done.2
  62.6 1.8 collective-permute-done.3
  64.3 1.2 pad_maximum_fusion.1
  65.5 30.6 %while.29 = (s32[]{:T(128)}, f32[512,256]{0,1:T(8,128)S(1)}, f32[16,256]{1,0:T(8,128)S(1)}, s32[16,256]{1,0:T(8,128)}, f32[512,768]{0,1:T(8,128)S(1)}, /*index=5*/s32[]{:T(128)}) while((s32[]{:T(128)}, f32[512,256]{0,1:T(8,128)S(1)}, f32[16,256]{1,0:T(8,128)S(1)}, s32[16,256]{1,0:T(8,128)}, f32[512,768]{0,1:T(8,128)S(1)}, ...), condition=%wide.region_3.5_spmd.clone, body=%wide.region_2.4_spmd.clone.sunk | while | flops 396290 | bytes 2635341 | solution.py:59
  66.2 1.0 gather_fusion.1
  70.1 1.0 gather_fusion.1
  72.0 1.0 gather_fusion.1
  75.8 1.0 gather_fusion.1
  79.6 1.0 gather_fusion.1
  83.5 1.0 gather_fusion.1
  85.4 1.0 gather_fusion.1
  89.2 1.0 gather_fusion.1
  93.0 1.0 gather_fusion.1
  94.9 1.0 gather_fusion.1
  96.1 1.0 copy.22
  97.1 21.2 %all-to-all-start = ((f32[8,64,256]{2,1,0:T(8,128)}), f32[8,64,256]{2,1,0:T(8,128)S(1)}, u32[]{:S(2)}, u32[]{:S(2)}) async-start(f32[8,64,256]{2,1,0:T(8,128)} %bitcast.1), calls=%async_computation | async-start | bytes 1048576 | tf_op jit(solution)/shard_map/all_to_all | solution.py:63
  118.3 8.9 all-to-all-done
  127.8 279.8 %psum.63 = f32[64,64]{0,1:T(8,128)S(1)} all-reduce(f32[64,64]{0,1:T(8,128)S(1)} %convolution_bitcast_fusion), channel_id=1, replica_groups=mesh['rows'=64,'cols'=8] {'rows'}, use_global_device_ids=true, to_apply=%region_4.6 | all-reduce | flops 4096 | bytes 32768 | tf_op jit(solution)/shard_map/psum | solution.py:80
  407.7 5.8 cholesky.59
  414.9 4.9 custom-call.7
  419.8 1.4 convolution_select_fusion.2
  421.3 61.5 %all-reduce.4.cloned.1.call-done = f32[64,2048]{1,0:T(8,128)} async-done(((f32[64,2048]{1,0:T(8,128)}), f32[64,2048]{1,0:T(8,128)}) %all-reduce.4.cloned.1.call-update) | async-done | bytes 524304 | tf_op jit(solution)/shard_map/psum | solution.py:33
  482.9 1.6 fusion.28
  484.5 280.2 %psum.65 = f32[64,64]{0,1:T(8,128)S(1)} all-reduce(f32[64,64]{0,1:T(8,128)S(1)} %fusion.28), channel_id=1, replica_groups=mesh['rows'=64,'cols'=8] {'rows'}, use_global_device_ids=true, to_apply=%region_8.12 | all-reduce | flops 4096 | bytes 32768 | tf_op jit(solution)/shard_map/psum | solution.py:85
  764.7 1.8 fusion.8
  767.0 273.9 %psum.66 = f32[64,64]{0,1:T(8,128)S(1)} all-reduce(f32[64,64]{0,1:T(8,128)S(1)} %fusion.29), channel_id=1, replica_groups=mesh['rows'=64,'cols'=8] {'rows'}, use_global_device_ids=true, to_apply=%region_9.13 | all-reduce | flops 4096 | bytes 32768 | tf_op jit(solution)/shard_map/psum | solution.py:80
  1041.1 5.8 cholesky.70
  1048.3 4.9 custom-call.8
  1053.2 1.4 convolution_select_fusion.1
  1054.7 62.1 %all-reduce.6.cloned.1.call-done = f32[64,2048]{1,0:T(8,128)} async-done(((f32[64,2048]{1,0:T(8,128)}), f32[64,2048]{1,0:T(8,128)}) %all-reduce.6.cloned.1.call-update) | async-done | bytes 524304 | tf_op jit(solution)/shard_map/psum | solution.py:33
  1116.8 1.6 fusion.30
  1118.4 280.3 %psum.68 = f32[64,64]{0,1:T(8,128)S(1)} all-reduce(f32[64,64]{0,1:T(8,128)S(1)} %fusion.30), channel_id=1, replica_groups=mesh['rows'=64,'cols'=8] {'rows'}, use_global_device_ids=true, to_apply=%region_11.15 | all-reduce | flops 4096 | bytes 32768 | tf_op jit(solution)/shard_map/psum | solution.py:85
  1398.7 1.8 fusion.7
  1401.1 273.9 %psum.69 = f32[64,64]{0,1:T(8,128)S(1)} all-reduce(f32[64,64]{0,1:T(8,128)S(1)} %fusion.31), channel_id=1, replica_groups=mesh['rows'=64,'cols'=8] {'rows'}, use_global_device_ids=true, to_apply=%region_12.16 | all-reduce | flops 4096 | bytes 32768 | tf_op jit(solution)/shard_map/psum | solution.py:80
  1675.2 5.8 cholesky.81
  1682.4 4.9 custom-call.9
  1687.3 1.4 convolution_select_fusion
  1688.7 62.3 %all-reduce.8.cloned.1.call-done = f32[64,2048]{1,0:T(8,128)} async-done(((f32[64,2048]{1,0:T(8,128)}), f32[64,2048]{1,0:T(8,128)}) %all-reduce.8.cloned.1.call-update) | async-done | bytes 524304 | tf_op jit(solution)/shard_map/psum | solution.py:33
  1751.0 1.6 fusion.32
  1752.6 280.1 %psum.71 = f32[64,64]{0,1:T(8,128)S(1)} all-reduce(f32[64,64]{0,1:T(8,128)S(1)} %fusion.32), channel_id=1, replica_groups=mesh['rows'=64,'cols'=8] {'rows'}, use_global_device_ids=true, to_apply=%region_14.18 | all-reduce | flops 4096 | bytes 32768 | tf_op jit(solution)/shard_map/psum | solution.py:85
  2032.7 2.6 fusion.6
  (200 shorter events, 44.5 us)
Async XLA Ops:
  7.8 10.5 collective-permute-start
  9.7 10.3 collective-permute-start.1
  51.8 10.8 collective-permute-start.2
  55.6 8.7 collective-permute-start.3
  97.1 30.1 %all-to-all-start = ((f32[8,64,256]{2,1,0:T(8,128)}), f32[8,64,256]{2,1,0:T(8,128)S(1)}, u32[]{:S(2)}, u32[]{:S(2)}) async-start(f32[8,64,256]{2,1,0:T(8,128)} %bitcast.1), calls=%async_computation | async-start | bytes 1048576 | tf_op jit(solution)/shard_map/all_to_all | solution.py:63
  118.3 364.6 %all-reduce.4.cloned.1.call-start = ((), (), s32[]{:S(2)}) async-start(), calls=%async_computation.1 | async-start | bytes 1048576 | tf_op jit(solution)/shard_map/psum | solution.py:33
  421.3 695.5 %all-reduce.6.cloned.1.call-start = ((), (), s32[]{:S(2)}) async-start(), calls=%async_computation.2 | async-start | bytes 1048576 | tf_op jit(solution)/shard_map/psum | solution.py:33
  1054.6 696.3 %all-reduce.8.cloned.1.call-start = ((), (), s32[]{:S(2)}) async-start(), calls=%async_computation.3 | async-start | bytes 1048576 | tf_op jit(solution)/shard_map/psum | solution.py:33
Sparse Core Ops, SparseCore 0:
  421.4 61.4 all-reduce.3
  1054.8 61.9 all-reduce.5
  1688.8 62.0 all-reduce.7
where the time goes:
time: 2040 us
  blocking collectives  1670 us (82%)
  waiting for transfers between devices  206 us (10%)
  local copies, waits for them, and re-layouts  56.6 us (3%)
  other arithmetic  46.2 us (2%)
  starting transfers between devices  32.7 us (2%)
    psum x3, blocking collectives, on_device(): lax.psum(jnp.dot(leader, local_block.T, precision=highest), 'rows')  841 us
    psum x3, blocking collectives, on_device(): lax.psum(jnp.dot(local_block, local_block.T, precision=highest), 'rows')  828 us
    psum x3, waiting for transfers between devices, spread(): return lax.psum(kept, axis)  186 us
  transfers between devices with their start and end apart: 8, of which 8 were waited for; matrix products, arithmetic and copies ran while one was open for 0% of the time, Pallas kernels for 0%

commit v1 on v0

v1 whole, which is shorter than its diff:
```python
import jax
import jax.numpy as jnp
import numpy as np
from jax import lax
from jax.experimental import pallas as pl
from jax.experimental.pallas import tpu as pltpu
from jax.sharding import Mesh, PartitionSpec as P

PI_BOND = -1.0
SIGMA_BOND = 0.178
DECAY_LENGTH = 0.319
LAYER_GAP = 2.36
SITE_MASS = 0.4
LAYER_BIAS = 0.25

BLOCK = 64
STEPS = 3
HEAD = BLOCK * STEPS
SLOTS = 16
REACH = 256
NV = 512
LOCAL = 256
WIDE = LOCAL + 2 * REACH
Y_SIZE = 4
F32 = jnp.float32
BF16 = jnp.bfloat16
HIGHEST = lax.Precision.HIGHEST
VMEM = pl.BlockSpec(memory_space=pltpu.VMEM)
PARAMS = pltpu.CompilerParams(vmem_limit_bytes=48 * 1024 * 1024)


def hop_rows(table):
    cosines = table[0:16]
    distances = table[16:32]
    offsets = table[32:48]
    counts = table[48:49]
    square = cosines * cosines
    bond = PI_BOND * jnp.exp(-(distances - 1.0) / DECAY_LENGTH) * (1.0 - square)
    bond = bond + SIGMA_BOND * jnp.exp(-(distances - LAYER_GAP) / DECAY_LENGTH) * square
    slot = lax.broadcasted_iota(jnp.int32, bond.shape, 0).astype(F32)
    hopping = jnp.where(slot < counts, bond, 0.0)
    onsite = SITE_MASS * (2.0 * table[49:50] - 1.0) + LAYER_BIAS * (2.0 * table[50:51] - 1.0)
    return hopping, offsets, onsite


def build_matrix(table, high_ref, low_ref):
    hopping, offsets, onsite = hop_rows(table)
    lane = lax.broadcasted_iota(jnp.int32, (1, 128), 1).astype(F32)
    row_index = lax.broadcasted_iota(jnp.int32, (16, 128), 0).astype(F32)
    for half in range(2):
        columns = slice(128 * half, 128 * half + 128)
        empty = 640 * (1 - half)
        high_ref[empty : empty + 128, columns] = jnp.zeros((128, 128), BF16)
        low_ref[empty : empty + 128, columns] = jnp.zeros((128, 128), BF16)
        home = lane + float(REACH)
        targets = [
            jnp.broadcast_to(offsets[k : k + 1, columns] + home, (16, 128)) for k in range(SLOTS)
        ]
        values = [jnp.broadcast_to(hopping[k : k + 1, columns], (16, 128)) for k in range(SLOTS)]
        homes = jnp.broadcast_to(home, (16, 128))
        own = jnp.broadcast_to(onsite[:, columns], (16, 128))

        def chunk(step, carry):
            base = step * 16
            rows = row_index + base.astype(F32)
            total = jnp.where(homes == rows, own, 0.0)
            for k in range(SLOTS):
                total = total + jnp.where(targets[k] == rows, values[k], 0.0)
            high = total.astype(BF16)
            low = (total - high.astype(F32)).astype(BF16)
            place = pl.ds(pl.multiple_of(base + 128 * half, 16), 16)
            high_ref[place, columns] = high
            low_ref[place, columns] = low
            return carry

        lax.fori_loop(0, 40, chunk, 0)


def own_matrix_kernel(table_ref, high_ref, low_ref):
    build_matrix(table_ref[...], high_ref, low_ref)


def split(value):
    high = value.astype(BF16)
    return high, (value - high.astype(F32)).astype(BF16)


def dot3(high, low, matrix_high, matrix_low):
    def dot(left, right):
        return jnp.dot(left, right, preferred_element_type=F32)

    return dot(high, matrix_high) + (dot(high, matrix_low) + dot(low, matrix_high))


def apply_kernel(
    left2_ref, left_ref, own_ref, right_ref, right2_ref, own_high_ref, own_low_ref,
    applied_ref, gram_ref, high_ref, low_ref, once_high_ref, once_low_ref, left_high_ref,
    left_low_ref, right_high_ref, right_low_ref,
):
    build_matrix(left_ref[NV:, :], left_high_ref, left_low_ref)
    build_matrix(right_ref[NV:, :], right_high_ref, right_low_ref)
    for place, ref in enumerate((left2_ref, left_ref, own_ref, right_ref, right2_ref)):
        columns = slice(LOCAL * place, LOCAL * place + LOCAL)
        high, low = split(ref[0:NV, :])
        high_ref[:, columns] = high
        low_ref[:, columns] = low
    matrices = (
        (left_high_ref, left_low_ref),
        (own_high_ref, own_low_ref),
        (right_high_ref, right_low_ref),
    )
    for place, (matrix_high, matrix_low) in enumerate(matrices):
        window = slice(LOCAL * place, LOCAL * place + WIDE)
        columns = slice(LOCAL * place, LOCAL * place + LOCAL)
        once = dot3(high_ref[:, window], low_ref[:, window], matrix_high[...], matrix_low[...])
        high, low = split(once)
        once_high_ref[:, columns] = high
        once_low_ref[:, columns] = low
    applied = dot3(once_high_ref[...], once_low_ref[...], own_high_ref[...], own_low_ref[...])
    applied_ref[...] = applied
    gram = lax.dot_general(
        applied[0:HEAD], applied, (((1,), (1,)), ((), ())), precision=HIGHEST,
        preferred_element_type=F32,
    )
    for part in range(NV // 128):
        gram_ref[part] = gram[:, 128 * part : 128 * part + 128]


def inverse_factor(pair):
    rows = lax.broadcasted_iota(jnp.int32, (BLOCK, 1), 0)
    work = pair
    scales = jnp.zeros((BLOCK, 1), F32)
    for j in range(BLOCK):
        row = work[j : j + 1, :]
        pivot = row[:, BLOCK + j : BLOCK + j + 1]
        scales = jnp.where(rows == j, lax.rsqrt(pivot), scales)
        column = jnp.where(rows > j, work[:, BLOCK + j : BLOCK + j + 1], 0.0)
        work = work - column * (row * (1.0 / pivot))
    return (work * scales)[:, 0:BLOCK]


def dot32(left, right, dims):
    return lax.dot_general(
        left, right, (dims, ((), ())), precision=HIGHEST, preferred_element_type=F32
    )


def finish_kernel(scale, gram_ref, applied_ref, basis_ref):
    gram = [
        jnp.concatenate(
            [gram_ref[part, BLOCK * s : BLOCK * s + BLOCK, :] for part in range(NV // 128)], axis=1
        )
        * scale
        for s in range(STEPS)
    ]
    lane = lax.broadcasted_iota(jnp.int32, (BLOCK, 128), 1)
    row = lax.broadcasted_iota(jnp.int32, (BLOCK, 128), 0)
    identity = jnp.where(lane == row, 1.0, 0.0).astype(F32)
    couplings = []
    inverses = []
    for s in range(STEPS):
        part = (BLOCK * s) // 128
        tile = gram[s][:, 128 * part : 128 * part + 128]
        if (BLOCK * s) % 128 == 0:
            tile = pltpu.roll(tile, BLOCK, axis=1)
        inverse = inverse_factor(jnp.where(lane < BLOCK, identity, tile))
        coupling = dot32(inverse, gram[s], ((1,), (0,)))
        for t in range(s + 1, STEPS):
            gram[t] = gram[t] - dot32(
                coupling[:, BLOCK * t : BLOCK * t + BLOCK], coupling, ((0,), (0,))
            )
        inverses.append(inverse)
        couplings.append(coupling)
    leaders = []
    for s in range(STEPS):
        block = applied_ref[BLOCK * s : BLOCK * s + BLOCK, :]
        for t in range(s):
            block = block - dot32(
                couplings[t][:, BLOCK * s : BLOCK * s + BLOCK], leaders[t], ((0,), (0,))
            )
        leader = dot32(inverses[s], block, ((1,), (0,)))
        leaders.append(leader)
        basis_ref[BLOCK * s : BLOCK * s + BLOCK, :] = leader
    stacked = jnp.concatenate([c[:, HEAD:] for c in couplings], axis=0)
    leading = jnp.concatenate(leaders, axis=0)
    basis_ref[HEAD:, :] = applied_ref[HEAD:, :] - dot32(stacked, leading, ((0,), (0,)))


def exchange(value, axes):
    return lax.all_to_all(value, axes, split_axis=0, concat_axis=0, tiled=True)


def on_device(vectors, offsets, counts, labels, cosines, distances):
    every = ("y", "z", "cols")
    plane = ("y", "cols")
    total = lax.axis_size(every)
    planes = lax.axis_size(plane)
    depth = lax.axis_size("z")

    def shift(value, step):
        return lax.ppermute(value, every, [(i, (i + step) % total) for i in range(total)])

    table = jnp.concatenate(
        [cosines, distances, offsets.astype(F32), counts.astype(F32)[None], labels.astype(F32),
         jnp.zeros((5, LOCAL), F32)], axis=0,
    )
    payload = jnp.concatenate([vectors, table], axis=0)
    left = shift(payload, 1)
    right = shift(payload, -1)
    left2 = shift(vectors, 2)
    right2 = shift(vectors, -2)
    matrix = jax.ShapeDtypeStruct((WIDE, LOCAL), BF16)
    own_high, own_low = pl.pallas_call(
        own_matrix_kernel, out_shape=(matrix, matrix), in_specs=[VMEM], out_specs=(VMEM, VMEM),
        compiler_params=PARAMS, name="own_matrix",
    )(table)
    wide = pltpu.VMEM((WIDE, LOCAL), BF16)
    applied, gram = pl.pallas_call(
        apply_kernel,
        out_shape=(
            jax.ShapeDtypeStruct((NV, LOCAL), F32),
            jax.ShapeDtypeStruct((NV // 128, HEAD, 128), F32),
        ),
        in_specs=[VMEM] * 7,
        out_specs=(VMEM, VMEM),
        scratch_shapes=[pltpu.VMEM((NV, 5 * LOCAL), BF16)] * 2
        + [pltpu.VMEM((NV, WIDE), BF16)] * 2 + [wide] * 4,
        compiler_params=PARAMS,
        name="apply_twice",
    )(left2, left, payload, right, right2, own_high, own_low)
    piece = (NV // 128) * HEAD // planes
    gram = gram.reshape(planes, piece, 128)
    gram = exchange(gram, plane).reshape(planes, piece, 128).sum(0)
    gram = exchange(jnp.broadcast_to(gram[None], (depth, piece, 128)), "z").sum(0)
    gram = exchange(jnp.broadcast_to(gram[None], (planes, piece, 128)), plane)
    gram = gram.reshape(NV // 128, HEAD, 128)
    scale = 1.0 / (LOCAL * total)
    basis = pl.pallas_call(
        lambda *refs: finish_kernel(scale, *refs),
        out_shape=jax.ShapeDtypeStruct((NV, LOCAL), F32),
        in_specs=[VMEM] * 2, out_specs=VMEM, compiler_params=PARAMS, name="finish",
    )(gram, applied)
    return lax.all_to_all(basis, "cols", split_axis=0, concat_axis=1, tiled=True)


def solution(mesh):
    rows = mesh.shape["rows"]
    cols = mesh.shape["cols"]
    cube = Mesh(mesh.devices.reshape(Y_SIZE, rows // Y_SIZE, cols), ("y", "z", "cols"))
    every = ("y", "z", "cols")
    placed = (P(None, every), P(None, every), P(every), P(None, every), P(None, every), P(None, every))
    return jax.shard_map(
        on_device, mesh=cube, in_specs=placed, out_specs=P("cols", ("y", "z")), check_vma=False
    )
```

time: 2040 us -> 138 us (0.07)
  the two profiles are of different devices: /device:TPU:2 before, /device:TPU:1 now
where the time goes in v1:
time: 138 us
  blocking collectives  61 us (44%)
  Pallas kernels  31.3 us (23%)
  starting transfers between devices  29.5 us (21%)
  waiting for transfers between devices  12.3 us (9%)
  local copies, waits for them, and re-layouts  2.08 us (2%)
  other arithmetic  1.49 us (1%)
    all_to_all x3, blocking collectives, exchange(): return lax.all_to_all(value, axes, split_axis=0, concat_axis=0, tiled=True)  48.9 us
    ppermute x4, starting transfers between devices, shift(): lax.ppermute(value, every, [(i, (i + step) % total) for i in range(total)])  29.5 us
    pallas_call x1, Pallas kernels, on_device(): pl.pallas_call(lambda *refs: finish_kernel(scale, *refs), out_shape=jax.S...  20.5 us
    ppermute x4, waiting for transfers between devices, shift(): lax.ppermute(value, every, [(i, (i + step) % total) for i in range(total)])  12.3 us
    all_to_all x1, blocking collectives, on_device(): lax.all_to_all(basis, 'cols', split_axis=0, concat_axis=1, tiled=True)  12.1 us
    pallas_call x1, Pallas kernels, on_device(): pl.pallas_call(apply_kernel, out_shape=(jax.ShapeDtypeStruct((NV, LOCAL),...  8.65 us
  transfers between devices with their start and end apart: 4, of which 1 were waited for; matrix products, arithmetic and copies ran while one was open for 0% of the time, Pallas kernels for 2%

profile of v1, /device:TPU:1, one launch (start us, length us, event | category | flops | bytes accessed | tf_op | source)
XLA Modules:
  0.0 137.8 jit_solution(6560848438911034917)
XLA Ops:
  0.0 0.0 copy-start.3
  0.0 0.7 convert_element_type.10
  0.7 0.0 copy-done.3
  0.7 0.0 copy-start.1
  0.7 0.0 copy-start.2
  0.7 0.7 convert_element_type.9
  1.5 0.0 copy-done.1
  1.5 0.0 copy-done.2
  1.5 0.0 copy-start
  1.5 1.1 concatenate.7.own_ref
  2.6 8.8 %collective-permute-start.2 = (f32[568,256]{1,0:T(8,128)S(1)}, f32[568,256]{1,0:T(8,128)S(1)}, u32[]{:S(2)}, u32[]{:S(2)}) collective-permute-start(f32[568,256]{1,0:T(8,128)S(1)} %concatenate.7.own_ref), channel_id=1, source_target_pairs={{0,511},{1,0},{2,1},{3,2},{4,3},{5,4},{6,5},{7,6},{8,7},{9,8},{10,... | collective-permute-start | bytes 1744904 | tf_op jit(solution)/shard_map/ppermute | solution.py:201
  11.4 1.9 %collective-permute-start.1 = (f32[568,256]{1,0:T(8,128)S(1)}, f32[568,256]{1,0:T(8,128)S(1)}, u32[]{:S(2)}, u32[]{:S(2)}) collective-permute-start(f32[568,256]{1,0:T(8,128)S(1)} %concatenate.7.own_ref), channel_id=1, source_target_pairs={{0,1},{1,2},{2,3},{3,4},{4,5},{5,6},{6,7},{7,8},{8,9},{9,10},{10,1... | collective-permute-start | bytes 1744904 | tf_op jit(solution)/shard_map/ppermute | solution.py:201
  13.3 0.0 copy-done
  13.4 1.9 %collective-permute-start = (f32[512,256]{1,0:T(8,128)S(1)}, f32[512,256]{1,0:T(8,128)S(1)}, u32[]{:S(2)}, u32[]{:S(2)}) collective-permute-start(f32[512,256]{1,0:T(8,128)S(1)} %copy-done), channel_id=1, source_target_pairs={{0,2},{1,3},{2,4},{3,5},{4,6},{5,7},{6,8},{7,9},{8,10},{9,11},{10,... | collective-permute-start | bytes 1572872 | tf_op jit(solution)/shard_map/ppermute | solution.py:201
  15.3 16.9 %collective-permute-start.3 = (f32[512,256]{1,0:T(8,128)S(1)}, f32[512,256]{1,0:T(8,128)S(1)}, u32[]{:S(2)}, u32[]{:S(2)}) collective-permute-start(f32[512,256]{1,0:T(8,128)S(1)} %copy-done), channel_id=1, source_target_pairs={{0,510},{1,511},{2,0},{3,1},{4,2},{5,3},{6,4},{7,5},{8,6},{9,7},{1... | collective-permute-start | bytes 1572872 | tf_op jit(solution)/shard_map/ppermute | solution.py:201
  32.2 2.2 %own_matrix.1 = (bf16[768,256]{1,0:T(8,128)(2,1)S(1)}, bf16[768,256]{1,0:T(8,128)(2,1)S(1)}) custom-call(f32[56,256]{1,0:T(8,128)S(1)} %concatenate.8.table_ref), custom_call_target="tpu_custom_call" | custom-call | tf_op jit(solution)/shard_map/own_matrix/pallas_call | solution.py:213
  34.4 12.3 %collective-permute-done.left2_ref = f32[512,256]{1,0:T(8,128)S(1)} collective-permute-done((f32[512,256]{1,0:T(8,128)S(1)}, f32[512,256]{1,0:T(8,128)S(1)}, u32[]{:S(2)}, u32[]{:S(2)}) %collective-permute-start) | collective-permute-done | bytes 524320 | tf_op jit(solution)/shard_map/ppermute | solution.py:201
  46.7 0.0 collective-permute-done.3.right2_ref
  46.7 0.0 collective-permute-done.2.right_ref
  46.7 0.0 collective-permute-done.1.left_ref
  46.7 8.6 %apply_twice.1 = (f32[512,256]{1,0:T(8,128)S(1)}, f32[4,192,128]{2,1,0:T(8,128)S(1)}) custom-call(f32[512,256]{1,0:T(8,128)S(1)} %collective-permute-done.left2_ref, f32[568,256]{1,0:T(8,128)S(1)} %collective-permute-done.1.left_ref, f32[568,256]{1,0:T(8,128)S(1)} %concatenate.7.own_ref, f32[568,256]{1,0:T(8,128)S(1)} %collective-permute-done.2.right_ref, ...), custom_call_target="tpu_custom_call" | custom-call | tf_op jit(solution)/shard_map/apply_twice/pallas_call | solution.py:218
  55.4 11.9 %all_to_all.34 = f32[32,24,128]{2,1,0:T(8,128)S(1)} all-to-all(f32[32,24,128]{2,1,0:T(8,128)S(1)} %bitcast.9), channel_id=1, replica_groups=mesh['y'=4,'z'=16,'cols'=8] {'y','cols'}, dimensions={0} | all-to-all | bytes 786432 | tf_op jit(solution)/shard_map/all_to_all | solution.py:190
  67.4 19.3 %all_to_all.35 = f32[16,24,128]{2,1,0:T(8,128)S(1)} all-to-all(f32[16,24,128]{2,1,0:T(8,128)S(1)} %broadcast_in_dim.20), channel_id=1, replica_groups=mesh['y'=4,'z'=16,'cols'=8] {'z'}, dimensions={0} | all-to-all | bytes 393216 | tf_op jit(solution)/shard_map/all_to_all | solution.py:190
  86.7 17.6 %all_to_all.36 = f32[32,24,128]{2,1,0:T(8,128)S(1)} all-to-all(f32[32,24,128]{2,1,0:T(8,128)S(1)} %broadcast_in_dim.21), channel_id=1, replica_groups=mesh['y'=4,'z'=16,'cols'=8] {'y','cols'}, dimensions={0} | all-to-all | bytes 786432 | tf_op jit(solution)/shard_map/all_to_all | solution.py:190
  104.4 20.5 %finish.1 = f32[512,256]{1,0:T(8,128)S(1)} custom-call(f32[4,192,128]{2,1,0:T(8,128)S(1)} %bitcast.8, f32[512,256]{1,0:T(8,128)S(1)} %get-tuple-element.12.refs_1_), custom_call_target="tpu_custom_call" | custom-call | tf_op jit(solution)/shard_map/finish/pallas_call | solution.py:238
  124.9 12.1 %all_to_all.37 = f32[8,64,256]{2,1,0:T(8,128)S(1)} all-to-all(f32[8,64,256]{2,1,0:T(8,128)S(1)} %bitcast.7), channel_id=1, replica_groups=mesh['y'=4,'z'=16,'cols'=8] {'cols'}, dimensions={0} | all-to-all | bytes 1048576 | tf_op jit(solution)/shard_map/all_to_all | solution.py:243
  137.0 0.8 copy.9
  (7 shorter events, 0.1 us)
Async XLA Ops:
  0.0 0.7 copy-start.3
  0.7 0.8 copy-start.1
  0.7 0.8 copy-start.2
  1.5 11.9 %copy-start = (f32[512,256]{1,0:T(8,128)S(1)}, f32[512,256]{1,0:T(8,128)}, u32[]{:S(2)}) copy-start(f32[512,256]{1,0:T(8,128)} %param.6) | copy-start | bytes 1572868
  2.6 44.1 %collective-permute-start.2 = (f32[568,256]{1,0:T(8,128)S(1)}, f32[568,256]{1,0:T(8,128)S(1)}, u32[]{:S(2)}, u32[]{:S(2)}) collective-permute-start(f32[568,256]{1,0:T(8,128)S(1)} %concatenate.7.own_ref), channel_id=1, source_target_pairs={{0,511},{1,0},{2,1},{3,2},{4,3},{5,4},{6,5},{7,6},{8,7},{9,8},{10,... | collective-permute-start | bytes 1744904 | tf_op jit(solution)/shard_map/ppermute | solution.py:201
  11.4 35.3 %collective-permute-start.1 = (f32[568,256]{1,0:T(8,128)S(1)}, f32[568,256]{1,0:T(8,128)S(1)}, u32[]{:S(2)}, u32[]{:S(2)}) collective-permute-start(f32[568,256]{1,0:T(8,128)S(1)} %concatenate.7.own_ref), channel_id=1, source_target_pairs={{0,1},{1,2},{2,3},{3,4},{4,5},{5,6},{6,7},{7,8},{8,9},{9,10},{10,1... | collective-permute-start | bytes 1744904 | tf_op jit(solution)/shard_map/ppermute | solution.py:201
  13.4 33.4 %collective-permute-start = (f32[512,256]{1,0:T(8,128)S(1)}, f32[512,256]{1,0:T(8,128)S(1)}, u32[]{:S(2)}, u32[]{:S(2)}) collective-permute-start(f32[512,256]{1,0:T(8,128)S(1)} %copy-done), channel_id=1, source_target_pairs={{0,2},{1,3},{2,4},{3,5},{4,6},{5,7},{6,8},{7,9},{8,10},{9,11},{10,... | collective-permute-start | bytes 1572872 | tf_op jit(solution)/shard_map/ppermute | solution.py:201
  15.3 31.4 %collective-permute-start.3 = (f32[512,256]{1,0:T(8,128)S(1)}, f32[512,256]{1,0:T(8,128)S(1)}, u32[]{:S(2)}, u32[]{:S(2)}) collective-permute-start(f32[512,256]{1,0:T(8,128)S(1)} %copy-done), channel_id=1, source_target_pairs={{0,510},{1,511},{2,0},{3,1},{4,2},{5,3},{6,4},{7,5},{8,6},{9,7},{1... | collective-permute-start | bytes 1572872 | tf_op jit(solution)/shard_map/ppermute | solution.py:201

commit v2 on v1

--- a/solution.py
+++ b/solution.py
@@ -126,17 +126,32 @@
         gram_ref[part] = gram[:, 128 * part : 128 * part + 128]
 
 
+def spread(value):
+    return jnp.broadcast_to(value, (8, 128))
+
+
 def inverse_factor(pair):
-    rows = lax.broadcasted_iota(jnp.int32, (BLOCK, 1), 0)
-    work = pair
-    scales = jnp.zeros((BLOCK, 1), F32)
-    for j in range(BLOCK):
-        row = work[j : j + 1, :]
-        pivot = row[:, BLOCK + j : BLOCK + j + 1]
-        scales = jnp.where(rows == j, lax.rsqrt(pivot), scales)
-        column = jnp.where(rows > j, work[:, BLOCK + j : BLOCK + j + 1], 0.0)
-        work = work - column * (row * (1.0 / pivot))
-    return (work * scales)[:, 0:BLOCK]
+    rows = [pair[8 * i : 8 * i + 8] for i in range(BLOCK // 8)]
+    sublane = lax.broadcasted_iota(jnp.int32, (8, 128), 0)
+    for p in range(BLOCK // 8):
+        start = BLOCK + 8 * p
+        columns = [
+            [spread(rows[i][:, start + b : start + b + 1]) for b in range(8)]
+            for i in range(p, BLOCK // 8)
+        ]
+        for j in range(8):
+            inverse = lax.rsqrt(spread(columns[0][j][j : j + 1]))
+            pivot_row = spread(rows[p][j : j + 1]) * inverse
+            heads = [spread(columns[0][b][j : j + 1]) * inverse for b in range(j + 1, 8)]
+            for i in range(p, BLOCK // 8):
+                factor = columns[i - p][j] * inverse
+                if i == p:
+                    factor = jnp.where(sublane > j, factor, 0.0)
+                rows[i] = rows[i] - factor * pivot_row
+                for b in range(j + 1, 8):
+                    columns[i - p][b] = columns[i - p][b] - factor * heads[b - j - 1]
+            rows[p] = jnp.where(sublane == j, pivot_row, rows[p])
+    return jnp.concatenate(rows, axis=0)[:, 0:BLOCK]
 
 
 def dot32(left, right, dims):

time: 138 us -> 126 us (0.913)
  Pallas kernels: 31.3 us -> 19 us
    pallas_call x1, Pallas kernels: 20.5 us -> 8.15 us  [on_device(): pl.pallas_call(lambda *refs: finish_kernel(scale, *refs), out_shape=jax.S...]
where the time goes in v2:
time: 126 us; the launch traced here: 125 us
  blocking collectives  61 us (48%)
  starting transfers between devices  29.5 us (23%)
  Pallas kernels  19 us (15%)
  waiting for transfers between devices  12.3 us (10%)
  local copies, waits for them, and re-layouts  2.08 us (2%)
  other arithmetic  1.49 us (1%)
    all_to_all x3, blocking collectives, exchange(): return lax.all_to_all(value, axes, split_axis=0, concat_axis=0, tiled=True)  48.9 us
    ppermute x4, starting transfers between devices, shift(): lax.ppermute(value, every, [(i, (i + step) % total) for i in range(total)])  29.5 us
    ppermute x4, waiting for transfers between devices, shift(): lax.ppermute(value, every, [(i, (i + step) % total) for i in range(total)])  12.3 us
    all_to_all x1, blocking collectives, on_device(): lax.all_to_all(basis, 'cols', split_axis=0, concat_axis=1, tiled=True)  12.1 us
    pallas_call x1, Pallas kernels, on_device(): pl.pallas_call(apply_kernel, out_shape=(jax.ShapeDtypeStruct((NV, LOCAL),...  8.65 us
    pallas_call x1, Pallas kernels, on_device(): pl.pallas_call(lambda *refs: finish_kernel(scale, *refs), out_shape=jax.S...  8.15 us
  transfers between devices with their start and end apart: 4, of which 1 were waited for; matrix products, arithmetic and copies ran while one was open for 0% of the time, Pallas kernels for 2%

profile of v2, /device:TPU:1, one launch (start us, length us, event | category | flops | bytes accessed | tf_op | source)
XLA Modules:
  0.0 125.5 jit_solution(8742786515712139380)
XLA Ops:
  0.0 0.0 copy-start.3
  0.0 0.7 convert_element_type.10
  0.7 0.0 copy-done.3
  0.7 0.0 copy-start.1
  0.7 0.0 copy-start.2
  0.7 0.7 convert_element_type.9
  1.5 0.0 copy-done.1
  1.5 0.0 copy-done.2
  1.5 0.0 copy-start
  1.5 1.1 concatenate.7.own_ref
  2.6 8.8 %collective-permute-start.2 = (f32[568,256]{1,0:T(8,128)S(1)}, f32[568,256]{1,0:T(8,128)S(1)}, u32[]{:S(2)}, u32[]{:S(2)}) collective-permute-start(f32[568,256]{1,0:T(8,128)S(1)} %concatenate.7.own_ref), channel_id=1, source_target_pairs={{0,511},{1,0},{2,1},{3,2},{4,3},{5,4},{6,5},{7,6},{8,7},{9,8},{10,... | collective-permute-start | bytes 1744904 | tf_op jit(solution)/shard_map/ppermute | solution.py:216
  11.4 1.9 %collective-permute-start.1 = (f32[568,256]{1,0:T(8,128)S(1)}, f32[568,256]{1,0:T(8,128)S(1)}, u32[]{:S(2)}, u32[]{:S(2)}) collective-permute-start(f32[568,256]{1,0:T(8,128)S(1)} %concatenate.7.own_ref), channel_id=1, source_target_pairs={{0,1},{1,2},{2,3},{3,4},{4,5},{5,6},{6,7},{7,8},{8,9},{9,10},{10,1... | collective-permute-start | bytes 1744904 | tf_op jit(solution)/shard_map/ppermute | solution.py:216
  13.3 0.0 copy-done
  13.4 1.9 %collective-permute-start = (f32[512,256]{1,0:T(8,128)S(1)}, f32[512,256]{1,0:T(8,128)S(1)}, u32[]{:S(2)}, u32[]{:S(2)}) collective-permute-start(f32[512,256]{1,0:T(8,128)S(1)} %copy-done), channel_id=1, source_target_pairs={{0,2},{1,3},{2,4},{3,5},{4,6},{5,7},{6,8},{7,9},{8,10},{9,11},{10,... | collective-permute-start | bytes 1572872 | tf_op jit(solution)/shard_map/ppermute | solution.py:216
  15.3 16.9 %collective-permute-start.3 = (f32[512,256]{1,0:T(8,128)S(1)}, f32[512,256]{1,0:T(8,128)S(1)}, u32[]{:S(2)}, u32[]{:S(2)}) collective-permute-start(f32[512,256]{1,0:T(8,128)S(1)} %copy-done), channel_id=1, source_target_pairs={{0,510},{1,511},{2,0},{3,1},{4,2},{5,3},{6,4},{7,5},{8,6},{9,7},{1... | collective-permute-start | bytes 1572872 | tf_op jit(solution)/shard_map/ppermute | solution.py:216
  32.2 2.2 %own_matrix.1 = (bf16[768,256]{1,0:T(8,128)(2,1)S(1)}, bf16[768,256]{1,0:T(8,128)(2,1)S(1)}) custom-call(f32[56,256]{1,0:T(8,128)S(1)} %concatenate.8.table_ref), custom_call_target="tpu_custom_call" | custom-call | tf_op jit(solution)/shard_map/own_matrix/pallas_call | solution.py:228
  34.4 12.3 %collective-permute-done.left2_ref = f32[512,256]{1,0:T(8,128)S(1)} collective-permute-done((f32[512,256]{1,0:T(8,128)S(1)}, f32[512,256]{1,0:T(8,128)S(1)}, u32[]{:S(2)}, u32[]{:S(2)}) %collective-permute-start) | collective-permute-done | bytes 524320 | tf_op jit(solution)/shard_map/ppermute | solution.py:216
  46.7 0.0 collective-permute-done.3.right2_ref
  46.7 0.0 collective-permute-done.2.right_ref
  46.7 0.0 collective-permute-done.1.left_ref
  46.7 8.6 %apply_twice.1 = (f32[512,256]{1,0:T(8,128)S(1)}, f32[4,192,128]{2,1,0:T(8,128)S(1)}) custom-call(f32[512,256]{1,0:T(8,128)S(1)} %collective-permute-done.left2_ref, f32[568,256]{1,0:T(8,128)S(1)} %collective-permute-done.1.left_ref, f32[568,256]{1,0:T(8,128)S(1)} %concatenate.7.own_ref, f32[568,256]{1,0:T(8,128)S(1)} %collective-permute-done.2.right_ref, ...), custom_call_target="tpu_custom_call" | custom-call | tf_op jit(solution)/shard_map/apply_twice/pallas_call | solution.py:233
  55.4 11.9 %all_to_all.34 = f32[32,24,128]{2,1,0:T(8,128)S(1)} all-to-all(f32[32,24,128]{2,1,0:T(8,128)S(1)} %bitcast.9), channel_id=1, replica_groups=mesh['y'=4,'z'=16,'cols'=8] {'y','cols'}, dimensions={0} | all-to-all | bytes 786432 | tf_op jit(solution)/shard_map/all_to_all | solution.py:205
  67.4 19.3 %all_to_all.35 = f32[16,24,128]{2,1,0:T(8,128)S(1)} all-to-all(f32[16,24,128]{2,1,0:T(8,128)S(1)} %broadcast_in_dim.20), channel_id=1, replica_groups=mesh['y'=4,'z'=16,'cols'=8] {'z'}, dimensions={0} | all-to-all | bytes 393216 | tf_op jit(solution)/shard_map/all_to_all | solution.py:205
  86.7 17.6 %all_to_all.36 = f32[32,24,128]{2,1,0:T(8,128)S(1)} all-to-all(f32[32,24,128]{2,1,0:T(8,128)S(1)} %broadcast_in_dim.21), channel_id=1, replica_groups=mesh['y'=4,'z'=16,'cols'=8] {'y','cols'}, dimensions={0} | all-to-all | bytes 786432 | tf_op jit(solution)/shard_map/all_to_all | solution.py:205
  104.4 8.1 %finish.1 = f32[512,256]{1,0:T(8,128)S(1)} custom-call(f32[4,192,128]{2,1,0:T(8,128)S(1)} %bitcast.8, f32[512,256]{1,0:T(8,128)S(1)} %get-tuple-element.12.refs_1_), custom_call_target="tpu_custom_call" | custom-call | tf_op jit(solution)/shard_map/finish/pallas_call | solution.py:253
  112.5 12.1 %all_to_all.37 = f32[8,64,256]{2,1,0:T(8,128)S(1)} all-to-all(f32[8,64,256]{2,1,0:T(8,128)S(1)} %bitcast.7), channel_id=1, replica_groups=mesh['y'=4,'z'=16,'cols'=8] {'cols'}, dimensions={0} | all-to-all | bytes 1048576 | tf_op jit(solution)/shard_map/all_to_all | solution.py:258
  124.7 0.8 copy.9
  (7 shorter events, 0.1 us)
Async XLA Ops:
  0.0 0.7 copy-start.3
  0.7 0.8 copy-start.1
  0.7 0.8 copy-start.2
  1.5 11.9 %copy-start = (f32[512,256]{1,0:T(8,128)S(1)}, f32[512,256]{1,0:T(8,128)}, u32[]{:S(2)}) copy-start(f32[512,256]{1,0:T(8,128)} %param.6) | copy-start | bytes 1572868
  2.6 44.1 %collective-permute-start.2 = (f32[568,256]{1,0:T(8,128)S(1)}, f32[568,256]{1,0:T(8,128)S(1)}, u32[]{:S(2)}, u32[]{:S(2)}) collective-permute-start(f32[568,256]{1,0:T(8,128)S(1)} %concatenate.7.own_ref), channel_id=1, source_target_pairs={{0,511},{1,0},{2,1},{3,2},{4,3},{5,4},{6,5},{7,6},{8,7},{9,8},{10,... | collective-permute-start | bytes 1744904 | tf_op jit(solution)/shard_map/ppermute | solution.py:216
  11.4 35.3 %collective-permute-start.1 = (f32[568,256]{1,0:T(8,128)S(1)}, f32[568,256]{1,0:T(8,128)S(1)}, u32[]{:S(2)}, u32[]{:S(2)}) collective-permute-start(f32[568,256]{1,0:T(8,128)S(1)} %concatenate.7.own_ref), channel_id=1, source_target_pairs={{0,1},{1,2},{2,3},{3,4},{4,5},{5,6},{6,7},{7,8},{8,9},{9,10},{10,1... | collective-permute-start | bytes 1744904 | tf_op jit(solution)/shard_map/ppermute | solution.py:216
  13.4 33.4 %collective-permute-start = (f32[512,256]{1,0:T(8,128)S(1)}, f32[512,256]{1,0:T(8,128)S(1)}, u32[]{:S(2)}, u32[]{:S(2)}) collective-permute-start(f32[512,256]{1,0:T(8,128)S(1)} %copy-done), channel_id=1, source_target_pairs={{0,2},{1,3},{2,4},{3,5},{4,6},{5,7},{6,8},{7,9},{8,10},{9,11},{10,... | collective-permute-start | bytes 1572872 | tf_op jit(solution)/shard_map/ppermute | solution.py:216
  15.3 31.4 %collective-permute-start.3 = (f32[512,256]{1,0:T(8,128)S(1)}, f32[512,256]{1,0:T(8,128)S(1)}, u32[]{:S(2)}, u32[]{:S(2)}) collective-permute-start(f32[512,256]{1,0:T(8,128)S(1)} %copy-done), channel_id=1, source_target_pairs={{0,510},{1,511},{2,0},{3,1},{4,2},{5,3},{6,4},{7,5},{8,6},{9,7},{1... | collective-permute-start | bytes 1572872 | tf_op jit(solution)/shard_map/ppermute | solution.py:216

commit v3 on v2

v3 whole, which is shorter than its diff:
```python
import jax
import jax.numpy as jnp
from jax import lax
from jax.experimental import pallas as pl
from jax.experimental.pallas import tpu as pltpu
from jax.sharding import Mesh, PartitionSpec as P

PI_BOND = -1.0
SIGMA_BOND = 0.178
DECAY_LENGTH = 0.319
LAYER_GAP = 2.36
SITE_MASS = 0.4
LAYER_BIAS = 0.25

BLOCK = 64
STEPS = 3
HEAD = BLOCK * STEPS
SLOTS = 16
REACH = 256
NV = 512
LOCAL = 256
WIDE = LOCAL + 2 * REACH
Y_SIZE = 4
CORES = 2
OWN = NV // CORES
TABLE = 40
CHIP = CORES * LOCAL
F32 = jnp.float32
BF16 = jnp.bfloat16
HIGHEST = lax.Precision.HIGHEST
VMEM = pl.BlockSpec(memory_space=pltpu.VMEM)
PARAMS = pltpu.CompilerParams(vmem_limit_bytes=48 * 1024 * 1024)


def pack_kernel(vectors_ref, cosines_ref, distances_ref, offsets_ref, counts_ref, labels_ref, out_ref):
    square = cosines_ref[...] * cosines_ref[...]
    distances = distances_ref[...]
    bond = PI_BOND * jnp.exp(-(distances - 1.0) / DECAY_LENGTH) * (1.0 - square)
    bond = bond + SIGMA_BOND * jnp.exp(-(distances - LAYER_GAP) / DECAY_LENGTH) * square
    slot = lax.broadcasted_iota(jnp.int32, bond.shape, 0)
    hopping = jnp.where(slot < counts_ref[...], bond, 0.0)
    offsets = offsets_ref[...].astype(F32)
    merged = jnp.zeros_like(hopping)
    for k in range(SLOTS):
        merged = merged + jnp.where(offsets == offsets[k : k + 1], hopping[k : k + 1], 0.0)
    labels = labels_ref[...].astype(F32)
    onsite = SITE_MASS * (2.0 * labels[0:1] - 1.0) + LAYER_BIAS * (2.0 * labels[1:2] - 1.0)
    for core in range(CORES):
        for p in range(OWN // BLOCK):
            source = BLOCK * (core + CORES * p)
            out_ref[core, BLOCK * p : BLOCK * p + BLOCK, :] = vectors_ref[source : source + BLOCK, :]
        out_ref[core, OWN : OWN + 16, :] = merged
        out_ref[core, OWN + 16 : OWN + 32, :] = offsets
        out_ref[core, OWN + 32 : OWN + 40, :] = jnp.broadcast_to(onsite, (8, LOCAL))


def build_matrix(table, high_ref, low_ref):
    hopping, offsets, onsite = table[0:16], table[16:32], table[32:33]
    lane = lax.broadcasted_iota(jnp.int32, (1, 128), 1).astype(F32)
    row_index = lax.broadcasted_iota(jnp.int32, (32, 128), 0).astype(F32)
    for half in range(2):
        columns = slice(128 * half, 128 * half + 128)
        empty = 640 * (1 - half)
        high_ref[empty : empty + 128, columns] = jnp.zeros((128, 128), BF16)
        low_ref[empty : empty + 128, columns] = jnp.zeros((128, 128), BF16)
        home = lane + float(REACH)
        targets = [
            jnp.broadcast_to(offsets[k : k + 1, columns] + home, (32, 128)) for k in range(SLOTS)
        ]
        values = [jnp.broadcast_to(hopping[k : k + 1, columns], (32, 128)) for k in range(SLOTS)]
        homes = jnp.broadcast_to(home, (32, 128))
        own = jnp.broadcast_to(onsite[:, columns], (32, 128))

        def chunk(step, carry):
            base = step * 32
            rows = row_index + base.astype(F32)
            total = jnp.where(homes == rows, own, 0.0)
            for k in range(SLOTS):
                total = jnp.where(targets[k] == rows, values[k], total)
            high = total.astype(BF16)
            low = (total - high.astype(F32)).astype(BF16)
            place = pl.ds(pl.multiple_of(base + 128 * half, 32), 32)
            high_ref[place, columns] = high
            low_ref[place, columns] = low
            return carry

        lax.fori_loop(0, 20, chunk, 0)


def own_matrix_kernel(slab_ref, *refs):
    for core in range(CORES):
        build_matrix(slab_ref[core, OWN:, :], refs[2 * core], refs[2 * core + 1])


def split(value):
    high = value.astype(BF16)
    return high, (value - high.astype(F32)).astype(BF16)


def dot3(high, low, matrix_high, matrix_low):
    def dot(left, right):
        return jnp.dot(left, right, preferred_element_type=F32)

    return dot(high, matrix_high) + (dot(high, matrix_low) + dot(low, matrix_high))


def apply_kernel(
    left_ref, own_ref, right_ref, first_high_ref, first_low_ref, second_high_ref, second_low_ref,
    applied_ref, head_ref, high_ref, low_ref, once_high_ref, once_low_ref,
    left_high_ref, left_low_ref, right_high_ref, right_low_ref,
):
    build_matrix(left_ref[1, OWN:, :], left_high_ref, left_low_ref)
    build_matrix(right_ref[0, OWN:, :], right_high_ref, right_low_ref)
    sources = [(ref, core) for ref in (left_ref, own_ref, right_ref) for core in range(CORES)]
    for place, (ref, core) in enumerate(sources):
        columns = slice(LOCAL * place, LOCAL * place + LOCAL)
        high, low = split(ref[core, 0:OWN, :])
        high_ref[:, columns] = high
        low_ref[:, columns] = low
    matrices = (
        (left_high_ref, left_low_ref),
        (first_high_ref, first_low_ref),
        (second_high_ref, second_low_ref),
        (right_high_ref, right_low_ref),
    )
    for place, (matrix_high, matrix_low) in enumerate(matrices):
        window = slice(LOCAL * place, LOCAL * place + WIDE)
        columns = slice(LOCAL * place, LOCAL * place + LOCAL)
        once = dot3(high_ref[:, window], low_ref[:, window], matrix_high[...], matrix_low[...])
        high, low = split(once)
        once_high_ref[:, columns] = high
        once_low_ref[:, columns] = low
    for place, (matrix_high, matrix_low) in enumerate(matrices[1:3]):
        window = slice(LOCAL * place, LOCAL * place + WIDE)
        columns = slice(LOCAL * place, LOCAL * place + LOCAL)
        twice = dot3(
            once_high_ref[:, window], once_low_ref[:, window], matrix_high[...], matrix_low[...]
        )
        applied_ref[:, columns] = twice
        for core in range(CORES):
            head_ref[core, :, columns] = twice[0 : 2 * BLOCK]


def head_blocks(head_ref):
    return head_ref[0, 0:BLOCK, :], head_ref[1, 0:BLOCK, :], head_ref[0, BLOCK:, :]


def gram_kernel(head_ref, applied_ref, gram_ref):
    head = jnp.concatenate(head_blocks(head_ref), axis=0)
    gram = dot32(head, applied_ref[...], ((1,), (1,)))
    for part in range(OWN // 128):
        gram_ref[part] = gram[:, 128 * part : 128 * part + 128]


def spread(value):
    return jnp.broadcast_to(value, (8, 128))


def inverse_factor(pair):
    rows = [pair[8 * i : 8 * i + 8] for i in range(BLOCK // 8)]
    sublane = lax.broadcasted_iota(jnp.int32, (8, 128), 0)
    for p in range(BLOCK // 8):
        start = BLOCK + 8 * p
        columns = [
            [spread(rows[i][:, start + b : start + b + 1]) for b in range(8)]
            for i in range(p, BLOCK // 8)
        ]
        for j in range(8):
            inverse = lax.rsqrt(spread(columns[0][j][j : j + 1]))
            pivot_row = spread(rows[p][j : j + 1]) * inverse
            heads = [spread(columns[0][b][j : j + 1]) * inverse for b in range(j + 1, 8)]
            for i in range(p, BLOCK // 8):
                factor = columns[i - p][j] * inverse
                if i == p:
                    factor = jnp.where(sublane > j, factor, 0.0)
                rows[i] = rows[i] - factor * pivot_row
                for b in range(j + 1, 8):
                    columns[i - p][b] = columns[i - p][b] - factor * heads[b - j - 1]
            rows[p] = jnp.where(sublane == j, pivot_row, rows[p])
    return jnp.concatenate(rows, axis=0)[:, 0:BLOCK]


def dot32(left, right, dims):
    return lax.dot_general(
        left, right, (dims, ((), ())), precision=HIGHEST, preferred_element_type=F32
    )


def finish_kernel(scale, core_ref, gram_ref, head_ref, applied_ref, basis_ref):
    second = core_ref[0] == 1
    tiles = gram_ref.shape[0] // 2

    def columns_of(part, core):
        return jnp.concatenate([gram_ref[part * tiles + m, core] for m in range(tiles)], axis=0)

    rest = jnp.where(second, columns_of(1, 1), columns_of(1, 0))
    full = jnp.concatenate([columns_of(0, 0), columns_of(0, 1), rest], axis=1) * scale
    gram = [full[BLOCK * s : BLOCK * s + BLOCK] for s in range(STEPS)]
    places = (0, 2 * BLOCK, BLOCK)
    lane = lax.broadcasted_iota(jnp.int32, (BLOCK, 128), 1)
    row = lax.broadcasted_iota(jnp.int32, (BLOCK, 128), 0)
    identity = jnp.where(lane == row, 1.0, 0.0).astype(F32)
    couplings = []
    inverses = []
    for s in range(STEPS):
        part = places[s] // 128
        tile = gram[s][:, 128 * part : 128 * part + 128]
        if places[s] % 128 == 0:
            tile = pltpu.roll(tile, BLOCK, axis=1)
        inverse = inverse_factor(jnp.where(lane < BLOCK, identity, tile))
        coupling = dot32(inverse, gram[s], ((1,), (0,)))
        for t in range(s + 1, STEPS):
            gram[t] = gram[t] - dot32(
                coupling[:, places[t] : places[t] + BLOCK], coupling, ((0,), (0,))
            )
        inverses.append(inverse)
        couplings.append(coupling)
    leaders = []
    heads = head_blocks(head_ref)
    for s in range(STEPS):
        block = heads[s]
        for t in range(s):
            block = block - dot32(
                couplings[t][:, places[s] : places[s] + BLOCK], leaders[t], ((0,), (0,))
            )
        leaders.append(dot32(inverses[s], block, ((1,), (0,))))
    stacked = jnp.concatenate([c[:, HEAD:] for c in couplings], axis=0)
    leading = jnp.concatenate(leaders, axis=0)
    later = applied_ref[BLOCK:, :] - dot32(stacked, leading, ((0,), (0,)))
    basis_ref[0:BLOCK, :] = jnp.where(second, leaders[1], leaders[0])
    basis_ref[BLOCK : 2 * BLOCK, :] = jnp.where(second, later[0:BLOCK], leaders[2])
    basis_ref[2 * BLOCK :, :] = later[BLOCK:]


def exchange(value, axes):
    return lax.all_to_all(value, axes, split_axis=0, concat_axis=0, tiled=True)


def call(kernel, name, out_shape, inputs, scratch=(), smem=0):
    single = not isinstance(out_shape, (tuple, list))
    return pl.pallas_call(
        kernel,
        out_shape=out_shape,
        in_specs=[pl.BlockSpec(memory_space=pltpu.SMEM)] * smem + [VMEM] * (len(inputs) - smem),
        out_specs=VMEM if single else (VMEM,) * len(out_shape),
        scratch_shapes=list(scratch),
        compiler_params=PARAMS,
        name=name,
    )(*inputs)


def on_device(vectors, offsets, counts, labels, cosines, distances):
    chips = ("y", "z", "x")
    plane = ("y", "x")
    chip_count = lax.axis_size(chips)
    planes = lax.axis_size(plane)
    depth = lax.axis_size("z")

    def shift(value, step):
        return lax.ppermute(value, chips, [(i, (i + step) % chip_count) for i in range(chip_count)])

    shape = jax.ShapeDtypeStruct
    slab = call(
        pack_kernel, "pack", shape((CORES, OWN + TABLE, LOCAL), F32),
        (vectors, cosines, distances, offsets, counts.reshape(1, LOCAL), labels),
    )
    slab = exchange(slab, "core")
    left = shift(slab, 1)
    right = shift(slab, -1)
    matrix = shape((WIDE, LOCAL), BF16)
    matrices = call(own_matrix_kernel, "own_matrix", (matrix,) * 4, (slab,))
    wide = pltpu.VMEM((WIDE, LOCAL), BF16)
    applied, head = call(
        apply_kernel,
        "apply_twice",
        (shape((OWN, CHIP), F32), shape((CORES, 2 * BLOCK, CHIP), F32)),
        (left, slab, right, *matrices),
        [pltpu.VMEM((OWN, 3 * CHIP), BF16)] * 2 + [pltpu.VMEM((OWN, 2 * CHIP), BF16)] * 2 + [wide] * 4,
    )
    head = exchange(head, "core")
    gram = call(gram_kernel, "gram", shape((OWN // 128, HEAD, 128), F32), (head, applied))
    piece = (OWN // 128) * HEAD // planes
    gram = exchange(gram.reshape(planes, piece, 128), plane).sum(0)
    gram = exchange(jnp.broadcast_to(gram[None], (depth, piece, 128)), "z").sum(0)
    everyone = planes * CORES
    gram = exchange(jnp.broadcast_to(gram[None], (everyone, piece, 128)), (*plane, "core"))
    gram = gram.reshape(planes, CORES, piece, 128)
    scale = 1.0 / (CHIP * chip_count)
    basis = call(
        lambda *refs: finish_kernel(scale, *refs), "finish", shape((OWN, CHIP), F32),
        (lax.axis_index("core").reshape(1), gram, head, applied), smem=1,
    )
    return lax.all_to_all(basis, "x", split_axis=0, concat_axis=1, tiled=True)


def solution(mesh):
    rows = mesh.shape["rows"]
    cols = mesh.shape["cols"]
    names = ("y", "z", "x", "core")
    cube = Mesh(mesh.devices.reshape(Y_SIZE, rows // Y_SIZE, cols // CORES, CORES), names)
    whole = P(None, names)
    placed = (whole, whole, P(names), whole, whole, whole)
    return jax.shard_map(
        on_device, mesh=cube, in_specs=placed, out_specs=P(("x", "core"), ("y", "z")),
        check_vma=False,
    )
```

time: 126 us -> 124 us (0.984)
  starting transfers between devices: 29.5 us -> 21.3 us
  waiting for transfers between devices: 12.3 us -> 20.5 us
  local copies, waits for them, and re-layouts: 2.08 us -> 6.17 us
  Pallas kernels: 19 us -> 15.7 us
  other arithmetic: 1.49 us -> 0.04 us
  blocking collectives: 61 us -> 59.7 us
    ppermute x4 -> x2, starting transfers between devices: 29.5 us -> 12.3 us  [shift(): lax.ppermute(value, chips, [(i, (i + step) % chip_count) for i in range(c...]
    all_to_all x0 -> x1, waiting for transfers between devices: none -> 10.2 us  [exchange(): return lax.all_to_all(value, axes, split_axis=0, concat_axis=0, tiled=True)]
    all_to_all x0 -> x1, starting transfers between devices: none -> 8.96 us  [exchange(): return lax.all_to_all(value, axes, split_axis=0, concat_axis=0, tiled=True)]
    unnamed x8 -> x12, local copies, waits for them, and re-layouts: 0.02 us -> 4.55 us
    pallas_call x3 -> x5, Pallas kernels: 19 us -> 15.7 us  [call(): pl.pallas_call(kernel, out_shape=out_shape, in_specs=[pl.BlockSpec(memory...]
    ppermute x4 -> x2, waiting for transfers between devices: 12.3 us -> 10.3 us  [shift(): lax.ppermute(value, chips, [(i, (i + step) % chip_count) for i in range(c...]
    convert_element_type x3 -> x0, other arithmetic: 1.43 us -> none  [the longest x1 0.74 us: on_device(): offsets.astype(F32)]
    all_to_all x3 -> x4, blocking collectives: 48.9 us -> 48.1 us  [exchange(): return lax.all_to_all(value, axes, split_axis=0, concat_axis=0, tiled=True)]
  transfers between devices with their start and end apart: 4 -> 3, of which waited for: 1 -> 3; matrix products, arithmetic and copies ran while one was open for 0% -> 0% of each run, Pallas kernels for 2% -> 2%
where the time goes in v3:
time: 124 us; the launch traced here: 123 us
  blocking collectives  59.7 us (48%)
  starting transfers between devices  21.3 us (17%)
  waiting for transfers between devices  20.5 us (17%)
  Pallas kernels  15.7 us (13%)
  local copies, waits for them, and re-layouts  6.17 us (5%)
    all_to_all x4, blocking collectives, exchange(): return lax.all_to_all(value, axes, split_axis=0, concat_axis=0, tiled=True)  48.1 us
    pallas_call x5, Pallas kernels, call(): pl.pallas_call(kernel, out_shape=out_shape, in_specs=[pl.BlockSpec(memory...  15.7 us
    ppermute x2, starting transfers between devices, shift(): lax.ppermute(value, chips, [(i, (i + step) % chip_count) for i in range(c...  12.3 us
    all_to_all x1, blocking collectives, on_device(): return lax.all_to_all(basis, 'x', split_axis=0, concat_axis=1, tiled=True)  11.6 us
    ppermute x2, waiting for transfers between devices, shift(): lax.ppermute(value, chips, [(i, (i + step) % chip_count) for i in range(c...  10.3 us
    all_to_all x1, waiting for transfers between devices, exchange(): return lax.all_to_all(value, axes, split_axis=0, concat_axis=0, tiled=True)  10.2 us
    all_to_all x1, starting transfers between devices, exchange(): return lax.all_to_all(value, axes, split_axis=0, concat_axis=0, tiled=True)  8.96 us
    unnamed x12, local copies, waits for them, and re-layouts  4.55 us
  transfers between devices with their start and end apart: 3, of which 3 were waited for; matrix products, arithmetic and copies ran while one was open for 0% of the time, Pallas kernels for 2%

profile of v3, /device:TPU:1, one launch (start us, length us, event | category | flops | bytes accessed | tf_op | source)
XLA Modules:
  0.0 123.4 jit_solution(2582922804527384778)
XLA Ops:
  0.0 0.0 copy-start.5
  0.0 0.7 copy-done.5
  0.7 0.0 copy-start
  0.7 1.0 copy-done
  1.7 0.0 copy-start.1
  1.7 0.7 copy-done.1
  2.4 0.0 copy-start.2
  2.4 0.7 copy-done.2
  3.2 0.0 copy-start.3
  3.2 0.7 copy-done.3
  3.9 0.0 copy-start.4
  3.9 0.7 copy-done.4
  4.6 0.1 pack.1
  4.6 10.7 %all_to_all.44.slab_ref.own_ref = f32[2,296,256]{2,1,0:T(8,128)S(1)} all-to-all(f32[2,296,256]{2,1,0:T(8,128)S(1)} %pack.1), channel_id=1, replica_groups=mesh['y'=4,'z'=16,'x'=4,'core'=2] {'core'}, dimensions={0} | all-to-all | bytes 1212416 | tf_op jit(solution)/shard_map/all_to_all | solution.py:236
  15.3 1.9 %collective-permute-start = (f32[2,296,256]{2,1,0:T(8,128)S(1)}, f32[2,296,256]{2,1,0:T(8,128)S(1)}, u32[]{:S(2)}, u32[]{:S(2)}) collective-permute-start(f32[2,296,256]{2,1,0:T(8,128)S(1)} %all_to_all.44.slab_ref.own_ref), channel_id=1, source_target_pairs={{0,2},{2,4},{4,6},{6,8},{8,10},{10,12},{12,14},{14,16},{16,18},{18... | collective-permute-start | bytes 1818632 | tf_op jit(solution)/shard_map/ppermute | solution.py:260
  17.2 10.4 %collective-permute-start.1 = (f32[2,296,256]{2,1,0:T(8,128)S(1)}, f32[2,296,256]{2,1,0:T(8,128)S(1)}, u32[]{:S(2)}, u32[]{:S(2)}) collective-permute-start(f32[2,296,256]{2,1,0:T(8,128)S(1)} %all_to_all.44.slab_ref.own_ref), channel_id=1, source_target_pairs={{0,510},{2,0},{4,2},{6,4},{8,6},{10,8},{12,10},{14,12},{16,14},{18... | collective-permute-start | bytes 1818632 | tf_op jit(solution)/shard_map/ppermute | solution.py:260
  27.7 2.4 %own_matrix.1 = (bf16[768,256]{1,0:T(8,128)(2,1)S(1)}, bf16[768,256]{1,0:T(8,128)(2,1)S(1)}, bf16[768,256]{1,0:T(8,128)(2,1)S(1)}, bf16[768,256]{1,0:T(8,128)(2,1)S(1)}) custom-call(f32[2,296,256]{2,1,0:T(8,128)S(1)} %all_to_all.44.slab_ref.own_ref), custom_call_target="tpu_custom_call" | custom-call | tf_op jit(solution)/shard_map/own_matrix/pallas_call | solution.py:241
  30.0 9.4 %collective-permute-done.left_ref = f32[2,296,256]{2,1,0:T(8,128)S(1)} collective-permute-done((f32[2,296,256]{2,1,0:T(8,128)S(1)}, f32[2,296,256]{2,1,0:T(8,128)S(1)}, u32[]{:S(2)}, u32[]{:S(2)}) %collective-permute-start) | collective-permute-done | bytes 606240 | tf_op jit(solution)/shard_map/ppermute | solution.py:260
  39.5 0.9 collective-permute-done.1.right_ref
  40.3 4.4 %apply_twice.1 = (f32[256,512]{1,0:T(8,128)S(1)}, f32[2,128,512]{2,1,0:T(8,128)S(1)}) custom-call(f32[2,296,256]{2,1,0:T(8,128)S(1)} %collective-permute-done.left_ref, f32[2,296,256]{2,1,0:T(8,128)S(1)} %all_to_all.44.slab_ref.own_ref, f32[2,296,256]{2,1,0:T(8,128)S(1)} %collective-permute-done.1.right_ref, ...), custom_call_target="tpu_custom_call" | custom-call | tf_op jit(solution)/shard_map/apply_twice/pallas_call | solution.py:241
  44.7 5.0 %all_to_all.45.head_ref.refs_2_ = f32[2,128,512]{2,1,0:T(8,128)S(1)} all-to-all(f32[2,128,512]{2,1,0:T(8,128)S(1)} %get-tuple-element.15), channel_id=1, replica_groups=mesh['y'=4,'z'=16,'x'=4,'core'=2] {'core'}, dimensions={0} | all-to-all | bytes 1048576 | tf_op jit(solution)/shard_map/all_to_all | solution.py:236
  49.7 0.7 gram.1
  50.4 10.3 %all_to_all.46 = f32[16,24,128]{2,1,0:T(8,128)S(1)} all-to-all(f32[16,24,128]{2,1,0:T(8,128)S(1)} %bitcast.10), channel_id=1, replica_groups=mesh['y'=4,'z'=16,'x'=4,'core'=2] {'y','x'}, dimensions={0} | all-to-all | bytes 393216 | tf_op jit(solution)/shard_map/all_to_all | solution.py:236
  60.7 22.1 %all_to_all.47 = f32[16,24,128]{2,1,0:T(8,128)S(1)} all-to-all(f32[16,24,128]{2,1,0:T(8,128)S(1)} %broadcast_in_dim.4), channel_id=1, replica_groups=mesh['y'=4,'z'=16,'x'=4,'core'=2] {'z'}, dimensions={0} | all-to-all | bytes 393216 | tf_op jit(solution)/shard_map/all_to_all | solution.py:236
  82.8 0.8 broadcast_in_dim.5
  83.6 9.0 %all-to-all-start.4 = ((f32[32,24,128]{2,1,0:T(8,128)}), f32[32,24,128]{2,1,0:T(8,128)S(1)}, u32[]{:S(2)}, u32[]{:S(2)}) async-start(f32[32,24,128]{2,1,0:T(8,128)} %broadcast_in_dim.5), calls=%async_computation.4 | async-start | bytes 786432 | tf_op jit(solution)/shard_map/all_to_all | solution.py:236
  92.6 10.2 %all-to-all-done.4 = f32[32,24,128]{2,1,0:T(8,128)S(1)} async-done(((f32[32,24,128]{2,1,0:T(8,128)}), f32[32,24,128]{2,1,0:T(8,128)S(1)}, u32[]{:S(2)}, u32[]{:S(2)}) %all-to-all-start.4) | async-done | bytes 393248 | tf_op jit(solution)/shard_map/all_to_all | solution.py:236
  102.8 8.2 %finish.1 = f32[256,512]{1,0:T(8,128)S(1)} custom-call(s32[1]{0:T(128)} %bitcast.refs_0_, f32[16,2,24,128]{3,2,1,0:T(8,128)S(1)} %bitcast.9, f32[2,128,512]{2,1,0:T(8,128)S(1)} %all_to_all.45.head_ref.refs_2_, f32[256,512]{1,0:T(8,128)S(1)} %get-tuple-element.16.applied_ref.refs_3_), custom_call_target="tpu_custom_call" | custom-call | tf_op jit(solution)/shard_map/finish/pallas_call | solution.py:241
  110.9 11.6 %all_to_all.48 = f32[4,64,512]{2,1,0:T(8,128)S(1)} all-to-all(f32[4,64,512]{2,1,0:T(8,128)S(1)} %bitcast.8), channel_id=1, replica_groups=mesh['y'=4,'z'=16,'x'=4,'core'=2] {'x'}, dimensions={0} | all-to-all | bytes 1048576 | tf_op jit(solution)/shard_map/all_to_all | solution.py:293
  122.5 0.8 copy.9
  (3 shorter events, 0.1 us)
Async XLA Ops:
  0.0 0.7 copy-start.5
  0.7 1.0 copy-start
  1.7 0.7 copy-start.1
  2.4 0.7 copy-start.2
  3.2 0.7 copy-start.3
  3.9 0.7 copy-start.4
  15.3 24.1 %collective-permute-start = (f32[2,296,256]{2,1,0:T(8,128)S(1)}, f32[2,296,256]{2,1,0:T(8,128)S(1)}, u32[]{:S(2)}, u32[]{:S(2)}) collective-permute-start(f32[2,296,256]{2,1,0:T(8,128)S(1)} %all_to_all.44.slab_ref.own_ref), channel_id=1, source_target_pairs={{0,2},{2,4},{4,6},{6,8},{8,10},{10,12},{12,14},{14,16},{16,18},{18... | collective-permute-start | bytes 1818632 | tf_op jit(solution)/shard_map/ppermute | solution.py:260
  17.2 23.1 %collective-permute-start.1 = (f32[2,296,256]{2,1,0:T(8,128)S(1)}, f32[2,296,256]{2,1,0:T(8,128)S(1)}, u32[]{:S(2)}, u32[]{:S(2)}) collective-permute-start(f32[2,296,256]{2,1,0:T(8,128)S(1)} %all_to_all.44.slab_ref.own_ref), channel_id=1, source_target_pairs={{0,510},{2,0},{4,2},{6,4},{8,6},{10,8},{12,10},{14,12},{16,14},{18... | collective-permute-start | bytes 1818632 | tf_op jit(solution)/shard_map/ppermute | solution.py:260
  83.6 19.1 %all-to-all-start.4 = ((f32[32,24,128]{2,1,0:T(8,128)}), f32[32,24,128]{2,1,0:T(8,128)S(1)}, u32[]{:S(2)}, u32[]{:S(2)}) async-start(f32[32,24,128]{2,1,0:T(8,128)} %broadcast_in_dim.5), calls=%async_computation.4 | async-start | bytes 786432 | tf_op jit(solution)/shard_map/all_to_all | solution.py:236

commit v4 on v3

--- a/solution.py
+++ b/solution.py
@@ -32,26 +32,56 @@
 PARAMS = pltpu.CompilerParams(vmem_limit_bytes=48 * 1024 * 1024)
 
 
-def pack_kernel(vectors_ref, cosines_ref, distances_ref, offsets_ref, counts_ref, labels_ref, out_ref):
-    square = cosines_ref[...] * cosines_ref[...]
-    distances = distances_ref[...]
-    bond = PI_BOND * jnp.exp(-(distances - 1.0) / DECAY_LENGTH) * (1.0 - square)
-    bond = bond + SIGMA_BOND * jnp.exp(-(distances - LAYER_GAP) / DECAY_LENGTH) * square
+def pack_kernel(
+    vectors_ref, cosines_ref, distances_ref, offsets_ref, counts_ref, labels_ref, out_ref,
+    cosines, distances, offsets, counts, labels, table_sems, block_sems,
+):
+    tables = (
+        (cosines_ref, cosines), (distances_ref, distances), (offsets_ref, offsets),
+        (counts_ref, counts), (labels_ref, labels),
+    )
+    table_copies = [
+        pltpu.make_async_copy(source, target, table_sems.at[i])
+        for i, (source, target) in enumerate(tables)
+    ]
+    block_copies = [
+        pltpu.make_async_copy(
+            vectors_ref.at[pl.ds(BLOCK * (core + CORES * p), BLOCK)],
+            out_ref.at[core, pl.ds(BLOCK * p, BLOCK)],
+            block_sems.at[core + CORES * p],
+        )
+        for core in range(CORES)
+        for p in range(OWN // BLOCK)
+    ]
+    for copy in table_copies + block_copies:
+        copy.start()
+    for copy in table_copies:
+        copy.wait()
+    square = cosines[...] * cosines[...]
+    bond = PI_BOND * jnp.exp(-(distances[...] - 1.0) / DECAY_LENGTH) * (1.0 - square)
+    bond = bond + SIGMA_BOND * jnp.exp(-(distances[...] - LAYER_GAP) / DECAY_LENGTH) * square
     slot = lax.broadcasted_iota(jnp.int32, bond.shape, 0)
-    hopping = jnp.where(slot < counts_ref[...], bond, 0.0)
-    offsets = offsets_ref[...].astype(F32)
+    hopping = jnp.where(slot < counts[...], bond, 0.0)
+    steps = offsets[...].astype(F32)
     merged = jnp.zeros_like(hopping)
     for k in range(SLOTS):
-        merged = merged + jnp.where(offsets == offsets[k : k + 1], hopping[k : k + 1], 0.0)
-    labels = labels_ref[...].astype(F32)
-    onsite = SITE_MASS * (2.0 * labels[0:1] - 1.0) + LAYER_BIAS * (2.0 * labels[1:2] - 1.0)
+        merged = merged + jnp.where(steps == steps[k : k + 1], hopping[k : k + 1], 0.0)
+    sides = labels[...].astype(F32)
+    onsite = SITE_MASS * (2.0 * sides[0:1] - 1.0) + LAYER_BIAS * (2.0 * sides[1:2] - 1.0)
     for core in range(CORES):
-        for p in range(OWN // BLOCK):
-            source = BLOCK * (core + CORES * p)
-            out_ref[core, BLOCK * p : BLOCK * p + BLOCK, :] = vectors_ref[source : source + BLOCK, :]
         out_ref[core, OWN : OWN + 16, :] = merged
-        out_ref[core, OWN + 16 : OWN + 32, :] = offsets
+        out_ref[core, OWN + 16 : OWN + 32, :] = steps
         out_ref[core, OWN + 32 : OWN + 40, :] = jnp.broadcast_to(onsite, (8, LOCAL))
+    for copy in block_copies:
+        copy.wait()
+
+
+def sum_kernel(pieces_ref, out_ref):
+    total = pieces_ref[0]
+    for i in range(1, pieces_ref.shape[0]):
+        total = total + pieces_ref[i]
+    for i in range(out_ref.shape[0]):
+        out_ref[i] = total
 
 
 def build_matrix(table, high_ref, low_ref):
@@ -106,7 +136,7 @@
 
 def apply_kernel(
     left_ref, own_ref, right_ref, first_high_ref, first_low_ref, second_high_ref, second_low_ref,
-    applied_ref, head_ref, high_ref, low_ref, once_high_ref, once_low_ref,
+    applied_ref, lead_ref, high_ref, low_ref, once_high_ref, once_low_ref,
     left_high_ref, left_low_ref, right_high_ref, right_low_ref,
 ):
     build_matrix(left_ref[1, OWN:, :], left_high_ref, left_low_ref)
@@ -137,17 +167,16 @@
             once_high_ref[:, window], once_low_ref[:, window], matrix_high[...], matrix_low[...]
         )
         applied_ref[:, columns] = twice
-        for core in range(CORES):
-            head_ref[core, :, columns] = twice[0 : 2 * BLOCK]
-
-
-def head_blocks(head_ref):
-    return head_ref[0, 0:BLOCK, :], head_ref[1, 0:BLOCK, :], head_ref[0, BLOCK:, :]
-
-
-def gram_kernel(head_ref, applied_ref, gram_ref):
-    head = jnp.concatenate(head_blocks(head_ref), axis=0)
-    gram = dot32(head, applied_ref[...], ((1,), (1,)))
+        lead_ref[:, columns] = twice[0 : 2 * BLOCK]
+
+
+def gram_kernel(core_ref, lead_ref, other_ref, applied_ref, gram_ref, head_ref):
+    second = core_ref[0] == 1
+    for s, place, core in ((0, 0, 0), (1, 0, 1), (2, BLOCK, 0)):
+        mine, theirs = lead_ref[place : place + BLOCK, :], other_ref[place : place + BLOCK, :]
+        pair = (mine, theirs) if core else (theirs, mine)
+        head_ref[BLOCK * s : BLOCK * s + BLOCK, :] = jnp.where(second, *pair)
+    gram = dot32(head_ref[...], applied_ref[...], ((1,), (1,)))
     for part in range(OWN // 128):
         gram_ref[part] = gram[:, 128 * part : 128 * part + 128]
 
@@ -216,9 +245,8 @@
         inverses.append(inverse)
         couplings.append(coupling)
     leaders = []
-    heads = head_blocks(head_ref)
     for s in range(STEPS):
-        block = heads[s]
+        block = head_ref[BLOCK * s : BLOCK * s + BLOCK, :]
         for t in range(s):
             block = block - dot32(
                 couplings[t][:, places[s] : places[s] + BLOCK], leaders[t], ((0,), (0,))
@@ -236,12 +264,16 @@
     return lax.all_to_all(value, axes, split_axis=0, concat_axis=0, tiled=True)
 
 
-def call(kernel, name, out_shape, inputs, scratch=(), smem=0):
+SMEM = pl.BlockSpec(memory_space=pltpu.SMEM)
+RAW = pl.BlockSpec(memory_space=pl.ANY)
+
+
+def call(kernel, name, out_shape, inputs, scratch=(), specs=None):
     single = not isinstance(out_shape, (tuple, list))
     return pl.pallas_call(
         kernel,
         out_shape=out_shape,
-        in_specs=[pl.BlockSpec(memory_space=pltpu.SMEM)] * smem + [VMEM] * (len(inputs) - smem),
+        in_specs=specs or [VMEM] * len(inputs),
         out_specs=VMEM if single else (VMEM,) * len(out_shape),
         scratch_shapes=list(scratch),
         compiler_params=PARAMS,
@@ -260,9 +292,12 @@
         return lax.ppermute(value, chips, [(i, (i + step) % chip_count) for i in range(chip_count)])
 
     shape = jax.ShapeDtypeStruct
+    tables = (cosines, distances, offsets, counts.reshape(1, LOCAL), labels)
     slab = call(
-        pack_kernel, "pack", shape((CORES, OWN + TABLE, LOCAL), F32),
-        (vectors, cosines, distances, offsets, counts.reshape(1, LOCAL), labels),
+        pack_kernel, "pack", shape((CORES, OWN + TABLE, LOCAL), F32), (vectors, *tables),
+        [pltpu.VMEM(t.shape, t.dtype) for t in tables]
+        + [pltpu.SemaphoreType.DMA((len(tables),)), pltpu.SemaphoreType.DMA((NV // BLOCK,))],
+        [RAW] * 6,
     )
     slab = exchange(slab, "core")
     left = shift(slab, 1)
@@ -270,25 +305,30 @@
     matrix = shape((WIDE, LOCAL), BF16)
     matrices = call(own_matrix_kernel, "own_matrix", (matrix,) * 4, (slab,))
     wide = pltpu.VMEM((WIDE, LOCAL), BF16)
-    applied, head = call(
+    applied, lead = call(
         apply_kernel,
         "apply_twice",
-        (shape((OWN, CHIP), F32), shape((CORES, 2 * BLOCK, CHIP), F32)),
+        (shape((OWN, CHIP), F32), shape((2 * BLOCK, CHIP), F32)),
         (left, slab, right, *matrices),
         [pltpu.VMEM((OWN, 3 * CHIP), BF16)] * 2 + [pltpu.VMEM((OWN, 2 * CHIP), BF16)] * 2 + [wide] * 4,
     )
-    head = exchange(head, "core")
-    gram = call(gram_kernel, "gram", shape((OWN // 128, HEAD, 128), F32), (head, applied))
+    other = lax.ppermute(lead, "core", [(0, 1), (1, 0)])
+    core = lax.axis_index("core").reshape(1)
+    gram, head = call(
+        gram_kernel, "gram", (shape((OWN // 128, HEAD, 128), F32), shape((HEAD, CHIP), F32)),
+        (core, lead, other, applied), (), [SMEM] + [VMEM] * 3,
+    )
     piece = (OWN // 128) * HEAD // planes
-    gram = exchange(gram.reshape(planes, piece, 128), plane).sum(0)
-    gram = exchange(jnp.broadcast_to(gram[None], (depth, piece, 128)), "z").sum(0)
     everyone = planes * CORES
-    gram = exchange(jnp.broadcast_to(gram[None], (everyone, piece, 128)), (*plane, "core"))
+    gram = exchange(gram.reshape(planes, piece, 128), plane)
+    gram = exchange(call(sum_kernel, "sum_plane", shape((depth, piece, 128), F32), (gram,)), "z")
+    gram = call(sum_kernel, "sum_depth", shape((everyone, piece, 128), F32), (gram,))
+    gram = exchange(gram, (*plane, "core"))
     gram = gram.reshape(planes, CORES, piece, 128)
     scale = 1.0 / (CHIP * chip_count)
     basis = call(
         lambda *refs: finish_kernel(scale, *refs), "finish", shape((OWN, CHIP), F32),
-        (lax.axis_index("core").reshape(1), gram, head, applied), smem=1,
+        (core, gram, head, applied), (), [SMEM] + [VMEM] * 3,
     )
     return lax.all_to_all(basis, "x", split_axis=0, concat_axis=1, tiled=True)
 

time: 124 us -> 123 us (level)
  blocking collectives: 59.7 us -> 73.7 us
  waiting for transfers between devices: 20.5 us -> 11.4 us
  starting transfers between devices: 21.3 us -> 15.4 us
    all_to_all x4, blocking collectives: 48.1 us -> 62 us  [exchange(): return lax.all_to_all(value, axes, split_axis=0, concat_axis=0, tiled=True)]
    all_to_all x1 -> x0, waiting for transfers between devices: 10.2 us -> none  [exchange(): return lax.all_to_all(value, axes, split_axis=0, concat_axis=0, tiled=True)]
    all_to_all x1 -> x0, starting transfers between devices: 8.96 us -> none  [exchange(): return lax.all_to_all(value, axes, split_axis=0, concat_axis=0, tiled=True)]
    ppermute x0 -> x1, starting transfers between devices: none -> 3.11 us  [on_device(): other = lax.ppermute(lead, 'core', [(0, 1), (1, 0)])]
    pallas_call x5 -> x7, Pallas kernels: 15.7 us -> 16.6 us  [call(): pl.pallas_call(kernel, out_shape=out_shape, in_specs=specs or [VMEM] * le...]
where the time goes in v4:
time: 123 us
  blocking collectives  73.7 us (60%)
  Pallas kernels  16.6 us (13%)
  starting transfers between devices  15.4 us (13%)
  waiting for transfers between devices  11.4 us (9%)
  local copies, waits for them, and re-layouts  5.39 us (4%)
    all_to_all x4, blocking collectives, exchange(): return lax.all_to_all(value, axes, split_axis=0, concat_axis=0, tiled=True)  62 us
    pallas_call x7, Pallas kernels, call(): pl.pallas_call(kernel, out_shape=out_shape, in_specs=specs or [VMEM] * le...  16.6 us
    ppermute x2, starting transfers between devices, shift(): lax.ppermute(value, chips, [(i, (i + step) % chip_count) for i in range(c...  12.3 us
    all_to_all x1, blocking collectives, on_device(): return lax.all_to_all(basis, 'x', split_axis=0, concat_axis=1, tiled=True)  11.6 us
    ppermute x2, waiting for transfers between devices, shift(): lax.ppermute(value, chips, [(i, (i + step) % chip_count) for i in range(c...  10.3 us
    unnamed x12, local copies, waits for them, and re-layouts  4.55 us
    ppermute x1, starting transfers between devices, on_device(): other = lax.ppermute(lead, 'core', [(0, 1), (1, 0)])  3.11 us
  transfers between devices with their start and end apart: 3, of which 3 were waited for; matrix products, arithmetic and copies ran while one was open for 0% of the time, Pallas kernels for 2%

profile of v4, /device:TPU:1, one launch (start us, length us, event | category | flops | bytes accessed | tf_op | source)
XLA Modules:
  0.0 122.5 jit_solution(6235826493932309158)
XLA Ops:
  0.0 0.0 copy-start.5
  0.0 0.7 copy-done.5
  0.7 0.0 copy-start
  0.7 1.0 copy-done
  1.7 0.0 copy-start.1
  1.7 0.7 copy-done.1
  2.4 0.0 copy-start.2
  2.4 0.7 copy-done.2
  3.2 0.0 copy-start.3
  3.2 0.7 copy-done.3
  3.9 0.0 copy-start.4
  3.9 0.7 copy-done.4
  4.6 0.9 pack.1
  5.5 10.7 %all_to_all.39.slab_ref.own_ref = f32[2,296,256]{2,1,0:T(8,128)S(1)} all-to-all(f32[2,296,256]{2,1,0:T(8,128)S(1)} %pack.1), channel_id=1, replica_groups=mesh['y'=4,'z'=16,'x'=4,'core'=2] {'core'}, dimensions={0} | all-to-all | bytes 1212416 | tf_op jit(solution)/shard_map/all_to_all | solution.py:264
  16.2 1.9 %collective-permute-start = (f32[2,296,256]{2,1,0:T(8,128)S(1)}, f32[2,296,256]{2,1,0:T(8,128)S(1)}, u32[]{:S(2)}, u32[]{:S(2)}) collective-permute-start(f32[2,296,256]{2,1,0:T(8,128)S(1)} %all_to_all.39.slab_ref.own_ref), channel_id=1, source_target_pairs={{0,2},{2,4},{4,6},{6,8},{8,10},{10,12},{12,14},{14,16},{16,18},{18... | collective-permute-start | bytes 1818632 | tf_op jit(solution)/shard_map/ppermute | solution.py:292
  18.1 10.4 %collective-permute-start.1 = (f32[2,296,256]{2,1,0:T(8,128)S(1)}, f32[2,296,256]{2,1,0:T(8,128)S(1)}, u32[]{:S(2)}, u32[]{:S(2)}) collective-permute-start(f32[2,296,256]{2,1,0:T(8,128)S(1)} %all_to_all.39.slab_ref.own_ref), channel_id=1, source_target_pairs={{0,510},{2,0},{4,2},{6,4},{8,6},{10,8},{12,10},{14,12},{16,14},{18... | collective-permute-start | bytes 1818632 | tf_op jit(solution)/shard_map/ppermute | solution.py:292
  28.5 2.4 %own_matrix.1 = (bf16[768,256]{1,0:T(8,128)(2,1)S(1)}, bf16[768,256]{1,0:T(8,128)(2,1)S(1)}, bf16[768,256]{1,0:T(8,128)(2,1)S(1)}, bf16[768,256]{1,0:T(8,128)(2,1)S(1)}) custom-call(f32[2,296,256]{2,1,0:T(8,128)S(1)} %all_to_all.39.slab_ref.own_ref), custom_call_target="tpu_custom_call" | custom-call | tf_op jit(solution)/shard_map/own_matrix/pallas_call | solution.py:273
  30.9 9.4 %collective-permute-done.left_ref = f32[2,296,256]{2,1,0:T(8,128)S(1)} collective-permute-done((f32[2,296,256]{2,1,0:T(8,128)S(1)}, f32[2,296,256]{2,1,0:T(8,128)S(1)}, u32[]{:S(2)}, u32[]{:S(2)}) %collective-permute-start) | collective-permute-done | bytes 606240 | tf_op jit(solution)/shard_map/ppermute | solution.py:292
  40.3 0.9 collective-permute-done.1.right_ref
  41.2 4.4 %apply_twice.1 = (f32[256,512]{1,0:T(8,128)S(1)}, f32[128,512]{1,0:T(8,128)S(1)}) custom-call(f32[2,296,256]{2,1,0:T(8,128)S(1)} %collective-permute-done.left_ref, f32[2,296,256]{2,1,0:T(8,128)S(1)} %all_to_all.39.slab_ref.own_ref, f32[2,296,256]{2,1,0:T(8,128)S(1)} %collective-permute-done.1.right_ref, ...), custom_call_target="tpu_custom_call" | custom-call | tf_op jit(solution)/shard_map/apply_twice/pallas_call | solution.py:273
  45.5 3.1 %collective-permute-start.2 = (f32[128,512]{1,0:T(8,128)S(1)}, f32[128,512]{1,0:T(8,128)S(1)}, u32[]{:S(2)}, u32[]{:S(2)}) collective-permute-start(f32[128,512]{1,0:T(8,128)S(1)} %get-tuple-element.17.lead_ref), channel_id=1, source_target_pairs={{0,1},{1,0},{2,3},{3,2},{4,5},{5,4},{6,7},{7,6},{8,9},{9,8},{10,11... | collective-permute-start | bytes 786440 | tf_op jit(solution)/shard_map/ppermute | solution.py:315
  48.7 1.1 collective-permute-done.2.other_ref
  49.8 0.7 gram.1
  50.5 10.3 %all_to_all.40.pieces_ref = f32[16,24,128]{2,1,0:T(8,128)S(1)} all-to-all(f32[16,24,128]{2,1,0:T(8,128)S(1)} %bitcast.10), channel_id=1, replica_groups=mesh['y'=4,'z'=16,'x'=4,'core'=2] {'y','x'}, dimensions={0} | all-to-all | bytes 393216 | tf_op jit(solution)/shard_map/all_to_all | solution.py:264
  60.9 22.1 %all_to_all.41.pieces_ref = f32[16,24,128]{2,1,0:T(8,128)S(1)} all-to-all(f32[16,24,128]{2,1,0:T(8,128)S(1)} %sum_plane.1), channel_id=1, replica_groups=mesh['y'=4,'z'=16,'x'=4,'core'=2] {'z'}, dimensions={0} | all-to-all | bytes 393216 | tf_op jit(solution)/shard_map/all_to_all | solution.py:264
  83.0 18.9 %all_to_all.42 = f32[32,24,128]{2,1,0:T(8,128)S(1)} all-to-all(f32[32,24,128]{2,1,0:T(8,128)S(1)} %sum_depth.1), channel_id=1, replica_groups=mesh['y'=4,'z'=16,'x'=4,'core'=2] {'y','x','core'}, dimensions={0} | all-to-all | bytes 786432 | tf_op jit(solution)/shard_map/all_to_all | solution.py:264
  101.9 8.2 %finish.1 = f32[256,512]{1,0:T(8,128)S(1)} custom-call(s32[1]{0:T(128)} %bitcast.core_ref.refs_0_, f32[16,2,24,128]{3,2,1,0:T(8,128)S(1)} %bitcast.9, f32[192,512]{1,0:T(8,128)S(1)} %get-tuple-element.20.refs_2_, f32[256,512]{1,0:T(8,128)S(1)} %get-tuple-element.18.applied_ref.refs_3_), custom_call_target="tpu_custom_call" | custom-call | tf_op jit(solution)/shard_map/finish/pallas_call | solution.py:273
  110.1 11.6 %all_to_all.43 = f32[4,64,512]{2,1,0:T(8,128)S(1)} all-to-all(f32[4,64,512]{2,1,0:T(8,128)S(1)} %bitcast.8), channel_id=1, replica_groups=mesh['y'=4,'z'=16,'x'=4,'core'=2] {'x'}, dimensions={0} | all-to-all | bytes 1048576 | tf_op jit(solution)/shard_map/all_to_all | solution.py:333
  121.7 0.8 copy.8
  (2 shorter events, 0.1 us)
Async XLA Ops:
  0.0 0.7 copy-start.5
  0.7 1.0 copy-start
  1.7 0.7 copy-start.1
  2.4 0.7 copy-start.2
  3.2 0.7 copy-start.3
  3.9 0.7 copy-start.4
  16.2 24.1 %collective-permute-start = (f32[2,296,256]{2,1,0:T(8,128)S(1)}, f32[2,296,256]{2,1,0:T(8,128)S(1)}, u32[]{:S(2)}, u32[]{:S(2)}) collective-permute-start(f32[2,296,256]{2,1,0:T(8,128)S(1)} %all_to_all.39.slab_ref.own_ref), channel_id=1, source_target_pairs={{0,2},{2,4},{4,6},{6,8},{8,10},{10,12},{12,14},{14,16},{16,18},{18... | collective-permute-start | bytes 1818632 | tf_op jit(solution)/shard_map/ppermute | solution.py:292
  18.1 23.1 %collective-permute-start.1 = (f32[2,296,256]{2,1,0:T(8,128)S(1)}, f32[2,296,256]{2,1,0:T(8,128)S(1)}, u32[]{:S(2)}, u32[]{:S(2)}) collective-permute-start(f32[2,296,256]{2,1,0:T(8,128)S(1)} %all_to_all.39.slab_ref.own_ref), channel_id=1, source_target_pairs={{0,510},{2,0},{4,2},{6,4},{8,6},{10,8},{12,10},{14,12},{16,14},{18... | collective-permute-start | bytes 1818632 | tf_op jit(solution)/shard_map/ppermute | solution.py:292
  45.5 4.3 %collective-permute-start.2 = (f32[128,512]{1,0:T(8,128)S(1)}, f32[128,512]{1,0:T(8,128)S(1)}, u32[]{:S(2)}, u32[]{:S(2)}) collective-permute-start(f32[128,512]{1,0:T(8,128)S(1)} %get-tuple-element.17.lead_ref), channel_id=1, source_target_pairs={{0,1},{1,0},{2,3},{3,2},{4,5},{5,4},{6,7},{7,6},{8,9},{9,8},{10,11... | collective-permute-start | bytes 786440 | tf_op jit(solution)/shard_map/ppermute | solution.py:315

commit v5 on v4

--- a/solution.py
+++ b/solution.py
@@ -24,6 +24,7 @@
 CORES = 2
 OWN = NV // CORES
 TABLE = 40
+SHARED = HEAD + OWN - BLOCK
 CHIP = CORES * LOCAL
 F32 = jnp.float32
 BF16 = jnp.bfloat16
@@ -170,13 +171,14 @@
         lead_ref[:, columns] = twice[0 : 2 * BLOCK]
 
 
-def gram_kernel(core_ref, lead_ref, other_ref, applied_ref, gram_ref, head_ref):
+def gram_kernel(core_ref, lead_ref, other_ref, applied_ref, gram_ref, shared_ref):
     second = core_ref[0] == 1
     for s, place, core in ((0, 0, 0), (1, 0, 1), (2, BLOCK, 0)):
         mine, theirs = lead_ref[place : place + BLOCK, :], other_ref[place : place + BLOCK, :]
         pair = (mine, theirs) if core else (theirs, mine)
-        head_ref[BLOCK * s : BLOCK * s + BLOCK, :] = jnp.where(second, *pair)
-    gram = dot32(head_ref[...], applied_ref[...], ((1,), (1,)))
+        shared_ref[BLOCK * s : BLOCK * s + BLOCK, :] = jnp.where(second, *pair)
+    shared_ref[HEAD:, :] = applied_ref[BLOCK:, :]
+    gram = dot32(shared_ref[0:HEAD, :], applied_ref[...], ((1,), (1,)))
     for part in range(OWN // 128):
         gram_ref[part] = gram[:, 128 * part : 128 * part + 128]
 
@@ -215,15 +217,39 @@
     )
 
 
-def finish_kernel(scale, core_ref, gram_ref, head_ref, applied_ref, basis_ref):
-    second = core_ref[0] == 1
+def finish_kernel(scale, place_ref, gram_ref, shared_ref, basis_ref, heads, later, results, sems):
+    chip, core = place_ref[0], place_ref[1]
+    second = core == 1
+    column = CORES * chip + core
+    count = shared_ref.shape[0]
+    start = pl.multiple_of(HEAD + BLOCK * jnp.maximum(chip - 1, 0), BLOCK)
+    copies = []
+    for q in range(count):
+        copies.append(
+            pltpu.make_async_copy(
+                shared_ref.at[q, pl.ds(0, HEAD)], heads.at[:, pl.ds(CHIP * q, CHIP)], sems.at[q]
+            )
+        )
+        copies.append(
+            pltpu.make_async_copy(
+                shared_ref.at[q, pl.ds(start, BLOCK)],
+                later.at[:, pl.ds(CHIP * q, CHIP)],
+                sems.at[count + q],
+            )
+        )
+    for copy in copies:
+        copy.start()
     tiles = gram_ref.shape[0] // 2
 
     def columns_of(part, core):
         return jnp.concatenate([gram_ref[part * tiles + m, core] for m in range(tiles)], axis=0)
 
-    rest = jnp.where(second, columns_of(1, 1), columns_of(1, 0))
-    full = jnp.concatenate([columns_of(0, 0), columns_of(0, 1), rest], axis=1) * scale
+    first_pair, second_pair = columns_of(0, 0), columns_of(0, 1)
+    low = jnp.where(second, second_pair, first_pair)
+    high = jnp.where(second, columns_of(1, 1), columns_of(1, 0))
+    mine = jnp.where(chip >= 2, high, low)
+    mine = jnp.where(chip % 2 == 1, pltpu.roll(mine, BLOCK, axis=1), mine)
+    full = jnp.concatenate([first_pair, second_pair, mine], axis=1) * scale
     gram = [full[BLOCK * s : BLOCK * s + BLOCK] for s in range(STEPS)]
     places = (0, 2 * BLOCK, BLOCK)
     lane = lax.broadcasted_iota(jnp.int32, (BLOCK, 128), 1)
@@ -244,20 +270,34 @@
             )
         inverses.append(inverse)
         couplings.append(coupling)
-    leaders = []
-    for s in range(STEPS):
-        block = head_ref[BLOCK * s : BLOCK * s + BLOCK, :]
-        for t in range(s):
-            block = block - dot32(
-                couplings[t][:, places[s] : places[s] + BLOCK], leaders[t], ((0,), (0,))
+    follows = column >= STEPS
+    weights = [None] * STEPS
+    for s in reversed(range(STEPS)):
+        leads = jnp.where(column == s, identity[:, 0:BLOCK], 0.0)
+        weight = jnp.where(follows, -couplings[s][:, 4 * BLOCK : 5 * BLOCK], leads)
+        for t in range(s + 1, STEPS):
+            weight = weight - dot32(
+                couplings[s][:, places[t] : places[t] + BLOCK], weights[t], ((1,), (0,))
             )
-        leaders.append(dot32(inverses[s], block, ((1,), (0,))))
-    stacked = jnp.concatenate([c[:, HEAD:] for c in couplings], axis=0)
-    leading = jnp.concatenate(leaders, axis=0)
-    later = applied_ref[BLOCK:, :] - dot32(stacked, leading, ((0,), (0,)))
-    basis_ref[0:BLOCK, :] = jnp.where(second, leaders[1], leaders[0])
-    basis_ref[BLOCK : 2 * BLOCK, :] = jnp.where(second, later[0:BLOCK], leaders[2])
-    basis_ref[2 * BLOCK :, :] = later[BLOCK:]
+        weights[s] = dot32(inverses[s], weight, ((0,), (0,)))
+    weight_high, weight_low = split(jnp.concatenate(weights, axis=0).T)
+    outs = []
+    for q in range(count):
+        columns = slice(CHIP * q, CHIP * q + CHIP)
+        copies[2 * q].wait()
+        copies[2 * q + 1].wait()
+        head_high, head_low = split(heads[:, columns])
+        result = jnp.where(follows, later[:, columns], 0.0)
+        results[:, columns] = result + dot3(weight_high, weight_low, head_high, head_low)
+        out = pltpu.make_async_copy(
+            results.at[:, pl.ds(CHIP * q, CHIP)],
+            basis_ref.at[:, pl.ds(CHIP * q, CHIP)],
+            sems.at[2 * count + q],
+        )
+        out.start()
+        outs.append(out)
+    for out in outs:
+        out.wait()
 
 
 def exchange(value, axes):
@@ -265,16 +305,21 @@
 
 
 SMEM = pl.BlockSpec(memory_space=pltpu.SMEM)
-RAW = pl.BlockSpec(memory_space=pl.ANY)
-
-
-def call(kernel, name, out_shape, inputs, scratch=(), specs=None):
+RAW = pl.BlockSpec(memory_space=pltpu.HBM)
+
+
+def call(kernel, name, out_shape, inputs, scratch=(), specs=None, out_specs=None):
     single = not isinstance(out_shape, (tuple, list))
+    if specs:
+        inputs = [
+            pltpu.with_memory_space_constraint(value, pltpu.HBM) if spec is RAW else value
+            for value, spec in zip(inputs, specs)
+        ]
     return pl.pallas_call(
         kernel,
         out_shape=out_shape,
         in_specs=specs or [VMEM] * len(inputs),
-        out_specs=VMEM if single else (VMEM,) * len(out_shape),
+        out_specs=out_specs or VMEM if single else (VMEM,) * len(out_shape),
         scratch_shapes=list(scratch),
         compiler_params=PARAMS,
         name=name,
@@ -314,10 +359,11 @@
     )
     other = lax.ppermute(lead, "core", [(0, 1), (1, 0)])
     core = lax.axis_index("core").reshape(1)
-    gram, head = call(
-        gram_kernel, "gram", (shape((OWN // 128, HEAD, 128), F32), shape((HEAD, CHIP), F32)),
+    gram, shared = call(
+        gram_kernel, "gram", (shape((OWN // 128, HEAD, 128), F32), shape((SHARED, CHIP), F32)),
         (core, lead, other, applied), (), [SMEM] + [VMEM] * 3,
     )
+    shared = lax.all_gather(shared, "x")
     piece = (OWN // 128) * HEAD // planes
     everyone = planes * CORES
     gram = exchange(gram.reshape(planes, piece, 128), plane)
@@ -326,11 +372,16 @@
     gram = exchange(gram, (*plane, "core"))
     gram = gram.reshape(planes, CORES, piece, 128)
     scale = 1.0 / (CHIP * chip_count)
-    basis = call(
-        lambda *refs: finish_kernel(scale, *refs), "finish", shape((OWN, CHIP), F32),
-        (core, gram, head, applied), (), [SMEM] + [VMEM] * 3,
-    )
-    return lax.all_to_all(basis, "x", split_axis=0, concat_axis=1, tiled=True)
+    count = lax.axis_size("x")
+    slab_width = CHIP * count
+    place = jnp.stack([lax.axis_index("x"), lax.axis_index("core")])
+    return call(
+        lambda *refs: finish_kernel(scale, *refs), "finish", shape((BLOCK, slab_width), F32),
+        (place, gram, shared),
+        [pltpu.VMEM((HEAD, slab_width), F32)] + [pltpu.VMEM((BLOCK, slab_width), F32)] * 2
+        + [pltpu.SemaphoreType.DMA((3 * count,))],
+        [SMEM, VMEM, RAW], RAW,
+    )
 
 
 def solution(mesh):

time: 123 us -> 124 us (level)
  blocking collectives: 73.7 us -> 36 us
  waiting for transfers between devices: 11.4 us -> 28.9 us
  between operations: 0.07 us -> 13.5 us
  starting transfers between devices: 15.4 us -> 24.3 us
  local copies, waits for them, and re-layouts: 5.39 us -> 0 us
  Pallas kernels: 16.6 us -> 20.3 us
    all_to_all x4 -> x3, blocking collectives: 62 us -> 36 us  [exchange(): return lax.all_to_all(value, axes, split_axis=0, concat_axis=0, tiled=True)]
    all_to_all x1 -> x0, blocking collectives: 11.6 us -> none  [on_device(): return lax.all_to_all(basis, 'x', split_axis=0, concat_axis=1, tiled=True)]
    all_to_all x0 -> x1, waiting for transfers between devices: none -> 10.2 us  [exchange(): return lax.all_to_all(value, axes, split_axis=0, concat_axis=0, tiled=True)]
    all_to_all x0 -> x1, starting transfers between devices: none -> 8.56 us  [exchange(): return lax.all_to_all(value, axes, split_axis=0, concat_axis=0, tiled=True)]
    ppermute x2, waiting for transfers between devices: 10.3 us -> 17.6 us  [shift(): lax.ppermute(value, chips, [(i, (i + step) % chip_count) for i in range(c...]
    unnamed x12 -> x0, local copies, waits for them, and re-layouts: 4.55 us -> none
    pallas_call x7, Pallas kernels: 16.6 us -> 20.3 us  [call(): pl.pallas_call(kernel, out_shape=out_shape, in_specs=specs or [VMEM] * le...]
  transfers between devices with their start and end apart: 3 -> 5, of which waited for: 3 -> 4; matrix products, arithmetic and copies ran while one was open for 0% -> 0% of each run, Pallas kernels for 2% -> 3%
where the time goes in v5:
time: 124 us; the launch traced here: 123 us
  blocking collectives  36 us (29%)
  waiting for transfers between devices  28.9 us (23%)
  starting transfers between devices  24.3 us (20%)
  Pallas kernels  20.3 us (16%)
  between operations  13.5 us (11%)
    all_to_all x3, blocking collectives, exchange(): return lax.all_to_all(value, axes, split_axis=0, concat_axis=0, tiled=True)  36 us
    pallas_call x7, Pallas kernels, call(): pl.pallas_call(kernel, out_shape=out_shape, in_specs=specs or [VMEM] * le...  20.3 us
    ppermute x2, waiting for transfers between devices, shift(): lax.ppermute(value, chips, [(i, (i + step) % chip_count) for i in range(c...  17.6 us
    ppermute x2, starting transfers between devices, shift(): lax.ppermute(value, chips, [(i, (i + step) % chip_count) for i in range(c...  12.3 us
    all_to_all x1, waiting for transfers between devices, exchange(): return lax.all_to_all(value, axes, split_axis=0, concat_axis=0, tiled=True)  10.2 us
    all_to_all x1, starting transfers between devices, exchange(): return lax.all_to_all(value, axes, split_axis=0, concat_axis=0, tiled=True)  8.56 us
    ppermute x1, starting transfers between devices, on_device(): other = lax.ppermute(lead, 'core', [(0, 1), (1, 0)])  3.43 us
  transfers between devices with their start and end apart: 5, of which 4 were waited for; matrix products, arithmetic and copies ran while one was open for 0% of the time, Pallas kernels for 3%

profile of v5, /device:TPU:1, one launch (start us, length us, event | category | flops | bytes accessed | tf_op | source)
XLA Modules:
  0.0 123.1 jit_solution(349559509313191755)
XLA Ops:
  6.5 0.0 all-gather.3.cloned.1.call-start
  6.5 1.2 pack.1
  7.8 10.7 %all_to_all.20.slab_ref.own_ref = f32[2,296,256]{2,1,0:T(8,128)S(1)} all-to-all(f32[2,296,256]{2,1,0:T(8,128)S(1)} %pack.1), channel_id=1, replica_groups=mesh['y'=4,'z'=16,'x'=4,'core'=2] {'core'}, dimensions={0} | all-to-all | bytes 1212416 | tf_op jit(solution)/shard_map/all_to_all | solution.py:304
  18.5 10.4 %collective-permute-start.1 = (f32[2,296,256]{2,1,0:T(8,128)S(1)}, f32[2,296,256]{2,1,0:T(8,128)S(1)}, u32[]{:S(2)}, u32[]{:S(2)}) collective-permute-start(f32[2,296,256]{2,1,0:T(8,128)S(1)} %all_to_all.20.slab_ref.own_ref), channel_id=1, source_target_pairs={{0,510},{2,0},{4,2},{6,4},{8,6},{10,8},{12,10},{14,12},{16,14},{18... | collective-permute-start | bytes 1818632 | tf_op jit(solution)/shard_map/ppermute | solution.py:337
  28.9 1.9 %collective-permute-start = (f32[2,296,256]{2,1,0:T(8,128)S(1)}, f32[2,296,256]{2,1,0:T(8,128)S(1)}, u32[]{:S(2)}, u32[]{:S(2)}) collective-permute-start(f32[2,296,256]{2,1,0:T(8,128)S(1)} %all_to_all.20.slab_ref.own_ref), channel_id=1, source_target_pairs={{0,2},{2,4},{4,6},{6,8},{8,10},{10,12},{12,14},{14,16},{16,18},{18... | collective-permute-start | bytes 1818632 | tf_op jit(solution)/shard_map/ppermute | solution.py:337
  30.8 2.4 %own_matrix.1 = (bf16[768,256]{1,0:T(8,128)(2,1)S(1)}, bf16[768,256]{1,0:T(8,128)(2,1)S(1)}, bf16[768,256]{1,0:T(8,128)(2,1)S(1)}, bf16[768,256]{1,0:T(8,128)(2,1)S(1)}) custom-call(f32[2,296,256]{2,1,0:T(8,128)S(1)} %all_to_all.20.slab_ref.own_ref), custom_call_target="tpu_custom_call" | custom-call | tf_op jit(solution)/shard_map/own_matrix/pallas_call | solution.py:318
  33.2 8.4 %collective-permute-done.1.right_ref = f32[2,296,256]{2,1,0:T(8,128)S(1)} collective-permute-done((f32[2,296,256]{2,1,0:T(8,128)S(1)}, f32[2,296,256]{2,1,0:T(8,128)S(1)}, u32[]{:S(2)}, u32[]{:S(2)}) %collective-permute-start.1) | collective-permute-done | bytes 606240 | tf_op jit(solution)/shard_map/ppermute | solution.py:337
  41.5 9.2 %collective-permute-done.left_ref = f32[2,296,256]{2,1,0:T(8,128)S(1)} collective-permute-done((f32[2,296,256]{2,1,0:T(8,128)S(1)}, f32[2,296,256]{2,1,0:T(8,128)S(1)}, u32[]{:S(2)}, u32[]{:S(2)}) %collective-permute-start) | collective-permute-done | bytes 606240 | tf_op jit(solution)/shard_map/ppermute | solution.py:337
  50.8 4.4 %apply_twice.1 = (f32[256,512]{1,0:T(8,128)S(1)}, f32[128,512]{1,0:T(8,128)S(1)}) custom-call(f32[2,296,256]{2,1,0:T(8,128)S(1)} %collective-permute-done.left_ref, f32[2,296,256]{2,1,0:T(8,128)S(1)} %all_to_all.20.slab_ref.own_ref, f32[2,296,256]{2,1,0:T(8,128)S(1)} %collective-permute-done.1.right_ref, ...), custom_call_target="tpu_custom_call" | custom-call | tf_op jit(solution)/shard_map/apply_twice/pallas_call | solution.py:318
  55.1 3.4 %collective-permute-start.2 = (f32[128,512]{1,0:T(8,128)S(1)}, f32[128,512]{1,0:T(8,128)S(1)}, u32[]{:S(2)}, u32[]{:S(2)}) collective-permute-start(f32[128,512]{1,0:T(8,128)S(1)} %get-tuple-element.17.lead_ref), channel_id=1, source_target_pairs={{0,1},{1,0},{2,3},{3,2},{4,5},{5,4},{6,7},{7,6},{8,9},{9,8},{10,11... | collective-permute-start | bytes 786440 | tf_op jit(solution)/shard_map/ppermute | solution.py:360
  58.6 1.1 collective-permute-done.2.other_ref
  59.7 1.5 %gram.1 = (f32[2,192,128]{2,1,0:T(8,128)S(1)}, f32[384,512]{1,0:T(8,128)}) custom-call(s32[1]{0:T(128)} %bitcast.1.core_ref, f32[128,512]{1,0:T(8,128)S(1)} %get-tuple-element.17.lead_ref, f32[128,512]{1,0:T(8,128)S(1)} %collective-permute-done.2.other_ref, f32[256,512]{1,0:T(8,128)S(1)} %get-tuple-element.18.applied_ref), custom_call_target="tpu_custom_call" | custom-call | tf_op jit(solution)/shard_map/gram/pallas_call | solution.py:318
  61.2 0.0 all-gather.3.cloned.1.call-update
  61.2 10.3 %all_to_all.21.pieces_ref = f32[16,24,128]{2,1,0:T(8,128)S(1)} all-to-all(f32[16,24,128]{2,1,0:T(8,128)S(1)} %bitcast.7), channel_id=1, replica_groups=mesh['y'=4,'z'=16,'x'=4,'core'=2] {'y','x'}, dimensions={0} | all-to-all | bytes 393216 | tf_op jit(solution)/shard_map/all_to_all | solution.py:304
  71.6 15.0 %all_to_all.22.pieces_ref = f32[16,24,128]{2,1,0:T(8,128)S(1)} all-to-all(f32[16,24,128]{2,1,0:T(8,128)S(1)} %sum_plane.1), channel_id=1, replica_groups=mesh['y'=4,'z'=16,'x'=4,'core'=2] {'z'}, dimensions={0} | all-to-all | bytes 393216 | tf_op jit(solution)/shard_map/all_to_all | solution.py:304
  86.6 0.8 sum_depth.1
  87.3 8.6 %all-to-all-start.3 = ((f32[32,24,128]{2,1,0:T(8,128)}), f32[32,24,128]{2,1,0:T(8,128)S(1)}, u32[]{:S(2)}, u32[]{:S(2)}) async-start(f32[32,24,128]{2,1,0:T(8,128)} %sum_depth.1), calls=%async_computation.3 | async-start | bytes 786432 | tf_op jit(solution)/shard_map/all_to_all | solution.py:304
  95.9 0.1 pad_add_fusion.refs_0_
  96.0 10.2 %all-to-all-done.3 = f32[32,24,128]{2,1,0:T(8,128)S(1)} async-done(((f32[32,24,128]{2,1,0:T(8,128)}), f32[32,24,128]{2,1,0:T(8,128)S(1)}, u32[]{:S(2)}, u32[]{:S(2)}) %all-to-all-start.3) | async-done | bytes 393248 | tf_op jit(solution)/shard_map/all_to_all | solution.py:304
  106.2 0.0 all-gather.3.cloned.1.call-done
  106.2 10.0 %finish.1 = f32[64,2048]{1,0:T(8,128)} custom-call(s32[2]{0:T(128)S(1)} %pad_add_fusion.refs_0_, f32[16,2,24,128]{3,2,1,0:T(8,128)S(1)} %bitcast.6, f32[4,384,512]{2,1,0:T(8,128)} %bitcast.8), custom_call_target="tpu_custom_call" | custom-call | tf_op jit(solution)/shard_map/finish/pallas_call | solution.py:318
  (1 shorter events, 0.0 us)
Async XLA Ops:
  6.5 99.7 %all-gather.3.cloned.1.call-start = ((), (), s32[]{:S(2)}) async-start(), calls=%async_computation.4 | async-start | bytes 3932160 | tf_op jit(solution)/shard_map/all_gather | solution.py:366
  18.5 23.1 %collective-permute-start.1 = (f32[2,296,256]{2,1,0:T(8,128)S(1)}, f32[2,296,256]{2,1,0:T(8,128)S(1)}, u32[]{:S(2)}, u32[]{:S(2)}) collective-permute-start(f32[2,296,256]{2,1,0:T(8,128)S(1)} %all_to_all.20.slab_ref.own_ref), channel_id=1, source_target_pairs={{0,510},{2,0},{4,2},{6,4},{8,6},{10,8},{12,10},{14,12},{16,14},{18... | collective-permute-start | bytes 1818632 | tf_op jit(solution)/shard_map/ppermute | solution.py:337
  28.9 21.9 %collective-permute-start = (f32[2,296,256]{2,1,0:T(8,128)S(1)}, f32[2,296,256]{2,1,0:T(8,128)S(1)}, u32[]{:S(2)}, u32[]{:S(2)}) collective-permute-start(f32[2,296,256]{2,1,0:T(8,128)S(1)} %all_to_all.20.slab_ref.own_ref), channel_id=1, source_target_pairs={{0,2},{2,4},{4,6},{6,8},{8,10},{10,12},{12,14},{14,16},{16,18},{18... | collective-permute-start | bytes 1818632 | tf_op jit(solution)/shard_map/ppermute | solution.py:337
  55.1 4.6 %collective-permute-start.2 = (f32[128,512]{1,0:T(8,128)S(1)}, f32[128,512]{1,0:T(8,128)S(1)}, u32[]{:S(2)}, u32[]{:S(2)}) collective-permute-start(f32[128,512]{1,0:T(8,128)S(1)} %get-tuple-element.17.lead_ref), channel_id=1, source_target_pairs={{0,1},{1,0},{2,3},{3,2},{4,5},{5,4},{6,7},{7,6},{8,9},{9,8},{10,11... | collective-permute-start | bytes 786440 | tf_op jit(solution)/shard_map/ppermute | solution.py:360
  87.3 18.9 %all-to-all-start.3 = ((f32[32,24,128]{2,1,0:T(8,128)}), f32[32,24,128]{2,1,0:T(8,128)S(1)}, u32[]{:S(2)}, u32[]{:S(2)}) async-start(f32[32,24,128]{2,1,0:T(8,128)} %sum_depth.1), calls=%async_computation.3 | async-start | bytes 786432 | tf_op jit(solution)/shard_map/all_to_all | solution.py:304
Sparse Core Ops, SparseCore 0:
  61.4 34.9 all-gather.2

commit v6 on v5

--- a/solution.py
+++ b/solution.py
@@ -24,7 +24,7 @@
 CORES = 2
 OWN = NV // CORES
 TABLE = 40
-SHARED = HEAD + OWN - BLOCK
+SHARED = HEAD + BLOCK
 CHIP = CORES * LOCAL
 F32 = jnp.float32
 BF16 = jnp.bfloat16
@@ -173,12 +173,16 @@
 
 def gram_kernel(core_ref, lead_ref, other_ref, applied_ref, gram_ref, shared_ref):
     second = core_ref[0] == 1
+    count = shared_ref.shape[0]
     for s, place, core in ((0, 0, 0), (1, 0, 1), (2, BLOCK, 0)):
         mine, theirs = lead_ref[place : place + BLOCK, :], other_ref[place : place + BLOCK, :]
         pair = (mine, theirs) if core else (theirs, mine)
-        shared_ref[BLOCK * s : BLOCK * s + BLOCK, :] = jnp.where(second, *pair)
-    shared_ref[HEAD:, :] = applied_ref[BLOCK:, :]
-    gram = dot32(shared_ref[0:HEAD, :], applied_ref[...], ((1,), (1,)))
+        block = jnp.where(second, *pair)
+        for q in range(count):
+            shared_ref[q, BLOCK * s : BLOCK * s + BLOCK, :] = block
+    for q in range(count):
+        shared_ref[q, HEAD:, :] = applied_ref[BLOCK * q : BLOCK * q + BLOCK, :]
+    gram = dot32(shared_ref[0, 0:HEAD, :], applied_ref[...], ((1,), (1,)))
     for part in range(OWN // 128):
         gram_ref[part] = gram[:, 128 * part : 128 * part + 128]
 
@@ -217,28 +221,11 @@
     )
 
 
-def finish_kernel(scale, place_ref, gram_ref, shared_ref, basis_ref, heads, later, results, sems):
+def finish_kernel(scale, place_ref, gram_ref, shared_ref, basis_ref, results, sems):
     chip, core = place_ref[0], place_ref[1]
     second = core == 1
     column = CORES * chip + core
     count = shared_ref.shape[0]
-    start = pl.multiple_of(HEAD + BLOCK * jnp.maximum(chip - 1, 0), BLOCK)
-    copies = []
-    for q in range(count):
-        copies.append(
-            pltpu.make_async_copy(
-                shared_ref.at[q, pl.ds(0, HEAD)], heads.at[:, pl.ds(CHIP * q, CHIP)], sems.at[q]
-            )
-        )
-        copies.append(
-            pltpu.make_async_copy(
-                shared_ref.at[q, pl.ds(start, BLOCK)],
-                later.at[:, pl.ds(CHIP * q, CHIP)],
-                sems.at[count + q],
-            )
-        )
-    for copy in copies:
-        copy.start()
     tiles = gram_ref.shape[0] // 2
 
     def columns_of(part, core):
@@ -284,15 +271,13 @@
     outs = []
     for q in range(count):
         columns = slice(CHIP * q, CHIP * q + CHIP)
-        copies[2 * q].wait()
-        copies[2 * q + 1].wait()
-        head_high, head_low = split(heads[:, columns])
-        result = jnp.where(follows, later[:, columns], 0.0)
+        head_high, head_low = split(shared_ref[q, 0:HEAD, :])
+        result = jnp.where(follows, shared_ref[q, HEAD:, :], 0.0)
         results[:, columns] = result + dot3(weight_high, weight_low, head_high, head_low)
         out = pltpu.make_async_copy(
             results.at[:, pl.ds(CHIP * q, CHIP)],
             basis_ref.at[:, pl.ds(CHIP * q, CHIP)],
-            sems.at[2 * count + q],
+            sems.at[q],
         )
         out.start()
         outs.append(out)
@@ -332,6 +317,7 @@
     chip_count = lax.axis_size(chips)
     planes = lax.axis_size(plane)
     depth = lax.axis_size("z")
+    count = lax.axis_size("x")
 
     def shift(value, step):
         return lax.ppermute(value, chips, [(i, (i + step) % chip_count) for i in range(chip_count)])
@@ -360,27 +346,27 @@
     other = lax.ppermute(lead, "core", [(0, 1), (1, 0)])
     core = lax.axis_index("core").reshape(1)
     gram, shared = call(
-        gram_kernel, "gram", (shape((OWN // 128, HEAD, 128), F32), shape((SHARED, CHIP), F32)),
+        gram_kernel, "gram", (shape((OWN // 128, HEAD, 128), F32), shape((count, SHARED, CHIP), F32)),
         (core, lead, other, applied), (), [SMEM] + [VMEM] * 3,
     )
-    shared = lax.all_gather(shared, "x")
     piece = (OWN // 128) * HEAD // planes
     everyone = planes * CORES
     gram = exchange(gram.reshape(planes, piece, 128), plane)
-    gram = exchange(call(sum_kernel, "sum_plane", shape((depth, piece, 128), F32), (gram,)), "z")
+    gram = call(sum_kernel, "sum_plane", shape((depth, piece, 128), F32), (gram,))
+    gram, shared = lax.optimization_barrier((gram, shared))
+    shared = exchange(shared, "x")
+    gram = exchange(gram, "z")
     gram = call(sum_kernel, "sum_depth", shape((everyone, piece, 128), F32), (gram,))
     gram = exchange(gram, (*plane, "core"))
     gram = gram.reshape(planes, CORES, piece, 128)
     scale = 1.0 / (CHIP * chip_count)
-    count = lax.axis_size("x")
     slab_width = CHIP * count
     place = jnp.stack([lax.axis_index("x"), lax.axis_index("core")])
     return call(
         lambda *refs: finish_kernel(scale, *refs), "finish", shape((BLOCK, slab_width), F32),
         (place, gram, shared),
-        [pltpu.VMEM((HEAD, slab_width), F32)] + [pltpu.VMEM((BLOCK, slab_width), F32)] * 2
-        + [pltpu.SemaphoreType.DMA((3 * count,))],
-        [SMEM, VMEM, RAW], RAW,
+        [pltpu.VMEM((BLOCK, slab_width), F32), pltpu.SemaphoreType.DMA((count,))],
+        [SMEM, VMEM, VMEM], RAW,
     )
 
 

time: 124 us -> 138 us (1.11)
  blocking collectives: 36 us -> 54.1 us
  waiting for transfers between devices: 28.9 us -> 44.7 us
  between operations: 13.5 us -> 0.09 us
  starting transfers between devices: 24.3 us -> 19.3 us
  Pallas kernels: 20.3 us -> 18.2 us
    all_to_all x3 -> x4, blocking collectives: 36 us -> 54.1 us  [exchange(): return lax.all_to_all(value, axes, split_axis=0, concat_axis=0, tiled=True)]
    all_to_all x1, waiting for transfers between devices: 10.2 us -> 26 us  [exchange(): return lax.all_to_all(value, axes, split_axis=0, concat_axis=0, tiled=True)]
    all_to_all x1, starting transfers between devices: 8.56 us -> 3.61 us  [exchange(): return lax.all_to_all(value, axes, split_axis=0, concat_axis=0, tiled=True)]
    pallas_call x7, Pallas kernels: 20.3 us -> 18.2 us  [call(): pl.pallas_call(kernel, out_shape=out_shape, in_specs=specs or [VMEM] * le...]
  transfers between devices with their start and end apart: 5 -> 4, of which waited for: 4 -> 4; matrix products, arithmetic and copies ran while one was open for 0% -> 0% of each run, Pallas kernels for 3% -> 2%
where the time goes in v6:
time: 138 us
  blocking collectives  54.1 us (39%)
  waiting for transfers between devices  44.7 us (32%)
  starting transfers between devices  19.3 us (14%)
  Pallas kernels  18.2 us (13%)
    all_to_all x4, blocking collectives, exchange(): return lax.all_to_all(value, axes, split_axis=0, concat_axis=0, tiled=True)  54.1 us
    all_to_all x1, waiting for transfers between devices, exchange(): return lax.all_to_all(value, axes, split_axis=0, concat_axis=0, tiled=True)  26 us
    pallas_call x7, Pallas kernels, call(): pl.pallas_call(kernel, out_shape=out_shape, in_specs=specs or [VMEM] * le...  18.2 us
    ppermute x2, waiting for transfers between devices, shift(): lax.ppermute(value, chips, [(i, (i + step) % chip_count) for i in range(c...  17.6 us
    ppermute x2, starting transfers between devices, shift(): lax.ppermute(value, chips, [(i, (i + step) % chip_count) for i in range(c...  12.3 us
    all_to_all x1, starting transfers between devices, exchange(): return lax.all_to_all(value, axes, split_axis=0, concat_axis=0, tiled=True)  3.61 us
    ppermute x1, starting transfers between devices, on_device(): other = lax.ppermute(lead, 'core', [(0, 1), (1, 0)])  3.43 us
  transfers between devices with their start and end apart: 4, of which 4 were waited for; matrix products, arithmetic and copies ran while one was open for 0% of the time, Pallas kernels for 2%

profile of v6, /device:TPU:1, one launch (start us, length us, event | category | flops | bytes accessed | tf_op | source)
XLA Modules:
  0.0 137.8 jit_solution(17943731226195010742)
XLA Ops:
  0.0 1.2 pack.1
  1.2 10.7 %all_to_all.25.slab_ref.own_ref = f32[2,296,256]{2,1,0:T(8,128)S(1)} all-to-all(f32[2,296,256]{2,1,0:T(8,128)S(1)} %pack.1), channel_id=1, replica_groups=mesh['y'=4,'z'=16,'x'=4,'core'=2] {'core'}, dimensions={0} | all-to-all | bytes 1212416 | tf_op jit(solution)/shard_map/all_to_all | solution.py:289
  11.9 10.4 %collective-permute-start.1 = (f32[2,296,256]{2,1,0:T(8,128)S(1)}, f32[2,296,256]{2,1,0:T(8,128)S(1)}, u32[]{:S(2)}, u32[]{:S(2)}) collective-permute-start(f32[2,296,256]{2,1,0:T(8,128)S(1)} %all_to_all.25.slab_ref.own_ref), channel_id=1, source_target_pairs={{0,510},{2,0},{4,2},{6,4},{8,6},{10,8},{12,10},{14,12},{16,14},{18... | collective-permute-start | bytes 1818632 | tf_op jit(solution)/shard_map/ppermute | solution.py:323
  22.3 1.9 %collective-permute-start = (f32[2,296,256]{2,1,0:T(8,128)S(1)}, f32[2,296,256]{2,1,0:T(8,128)S(1)}, u32[]{:S(2)}, u32[]{:S(2)}) collective-permute-start(f32[2,296,256]{2,1,0:T(8,128)S(1)} %all_to_all.25.slab_ref.own_ref), channel_id=1, source_target_pairs={{0,2},{2,4},{4,6},{6,8},{8,10},{10,12},{12,14},{14,16},{16,18},{18... | collective-permute-start | bytes 1818632 | tf_op jit(solution)/shard_map/ppermute | solution.py:323
  24.3 2.4 %own_matrix.1 = (bf16[768,256]{1,0:T(8,128)(2,1)S(1)}, bf16[768,256]{1,0:T(8,128)(2,1)S(1)}, bf16[768,256]{1,0:T(8,128)(2,1)S(1)}, bf16[768,256]{1,0:T(8,128)(2,1)S(1)}) custom-call(f32[2,296,256]{2,1,0:T(8,128)S(1)} %all_to_all.25.slab_ref.own_ref), custom_call_target="tpu_custom_call" | custom-call | tf_op jit(solution)/shard_map/own_matrix/pallas_call | solution.py:303
  26.6 8.4 %collective-permute-done.1.right_ref = f32[2,296,256]{2,1,0:T(8,128)S(1)} collective-permute-done((f32[2,296,256]{2,1,0:T(8,128)S(1)}, f32[2,296,256]{2,1,0:T(8,128)S(1)}, u32[]{:S(2)}, u32[]{:S(2)}) %collective-permute-start.1) | collective-permute-done | bytes 606240 | tf_op jit(solution)/shard_map/ppermute | solution.py:323
  35.0 9.2 %collective-permute-done.left_ref = f32[2,296,256]{2,1,0:T(8,128)S(1)} collective-permute-done((f32[2,296,256]{2,1,0:T(8,128)S(1)}, f32[2,296,256]{2,1,0:T(8,128)S(1)}, u32[]{:S(2)}, u32[]{:S(2)}) %collective-permute-start) | collective-permute-done | bytes 606240 | tf_op jit(solution)/shard_map/ppermute | solution.py:323
  44.2 4.4 %apply_twice.1 = (f32[256,512]{1,0:T(8,128)S(1)}, f32[128,512]{1,0:T(8,128)S(1)}) custom-call(f32[2,296,256]{2,1,0:T(8,128)S(1)} %collective-permute-done.left_ref, f32[2,296,256]{2,1,0:T(8,128)S(1)} %all_to_all.25.slab_ref.own_ref, f32[2,296,256]{2,1,0:T(8,128)S(1)} %collective-permute-done.1.right_ref, ...), custom_call_target="tpu_custom_call" | custom-call | tf_op jit(solution)/shard_map/apply_twice/pallas_call | solution.py:303
  48.6 3.4 %collective-permute-start.2 = (f32[128,512]{1,0:T(8,128)S(1)}, f32[128,512]{1,0:T(8,128)S(1)}, u32[]{:S(2)}, u32[]{:S(2)}) collective-permute-start(f32[128,512]{1,0:T(8,128)S(1)} %get-tuple-element.19.lead_ref), channel_id=1, source_target_pairs={{0,1},{1,0},{2,3},{3,2},{4,5},{5,4},{6,7},{7,6},{8,9},{9,8},{10,11... | collective-permute-start | bytes 786440 | tf_op jit(solution)/shard_map/ppermute | solution.py:346
  52.0 1.1 collective-permute-done.2.other_ref
  53.2 0.8 gram.1
  54.0 0.0 copy-start
  54.0 1.3 copy-done
  55.3 10.3 %all_to_all.26.pieces_ref = f32[16,24,128]{2,1,0:T(8,128)S(1)} all-to-all(f32[16,24,128]{2,1,0:T(8,128)S(1)} %bitcast.6), channel_id=1, replica_groups=mesh['y'=4,'z'=16,'x'=4,'core'=2] {'y','x'}, dimensions={0} | all-to-all | bytes 393216 | tf_op jit(solution)/shard_map/all_to_all | solution.py:289
  65.6 15.0 %all_to_all.27.pieces_ref = f32[16,24,128]{2,1,0:T(8,128)S(1)} all-to-all(f32[16,24,128]{2,1,0:T(8,128)S(1)} %sum_plane.1), channel_id=1, replica_groups=mesh['y'=4,'z'=16,'x'=4,'core'=2] {'z'}, dimensions={0} | all-to-all | bytes 393216 | tf_op jit(solution)/shard_map/all_to_all | solution.py:289
  80.7 18.1 %all_to_all.28 = f32[32,24,128]{2,1,0:T(8,128)S(1)} all-to-all(f32[32,24,128]{2,1,0:T(8,128)S(1)} %sum_depth.1), channel_id=1, replica_groups=mesh['y'=4,'z'=16,'x'=4,'core'=2] {'y','x','core'}, dimensions={0} | all-to-all | bytes 786432 | tf_op jit(solution)/shard_map/all_to_all | solution.py:289
  98.8 3.6 %all-to-all-start.4 = ((f32[4,256,512]{2,1,0:T(8,128)}), f32[4,256,512]{2,1,0:T(8,128)S(1)}, u32[]{:S(2)}, u32[]{:S(2)}) async-start(f32[4,256,512]{2,1,0:T(8,128)} %copy-done), calls=%async_computation.4 | async-start | bytes 4194304 | tf_op jit(solution)/shard_map/all_to_all | solution.py:289
  102.4 0.1 pad_add_fusion.refs_0_
  102.5 26.0 %all-to-all-done.4.refs_2_ = f32[4,256,512]{2,1,0:T(8,128)S(1)} async-done(((f32[4,256,512]{2,1,0:T(8,128)}), f32[4,256,512]{2,1,0:T(8,128)S(1)}, u32[]{:S(2)}, u32[]{:S(2)}) %all-to-all-start.4) | async-done | bytes 2097184 | tf_op jit(solution)/shard_map/all_to_all | solution.py:289
  128.5 9.4 %finish.1 = f32[64,2048]{1,0:T(8,128)} custom-call(s32[2]{0:T(128)S(1)} %pad_add_fusion.refs_0_, f32[16,2,24,128]{3,2,1,0:T(8,128)S(1)} %bitcast.5, f32[4,256,512]{2,1,0:T(8,128)S(1)} %all-to-all-done.4.refs_2_), custom_call_target="tpu_custom_call" | custom-call | tf_op jit(solution)/shard_map/finish/pallas_call | solution.py:303
  (2 shorter events, 0.1 us)
Async XLA Ops:
  11.9 23.1 %collective-permute-start.1 = (f32[2,296,256]{2,1,0:T(8,128)S(1)}, f32[2,296,256]{2,1,0:T(8,128)S(1)}, u32[]{:S(2)}, u32[]{:S(2)}) collective-permute-start(f32[2,296,256]{2,1,0:T(8,128)S(1)} %all_to_all.25.slab_ref.own_ref), channel_id=1, source_target_pairs={{0,510},{2,0},{4,2},{6,4},{8,6},{10,8},{12,10},{14,12},{16,14},{18... | collective-permute-start | bytes 1818632 | tf_op jit(solution)/shard_map/ppermute | solution.py:323
  22.3 21.9 %collective-permute-start = (f32[2,296,256]{2,1,0:T(8,128)S(1)}, f32[2,296,256]{2,1,0:T(8,128)S(1)}, u32[]{:S(2)}, u32[]{:S(2)}) collective-permute-start(f32[2,296,256]{2,1,0:T(8,128)S(1)} %all_to_all.25.slab_ref.own_ref), channel_id=1, source_target_pairs={{0,2},{2,4},{4,6},{6,8},{8,10},{10,12},{12,14},{14,16},{16,18},{18... | collective-permute-start | bytes 1818632 | tf_op jit(solution)/shard_map/ppermute | solution.py:323
  48.6 4.6 %collective-permute-start.2 = (f32[128,512]{1,0:T(8,128)S(1)}, f32[128,512]{1,0:T(8,128)S(1)}, u32[]{:S(2)}, u32[]{:S(2)}) collective-permute-start(f32[128,512]{1,0:T(8,128)S(1)} %get-tuple-element.19.lead_ref), channel_id=1, source_target_pairs={{0,1},{1,0},{2,3},{3,2},{4,5},{5,4},{6,7},{7,6},{8,9},{9,8},{10,11... | collective-permute-start | bytes 786440 | tf_op jit(solution)/shard_map/ppermute | solution.py:346
  54.0 1.3 copy-start
  98.8 29.7 %all-to-all-start.4 = ((f32[4,256,512]{2,1,0:T(8,128)}), f32[4,256,512]{2,1,0:T(8,128)S(1)}, u32[]{:S(2)}, u32[]{:S(2)}) async-start(f32[4,256,512]{2,1,0:T(8,128)} %copy-done), calls=%async_computation.4 | async-start | bytes 4194304 | tf_op jit(solution)/shard_map/all_to_all | solution.py:289

commit v7 on v6

--- a/solution.py
+++ b/solution.py
@@ -171,18 +171,19 @@
         lead_ref[:, columns] = twice[0 : 2 * BLOCK]
 
 
-def gram_kernel(core_ref, lead_ref, other_ref, applied_ref, gram_ref, shared_ref):
-    second = core_ref[0] == 1
-    count = shared_ref.shape[0]
+def gram_kernel(place_ref, lead_ref, other_ref, applied_ref, gram_ref, *shared_refs):
+    chip, second = place_ref[0], place_ref[1] == 1
+    count = len(shared_refs)
     for s, place, core in ((0, 0, 0), (1, 0, 1), (2, BLOCK, 0)):
         mine, theirs = lead_ref[place : place + BLOCK, :], other_ref[place : place + BLOCK, :]
         pair = (mine, theirs) if core else (theirs, mine)
         block = jnp.where(second, *pair)
-        for q in range(count):
-            shared_ref[q, BLOCK * s : BLOCK * s + BLOCK, :] = block
-    for q in range(count):
-        shared_ref[q, HEAD:, :] = applied_ref[BLOCK * q : BLOCK * q + BLOCK, :]
-    gram = dot32(shared_ref[0, 0:HEAD, :], applied_ref[...], ((1,), (1,)))
+        for ref in shared_refs:
+            ref[BLOCK * s : BLOCK * s + BLOCK, :] = block
+    for step, ref in enumerate(shared_refs):
+        start = pl.multiple_of(lax.rem(chip + step, count) * BLOCK, BLOCK)
+        ref[HEAD:, :] = applied_ref[pl.ds(start, BLOCK), :]
+    gram = dot32(shared_refs[0][0:HEAD, :], applied_ref[...], ((1,), (1,)))
     for part in range(OWN // 128):
         gram_ref[part] = gram[:, 128 * part : 128 * part + 128]
 
@@ -221,11 +222,12 @@
     )
 
 
-def finish_kernel(scale, place_ref, gram_ref, shared_ref, basis_ref, results, sems):
+def finish_kernel(scale, place_ref, gram_ref, *refs):
+    *shared_refs, basis_ref, results, sems = refs
     chip, core = place_ref[0], place_ref[1]
     second = core == 1
     column = CORES * chip + core
-    count = shared_ref.shape[0]
+    count = len(shared_refs)
     tiles = gram_ref.shape[0] // 2
 
     def columns_of(part, core):
@@ -269,16 +271,13 @@
         weights[s] = dot32(inverses[s], weight, ((0,), (0,)))
     weight_high, weight_low = split(jnp.concatenate(weights, axis=0).T)
     outs = []
-    for q in range(count):
-        columns = slice(CHIP * q, CHIP * q + CHIP)
-        head_high, head_low = split(shared_ref[q, 0:HEAD, :])
-        result = jnp.where(follows, shared_ref[q, HEAD:, :], 0.0)
-        results[:, columns] = result + dot3(weight_high, weight_low, head_high, head_low)
-        out = pltpu.make_async_copy(
-            results.at[:, pl.ds(CHIP * q, CHIP)],
-            basis_ref.at[:, pl.ds(CHIP * q, CHIP)],
-            sems.at[q],
-        )
+    for step, ref in enumerate(shared_refs):
+        head_high, head_low = split(ref[0:HEAD, :])
+        result = jnp.where(follows, ref[HEAD:, :], 0.0)
+        results[step] = result + dot3(weight_high, weight_low, head_high, head_low)
+        source = lax.rem(chip + count - step, count)
+        columns = pl.ds(pl.multiple_of(source * CHIP, CHIP), CHIP)
+        out = pltpu.make_async_copy(results.at[step], basis_ref.at[:, columns], sems.at[step])
         out.start()
         outs.append(out)
     for out in outs:
@@ -344,29 +343,32 @@
         [pltpu.VMEM((OWN, 3 * CHIP), BF16)] * 2 + [pltpu.VMEM((OWN, 2 * CHIP), BF16)] * 2 + [wide] * 4,
     )
     other = lax.ppermute(lead, "core", [(0, 1), (1, 0)])
-    core = lax.axis_index("core").reshape(1)
-    gram, shared = call(
-        gram_kernel, "gram", (shape((OWN // 128, HEAD, 128), F32), shape((count, SHARED, CHIP), F32)),
-        (core, lead, other, applied), (), [SMEM] + [VMEM] * 3,
+    place = jnp.stack([lax.axis_index("x"), lax.axis_index("core")])
+    gram, *shared = call(
+        gram_kernel, "gram",
+        (shape((OWN // 128, HEAD, 128), F32),) + (shape((SHARED, CHIP), F32),) * count,
+        (place, lead, other, applied), (), [SMEM] + [VMEM] * 3,
     )
     piece = (OWN // 128) * HEAD // planes
     everyone = planes * CORES
     gram = exchange(gram.reshape(planes, piece, 128), plane)
     gram = call(sum_kernel, "sum_plane", shape((depth, piece, 128), F32), (gram,))
-    gram, shared = lax.optimization_barrier((gram, shared))
-    shared = exchange(shared, "x")
+    gram, *shared = lax.optimization_barrier((gram, *shared))
+    shared = [shared[0]] + [
+        lax.ppermute(shared[step], "x", [(i, (i + step) % count) for i in range(count)])
+        for step in range(1, count)
+    ]
     gram = exchange(gram, "z")
     gram = call(sum_kernel, "sum_depth", shape((everyone, piece, 128), F32), (gram,))
     gram = exchange(gram, (*plane, "core"))
     gram = gram.reshape(planes, CORES, piece, 128)
     scale = 1.0 / (CHIP * chip_count)
     slab_width = CHIP * count
-    place = jnp.stack([lax.axis_index("x"), lax.axis_index("core")])
     return call(
         lambda *refs: finish_kernel(scale, *refs), "finish", shape((BLOCK, slab_width), F32),
-        (place, gram, shared),
-        [pltpu.VMEM((BLOCK, slab_width), F32), pltpu.SemaphoreType.DMA((count,))],
-        [SMEM, VMEM, VMEM], RAW,
+        (place, gram, *shared),
+        [pltpu.VMEM((count, BLOCK, CHIP), F32), pltpu.SemaphoreType.DMA((count,))],
+        [SMEM] + [VMEM] * (1 + count), RAW,
     )
 
 

time: 138 us -> 113 us (0.82)
  blocking collectives: 54.1 us -> 21 us
  starting transfers between devices: 19.3 us -> 43.2 us
  waiting for transfers between devices: 44.7 us -> 27.3 us
  Pallas kernels: 18.2 us -> 20.8 us
    all_to_all x4 -> x2, blocking collectives: 54.1 us -> 21 us  [exchange(): return lax.all_to_all(value, axes, split_axis=0, concat_axis=0, tiled=True)]
    all_to_all x1 -> x2, waiting for transfers between devices: 26 us -> 7.58 us  [exchange(): return lax.all_to_all(value, axes, split_axis=0, concat_axis=0, tiled=True)]
    all_to_all x1 -> x2, starting transfers between devices: 3.61 us -> 18.9 us  [exchange(): return lax.all_to_all(value, axes, split_axis=0, concat_axis=0, tiled=True)]
    ppermute x0 -> x3, starting transfers between devices: none -> 8.87 us  [on_device(): lax.ppermute(shared[step], 'x', [(i, (i + step) % count) for i in range(c...]
    ppermute x0 -> x3, waiting for transfers between devices: none -> 8.35 us  [on_device(): lax.ppermute(shared[step], 'x', [(i, (i + step) % count) for i in range(c...]
    ppermute x2, waiting for transfers between devices: 17.6 us -> 10.3 us  [shift(): lax.ppermute(value, chips, [(i, (i + step) % chip_count) for i in range(c...]
    pallas_call x7, Pallas kernels: 18.2 us -> 20.8 us  [call(): pl.pallas_call(kernel, out_shape=out_shape, in_specs=specs or [VMEM] * le...]
  transfers between devices with their start and end apart: 4 -> 8, of which waited for: 4 -> 7; matrix products, arithmetic and copies ran while one was open for 0% -> 0% of each run, Pallas kernels for 2% -> 3%
where the time goes in v7:
time: 113 us; the launch traced here: 112 us
  starting transfers between devices  43.2 us (38%)
  waiting for transfers between devices  27.3 us (24%)
  blocking collectives  21 us (19%)
  Pallas kernels  20.8 us (18%)
    all_to_all x2, blocking collectives, exchange(): return lax.all_to_all(value, axes, split_axis=0, concat_axis=0, tiled=True)  21 us
    pallas_call x7, Pallas kernels, call(): pl.pallas_call(kernel, out_shape=out_shape, in_specs=specs or [VMEM] * le...  20.8 us
    all_to_all x2, starting transfers between devices, exchange(): return lax.all_to_all(value, axes, split_axis=0, concat_axis=0, tiled=True)  18.9 us
    ppermute x2, starting transfers between devices, shift(): lax.ppermute(value, chips, [(i, (i + step) % chip_count) for i in range(c...  12.3 us
    ppermute x2, waiting for transfers between devices, shift(): lax.ppermute(value, chips, [(i, (i + step) % chip_count) for i in range(c...  10.3 us
    ppermute x3, starting transfers between devices, on_device(): lax.ppermute(shared[step], 'x', [(i, (i + step) % count) for i in range(c...  8.87 us
    ppermute x3, waiting for transfers between devices, on_device(): lax.ppermute(shared[step], 'x', [(i, (i + step) % count) for i in range(c...  8.35 us
    all_to_all x2, waiting for transfers between devices, exchange(): return lax.all_to_all(value, axes, split_axis=0, concat_axis=0, tiled=True)  7.58 us
  transfers between devices with their start and end apart: 8, of which 7 were waited for; matrix products, arithmetic and copies ran while one was open for 0% of the time, Pallas kernels for 3%

profile of v7, /device:TPU:1, one launch (start us, length us, event | category | flops | bytes accessed | tf_op | source)
XLA Modules:
  0.0 112.4 jit_solution(17172184370101571945)
XLA Ops:
  0.0 1.2 %pack.1 = f32[2,296,256]{2,1,0:T(8,128)S(1)} custom-call(f32[512,256]{1,0:T(8,128)} %vectors_ref.1, f32[16,256]{1,0:T(8,128)} %cosines_ref.1, f32[16,256]{1,0:T(8,128)} %distances_ref.1, s32[16,256]{1,0:T(8,128)} %offsets_ref.1, s32[1,256]{1,0:T(1,128)} %bitcast.7, s32[2,256]{1,0:T(2,128)} %labels_ref.1), custom_call_target="tpu_custom_call" | custom-call | tf_op jit(solution)/shard_map/pack/pallas_call | solution.py:302
  1.2 10.7 %all_to_all.20.slab_ref.own_ref = f32[2,296,256]{2,1,0:T(8,128)S(1)} all-to-all(f32[2,296,256]{2,1,0:T(8,128)S(1)} %pack.1), channel_id=1, replica_groups=mesh['y'=4,'z'=16,'x'=4,'core'=2] {'core'}, dimensions={0} | all-to-all | bytes 1212416 | tf_op jit(solution)/shard_map/all_to_all | solution.py:288
  11.9 1.9 %collective-permute-start = (f32[2,296,256]{2,1,0:T(8,128)S(1)}, f32[2,296,256]{2,1,0:T(8,128)S(1)}, u32[]{:S(2)}, u32[]{:S(2)}) collective-permute-start(f32[2,296,256]{2,1,0:T(8,128)S(1)} %all_to_all.20.slab_ref.own_ref), channel_id=1, source_target_pairs={{0,2},{2,4},{4,6},{6,8},{8,10},{10,12},{12,14},{14,16},{16,18},{18... | collective-permute-start | bytes 1818632 | tf_op jit(solution)/shard_map/ppermute | solution.py:322
  13.9 10.4 %collective-permute-start.1 = (f32[2,296,256]{2,1,0:T(8,128)S(1)}, f32[2,296,256]{2,1,0:T(8,128)S(1)}, u32[]{:S(2)}, u32[]{:S(2)}) collective-permute-start(f32[2,296,256]{2,1,0:T(8,128)S(1)} %all_to_all.20.slab_ref.own_ref), channel_id=1, source_target_pairs={{0,510},{2,0},{4,2},{6,4},{8,6},{10,8},{12,10},{14,12},{16,14},{18... | collective-permute-start | bytes 1818632 | tf_op jit(solution)/shard_map/ppermute | solution.py:322
  24.3 2.4 %own_matrix.1 = (bf16[768,256]{1,0:T(8,128)(2,1)S(1)}, bf16[768,256]{1,0:T(8,128)(2,1)S(1)}, bf16[768,256]{1,0:T(8,128)(2,1)S(1)}, bf16[768,256]{1,0:T(8,128)(2,1)S(1)}) custom-call(f32[2,296,256]{2,1,0:T(8,128)S(1)} %all_to_all.20.slab_ref.own_ref), custom_call_target="tpu_custom_call" | custom-call | tf_op jit(solution)/shard_map/own_matrix/pallas_call | solution.py:302
  26.6 9.4 %collective-permute-done.left_ref = f32[2,296,256]{2,1,0:T(8,128)S(1)} collective-permute-done((f32[2,296,256]{2,1,0:T(8,128)S(1)}, f32[2,296,256]{2,1,0:T(8,128)S(1)}, u32[]{:S(2)}, u32[]{:S(2)}) %collective-permute-start) | collective-permute-done | bytes 606240 | tf_op jit(solution)/shard_map/ppermute | solution.py:322
  36.1 0.9 collective-permute-done.1.right_ref
  36.9 4.4 %apply_twice.1 = (f32[256,512]{1,0:T(8,128)S(1)}, f32[128,512]{1,0:T(8,128)S(1)}) custom-call(f32[2,296,256]{2,1,0:T(8,128)S(1)} %collective-permute-done.left_ref, f32[2,296,256]{2,1,0:T(8,128)S(1)} %all_to_all.20.slab_ref.own_ref, f32[2,296,256]{2,1,0:T(8,128)S(1)} %collective-permute-done.1.right_ref, ...), custom_call_target="tpu_custom_call" | custom-call | tf_op jit(solution)/shard_map/apply_twice/pallas_call | solution.py:302
  41.3 3.1 %collective-permute-start.2 = (f32[128,512]{1,0:T(8,128)S(1)}, f32[128,512]{1,0:T(8,128)S(1)}, u32[]{:S(2)}, u32[]{:S(2)}) collective-permute-start(f32[128,512]{1,0:T(8,128)S(1)} %get-tuple-element.25.lead_ref), channel_id=1, source_target_pairs={{0,1},{1,0},{2,3},{3,2},{4,5},{5,4},{6,7},{7,6},{8,9},{9,8},{10,11... | collective-permute-start | bytes 786440 | tf_op jit(solution)/shard_map/ppermute | solution.py:345
  44.4 0.1 pad_add_fusion.place_ref.refs_0_
  44.5 1.1 collective-permute-done.2.other_ref
  45.6 2.0 %gram.1 = (f32[2,192,128]{2,1,0:T(8,128)S(1)}, f32[256,512]{1,0:T(8,128)S(1)}, f32[256,512]{1,0:T(8,128)}, f32[256,512]{1,0:T(8,128)S(1)}, f32[256,512]{1,0:T(8,128)S(1)}) custom-call(s32[2]{0:T(128)S(1)} %pad_add_fusion.place_ref.refs_0_, f32[128,512]{1,0:T(8,128)S(1)} %get-tuple-element.25.lead_ref, f32[128,512]{1,0:T(8,128)S(1)} %collective-permute-done.2.other_ref, ...), custom_call_target="tpu_custom_call" | custom-call | tf_op jit(solution)/shard_map/gram/pallas_call | solution.py:302
  47.5 10.3 %all_to_all.21.pieces_ref = f32[16,24,128]{2,1,0:T(8,128)S(1)} all-to-all(f32[16,24,128]{2,1,0:T(8,128)S(1)} %bitcast.6), channel_id=1, replica_groups=mesh['y'=4,'z'=16,'x'=4,'core'=2] {'y','x'}, dimensions={0} | all-to-all | bytes 393216 | tf_op jit(solution)/shard_map/all_to_all | solution.py:288
  57.8 0.7 sum_plane.1
  58.5 9.9 %all-to-all-start.2 = ((f32[16,24,128]{2,1,0:T(8,128)}), f32[16,24,128]{2,1,0:T(8,128)S(1)}, u32[]{:S(2)}, u32[]{:S(2)}) async-start(f32[16,24,128]{2,1,0:T(8,128)} %sum_plane.1), calls=%async_computation.2 | async-start | bytes 393216 | tf_op jit(solution)/shard_map/all_to_all | solution.py:288
  68.5 2.5 %collective-permute-start.3 = (f32[256,512]{1,0:T(8,128)}, f32[256,512]{1,0:T(8,128)S(1)}, u32[]{:S(2)}, u32[]{:S(2)}) collective-permute-start(f32[256,512]{1,0:T(8,128)} %get-tuple-element.34), channel_id=1, source_target_pairs={{0,2},{2,4},{4,6},{6,0},{1,3},{3,5},{5,7},{7,1},{8,10},{10,12},{12... | collective-permute-start | bytes 1572872 | tf_op jit(solution)/shard_map/ppermute | solution.py:358
  71.0 3.2 %collective-permute-start.4 = (f32[256,512]{1,0:T(8,128)S(1)}, f32[256,512]{1,0:T(8,128)S(1)}, u32[]{:S(2)}, u32[]{:S(2)}) collective-permute-start(f32[256,512]{1,0:T(8,128)S(1)} %get-tuple-element.35), channel_id=1, source_target_pairs={{0,4},{2,6},{4,0},{6,2},{1,5},{3,7},{5,1},{7,3},{8,12},{10,14},{12... | collective-permute-start | bytes 1572872 | tf_op jit(solution)/shard_map/ppermute | solution.py:358
  74.2 3.2 %collective-permute-start.5 = (f32[256,512]{1,0:T(8,128)S(1)}, f32[256,512]{1,0:T(8,128)S(1)}, u32[]{:S(2)}, u32[]{:S(2)}) collective-permute-start(f32[256,512]{1,0:T(8,128)S(1)} %get-tuple-element.36), channel_id=1, source_target_pairs={{0,6},{2,0},{4,2},{6,4},{1,7},{3,1},{5,3},{7,5},{8,14},{10,8},{12,... | collective-permute-start | bytes 1572872 | tf_op jit(solution)/shard_map/ppermute | solution.py:358
  77.4 3.4 %all-to-all-done.2.pieces_ref = f32[16,24,128]{2,1,0:T(8,128)S(1)} async-done(((f32[16,24,128]{2,1,0:T(8,128)}), f32[16,24,128]{2,1,0:T(8,128)S(1)}, u32[]{:S(2)}, u32[]{:S(2)}) %all-to-all-start.2) | async-done | bytes 196640 | tf_op jit(solution)/shard_map/all_to_all | solution.py:288
  80.8 0.8 sum_depth.1
  81.6 9.0 %all-to-all-start.3 = ((f32[32,24,128]{2,1,0:T(8,128)}), f32[32,24,128]{2,1,0:T(8,128)S(1)}, u32[]{:S(2)}, u32[]{:S(2)}) async-start(f32[32,24,128]{2,1,0:T(8,128)} %sum_depth.1), calls=%async_computation.3 | async-start | bytes 786432 | tf_op jit(solution)/shard_map/all_to_all | solution.py:288
  90.6 0.0 collective-permute-done.3.refs_3_
  90.6 3.1 %collective-permute-done.4.refs_4_ = f32[256,512]{1,0:T(8,128)S(1)} collective-permute-done((f32[256,512]{1,0:T(8,128)S(1)}, f32[256,512]{1,0:T(8,128)S(1)}, u32[]{:S(2)}, u32[]{:S(2)}) %collective-permute-start.4) | collective-permute-done | bytes 524320 | tf_op jit(solution)/shard_map/ppermute | solution.py:358
  93.7 5.2 %collective-permute-done.5.refs_5_ = f32[256,512]{1,0:T(8,128)S(1)} collective-permute-done((f32[256,512]{1,0:T(8,128)S(1)}, f32[256,512]{1,0:T(8,128)S(1)}, u32[]{:S(2)}, u32[]{:S(2)}) %collective-permute-start.5) | collective-permute-done | bytes 524320 | tf_op jit(solution)/shard_map/ppermute | solution.py:358
  98.9 4.1 %all-to-all-done.3 = f32[32,24,128]{2,1,0:T(8,128)S(1)} async-done(((f32[32,24,128]{2,1,0:T(8,128)}), f32[32,24,128]{2,1,0:T(8,128)S(1)}, u32[]{:S(2)}, u32[]{:S(2)}) %all-to-all-start.3) | async-done | bytes 393248 | tf_op jit(solution)/shard_map/all_to_all | solution.py:288
  103.1 9.4 %finish.1 = f32[64,2048]{1,0:T(8,128)} custom-call(s32[2]{0:T(128)S(1)} %pad_add_fusion.place_ref.refs_0_, f32[16,2,24,128]{3,2,1,0:T(8,128)S(1)} %bitcast.5, f32[256,512]{1,0:T(8,128)S(1)} %get-tuple-element.33.refs_2_, f32[256,512]{1,0:T(8,128)S(1)} %collective-permute-done.3.refs_3_, f32[256,512]{1,0:T(8,128)S(1)} %collective-permute-done.4.refs_4_, ...), custom_call_target="tpu_custom_call" | custom-call | tf_op jit(solution)/shard_map/finish/pallas_call | solution.py:302
Async XLA Ops:
  11.9 24.1 %collective-permute-start = (f32[2,296,256]{2,1,0:T(8,128)S(1)}, f32[2,296,256]{2,1,0:T(8,128)S(1)}, u32[]{:S(2)}, u32[]{:S(2)}) collective-permute-start(f32[2,296,256]{2,1,0:T(8,128)S(1)} %all_to_all.20.slab_ref.own_ref), channel_id=1, source_target_pairs={{0,2},{2,4},{4,6},{6,8},{8,10},{10,12},{12,14},{14,16},{16,18},{18... | collective-permute-start | bytes 1818632 | tf_op jit(solution)/shard_map/ppermute | solution.py:322
  13.9 23.1 %collective-permute-start.1 = (f32[2,296,256]{2,1,0:T(8,128)S(1)}, f32[2,296,256]{2,1,0:T(8,128)S(1)}, u32[]{:S(2)}, u32[]{:S(2)}) collective-permute-start(f32[2,296,256]{2,1,0:T(8,128)S(1)} %all_to_all.20.slab_ref.own_ref), channel_id=1, source_target_pairs={{0,510},{2,0},{4,2},{6,4},{8,6},{10,8},{12,10},{14,12},{16,14},{18... | collective-permute-start | bytes 1818632 | tf_op jit(solution)/shard_map/ppermute | solution.py:322
  41.3 4.3 %collective-permute-start.2 = (f32[128,512]{1,0:T(8,128)S(1)}, f32[128,512]{1,0:T(8,128)S(1)}, u32[]{:S(2)}, u32[]{:S(2)}) collective-permute-start(f32[128,512]{1,0:T(8,128)S(1)} %get-tuple-element.25.lead_ref), channel_id=1, source_target_pairs={{0,1},{1,0},{2,3},{3,2},{4,5},{5,4},{6,7},{7,6},{8,9},{9,8},{10,11... | collective-permute-start | bytes 786440 | tf_op jit(solution)/shard_map/ppermute | solution.py:345
  58.5 22.3 %all-to-all-start.2 = ((f32[16,24,128]{2,1,0:T(8,128)}), f32[16,24,128]{2,1,0:T(8,128)S(1)}, u32[]{:S(2)}, u32[]{:S(2)}) async-start(f32[16,24,128]{2,1,0:T(8,128)} %sum_plane.1), calls=%async_computation.2 | async-start | bytes 393216 | tf_op jit(solution)/shard_map/all_to_all | solution.py:288
  68.5 22.1 %collective-permute-start.3 = (f32[256,512]{1,0:T(8,128)}, f32[256,512]{1,0:T(8,128)S(1)}, u32[]{:S(2)}, u32[]{:S(2)}) collective-permute-start(f32[256,512]{1,0:T(8,128)} %get-tuple-element.34), channel_id=1, source_target_pairs={{0,2},{2,4},{4,6},{6,0},{1,3},{3,5},{5,7},{7,1},{8,10},{10,12},{12... | collective-permute-start | bytes 1572872 | tf_op jit(solution)/shard_map/ppermute | solution.py:358
  71.0 22.7 %collective-permute-start.4 = (f32[256,512]{1,0:T(8,128)S(1)}, f32[256,512]{1,0:T(8,128)S(1)}, u32[]{:S(2)}, u32[]{:S(2)}) collective-permute-start(f32[256,512]{1,0:T(8,128)S(1)} %get-tuple-element.35), channel_id=1, source_target_pairs={{0,4},{2,6},{4,0},{6,2},{1,5},{3,7},{5,1},{7,3},{8,12},{10,14},{12... | collective-permute-start | bytes 1572872 | tf_op jit(solution)/shard_map/ppermute | solution.py:358
  74.2 24.7 %collective-permute-start.5 = (f32[256,512]{1,0:T(8,128)S(1)}, f32[256,512]{1,0:T(8,128)S(1)}, u32[]{:S(2)}, u32[]{:S(2)}) collective-permute-start(f32[256,512]{1,0:T(8,128)S(1)} %get-tuple-element.36), channel_id=1, source_target_pairs={{0,6},{2,0},{4,2},{6,4},{1,7},{3,1},{5,3},{7,5},{8,14},{10,8},{12,... | collective-permute-start | bytes 1572872 | tf_op jit(solution)/shard_map/ppermute | solution.py:358
  81.6 21.5 %all-to-all-start.3 = ((f32[32,24,128]{2,1,0:T(8,128)}), f32[32,24,128]{2,1,0:T(8,128)S(1)}, u32[]{:S(2)}, u32[]{:S(2)}) async-start(f32[32,24,128]{2,1,0:T(8,128)} %sum_depth.1), calls=%async_computation.3 | async-start | bytes 786432 | tf_op jit(solution)/shard_map/all_to_all | solution.py:288

commit v8 on v7

--- a/solution.py
+++ b/solution.py
@@ -34,8 +34,8 @@
 
 
 def pack_kernel(
-    vectors_ref, cosines_ref, distances_ref, offsets_ref, counts_ref, labels_ref, out_ref,
-    cosines, distances, offsets, counts, labels, table_sems, block_sems,
+    core_ref, vectors_ref, cosines_ref, distances_ref, offsets_ref, counts_ref, labels_ref,
+    own_ref, send_ref, cosines, distances, offsets, counts, labels, table_sems, block_sems,
 ):
     tables = (
         (cosines_ref, cosines), (distances_ref, distances), (offsets_ref, offsets),
@@ -45,15 +45,17 @@
         pltpu.make_async_copy(source, target, table_sems.at[i])
         for i, (source, target) in enumerate(tables)
     ]
-    block_copies = [
-        pltpu.make_async_copy(
-            vectors_ref.at[pl.ds(BLOCK * (core + CORES * p), BLOCK)],
-            out_ref.at[core, pl.ds(BLOCK * p, BLOCK)],
-            block_sems.at[core + CORES * p],
-        )
-        for core in range(CORES)
-        for p in range(OWN // BLOCK)
-    ]
+    block_copies = []
+    for owner, ref in ((core_ref[0], own_ref), (1 - core_ref[0], send_ref)):
+        for p in range(OWN // BLOCK):
+            start = pl.multiple_of((owner + CORES * p) * BLOCK, BLOCK)
+            block_copies.append(
+                pltpu.make_async_copy(
+                    vectors_ref.at[pl.ds(start, BLOCK)],
+                    ref.at[pl.ds(BLOCK * p, BLOCK)],
+                    block_sems.at[len(block_copies)],
+                )
+            )
     for copy in table_copies + block_copies:
         copy.start()
     for copy in table_copies:
@@ -69,10 +71,10 @@
         merged = merged + jnp.where(steps == steps[k : k + 1], hopping[k : k + 1], 0.0)
     sides = labels[...].astype(F32)
     onsite = SITE_MASS * (2.0 * sides[0:1] - 1.0) + LAYER_BIAS * (2.0 * sides[1:2] - 1.0)
-    for core in range(CORES):
-        out_ref[core, OWN : OWN + 16, :] = merged
-        out_ref[core, OWN + 16 : OWN + 32, :] = steps
-        out_ref[core, OWN + 32 : OWN + 40, :] = jnp.broadcast_to(onsite, (8, LOCAL))
+    for ref in (own_ref, send_ref):
+        ref[OWN : OWN + 16, :] = merged
+        ref[OWN + 16 : OWN + 32, :] = steps
+        ref[OWN + 32 : OWN + 40, :] = jnp.broadcast_to(onsite, (8, LOCAL))
     for copy in block_copies:
         copy.wait()
 
@@ -118,9 +120,11 @@
         lax.fori_loop(0, 20, chunk, 0)
 
 
-def own_matrix_kernel(slab_ref, *refs):
-    for core in range(CORES):
-        build_matrix(slab_ref[core, OWN:, :], refs[2 * core], refs[2 * core + 1])
+def own_matrix_kernel(core_ref, own_ref, mate_ref, *refs):
+    second = core_ref[0] == 1
+    own, mate = own_ref[OWN:, :], mate_ref[OWN:, :]
+    build_matrix(jnp.where(second, mate, own), refs[0], refs[1])
+    build_matrix(jnp.where(second, own, mate), refs[2], refs[3])
 
 
 def split(value):
@@ -136,18 +140,24 @@
 
 
 def apply_kernel(
-    left_ref, own_ref, right_ref, first_high_ref, first_low_ref, second_high_ref, second_low_ref,
+    core_ref, left_ref, left_mate_ref, own_ref, mate_ref, right_ref, right_mate_ref,
+    first_high_ref, first_low_ref, second_high_ref, second_low_ref,
     applied_ref, lead_ref, high_ref, low_ref, once_high_ref, once_low_ref,
     left_high_ref, left_low_ref, right_high_ref, right_low_ref,
 ):
-    build_matrix(left_ref[1, OWN:, :], left_high_ref, left_low_ref)
-    build_matrix(right_ref[0, OWN:, :], right_high_ref, right_low_ref)
-    sources = [(ref, core) for ref in (left_ref, own_ref, right_ref) for core in range(CORES)]
-    for place, (ref, core) in enumerate(sources):
-        columns = slice(LOCAL * place, LOCAL * place + LOCAL)
-        high, low = split(ref[core, 0:OWN, :])
-        high_ref[:, columns] = high
-        low_ref[:, columns] = low
+    core = core_ref[0]
+    second = core == 1
+    left_table = jnp.where(second, left_ref[OWN:, :], left_mate_ref[OWN:, :])
+    right_table = jnp.where(second, right_mate_ref[OWN:, :], right_ref[OWN:, :])
+    build_matrix(left_table, left_high_ref, left_low_ref)
+    build_matrix(right_table, right_high_ref, right_low_ref)
+    pairs = ((left_ref, left_mate_ref), (own_ref, mate_ref), (right_ref, right_mate_ref))
+    for chip, pair in enumerate(pairs):
+        for place, ref in zip((core, 1 - core), pair):
+            start = pl.multiple_of((CORES * chip + place) * LOCAL, LOCAL)
+            high, low = split(ref[0:OWN, :])
+            high_ref[:, pl.ds(start, LOCAL)] = high
+            low_ref[:, pl.ds(start, LOCAL)] = low
     matrices = (
         (left_high_ref, left_low_ref),
         (first_high_ref, first_low_ref),
@@ -171,21 +181,28 @@
         lead_ref[:, columns] = twice[0 : 2 * BLOCK]
 
 
-def gram_kernel(place_ref, lead_ref, other_ref, applied_ref, gram_ref, *shared_refs):
-    chip, second = place_ref[0], place_ref[1] == 1
+def head_block(s, core_ref, lead_ref, other_ref):
+    place, core = ((0, 0), (0, 1), (BLOCK, 0))[s]
+    mine, theirs = lead_ref[place : place + BLOCK, :], other_ref[place : place + BLOCK, :]
+    return jnp.where(core_ref[0] == core, mine, theirs)
+
+
+def gram_kernel(core_ref, lead_ref, other_ref, applied_ref, gram_ref):
+    blocks = [head_block(s, core_ref, lead_ref, other_ref) for s in range(STEPS)]
+    gram = dot32(jnp.concatenate(blocks, axis=0), applied_ref[...], ((1,), (1,)))
+    for part in range(OWN // 128):
+        gram_ref[part] = gram[:, 128 * part : 128 * part + 128]
+
+
+def share_kernel(core_ref, chip_ref, lead_ref, other_ref, applied_ref, *shared_refs):
     count = len(shared_refs)
-    for s, place, core in ((0, 0, 0), (1, 0, 1), (2, BLOCK, 0)):
-        mine, theirs = lead_ref[place : place + BLOCK, :], other_ref[place : place + BLOCK, :]
-        pair = (mine, theirs) if core else (theirs, mine)
-        block = jnp.where(second, *pair)
+    for s in range(STEPS):
+        block = head_block(s, core_ref, lead_ref, other_ref)
         for ref in shared_refs:
             ref[BLOCK * s : BLOCK * s + BLOCK, :] = block
     for step, ref in enumerate(shared_refs):
-        start = pl.multiple_of(lax.rem(chip + step, count) * BLOCK, BLOCK)
+        start = pl.multiple_of(lax.rem(chip_ref[0] + step, count) * BLOCK, BLOCK)
         ref[HEAD:, :] = applied_ref[pl.ds(start, BLOCK), :]
-    gram = dot32(shared_refs[0][0:HEAD, :], applied_ref[...], ((1,), (1,)))
-    for part in range(OWN // 128):
-        gram_ref[part] = gram[:, 128 * part : 128 * part + 128]
 
 
 def spread(value):
@@ -222,9 +239,9 @@
     )
 
 
-def finish_kernel(scale, place_ref, gram_ref, *refs):
+def finish_kernel(scale, core_ref, chip_ref, gram_ref, *refs):
     *shared_refs, basis_ref, results, sems = refs
-    chip, core = place_ref[0], place_ref[1]
+    chip, core = chip_ref[0], core_ref[0]
     second = core == 1
     column = CORES * chip + core
     count = len(shared_refs)
@@ -322,38 +339,47 @@
         return lax.ppermute(value, chips, [(i, (i + step) % chip_count) for i in range(chip_count)])
 
     shape = jax.ShapeDtypeStruct
+    core = lax.axis_index("core").reshape(1)
+    chip = lax.axis_index("x").reshape(1)
     tables = (cosines, distances, offsets, counts.reshape(1, LOCAL), labels)
-    slab = call(
-        pack_kernel, "pack", shape((CORES, OWN + TABLE, LOCAL), F32), (vectors, *tables),
+    part = shape((OWN + TABLE, LOCAL), F32)
+    own, send = call(
+        pack_kernel, "pack", (part, part), (core, vectors, *tables),
         [pltpu.VMEM(t.shape, t.dtype) for t in tables]
         + [pltpu.SemaphoreType.DMA((len(tables),)), pltpu.SemaphoreType.DMA((NV // BLOCK,))],
-        [RAW] * 6,
-    )
-    slab = exchange(slab, "core")
-    left = shift(slab, 1)
-    right = shift(slab, -1)
+        [SMEM] + [RAW] * 6,
+    )
+    left = shift(own, 1)
+    right = shift(own, -1)
+    mate = lax.ppermute(send, "core", [(0, 1), (1, 0)])
+    left_mate = shift(mate, 1)
+    right_mate = shift(mate, -1)
     matrix = shape((WIDE, LOCAL), BF16)
-    matrices = call(own_matrix_kernel, "own_matrix", (matrix,) * 4, (slab,))
+    matrices = call(
+        own_matrix_kernel, "own_matrix", (matrix,) * 4, (core, own, mate), (), [SMEM] + [VMEM] * 2
+    )
     wide = pltpu.VMEM((WIDE, LOCAL), BF16)
     applied, lead = call(
         apply_kernel,
         "apply_twice",
         (shape((OWN, CHIP), F32), shape((2 * BLOCK, CHIP), F32)),
-        (left, slab, right, *matrices),
+        (core, left, left_mate, own, mate, right, right_mate, *matrices),
         [pltpu.VMEM((OWN, 3 * CHIP), BF16)] * 2 + [pltpu.VMEM((OWN, 2 * CHIP), BF16)] * 2 + [wide] * 4,
+        [SMEM] + [VMEM] * 10,
     )
     other = lax.ppermute(lead, "core", [(0, 1), (1, 0)])
-    place = jnp.stack([lax.axis_index("x"), lax.axis_index("core")])
-    gram, *shared = call(
-        gram_kernel, "gram",
-        (shape((OWN // 128, HEAD, 128), F32),) + (shape((SHARED, CHIP), F32),) * count,
-        (place, lead, other, applied), (), [SMEM] + [VMEM] * 3,
+    gram = call(
+        gram_kernel, "gram", shape((OWN // 128, HEAD, 128), F32),
+        (core, lead, other, applied), (), [SMEM] + [VMEM] * 3,
+    )
+    shared = call(
+        share_kernel, "share", (shape((SHARED, CHIP), F32),) * count,
+        (core, chip, lead, other, applied), (), [SMEM] * 2 + [VMEM] * 3,
     )
     piece = (OWN // 128) * HEAD // planes
     everyone = planes * CORES
     gram = exchange(gram.reshape(planes, piece, 128), plane)
     gram = call(sum_kernel, "sum_plane", shape((depth, piece, 128), F32), (gram,))
-    gram, *shared = lax.optimization_barrier((gram, *shared))
     shared = [shared[0]] + [
         lax.ppermute(shared[step], "x", [(i, (i + step) % count) for i in range(count)])
         for step in range(1, count)
@@ -366,9 +392,9 @@
     slab_width = CHIP * count
     return call(
         lambda *refs: finish_kernel(scale, *refs), "finish", shape((BLOCK, slab_width), F32),
-        (place, gram, *shared),
+        (core, chip, gram, *shared),
         [pltpu.VMEM((count, BLOCK, CHIP), F32), pltpu.SemaphoreType.DMA((count,))],
-        [SMEM] + [VMEM] * (1 + count), RAW,
+        [SMEM] * 2 + [VMEM] * (1 + count), RAW,
     )
 
 

time: 113 us -> 116 us (1.027)
  starting transfers between devices: 43.2 us -> 56 us
  blocking collectives: 21 us -> 10.3 us
  waiting for transfers between devices: 27.3 us -> 28.9 us
    ppermute x2 -> x4, starting transfers between devices: 12.3 us -> 23 us  [shift(): lax.ppermute(value, chips, [(i, (i + step) % chip_count) for i in range(c...]
    all_to_all x2 -> x1, blocking collectives: 21 us -> 10.3 us  [exchange(): return lax.all_to_all(value, axes, split_axis=0, concat_axis=0, tiled=True)]
    ppermute x0 -> x1, starting transfers between devices: none -> 8.79 us  [on_device(): mate = lax.ppermute(send, 'core', [(0, 1), (1, 0)])]
    all_to_all x2, starting transfers between devices: 18.9 us -> 12.1 us  [exchange(): return lax.all_to_all(value, axes, split_axis=0, concat_axis=0, tiled=True)]
    ppermute x3, waiting for transfers between devices: 8.35 us -> 9.6 us  [on_device(): lax.ppermute(shared[step], 'x', [(i, (i + step) % count) for i in range(c...]
    ppermute x2 -> x4, waiting for transfers between devices: 10.3 us -> 10.9 us  [shift(): lax.ppermute(value, chips, [(i, (i + step) % chip_count) for i in range(c...]
    pallas_call x7 -> x8, Pallas kernels: 20.8 us -> 20.4 us  [call(): pl.pallas_call(kernel, out_shape=out_shape, in_specs=specs or [VMEM] * le...]
  transfers between devices with their start and end apart: 8 -> 11, of which waited for: 7 -> 8; matrix products, arithmetic and copies ran while one was open for 0% -> 0% of each run, Pallas kernels for 3% -> 4%
where the time goes in v8:
time: 116 us
  starting transfers between devices  56 us (48%)
  waiting for transfers between devices  28.9 us (25%)
  Pallas kernels  20.4 us (18%)
  blocking collectives  10.3 us (9%)
    ppermute x4, starting transfers between devices, shift(): lax.ppermute(value, chips, [(i, (i + step) % chip_count) for i in range(c...  23 us
    pallas_call x8, Pallas kernels, call(): pl.pallas_call(kernel, out_shape=out_shape, in_specs=specs or [VMEM] * le...  20.4 us
    all_to_all x2, starting transfers between devices, exchange(): return lax.all_to_all(value, axes, split_axis=0, concat_axis=0, tiled=True)  12.1 us
    ppermute x4, waiting for transfers between devices, shift(): lax.ppermute(value, chips, [(i, (i + step) % chip_count) for i in range(c...  10.9 us
    all_to_all x1, blocking collectives, exchange(): return lax.all_to_all(value, axes, split_axis=0, concat_axis=0, tiled=True)  10.3 us
    ppermute x3, waiting for transfers between devices, on_device(): lax.ppermute(shared[step], 'x', [(i, (i + step) % count) for i in range(c...  9.6 us
    ppermute x1, starting transfers between devices, on_device(): mate = lax.ppermute(send, 'core', [(0, 1), (1, 0)])  8.79 us
    ppermute x3, starting transfers between devices, on_device(): lax.ppermute(shared[step], 'x', [(i, (i + step) % count) for i in range(c...  8.41 us
  transfers between devices with their start and end apart: 11, of which 8 were waited for; matrix products, arithmetic and copies ran while one was open for 0% of the time, Pallas kernels for 4%

profile of v8, /device:TPU:1, one launch (start us, length us, event | category | flops | bytes accessed | tf_op | source)
XLA Modules:
  0.0 115.7 jit_solution(9341079190889655910)
XLA Ops:
  0.0 1.2 %pack.1 = (f32[296,256]{1,0:T(8,128)S(1)}, f32[296,256]{1,0:T(8,128)S(1)}) custom-call(s32[1]{0:T(128)} %bitcast.core_ref.refs_0_, f32[512,256]{1,0:T(8,128)} %vectors_ref.1, f32[16,256]{1,0:T(8,128)} %cosines_ref.1, f32[16,256]{1,0:T(8,128)} %distances_ref.1, s32[16,256]{1,0:T(8,128)} %offsets_ref.1, s32[1,256]{1,0:T(1,128)} %bitcast.7, s32[2,256]{1,0:T(2,128)} %labels_ref.1), custom_call_target="tpu_custom_call" | custom-call | tf_op jit(solution)/shard_map/pack/pallas_call | solution.py:319
  1.2 8.8 %collective-permute-start.1 = (f32[296,256]{1,0:T(8,128)S(1)}, f32[296,256]{1,0:T(8,128)S(1)}, u32[]{:S(2)}, u32[]{:S(2)}) collective-permute-start(f32[296,256]{1,0:T(8,128)S(1)} %get-tuple-element.18), channel_id=1, source_target_pairs={{0,1},{1,0},{2,3},{3,2},{4,5},{5,4},{6,7},{7,6},{8,9},{9,8},{10,11... | collective-permute-start | bytes 909320 | tf_op jit(solution)/shard_map/ppermute | solution.py:354
  10.0 10.4 %collective-permute-start.3 = (f32[296,256]{1,0:T(8,128)S(1)}, f32[296,256]{1,0:T(8,128)S(1)}, u32[]{:S(2)}, u32[]{:S(2)}) collective-permute-start(f32[296,256]{1,0:T(8,128)S(1)} %get-tuple-element.17.own_ref), channel_id=1, source_target_pairs={{0,510},{2,0},{4,2},{6,4},{8,6},{10,8},{12,10},{14,12},{16,14},{18... | collective-permute-start | bytes 909320 | tf_op jit(solution)/shard_map/ppermute | solution.py:339
  20.4 1.9 %collective-permute-start = (f32[296,256]{1,0:T(8,128)S(1)}, f32[296,256]{1,0:T(8,128)S(1)}, u32[]{:S(2)}, u32[]{:S(2)}) collective-permute-start(f32[296,256]{1,0:T(8,128)S(1)} %get-tuple-element.17.own_ref), channel_id=1, source_target_pairs={{0,2},{2,4},{4,6},{6,8},{8,10},{10,12},{12,14},{14,16},{16,18},{18... | collective-permute-start | bytes 909320 | tf_op jit(solution)/shard_map/ppermute | solution.py:339
  22.4 0.0 collective-permute-done.1.mate_ref
  22.4 8.8 %collective-permute-start.4 = (f32[296,256]{1,0:T(8,128)S(1)}, f32[296,256]{1,0:T(8,128)S(1)}, u32[]{:S(2)}, u32[]{:S(2)}) collective-permute-start(f32[296,256]{1,0:T(8,128)S(1)} %collective-permute-done.1.mate_ref), channel_id=1, source_target_pairs={{0,510},{2,0},{4,2},{6,4},{8,6},{10,8},{12,10},{14,12},{16,14},{18... | collective-permute-start | bytes 909320 | tf_op jit(solution)/shard_map/ppermute | solution.py:339
  31.2 1.9 %collective-permute-start.2 = (f32[296,256]{1,0:T(8,128)S(1)}, f32[296,256]{1,0:T(8,128)S(1)}, u32[]{:S(2)}, u32[]{:S(2)}) collective-permute-start(f32[296,256]{1,0:T(8,128)S(1)} %collective-permute-done.1.mate_ref), channel_id=1, source_target_pairs={{0,2},{2,4},{4,6},{6,8},{8,10},{10,12},{12,14},{14,16},{16,18},{18... | collective-permute-start | bytes 909320 | tf_op jit(solution)/shard_map/ppermute | solution.py:339
  33.1 2.4 %own_matrix.1 = (bf16[768,256]{1,0:T(8,128)(2,1)S(1)}, bf16[768,256]{1,0:T(8,128)(2,1)S(1)}, bf16[768,256]{1,0:T(8,128)(2,1)S(1)}, bf16[768,256]{1,0:T(8,128)(2,1)S(1)}) custom-call(s32[1]{0:T(128)} %bitcast.core_ref.refs_0_, f32[296,256]{1,0:T(8,128)S(1)} %get-tuple-element.17.own_ref, f32[296,256]{1,0:T(8,128)S(1)} %collective-permute-done.1.mate_ref), custom_call_target="tpu_custom_call" | custom-call | tf_op jit(solution)/shard_map/own_matrix/pallas_call | solution.py:319
  35.5 0.0 collective-permute-done.3.right_ref
  35.5 0.8 collective-permute-done.left_ref
  36.2 0.9 collective-permute-done.4.right_mate_ref
  37.1 9.2 %collective-permute-done.2.left_mate_ref = f32[296,256]{1,0:T(8,128)S(1)} collective-permute-done((f32[296,256]{1,0:T(8,128)S(1)}, f32[296,256]{1,0:T(8,128)S(1)}, u32[]{:S(2)}, u32[]{:S(2)}) %collective-permute-start.2) | collective-permute-done | bytes 303136 | tf_op jit(solution)/shard_map/ppermute | solution.py:339
  46.3 4.7 %apply_twice.1 = (f32[256,512]{1,0:T(8,128)S(1)}, f32[128,512]{1,0:T(8,128)S(1)}) custom-call(s32[1]{0:T(128)} %bitcast.core_ref.refs_0_, f32[296,256]{1,0:T(8,128)S(1)} %collective-permute-done.left_ref, f32[296,256]{1,0:T(8,128)S(1)} %collective-permute-done.2.left_mate_ref, f32[296,256]{1,0:T(8,128)S(1)} %get-tuple-element.17.own_ref, ...), custom_call_target="tpu_custom_call" | custom-call | tf_op jit(solution)/shard_map/apply_twice/pallas_call | solution.py:319
  51.1 3.7 %collective-permute-start.5 = (f32[128,512]{1,0:T(8,128)S(1)}, f32[128,512]{1,0:T(8,128)S(1)}, u32[]{:S(2)}, u32[]{:S(2)}) collective-permute-start(f32[128,512]{1,0:T(8,128)S(1)} %get-tuple-element.23.lead_ref), channel_id=1, source_target_pairs={{0,1},{1,0},{2,3},{3,2},{4,5},{5,4},{6,7},{7,6},{8,9},{9,8},{10,11... | collective-permute-start | bytes 786440 | tf_op jit(solution)/shard_map/ppermute | solution.py:370
  54.7 1.1 collective-permute-done.5.other_ref
  55.9 0.7 gram.1
  56.6 10.3 %all_to_all.15.pieces_ref = f32[16,24,128]{2,1,0:T(8,128)S(1)} all-to-all(f32[16,24,128]{2,1,0:T(8,128)S(1)} %bitcast.6), channel_id=1, replica_groups=mesh['y'=4,'z'=16,'x'=4,'core'=2] {'y','x'}, dimensions={0} | all-to-all | bytes 393216 | tf_op jit(solution)/shard_map/all_to_all | solution.py:305
  66.9 0.7 sum_plane.1
  67.6 3.5 %all-to-all-start.1 = ((f32[16,24,128]{2,1,0:T(8,128)}), f32[16,24,128]{2,1,0:T(8,128)S(1)}, u32[]{:S(2)}, u32[]{:S(2)}) async-start(f32[16,24,128]{2,1,0:T(8,128)} %sum_plane.1), calls=%async_computation.1 | async-start | bytes 393216 | tf_op jit(solution)/shard_map/all_to_all | solution.py:305
  71.1 1.1 share.1
  72.2 2.2 %collective-permute-start.6 = (f32[256,512]{1,0:T(8,128)}, f32[256,512]{1,0:T(8,128)S(1)}, u32[]{:S(2)}, u32[]{:S(2)}) collective-permute-start(f32[256,512]{1,0:T(8,128)} %get-tuple-element.26), channel_id=1, source_target_pairs={{0,2},{2,4},{4,6},{6,0},{1,3},{3,5},{5,7},{7,1},{8,10},{10,12},{12... | collective-permute-start | bytes 1572872 | tf_op jit(solution)/shard_map/ppermute | solution.py:384
  74.4 2.9 %collective-permute-start.7 = (f32[256,512]{1,0:T(8,128)}, f32[256,512]{1,0:T(8,128)S(1)}, u32[]{:S(2)}, u32[]{:S(2)}) collective-permute-start(f32[256,512]{1,0:T(8,128)} %get-tuple-element.27), channel_id=1, source_target_pairs={{0,4},{2,6},{4,0},{6,2},{1,5},{3,7},{5,1},{7,3},{8,12},{10,14},{12... | collective-permute-start | bytes 1572872 | tf_op jit(solution)/shard_map/ppermute | solution.py:384
  77.3 3.3 %collective-permute-start.8 = (f32[256,512]{1,0:T(8,128)S(1)}, f32[256,512]{1,0:T(8,128)S(1)}, u32[]{:S(2)}, u32[]{:S(2)}) collective-permute-start(f32[256,512]{1,0:T(8,128)S(1)} %get-tuple-element.28), channel_id=1, source_target_pairs={{0,6},{2,0},{4,2},{6,4},{1,7},{3,1},{5,3},{7,5},{8,14},{10,8},{12,... | collective-permute-start | bytes 1572872 | tf_op jit(solution)/shard_map/ppermute | solution.py:384
  80.7 2.8 %all-to-all-done.1.pieces_ref = f32[16,24,128]{2,1,0:T(8,128)S(1)} async-done(((f32[16,24,128]{2,1,0:T(8,128)}), f32[16,24,128]{2,1,0:T(8,128)S(1)}, u32[]{:S(2)}, u32[]{:S(2)}) %all-to-all-start.1) | async-done | bytes 196640 | tf_op jit(solution)/shard_map/all_to_all | solution.py:305
  83.5 0.8 sum_depth.1
  84.2 8.6 %all-to-all-start.2 = ((f32[32,24,128]{2,1,0:T(8,128)}), f32[32,24,128]{2,1,0:T(8,128)S(1)}, u32[]{:S(2)}, u32[]{:S(2)}) async-start(f32[32,24,128]{2,1,0:T(8,128)} %sum_depth.1), calls=%async_computation.2 | async-start | bytes 786432 | tf_op jit(solution)/shard_map/all_to_all | solution.py:305
  92.8 0.0 collective-permute-done.6.refs_4_
  92.8 4.4 %collective-permute-done.7.refs_5_ = f32[256,512]{1,0:T(8,128)S(1)} collective-permute-done((f32[256,512]{1,0:T(8,128)}, f32[256,512]{1,0:T(8,128)S(1)}, u32[]{:S(2)}, u32[]{:S(2)}) %collective-permute-start.7) | collective-permute-done | bytes 524320 | tf_op jit(solution)/shard_map/ppermute | solution.py:384
  97.2 5.2 %collective-permute-done.8.refs_6_ = f32[256,512]{1,0:T(8,128)S(1)} collective-permute-done((f32[256,512]{1,0:T(8,128)S(1)}, f32[256,512]{1,0:T(8,128)S(1)}, u32[]{:S(2)}, u32[]{:S(2)}) %collective-permute-start.8) | collective-permute-done | bytes 524320 | tf_op jit(solution)/shard_map/ppermute | solution.py:384
  102.4 4.5 %all-to-all-done.2 = f32[32,24,128]{2,1,0:T(8,128)S(1)} async-done(((f32[32,24,128]{2,1,0:T(8,128)}), f32[32,24,128]{2,1,0:T(8,128)S(1)}, u32[]{:S(2)}, u32[]{:S(2)}) %all-to-all-start.2) | async-done | bytes 393248 | tf_op jit(solution)/shard_map/all_to_all | solution.py:305
  106.9 8.8 %finish.1 = f32[64,2048]{1,0:T(8,128)} custom-call(s32[1]{0:T(128)} %bitcast.core_ref.refs_0_, s32[1]{0:T(128)} %bitcast.1.chip_ref.refs_1_, f32[16,2,24,128]{3,2,1,0:T(8,128)S(1)} %bitcast.5, f32[256,512]{1,0:T(8,128)S(1)} %get-tuple-element.25.refs_3_, f32[256,512]{1,0:T(8,128)S(1)} %collective-permute-done.6.refs_4_, ...), custom_call_target="tpu_custom_call" | custom-call | tf_op jit(solution)/shard_map/finish/pallas_call | solution.py:319
Async XLA Ops:
  1.2 21.1 %collective-permute-start.1 = (f32[296,256]{1,0:T(8,128)S(1)}, f32[296,256]{1,0:T(8,128)S(1)}, u32[]{:S(2)}, u32[]{:S(2)}) collective-permute-start(f32[296,256]{1,0:T(8,128)S(1)} %get-tuple-element.18), channel_id=1, source_target_pairs={{0,1},{1,0},{2,3},{3,2},{4,5},{5,4},{6,7},{7,6},{8,9},{9,8},{10,11... | collective-permute-start | bytes 909320 | tf_op jit(solution)/shard_map/ppermute | solution.py:354
  10.0 25.5 %collective-permute-start.3 = (f32[296,256]{1,0:T(8,128)S(1)}, f32[296,256]{1,0:T(8,128)S(1)}, u32[]{:S(2)}, u32[]{:S(2)}) collective-permute-start(f32[296,256]{1,0:T(8,128)S(1)} %get-tuple-element.17.own_ref), channel_id=1, source_target_pairs={{0,510},{2,0},{4,2},{6,4},{8,6},{10,8},{12,10},{14,12},{16,14},{18... | collective-permute-start | bytes 909320 | tf_op jit(solution)/shard_map/ppermute | solution.py:339
  20.4 15.8 %collective-permute-start = (f32[296,256]{1,0:T(8,128)S(1)}, f32[296,256]{1,0:T(8,128)S(1)}, u32[]{:S(2)}, u32[]{:S(2)}) collective-permute-start(f32[296,256]{1,0:T(8,128)S(1)} %get-tuple-element.17.own_ref), channel_id=1, source_target_pairs={{0,2},{2,4},{4,6},{6,8},{8,10},{10,12},{12,14},{14,16},{16,18},{18... | collective-permute-start | bytes 909320 | tf_op jit(solution)/shard_map/ppermute | solution.py:339
  22.4 14.7 %collective-permute-start.4 = (f32[296,256]{1,0:T(8,128)S(1)}, f32[296,256]{1,0:T(8,128)S(1)}, u32[]{:S(2)}, u32[]{:S(2)}) collective-permute-start(f32[296,256]{1,0:T(8,128)S(1)} %collective-permute-done.1.mate_ref), channel_id=1, source_target_pairs={{0,510},{2,0},{4,2},{6,4},{8,6},{10,8},{12,10},{14,12},{16,14},{18... | collective-permute-start | bytes 909320 | tf_op jit(solution)/shard_map/ppermute | solution.py:339
  31.2 15.2 %collective-permute-start.2 = (f32[296,256]{1,0:T(8,128)S(1)}, f32[296,256]{1,0:T(8,128)S(1)}, u32[]{:S(2)}, u32[]{:S(2)}) collective-permute-start(f32[296,256]{1,0:T(8,128)S(1)} %collective-permute-done.1.mate_ref), channel_id=1, source_target_pairs={{0,2},{2,4},{4,6},{6,8},{8,10},{10,12},{12,14},{14,16},{16,18},{18... | collective-permute-start | bytes 909320 | tf_op jit(solution)/shard_map/ppermute | solution.py:339
  51.1 4.8 %collective-permute-start.5 = (f32[128,512]{1,0:T(8,128)S(1)}, f32[128,512]{1,0:T(8,128)S(1)}, u32[]{:S(2)}, u32[]{:S(2)}) collective-permute-start(f32[128,512]{1,0:T(8,128)S(1)} %get-tuple-element.23.lead_ref), channel_id=1, source_target_pairs={{0,1},{1,0},{2,3},{3,2},{4,5},{5,4},{6,7},{7,6},{8,9},{9,8},{10,11... | collective-permute-start | bytes 786440 | tf_op jit(solution)/shard_map/ppermute | solution.py:370
  67.6 15.9 %all-to-all-start.1 = ((f32[16,24,128]{2,1,0:T(8,128)}), f32[16,24,128]{2,1,0:T(8,128)S(1)}, u32[]{:S(2)}, u32[]{:S(2)}) async-start(f32[16,24,128]{2,1,0:T(8,128)} %sum_plane.1), calls=%async_computation.1 | async-start | bytes 393216 | tf_op jit(solution)/shard_map/all_to_all | solution.py:305
  72.2 20.6 %collective-permute-start.6 = (f32[256,512]{1,0:T(8,128)}, f32[256,512]{1,0:T(8,128)S(1)}, u32[]{:S(2)}, u32[]{:S(2)}) collective-permute-start(f32[256,512]{1,0:T(8,128)} %get-tuple-element.26), channel_id=1, source_target_pairs={{0,2},{2,4},{4,6},{6,0},{1,3},{3,5},{5,7},{7,1},{8,10},{10,12},{12... | collective-permute-start | bytes 1572872 | tf_op jit(solution)/shard_map/ppermute | solution.py:384
  74.4 22.7 %collective-permute-start.7 = (f32[256,512]{1,0:T(8,128)}, f32[256,512]{1,0:T(8,128)S(1)}, u32[]{:S(2)}, u32[]{:S(2)}) collective-permute-start(f32[256,512]{1,0:T(8,128)} %get-tuple-element.27), channel_id=1, source_target_pairs={{0,4},{2,6},{4,0},{6,2},{1,5},{3,7},{5,1},{7,3},{8,12},{10,14},{12... | collective-permute-start | bytes 1572872 | tf_op jit(solution)/shard_map/ppermute | solution.py:384
  77.3 25.1 %collective-permute-start.8 = (f32[256,512]{1,0:T(8,128)S(1)}, f32[256,512]{1,0:T(8,128)S(1)}, u32[]{:S(2)}, u32[]{:S(2)}) collective-permute-start(f32[256,512]{1,0:T(8,128)S(1)} %get-tuple-element.28), channel_id=1, source_target_pairs={{0,6},{2,0},{4,2},{6,4},{1,7},{3,1},{5,3},{7,5},{8,14},{10,8},{12,... | collective-permute-start | bytes 1572872 | tf_op jit(solution)/shard_map/ppermute | solution.py:384
  84.2 22.7 %all-to-all-start.2 = ((f32[32,24,128]{2,1,0:T(8,128)}), f32[32,24,128]{2,1,0:T(8,128)S(1)}, u32[]{:S(2)}, u32[]{:S(2)}) async-start(f32[32,24,128]{2,1,0:T(8,128)} %sum_depth.1), calls=%async_computation.2 | async-start | bytes 786432 | tf_op jit(solution)/shard_map/all_to_all | solution.py:305

commit v9 on v7

--- a/solution.py
+++ b/solution.py
@@ -171,21 +171,28 @@
         lead_ref[:, columns] = twice[0 : 2 * BLOCK]
 
 
-def gram_kernel(place_ref, lead_ref, other_ref, applied_ref, gram_ref, *shared_refs):
-    chip, second = place_ref[0], place_ref[1] == 1
+def head_block(s, core_ref, lead_ref, other_ref):
+    place, core = ((0, 0), (0, 1), (BLOCK, 0))[s]
+    mine, theirs = lead_ref[place : place + BLOCK, :], other_ref[place : place + BLOCK, :]
+    return jnp.where(core_ref[0] == core, mine, theirs)
+
+
+def gram_kernel(core_ref, lead_ref, other_ref, applied_ref, gram_ref):
+    blocks = [head_block(s, core_ref, lead_ref, other_ref) for s in range(STEPS)]
+    gram = dot32(jnp.concatenate(blocks, axis=0), applied_ref[...], ((1,), (1,)))
+    for part in range(OWN // 128):
+        gram_ref[part] = gram[:, 128 * part : 128 * part + 128]
+
+
+def share_kernel(core_ref, chip_ref, lead_ref, other_ref, applied_ref, *shared_refs):
     count = len(shared_refs)
-    for s, place, core in ((0, 0, 0), (1, 0, 1), (2, BLOCK, 0)):
-        mine, theirs = lead_ref[place : place + BLOCK, :], other_ref[place : place + BLOCK, :]
-        pair = (mine, theirs) if core else (theirs, mine)
-        block = jnp.where(second, *pair)
+    for s in range(STEPS):
+        block = head_block(s, core_ref, lead_ref, other_ref)
         for ref in shared_refs:
             ref[BLOCK * s : BLOCK * s + BLOCK, :] = block
     for step, ref in enumerate(shared_refs):
-        start = pl.multiple_of(lax.rem(chip + step, count) * BLOCK, BLOCK)
+        start = pl.multiple_of(lax.rem(chip_ref[0] + step, count) * BLOCK, BLOCK)
         ref[HEAD:, :] = applied_ref[pl.ds(start, BLOCK), :]
-    gram = dot32(shared_refs[0][0:HEAD, :], applied_ref[...], ((1,), (1,)))
-    for part in range(OWN // 128):
-        gram_ref[part] = gram[:, 128 * part : 128 * part + 128]
 
 
 def spread(value):
@@ -222,9 +229,9 @@
     )
 
 
-def finish_kernel(scale, place_ref, gram_ref, *refs):
+def finish_kernel(scale, core_ref, chip_ref, gram_ref, *refs):
     *shared_refs, basis_ref, results, sems = refs
-    chip, core = place_ref[0], place_ref[1]
+    chip, core = chip_ref[0], core_ref[0]
     second = core == 1
     column = CORES * chip + core
     count = len(shared_refs)
@@ -343,17 +350,20 @@
         [pltpu.VMEM((OWN, 3 * CHIP), BF16)] * 2 + [pltpu.VMEM((OWN, 2 * CHIP), BF16)] * 2 + [wide] * 4,
     )
     other = lax.ppermute(lead, "core", [(0, 1), (1, 0)])
-    place = jnp.stack([lax.axis_index("x"), lax.axis_index("core")])
-    gram, *shared = call(
-        gram_kernel, "gram",
-        (shape((OWN // 128, HEAD, 128), F32),) + (shape((SHARED, CHIP), F32),) * count,
-        (place, lead, other, applied), (), [SMEM] + [VMEM] * 3,
+    core = lax.axis_index("core").reshape(1)
+    chip = lax.axis_index("x").reshape(1)
+    gram = call(
+        gram_kernel, "gram", shape((OWN // 128, HEAD, 128), F32),
+        (core, lead, other, applied), (), [SMEM] + [VMEM] * 3,
+    )
+    shared = call(
+        share_kernel, "share", (shape((SHARED, CHIP), F32),) * count,
+        (core, chip, lead, other, applied), (), [SMEM] * 2 + [VMEM] * 3,
     )
     piece = (OWN // 128) * HEAD // planes
     everyone = planes * CORES
     gram = exchange(gram.reshape(planes, piece, 128), plane)
     gram = call(sum_kernel, "sum_plane", shape((depth, piece, 128), F32), (gram,))
-    gram, *shared = lax.optimization_barrier((gram, *shared))
     shared = [shared[0]] + [
         lax.ppermute(shared[step], "x", [(i, (i + step) % count) for i in range(count)])
         for step in range(1, count)
@@ -366,9 +376,9 @@
     slab_width = CHIP * count
     return call(
         lambda *refs: finish_kernel(scale, *refs), "finish", shape((BLOCK, slab_width), F32),
-        (place, gram, *shared),
+        (core, chip, gram, *shared),
         [pltpu.VMEM((count, BLOCK, CHIP), F32), pltpu.SemaphoreType.DMA((count,))],
-        [SMEM] + [VMEM] * (1 + count), RAW,
+        [SMEM] * 2 + [VMEM] * (1 + count), RAW,
     )
 
 

time: 113 us -> 113 us (level)
    ppermute x3, waiting for transfers between devices: 8.35 us -> 9.66 us  [on_device(): lax.ppermute(shared[step], 'x', [(i, (i + step) % count) for i in range(c...]
    pallas_call x7 -> x8, Pallas kernels: 20.8 us -> 20.1 us  [call(): pl.pallas_call(kernel, out_shape=out_shape, in_specs=specs or [VMEM] * le...]
  transfers between devices with their start and end apart: 8 -> 8, of which waited for: 7 -> 7; matrix products, arithmetic and copies ran while one was open for 0% -> 0% of each run, Pallas kernels for 3% -> 4%
where the time goes in v9:
time: 113 us; the launch traced here: 112 us
  starting transfers between devices  43.2 us (38%)
  waiting for transfers between devices  27.6 us (24%)
  blocking collectives  21 us (19%)
  Pallas kernels  20.1 us (18%)
    all_to_all x2, blocking collectives, exchange(): return lax.all_to_all(value, axes, split_axis=0, concat_axis=0, tiled=True)  21 us
    pallas_call x8, Pallas kernels, call(): pl.pallas_call(kernel, out_shape=out_shape, in_specs=specs or [VMEM] * le...  20.1 us
    all_to_all x2, starting transfers between devices, exchange(): return lax.all_to_all(value, axes, split_axis=0, concat_axis=0, tiled=True)  18.9 us
    ppermute x2, starting transfers between devices, shift(): lax.ppermute(value, chips, [(i, (i + step) % chip_count) for i in range(c...  12.3 us
    ppermute x2, waiting for transfers between devices, shift(): lax.ppermute(value, chips, [(i, (i + step) % chip_count) for i in range(c...  10.3 us
    ppermute x3, waiting for transfers between devices, on_device(): lax.ppermute(shared[step], 'x', [(i, (i + step) % count) for i in range(c...  9.66 us
    ppermute x3, starting transfers between devices, on_device(): lax.ppermute(shared[step], 'x', [(i, (i + step) % count) for i in range(c...  8.86 us
    all_to_all x2, waiting for transfers between devices, exchange(): return lax.all_to_all(value, axes, split_axis=0, concat_axis=0, tiled=True)  6.47 us
  transfers between devices with their start and end apart: 8, of which 7 were waited for; matrix products, arithmetic and copies ran while one was open for 0% of the time, Pallas kernels for 4%

profile of v9, /device:TPU:1, one launch (start us, length us, event | category | flops | bytes accessed | tf_op | source)
XLA Modules:
  0.0 112.0 jit_solution(4090861563418299348)
XLA Ops:
  0.0 1.2 %pack.1 = f32[2,296,256]{2,1,0:T(8,128)S(1)} custom-call(f32[512,256]{1,0:T(8,128)} %vectors_ref.1, f32[16,256]{1,0:T(8,128)} %cosines_ref.1, f32[16,256]{1,0:T(8,128)} %distances_ref.1, s32[16,256]{1,0:T(8,128)} %offsets_ref.1, s32[1,256]{1,0:T(1,128)} %bitcast.7, s32[2,256]{1,0:T(2,128)} %labels_ref.1), custom_call_target="tpu_custom_call" | custom-call | tf_op jit(solution)/shard_map/pack/pallas_call | solution.py:309
  1.2 10.7 %all_to_all.20.slab_ref.own_ref = f32[2,296,256]{2,1,0:T(8,128)S(1)} all-to-all(f32[2,296,256]{2,1,0:T(8,128)S(1)} %pack.1), channel_id=1, replica_groups=mesh['y'=4,'z'=16,'x'=4,'core'=2] {'core'}, dimensions={0} | all-to-all | bytes 1212416 | tf_op jit(solution)/shard_map/all_to_all | solution.py:295
  11.9 1.9 %collective-permute-start = (f32[2,296,256]{2,1,0:T(8,128)S(1)}, f32[2,296,256]{2,1,0:T(8,128)S(1)}, u32[]{:S(2)}, u32[]{:S(2)}) collective-permute-start(f32[2,296,256]{2,1,0:T(8,128)S(1)} %all_to_all.20.slab_ref.own_ref), channel_id=1, source_target_pairs={{0,2},{2,4},{4,6},{6,8},{8,10},{10,12},{12,14},{14,16},{16,18},{18... | collective-permute-start | bytes 1818632 | tf_op jit(solution)/shard_map/ppermute | solution.py:329
  13.9 10.4 %collective-permute-start.1 = (f32[2,296,256]{2,1,0:T(8,128)S(1)}, f32[2,296,256]{2,1,0:T(8,128)S(1)}, u32[]{:S(2)}, u32[]{:S(2)}) collective-permute-start(f32[2,296,256]{2,1,0:T(8,128)S(1)} %all_to_all.20.slab_ref.own_ref), channel_id=1, source_target_pairs={{0,510},{2,0},{4,2},{6,4},{8,6},{10,8},{12,10},{14,12},{16,14},{18... | collective-permute-start | bytes 1818632 | tf_op jit(solution)/shard_map/ppermute | solution.py:329
  24.3 2.4 %own_matrix.1 = (bf16[768,256]{1,0:T(8,128)(2,1)S(1)}, bf16[768,256]{1,0:T(8,128)(2,1)S(1)}, bf16[768,256]{1,0:T(8,128)(2,1)S(1)}, bf16[768,256]{1,0:T(8,128)(2,1)S(1)}) custom-call(f32[2,296,256]{2,1,0:T(8,128)S(1)} %all_to_all.20.slab_ref.own_ref), custom_call_target="tpu_custom_call" | custom-call | tf_op jit(solution)/shard_map/own_matrix/pallas_call | solution.py:309
  26.6 9.4 %collective-permute-done.left_ref = f32[2,296,256]{2,1,0:T(8,128)S(1)} collective-permute-done((f32[2,296,256]{2,1,0:T(8,128)S(1)}, f32[2,296,256]{2,1,0:T(8,128)S(1)}, u32[]{:S(2)}, u32[]{:S(2)}) %collective-permute-start) | collective-permute-done | bytes 606240 | tf_op jit(solution)/shard_map/ppermute | solution.py:329
  36.1 0.9 collective-permute-done.1.right_ref
  36.9 4.4 %apply_twice.1 = (f32[256,512]{1,0:T(8,128)S(1)}, f32[128,512]{1,0:T(8,128)S(1)}) custom-call(f32[2,296,256]{2,1,0:T(8,128)S(1)} %collective-permute-done.left_ref, f32[2,296,256]{2,1,0:T(8,128)S(1)} %all_to_all.20.slab_ref.own_ref, f32[2,296,256]{2,1,0:T(8,128)S(1)} %collective-permute-done.1.right_ref, ...), custom_call_target="tpu_custom_call" | custom-call | tf_op jit(solution)/shard_map/apply_twice/pallas_call | solution.py:309
  41.3 3.1 %collective-permute-start.2 = (f32[128,512]{1,0:T(8,128)S(1)}, f32[128,512]{1,0:T(8,128)S(1)}, u32[]{:S(2)}, u32[]{:S(2)}) collective-permute-start(f32[128,512]{1,0:T(8,128)S(1)} %get-tuple-element.19.lead_ref), channel_id=1, source_target_pairs={{0,1},{1,0},{2,3},{3,2},{4,5},{5,4},{6,7},{7,6},{8,9},{9,8},{10,11... | collective-permute-start | bytes 786440 | tf_op jit(solution)/shard_map/ppermute | solution.py:352
  44.4 1.1 %collective-permute-done.2.other_ref = f32[128,512]{1,0:T(8,128)S(1)} collective-permute-done((f32[128,512]{1,0:T(8,128)S(1)}, f32[128,512]{1,0:T(8,128)S(1)}, u32[]{:S(2)}, u32[]{:S(2)}) %collective-permute-start.2) | collective-permute-done | bytes 262176 | tf_op jit(solution)/shard_map/ppermute | solution.py:352
  45.6 0.7 gram.1
  46.3 10.3 %all_to_all.21.pieces_ref = f32[16,24,128]{2,1,0:T(8,128)S(1)} all-to-all(f32[16,24,128]{2,1,0:T(8,128)S(1)} %bitcast.6), channel_id=1, replica_groups=mesh['y'=4,'z'=16,'x'=4,'core'=2] {'y','x'}, dimensions={0} | all-to-all | bytes 393216 | tf_op jit(solution)/shard_map/all_to_all | solution.py:295
  56.6 0.7 sum_plane.1
  57.3 9.9 %all-to-all-start.2 = ((f32[16,24,128]{2,1,0:T(8,128)}), f32[16,24,128]{2,1,0:T(8,128)S(1)}, u32[]{:S(2)}, u32[]{:S(2)}) async-start(f32[16,24,128]{2,1,0:T(8,128)} %sum_plane.1), calls=%async_computation.2 | async-start | bytes 393216 | tf_op jit(solution)/shard_map/all_to_all | solution.py:295
  67.2 1.1 %share.1 = (f32[256,512]{1,0:T(8,128)S(1)}, f32[256,512]{1,0:T(8,128)}, f32[256,512]{1,0:T(8,128)}, f32[256,512]{1,0:T(8,128)S(1)}) custom-call(s32[1]{0:T(128)} %bitcast.core_ref.refs_0_, s32[1]{0:T(128)} %bitcast.1.chip_ref.refs_1_, f32[128,512]{1,0:T(8,128)S(1)} %get-tuple-element.19.lead_ref, f32[128,512]{1,0:T(8,128)S(1)} %collective-permute-done.2.other_ref, ...), custom_call_target="tpu_custom_call" | custom-call | tf_op jit(solution)/shard_map/share/pallas_call | solution.py:309
  68.4 2.5 %collective-permute-start.3 = (f32[256,512]{1,0:T(8,128)}, f32[256,512]{1,0:T(8,128)S(1)}, u32[]{:S(2)}, u32[]{:S(2)}) collective-permute-start(f32[256,512]{1,0:T(8,128)} %get-tuple-element.22), channel_id=1, source_target_pairs={{0,2},{2,4},{4,6},{6,0},{1,3},{3,5},{5,7},{7,1},{8,10},{10,12},{12... | collective-permute-start | bytes 1572872 | tf_op jit(solution)/shard_map/ppermute | solution.py:368
  70.8 3.2 %collective-permute-start.4 = (f32[256,512]{1,0:T(8,128)}, f32[256,512]{1,0:T(8,128)S(1)}, u32[]{:S(2)}, u32[]{:S(2)}) collective-permute-start(f32[256,512]{1,0:T(8,128)} %get-tuple-element.23), channel_id=1, source_target_pairs={{0,4},{2,6},{4,0},{6,2},{1,5},{3,7},{5,1},{7,3},{8,12},{10,14},{12... | collective-permute-start | bytes 1572872 | tf_op jit(solution)/shard_map/ppermute | solution.py:368
  74.0 3.2 %collective-permute-start.5 = (f32[256,512]{1,0:T(8,128)S(1)}, f32[256,512]{1,0:T(8,128)S(1)}, u32[]{:S(2)}, u32[]{:S(2)}) collective-permute-start(f32[256,512]{1,0:T(8,128)S(1)} %get-tuple-element.24), channel_id=1, source_target_pairs={{0,6},{2,0},{4,2},{6,4},{1,7},{3,1},{5,3},{7,5},{8,14},{10,8},{12,... | collective-permute-start | bytes 1572872 | tf_op jit(solution)/shard_map/ppermute | solution.py:368
  77.2 2.3 %all-to-all-done.2.pieces_ref = f32[16,24,128]{2,1,0:T(8,128)S(1)} async-done(((f32[16,24,128]{2,1,0:T(8,128)}), f32[16,24,128]{2,1,0:T(8,128)S(1)}, u32[]{:S(2)}, u32[]{:S(2)}) %all-to-all-start.2) | async-done | bytes 196640 | tf_op jit(solution)/shard_map/all_to_all | solution.py:295
  79.6 0.8 sum_depth.1
  80.4 9.0 %all-to-all-start.3 = ((f32[32,24,128]{2,1,0:T(8,128)}), f32[32,24,128]{2,1,0:T(8,128)S(1)}, u32[]{:S(2)}, u32[]{:S(2)}) async-start(f32[32,24,128]{2,1,0:T(8,128)} %sum_depth.1), calls=%async_computation.3 | async-start | bytes 786432 | tf_op jit(solution)/shard_map/all_to_all | solution.py:295
  89.3 0.0 collective-permute-done.3.refs_4_
  89.3 4.2 %collective-permute-done.4.refs_5_ = f32[256,512]{1,0:T(8,128)S(1)} collective-permute-done((f32[256,512]{1,0:T(8,128)}, f32[256,512]{1,0:T(8,128)S(1)}, u32[]{:S(2)}, u32[]{:S(2)}) %collective-permute-start.4) | collective-permute-done | bytes 524320 | tf_op jit(solution)/shard_map/ppermute | solution.py:368
  93.6 5.4 %collective-permute-done.5.refs_6_ = f32[256,512]{1,0:T(8,128)S(1)} collective-permute-done((f32[256,512]{1,0:T(8,128)S(1)}, f32[256,512]{1,0:T(8,128)S(1)}, u32[]{:S(2)}, u32[]{:S(2)}) %collective-permute-start.5) | collective-permute-done | bytes 524320 | tf_op jit(solution)/shard_map/ppermute | solution.py:368
  99.0 4.1 %all-to-all-done.3 = f32[32,24,128]{2,1,0:T(8,128)S(1)} async-done(((f32[32,24,128]{2,1,0:T(8,128)}), f32[32,24,128]{2,1,0:T(8,128)S(1)}, u32[]{:S(2)}, u32[]{:S(2)}) %all-to-all-start.3) | async-done | bytes 393248 | tf_op jit(solution)/shard_map/all_to_all | solution.py:295
  103.1 8.8 %finish.1 = f32[64,2048]{1,0:T(8,128)} custom-call(s32[1]{0:T(128)} %bitcast.core_ref.refs_0_, s32[1]{0:T(128)} %bitcast.1.chip_ref.refs_1_, f32[16,2,24,128]{3,2,1,0:T(8,128)S(1)} %bitcast.5, f32[256,512]{1,0:T(8,128)S(1)} %get-tuple-element.21.refs_3_, f32[256,512]{1,0:T(8,128)S(1)} %collective-permute-done.3.refs_4_, ...), custom_call_target="tpu_custom_call" | custom-call | tf_op jit(solution)/shard_map/finish/pallas_call | solution.py:309
Async XLA Ops:
  11.9 24.1 %collective-permute-start = (f32[2,296,256]{2,1,0:T(8,128)S(1)}, f32[2,296,256]{2,1,0:T(8,128)S(1)}, u32[]{:S(2)}, u32[]{:S(2)}) collective-permute-start(f32[2,296,256]{2,1,0:T(8,128)S(1)} %all_to_all.20.slab_ref.own_ref), channel_id=1, source_target_pairs={{0,2},{2,4},{4,6},{6,8},{8,10},{10,12},{12,14},{14,16},{16,18},{18... | collective-permute-start | bytes 1818632 | tf_op jit(solution)/shard_map/ppermute | solution.py:329
  13.9 23.1 %collective-permute-start.1 = (f32[2,296,256]{2,1,0:T(8,128)S(1)}, f32[2,296,256]{2,1,0:T(8,128)S(1)}, u32[]{:S(2)}, u32[]{:S(2)}) collective-permute-start(f32[2,296,256]{2,1,0:T(8,128)S(1)} %all_to_all.20.slab_ref.own_ref), channel_id=1, source_target_pairs={{0,510},{2,0},{4,2},{6,4},{8,6},{10,8},{12,10},{14,12},{16,14},{18... | collective-permute-start | bytes 1818632 | tf_op jit(solution)/shard_map/ppermute | solution.py:329
  41.3 4.3 %collective-permute-start.2 = (f32[128,512]{1,0:T(8,128)S(1)}, f32[128,512]{1,0:T(8,128)S(1)}, u32[]{:S(2)}, u32[]{:S(2)}) collective-permute-start(f32[128,512]{1,0:T(8,128)S(1)} %get-tuple-element.19.lead_ref), channel_id=1, source_target_pairs={{0,1},{1,0},{2,3},{3,2},{4,5},{5,4},{6,7},{7,6},{8,9},{9,8},{10,11... | collective-permute-start | bytes 786440 | tf_op jit(solution)/shard_map/ppermute | solution.py:352
  57.3 22.3 %all-to-all-start.2 = ((f32[16,24,128]{2,1,0:T(8,128)}), f32[16,24,128]{2,1,0:T(8,128)S(1)}, u32[]{:S(2)}, u32[]{:S(2)}) async-start(f32[16,24,128]{2,1,0:T(8,128)} %sum_plane.1), calls=%async_computation.2 | async-start | bytes 393216 | tf_op jit(solution)/shard_map/all_to_all | solution.py:295
  68.4 21.0 %collective-permute-start.3 = (f32[256,512]{1,0:T(8,128)}, f32[256,512]{1,0:T(8,128)S(1)}, u32[]{:S(2)}, u32[]{:S(2)}) collective-permute-start(f32[256,512]{1,0:T(8,128)} %get-tuple-element.22), channel_id=1, source_target_pairs={{0,2},{2,4},{4,6},{6,0},{1,3},{3,5},{5,7},{7,1},{8,10},{10,12},{12... | collective-permute-start | bytes 1572872 | tf_op jit(solution)/shard_map/ppermute | solution.py:368
  70.8 22.7 %collective-permute-start.4 = (f32[256,512]{1,0:T(8,128)}, f32[256,512]{1,0:T(8,128)S(1)}, u32[]{:S(2)}, u32[]{:S(2)}) collective-permute-start(f32[256,512]{1,0:T(8,128)} %get-tuple-element.23), channel_id=1, source_target_pairs={{0,4},{2,6},{4,0},{6,2},{1,5},{3,7},{5,1},{7,3},{8,12},{10,14},{12... | collective-permute-start | bytes 1572872 | tf_op jit(solution)/shard_map/ppermute | solution.py:368
  74.0 25.0 %collective-permute-start.5 = (f32[256,512]{1,0:T(8,128)S(1)}, f32[256,512]{1,0:T(8,128)S(1)}, u32[]{:S(2)}, u32[]{:S(2)}) collective-permute-start(f32[256,512]{1,0:T(8,128)S(1)} %get-tuple-element.24), channel_id=1, source_target_pairs={{0,6},{2,0},{4,2},{6,4},{1,7},{3,1},{5,3},{7,5},{8,14},{10,8},{12,... | collective-permute-start | bytes 1572872 | tf_op jit(solution)/shard_map/ppermute | solution.py:368
  80.4 22.8 %all-to-all-start.3 = ((f32[32,24,128]{2,1,0:T(8,128)}), f32[32,24,128]{2,1,0:T(8,128)S(1)}, u32[]{:S(2)}, u32[]{:S(2)}) async-start(f32[32,24,128]{2,1,0:T(8,128)} %sum_depth.1), calls=%async_computation.3 | async-start | bytes 786432 | tf_op jit(solution)/shard_map/all_to_all | solution.py:295

commit v10 on v9

--- a/solution.py
+++ b/solution.py
@@ -24,7 +24,7 @@
 CORES = 2
 OWN = NV // CORES
 TABLE = 40
-SHARED = HEAD + BLOCK
+HALF = HEAD // CORES
 CHIP = CORES * LOCAL
 F32 = jnp.float32
 BF16 = jnp.bfloat16
@@ -184,15 +184,24 @@
         gram_ref[part] = gram[:, 128 * part : 128 * part + 128]
 
 
-def share_kernel(core_ref, chip_ref, lead_ref, other_ref, applied_ref, *shared_refs):
-    count = len(shared_refs)
+def share_kernel(core_ref, chip_ref, lead_ref, other_ref, applied_ref, home_ref, *sent_refs):
+    count = 1 + len(sent_refs)
+    second = core_ref[0] == 1
+    head = [head_block(s, core_ref, lead_ref, other_ref) for s in range(STEPS)]
     for s in range(STEPS):
-        block = head_block(s, core_ref, lead_ref, other_ref)
-        for ref in shared_refs:
-            ref[BLOCK * s : BLOCK * s + BLOCK, :] = block
-    for step, ref in enumerate(shared_refs):
+        home_ref[BLOCK * s : BLOCK * s + BLOCK, :] = head[s]
+    middle = HALF - BLOCK
+    half = (
+        jnp.where(second, head[1][middle:], head[0][0 : BLOCK - middle]),
+        jnp.where(second, head[2][0:BLOCK], jnp.concatenate(
+            [head[0][BLOCK - middle :], head[1][0:middle]], axis=0)),
+    )
+    for ref in sent_refs:
+        ref[0 : BLOCK - middle, :] = half[0]
+        ref[BLOCK - middle : HALF, :] = half[1]
+    for step, ref in enumerate((home_ref, *sent_refs)):
         start = pl.multiple_of(lax.rem(chip_ref[0] + step, count) * BLOCK, BLOCK)
-        ref[HEAD:, :] = applied_ref[pl.ds(start, BLOCK), :]
+        ref[ref.shape[0] - BLOCK :, :] = applied_ref[pl.ds(start, BLOCK), :]
 
 
 def spread(value):
@@ -230,11 +239,12 @@
 
 
 def finish_kernel(scale, core_ref, chip_ref, gram_ref, *refs):
-    *shared_refs, basis_ref, results, sems = refs
+    home_ref, *others, basis_ref, results, sems = refs
+    count = 1 + len(others) // 2
+    got_refs, mate_refs = others[: count - 1], others[count - 1 :]
     chip, core = chip_ref[0], core_ref[0]
     second = core == 1
     column = CORES * chip + core
-    count = len(shared_refs)
     tiles = gram_ref.shape[0] // 2
 
     def columns_of(part, core):
@@ -276,12 +286,20 @@
                 couplings[s][:, places[t] : places[t] + BLOCK], weights[t], ((1,), (0,))
             )
         weights[s] = dot32(inverses[s], weight, ((0,), (0,)))
-    weight_high, weight_low = split(jnp.concatenate(weights, axis=0).T)
+    weights = jnp.concatenate(weights, axis=0)
+    swapped = jnp.concatenate([weights[HALF:], weights[0:HALF]], axis=0)
+    home_weights = split(weights.T)
+    other_weights = split(jnp.where(second, swapped, weights).T)
     outs = []
-    for step, ref in enumerate(shared_refs):
-        head_high, head_low = split(ref[0:HEAD, :])
-        result = jnp.where(follows, ref[HEAD:, :], 0.0)
-        results[step] = result + dot3(weight_high, weight_low, head_high, head_low)
+    for step in range(count):
+        if step == 0:
+            head, block, parts = home_ref[0:HEAD, :], home_ref[HEAD:, :], home_weights
+        else:
+            got = got_refs[step - 1]
+            head = jnp.concatenate([got[0:HALF, :], mate_refs[step - 1][0:HALF, :]], axis=0)
+            block, parts = got[HALF:, :], other_weights
+        head_high, head_low = split(head)
+        results[step] = jnp.where(follows, block, 0.0) + dot3(*parts, head_high, head_low)
         source = lax.rem(chip + count - step, count)
         columns = pl.ds(pl.multiple_of(source * CHIP, CHIP), CHIP)
         out = pltpu.make_async_copy(results.at[step], basis_ref.at[:, columns], sems.at[step])
@@ -356,18 +374,20 @@
         gram_kernel, "gram", shape((OWN // 128, HEAD, 128), F32),
         (core, lead, other, applied), (), [SMEM] + [VMEM] * 3,
     )
-    shared = call(
-        share_kernel, "share", (shape((SHARED, CHIP), F32),) * count,
+    home, *sent = call(
+        share_kernel, "share",
+        (shape((HEAD + BLOCK, CHIP), F32),) + (shape((HALF + BLOCK, CHIP), F32),) * (count - 1),
         (core, chip, lead, other, applied), (), [SMEM] * 2 + [VMEM] * 3,
     )
+    got = [
+        lax.ppermute(value, "x", [(i, (i + step + 1) % count) for i in range(count)])
+        for step, value in enumerate(sent)
+    ]
+    theirs = [lax.ppermute(value, "core", [(0, 1), (1, 0)]) for value in got]
     piece = (OWN // 128) * HEAD // planes
     everyone = planes * CORES
     gram = exchange(gram.reshape(planes, piece, 128), plane)
     gram = call(sum_kernel, "sum_plane", shape((depth, piece, 128), F32), (gram,))
-    shared = [shared[0]] + [
-        lax.ppermute(shared[step], "x", [(i, (i + step) % count) for i in range(count)])
-        for step in range(1, count)
-    ]
     gram = exchange(gram, "z")
     gram = call(sum_kernel, "sum_depth", shape((everyone, piece, 128), F32), (gram,))
     gram = exchange(gram, (*plane, "core"))
@@ -376,9 +396,9 @@
     slab_width = CHIP * count
     return call(
         lambda *refs: finish_kernel(scale, *refs), "finish", shape((BLOCK, slab_width), F32),
-        (core, chip, gram, *shared),
+        (core, chip, gram, home, *got, *theirs),
         [pltpu.VMEM((count, BLOCK, CHIP), F32), pltpu.SemaphoreType.DMA((count,))],
-        [SMEM] * 2 + [VMEM] * (1 + count), RAW,
+        [SMEM] * 2 + [VMEM] * (2 * count), RAW,
     )
 
 

time: 113 us -> 109 us (0.965)
  waiting for transfers between devices: 27.6 us -> 18.4 us
  starting transfers between devices: 43.2 us -> 49.6 us
    ppermute x3 -> x6, waiting for transfers between devices: 9.66 us -> 1.36 us  [the longest x3 1.35 us: on_device(): theirs = [lax.ppermute(value, 'core', [(0, 1), (1, 0)]) for value in got]]
    ppermute x3 -> x6, starting transfers between devices: 8.86 us -> 15.3 us  [the longest x3 8.87 us: on_device(): lax.ppermute(value, 'x', [(i, (i + step + 1) % count) for i in range(coun...]
  transfers between devices with their start and end apart: 8 -> 11, of which waited for: 7 -> 6; matrix products, arithmetic and copies ran while one was open for 0% -> 0% of each run, Pallas kernels for 4% -> 3%
where the time goes in v10:
time: 109 us; the launch traced here: 108 us
  starting transfers between devices  49.6 us (46%)
  blocking collectives  21 us (19%)
  Pallas kernels  19.1 us (18%)
  waiting for transfers between devices  18.4 us (17%)
    all_to_all x2, blocking collectives, exchange(): return lax.all_to_all(value, axes, split_axis=0, concat_axis=0, tiled=True)  21 us
    pallas_call x8, Pallas kernels, call(): pl.pallas_call(kernel, out_shape=out_shape, in_specs=specs or [VMEM] * le...  19.1 us
    all_to_all x2, starting transfers between devices, exchange(): return lax.all_to_all(value, axes, split_axis=0, concat_axis=0, tiled=True)  18.9 us
    ppermute x2, starting transfers between devices, shift(): lax.ppermute(value, chips, [(i, (i + step) % chip_count) for i in range(c...  12.3 us
    ppermute x2, waiting for transfers between devices, shift(): lax.ppermute(value, chips, [(i, (i + step) % chip_count) for i in range(c...  10.3 us
    ppermute x3, starting transfers between devices, on_device(): lax.ppermute(value, 'x', [(i, (i + step + 1) % count) for i in range(coun...  8.87 us
    ppermute x3, starting transfers between devices, on_device(): theirs = [lax.ppermute(value, 'core', [(0, 1), (1, 0)]) for value in got]  6.47 us
    all_to_all x2, waiting for transfers between devices, exchange(): return lax.all_to_all(value, axes, split_axis=0, concat_axis=0, tiled=True)  5.59 us
  transfers between devices with their start and end apart: 11, of which 6 were waited for; matrix products, arithmetic and copies ran while one was open for 0% of the time, Pallas kernels for 3%

profile of v10, /device:TPU:1, one launch (start us, length us, event | category | flops | bytes accessed | tf_op | source)
XLA Modules:
  0.0 108.3 jit_solution(13686387138177656266)
XLA Ops:
  0.0 1.2 %pack.1 = f32[2,296,256]{2,1,0:T(8,128)S(1)} custom-call(f32[512,256]{1,0:T(8,128)} %vectors_ref.1, f32[16,256]{1,0:T(8,128)} %cosines_ref.1, f32[16,256]{1,0:T(8,128)} %distances_ref.1, s32[16,256]{1,0:T(8,128)} %offsets_ref.1, s32[1,256]{1,0:T(1,128)} %bitcast.7, s32[2,256]{1,0:T(2,128)} %labels_ref.1), custom_call_target="tpu_custom_call" | custom-call | tf_op jit(solution)/shard_map/pack/pallas_call | solution.py:327
  1.2 10.7 %all_to_all.20.slab_ref.own_ref = f32[2,296,256]{2,1,0:T(8,128)S(1)} all-to-all(f32[2,296,256]{2,1,0:T(8,128)S(1)} %pack.1), channel_id=1, replica_groups=mesh['y'=4,'z'=16,'x'=4,'core'=2] {'core'}, dimensions={0} | all-to-all | bytes 1212416 | tf_op jit(solution)/shard_map/all_to_all | solution.py:313
  11.9 1.9 %collective-permute-start = (f32[2,296,256]{2,1,0:T(8,128)S(1)}, f32[2,296,256]{2,1,0:T(8,128)S(1)}, u32[]{:S(2)}, u32[]{:S(2)}) collective-permute-start(f32[2,296,256]{2,1,0:T(8,128)S(1)} %all_to_all.20.slab_ref.own_ref), channel_id=1, source_target_pairs={{0,2},{2,4},{4,6},{6,8},{8,10},{10,12},{12,14},{14,16},{16,18},{18... | collective-permute-start | bytes 1818632 | tf_op jit(solution)/shard_map/ppermute | solution.py:347
  13.9 10.4 %collective-permute-start.1 = (f32[2,296,256]{2,1,0:T(8,128)S(1)}, f32[2,296,256]{2,1,0:T(8,128)S(1)}, u32[]{:S(2)}, u32[]{:S(2)}) collective-permute-start(f32[2,296,256]{2,1,0:T(8,128)S(1)} %all_to_all.20.slab_ref.own_ref), channel_id=1, source_target_pairs={{0,510},{2,0},{4,2},{6,4},{8,6},{10,8},{12,10},{14,12},{16,14},{18... | collective-permute-start | bytes 1818632 | tf_op jit(solution)/shard_map/ppermute | solution.py:347
  24.3 2.4 %own_matrix.1 = (bf16[768,256]{1,0:T(8,128)(2,1)S(1)}, bf16[768,256]{1,0:T(8,128)(2,1)S(1)}, bf16[768,256]{1,0:T(8,128)(2,1)S(1)}, bf16[768,256]{1,0:T(8,128)(2,1)S(1)}) custom-call(f32[2,296,256]{2,1,0:T(8,128)S(1)} %all_to_all.20.slab_ref.own_ref), custom_call_target="tpu_custom_call" | custom-call | tf_op jit(solution)/shard_map/own_matrix/pallas_call | solution.py:327
  26.6 9.4 %collective-permute-done.left_ref = f32[2,296,256]{2,1,0:T(8,128)S(1)} collective-permute-done((f32[2,296,256]{2,1,0:T(8,128)S(1)}, f32[2,296,256]{2,1,0:T(8,128)S(1)}, u32[]{:S(2)}, u32[]{:S(2)}) %collective-permute-start) | collective-permute-done | bytes 606240 | tf_op jit(solution)/shard_map/ppermute | solution.py:347
  36.1 0.9 collective-permute-done.1.right_ref
  36.9 4.4 %apply_twice.1 = (f32[256,512]{1,0:T(8,128)S(1)}, f32[128,512]{1,0:T(8,128)S(1)}) custom-call(f32[2,296,256]{2,1,0:T(8,128)S(1)} %collective-permute-done.left_ref, f32[2,296,256]{2,1,0:T(8,128)S(1)} %all_to_all.20.slab_ref.own_ref, f32[2,296,256]{2,1,0:T(8,128)S(1)} %collective-permute-done.1.right_ref, ...), custom_call_target="tpu_custom_call" | custom-call | tf_op jit(solution)/shard_map/apply_twice/pallas_call | solution.py:327
  41.3 3.1 %collective-permute-start.2 = (f32[128,512]{1,0:T(8,128)S(1)}, f32[128,512]{1,0:T(8,128)S(1)}, u32[]{:S(2)}, u32[]{:S(2)}) collective-permute-start(f32[128,512]{1,0:T(8,128)S(1)} %get-tuple-element.19.lead_ref), channel_id=1, source_target_pairs={{0,1},{1,0},{2,3},{3,2},{4,5},{5,4},{6,7},{7,6},{8,9},{9,8},{10,11... | collective-permute-start | bytes 786440 | tf_op jit(solution)/shard_map/ppermute | solution.py:370
  44.4 1.1 %collective-permute-done.2.other_ref = f32[128,512]{1,0:T(8,128)S(1)} collective-permute-done((f32[128,512]{1,0:T(8,128)S(1)}, f32[128,512]{1,0:T(8,128)S(1)}, u32[]{:S(2)}, u32[]{:S(2)}) %collective-permute-start.2) | collective-permute-done | bytes 262176 | tf_op jit(solution)/shard_map/ppermute | solution.py:370
  45.6 0.7 gram.1
  46.3 10.3 %all_to_all.21.pieces_ref = f32[16,24,128]{2,1,0:T(8,128)S(1)} all-to-all(f32[16,24,128]{2,1,0:T(8,128)S(1)} %bitcast.6), channel_id=1, replica_groups=mesh['y'=4,'z'=16,'x'=4,'core'=2] {'y','x'}, dimensions={0} | all-to-all | bytes 393216 | tf_op jit(solution)/shard_map/all_to_all | solution.py:313
  56.6 0.7 sum_plane.1
  57.3 9.9 %all-to-all-start.2 = ((f32[16,24,128]{2,1,0:T(8,128)}), f32[16,24,128]{2,1,0:T(8,128)S(1)}, u32[]{:S(2)}, u32[]{:S(2)}) async-start(f32[16,24,128]{2,1,0:T(8,128)} %sum_plane.1), calls=%async_computation.2 | async-start | bytes 393216 | tf_op jit(solution)/shard_map/all_to_all | solution.py:313
  67.2 0.1 share.1
  67.3 2.5 %collective-permute-start.3 = (f32[160,512]{1,0:T(8,128)S(1)}, f32[160,512]{1,0:T(8,128)S(1)}, u32[]{:S(2)}, u32[]{:S(2)}) collective-permute-start(f32[160,512]{1,0:T(8,128)S(1)} %get-tuple-element.22), channel_id=1, source_target_pairs={{0,2},{2,4},{4,6},{6,0},{1,3},{3,5},{5,7},{7,1},{8,10},{10,12},{12... | collective-permute-start | bytes 983048 | tf_op jit(solution)/shard_map/ppermute | solution.py:383
  69.8 3.2 %collective-permute-start.4 = (f32[160,512]{1,0:T(8,128)S(1)}, f32[160,512]{1,0:T(8,128)S(1)}, u32[]{:S(2)}, u32[]{:S(2)}) collective-permute-start(f32[160,512]{1,0:T(8,128)S(1)} %get-tuple-element.23), channel_id=1, source_target_pairs={{0,4},{2,6},{4,0},{6,2},{1,5},{3,7},{5,1},{7,3},{8,12},{10,14},{12... | collective-permute-start | bytes 983048 | tf_op jit(solution)/shard_map/ppermute | solution.py:383
  73.0 3.2 %collective-permute-start.5 = (f32[160,512]{1,0:T(8,128)S(1)}, f32[160,512]{1,0:T(8,128)S(1)}, u32[]{:S(2)}, u32[]{:S(2)}) collective-permute-start(f32[160,512]{1,0:T(8,128)S(1)} %get-tuple-element.24), channel_id=1, source_target_pairs={{0,6},{2,0},{4,2},{6,4},{1,7},{3,1},{5,3},{7,5},{8,14},{10,8},{12,... | collective-permute-start | bytes 983048 | tf_op jit(solution)/shard_map/ppermute | solution.py:383
  76.2 3.3 %all-to-all-done.2.pieces_ref = f32[16,24,128]{2,1,0:T(8,128)S(1)} async-done(((f32[16,24,128]{2,1,0:T(8,128)}), f32[16,24,128]{2,1,0:T(8,128)S(1)}, u32[]{:S(2)}, u32[]{:S(2)}) %all-to-all-start.2) | async-done | bytes 196640 | tf_op jit(solution)/shard_map/all_to_all | solution.py:313
  79.6 0.8 sum_depth.1
  80.4 9.0 %all-to-all-start.3 = ((f32[32,24,128]{2,1,0:T(8,128)}), f32[32,24,128]{2,1,0:T(8,128)S(1)}, u32[]{:S(2)}, u32[]{:S(2)}) async-start(f32[32,24,128]{2,1,0:T(8,128)} %sum_depth.1), calls=%async_computation.3 | async-start | bytes 786432 | tf_op jit(solution)/shard_map/all_to_all | solution.py:313
  89.3 0.0 collective-permute-done.3.refs_4_
  89.3 2.1 %collective-permute-start.6 = (f32[160,512]{1,0:T(8,128)S(1)}, f32[160,512]{1,0:T(8,128)S(1)}, u32[]{:S(2)}, u32[]{:S(2)}) collective-permute-start(f32[160,512]{1,0:T(8,128)S(1)} %collective-permute-done.3.refs_4_), channel_id=1, source_target_pairs={{0,1},{1,0},{2,3},{3,2},{4,5},{5,4},{6,7},{7,6},{8,9},{9,8},{10,11... | collective-permute-start | bytes 983048 | tf_op jit(solution)/shard_map/ppermute | solution.py:386
  91.5 0.0 collective-permute-done.4.refs_5_
  91.5 2.2 %collective-permute-start.7 = (f32[160,512]{1,0:T(8,128)S(1)}, f32[160,512]{1,0:T(8,128)S(1)}, u32[]{:S(2)}, u32[]{:S(2)}) collective-permute-start(f32[160,512]{1,0:T(8,128)S(1)} %collective-permute-done.4.refs_5_), channel_id=1, source_target_pairs={{0,1},{1,0},{2,3},{3,2},{4,5},{5,4},{6,7},{7,6},{8,9},{9,8},{10,11... | collective-permute-start | bytes 983048 | tf_op jit(solution)/shard_map/ppermute | solution.py:386
  93.7 0.0 collective-permute-done.5.refs_6_
  93.7 2.1 %collective-permute-start.8 = (f32[160,512]{1,0:T(8,128)S(1)}, f32[160,512]{1,0:T(8,128)S(1)}, u32[]{:S(2)}, u32[]{:S(2)}) collective-permute-start(f32[160,512]{1,0:T(8,128)S(1)} %collective-permute-done.5.refs_6_), channel_id=1, source_target_pairs={{0,1},{1,0},{2,3},{3,2},{4,5},{5,4},{6,7},{7,6},{8,9},{9,8},{10,11... | collective-permute-start | bytes 983048 | tf_op jit(solution)/shard_map/ppermute | solution.py:386
  95.8 0.0 collective-permute-done.6.refs_7_
  95.9 0.0 collective-permute-done.7.refs_8_
  95.9 1.3 %collective-permute-done.8.refs_9_ = f32[160,512]{1,0:T(8,128)S(1)} collective-permute-done((f32[160,512]{1,0:T(8,128)S(1)}, f32[160,512]{1,0:T(8,128)S(1)}, u32[]{:S(2)}, u32[]{:S(2)}) %collective-permute-start.8) | collective-permute-done | bytes 327712 | tf_op jit(solution)/shard_map/ppermute | solution.py:386
  97.2 2.3 %all-to-all-done.3 = f32[32,24,128]{2,1,0:T(8,128)S(1)} async-done(((f32[32,24,128]{2,1,0:T(8,128)}), f32[32,24,128]{2,1,0:T(8,128)S(1)}, u32[]{:S(2)}, u32[]{:S(2)}) %all-to-all-start.3) | async-done | bytes 393248 | tf_op jit(solution)/shard_map/all_to_all | solution.py:313
  99.5 8.8 %finish.1 = f32[64,2048]{1,0:T(8,128)} custom-call(s32[1]{0:T(128)} %bitcast.core_ref.refs_0_, s32[1]{0:T(128)} %bitcast.1.chip_ref.refs_1_, f32[16,2,24,128]{3,2,1,0:T(8,128)S(1)} %bitcast.5, f32[256,512]{1,0:T(8,128)S(1)} %get-tuple-element.21.refs_3_, f32[160,512]{1,0:T(8,128)S(1)} %collective-permute-done.3.refs_4_, ...), custom_call_target="tpu_custom_call" | custom-call | tf_op jit(solution)/shard_map/finish/pallas_call | solution.py:327
Async XLA Ops:
  11.9 24.1 %collective-permute-start = (f32[2,296,256]{2,1,0:T(8,128)S(1)}, f32[2,296,256]{2,1,0:T(8,128)S(1)}, u32[]{:S(2)}, u32[]{:S(2)}) collective-permute-start(f32[2,296,256]{2,1,0:T(8,128)S(1)} %all_to_all.20.slab_ref.own_ref), channel_id=1, source_target_pairs={{0,2},{2,4},{4,6},{6,8},{8,10},{10,12},{12,14},{14,16},{16,18},{18... | collective-permute-start | bytes 1818632 | tf_op jit(solution)/shard_map/ppermute | solution.py:347
  13.9 23.1 %collective-permute-start.1 = (f32[2,296,256]{2,1,0:T(8,128)S(1)}, f32[2,296,256]{2,1,0:T(8,128)S(1)}, u32[]{:S(2)}, u32[]{:S(2)}) collective-permute-start(f32[2,296,256]{2,1,0:T(8,128)S(1)} %all_to_all.20.slab_ref.own_ref), channel_id=1, source_target_pairs={{0,510},{2,0},{4,2},{6,4},{8,6},{10,8},{12,10},{14,12},{16,14},{18... | collective-permute-start | bytes 1818632 | tf_op jit(solution)/shard_map/ppermute | solution.py:347
  41.3 4.3 %collective-permute-start.2 = (f32[128,512]{1,0:T(8,128)S(1)}, f32[128,512]{1,0:T(8,128)S(1)}, u32[]{:S(2)}, u32[]{:S(2)}) collective-permute-start(f32[128,512]{1,0:T(8,128)S(1)} %get-tuple-element.19.lead_ref), channel_id=1, source_target_pairs={{0,1},{1,0},{2,3},{3,2},{4,5},{5,4},{6,7},{7,6},{8,9},{9,8},{10,11... | collective-permute-start | bytes 786440 | tf_op jit(solution)/shard_map/ppermute | solution.py:370
  57.3 22.3 %all-to-all-start.2 = ((f32[16,24,128]{2,1,0:T(8,128)}), f32[16,24,128]{2,1,0:T(8,128)S(1)}, u32[]{:S(2)}, u32[]{:S(2)}) async-start(f32[16,24,128]{2,1,0:T(8,128)} %sum_plane.1), calls=%async_computation.2 | async-start | bytes 393216 | tf_op jit(solution)/shard_map/all_to_all | solution.py:313
  67.3 22.0 %collective-permute-start.3 = (f32[160,512]{1,0:T(8,128)S(1)}, f32[160,512]{1,0:T(8,128)S(1)}, u32[]{:S(2)}, u32[]{:S(2)}) collective-permute-start(f32[160,512]{1,0:T(8,128)S(1)} %get-tuple-element.22), channel_id=1, source_target_pairs={{0,2},{2,4},{4,6},{6,0},{1,3},{3,5},{5,7},{7,1},{8,10},{10,12},{12... | collective-permute-start | bytes 983048 | tf_op jit(solution)/shard_map/ppermute | solution.py:383
  69.8 21.6 %collective-permute-start.4 = (f32[160,512]{1,0:T(8,128)S(1)}, f32[160,512]{1,0:T(8,128)S(1)}, u32[]{:S(2)}, u32[]{:S(2)}) collective-permute-start(f32[160,512]{1,0:T(8,128)S(1)} %get-tuple-element.23), channel_id=1, source_target_pairs={{0,4},{2,6},{4,0},{6,2},{1,5},{3,7},{5,1},{7,3},{8,12},{10,14},{12... | collective-permute-start | bytes 983048 | tf_op jit(solution)/shard_map/ppermute | solution.py:383
  73.0 20.6 %collective-permute-start.5 = (f32[160,512]{1,0:T(8,128)S(1)}, f32[160,512]{1,0:T(8,128)S(1)}, u32[]{:S(2)}, u32[]{:S(2)}) collective-permute-start(f32[160,512]{1,0:T(8,128)S(1)} %get-tuple-element.24), channel_id=1, source_target_pairs={{0,6},{2,0},{4,2},{6,4},{1,7},{3,1},{5,3},{7,5},{8,14},{10,8},{12,... | collective-permute-start | bytes 983048 | tf_op jit(solution)/shard_map/ppermute | solution.py:383
  80.4 19.1 %all-to-all-start.3 = ((f32[32,24,128]{2,1,0:T(8,128)}), f32[32,24,128]{2,1,0:T(8,128)S(1)}, u32[]{:S(2)}, u32[]{:S(2)}) async-start(f32[32,24,128]{2,1,0:T(8,128)} %sum_depth.1), calls=%async_computation.3 | async-start | bytes 786432 | tf_op jit(solution)/shard_map/all_to_all | solution.py:313
  89.3 6.5 %collective-permute-start.6 = (f32[160,512]{1,0:T(8,128)S(1)}, f32[160,512]{1,0:T(8,128)S(1)}, u32[]{:S(2)}, u32[]{:S(2)}) collective-permute-start(f32[160,512]{1,0:T(8,128)S(1)} %collective-permute-done.3.refs_4_), channel_id=1, source_target_pairs={{0,1},{1,0},{2,3},{3,2},{4,5},{5,4},{6,7},{7,6},{8,9},{9,8},{10,11... | collective-permute-start | bytes 983048 | tf_op jit(solution)/shard_map/ppermute | solution.py:386
  91.5 4.4 %collective-permute-start.7 = (f32[160,512]{1,0:T(8,128)S(1)}, f32[160,512]{1,0:T(8,128)S(1)}, u32[]{:S(2)}, u32[]{:S(2)}) collective-permute-start(f32[160,512]{1,0:T(8,128)S(1)} %collective-permute-done.4.refs_5_), channel_id=1, source_target_pairs={{0,1},{1,0},{2,3},{3,2},{4,5},{5,4},{6,7},{7,6},{8,9},{9,8},{10,11... | collective-permute-start | bytes 983048 | tf_op jit(solution)/shard_map/ppermute | solution.py:386
  93.7 3.5 %collective-permute-start.8 = (f32[160,512]{1,0:T(8,128)S(1)}, f32[160,512]{1,0:T(8,128)S(1)}, u32[]{:S(2)}, u32[]{:S(2)}) collective-permute-start(f32[160,512]{1,0:T(8,128)S(1)} %collective-permute-done.5.refs_6_), channel_id=1, source_target_pairs={{0,1},{1,0},{2,3},{3,2},{4,5},{5,4},{6,7},{7,6},{8,9},{9,8},{10,11... | collective-permute-start | bytes 983048 | tf_op jit(solution)/shard_map/ppermute | solution.py:386

commit v11 on v10

--- a/solution.py
+++ b/solution.py
@@ -20,6 +20,7 @@
 NV = 512
 LOCAL = 256
 WIDE = LOCAL + 2 * REACH
+CHUNK = 128
 Y_SIZE = 4
 CORES = 2
 OWN = NV // CORES
@@ -88,7 +89,7 @@
 def build_matrix(table, high_ref, low_ref):
     hopping, offsets, onsite = table[0:16], table[16:32], table[32:33]
     lane = lax.broadcasted_iota(jnp.int32, (1, 128), 1).astype(F32)
-    row_index = lax.broadcasted_iota(jnp.int32, (32, 128), 0).astype(F32)
+    row_index = lax.broadcasted_iota(jnp.int32, (CHUNK, 128), 0).astype(F32)
     for half in range(2):
         columns = slice(128 * half, 128 * half + 128)
         empty = 640 * (1 - half)
@@ -96,26 +97,26 @@
         low_ref[empty : empty + 128, columns] = jnp.zeros((128, 128), BF16)
         home = lane + float(REACH)
         targets = [
-            jnp.broadcast_to(offsets[k : k + 1, columns] + home, (32, 128)) for k in range(SLOTS)
+            jnp.broadcast_to(offsets[k : k + 1, columns] + home, (CHUNK, 128)) for k in range(SLOTS)
         ]
-        values = [jnp.broadcast_to(hopping[k : k + 1, columns], (32, 128)) for k in range(SLOTS)]
-        homes = jnp.broadcast_to(home, (32, 128))
-        own = jnp.broadcast_to(onsite[:, columns], (32, 128))
+        values = [jnp.broadcast_to(hopping[k : k + 1, columns], (CHUNK, 128)) for k in range(SLOTS)]
+        homes = jnp.broadcast_to(home, (CHUNK, 128))
+        own = jnp.broadcast_to(onsite[:, columns], (CHUNK, 128))
 
         def chunk(step, carry):
-            base = step * 32
+            base = step * CHUNK
             rows = row_index + base.astype(F32)
             total = jnp.where(homes == rows, own, 0.0)
             for k in range(SLOTS):
                 total = jnp.where(targets[k] == rows, values[k], total)
             high = total.astype(BF16)
             low = (total - high.astype(F32)).astype(BF16)
-            place = pl.ds(pl.multiple_of(base + 128 * half, 32), 32)
+            place = pl.ds(pl.multiple_of(base + 128 * half, 128), CHUNK)
             high_ref[place, columns] = high
             low_ref[place, columns] = low
             return carry
 
-        lax.fori_loop(0, 20, chunk, 0)
+        lax.fori_loop(0, (WIDE - 128) // CHUNK, chunk, 0)
 
 
 def own_matrix_kernel(slab_ref, *refs):
@@ -261,8 +262,11 @@
     lane = lax.broadcasted_iota(jnp.int32, (BLOCK, 128), 1)
     row = lax.broadcasted_iota(jnp.int32, (BLOCK, 128), 0)
     identity = jnp.where(lane == row, 1.0, 0.0).astype(F32)
+    zero = jnp.zeros((BLOCK, BLOCK), F32)
+    for s in range(STEPS):
+        unit = [identity[:, 0:BLOCK] if t == s else zero for t in range(STEPS)]
+        gram[s] = jnp.concatenate([gram[s], *unit], axis=1)
     couplings = []
-    inverses = []
     for s in range(STEPS):
         part = places[s] // 128
         tile = gram[s][:, 128 * part : 128 * part + 128]
@@ -274,30 +278,28 @@
             gram[t] = gram[t] - dot32(
                 coupling[:, places[t] : places[t] + BLOCK], coupling, ((0,), (0,))
             )
-        inverses.append(inverse)
         couplings.append(coupling)
     follows = column >= STEPS
-    weights = [None] * STEPS
-    for s in reversed(range(STEPS)):
-        leads = jnp.where(column == s, identity[:, 0:BLOCK], 0.0)
-        weight = jnp.where(follows, -couplings[s][:, 4 * BLOCK : 5 * BLOCK], leads)
-        for t in range(s + 1, STEPS):
-            weight = weight - dot32(
-                couplings[s][:, places[t] : places[t] + BLOCK], weights[t], ((1,), (0,))
-            )
-        weights[s] = dot32(inverses[s], weight, ((0,), (0,)))
-    weights = jnp.concatenate(weights, axis=0)
-    swapped = jnp.concatenate([weights[HALF:], weights[0:HALF]], axis=0)
-    home_weights = split(weights.T)
-    other_weights = split(jnp.where(second, swapped, weights).T)
+    units = 6 * BLOCK
+    mine = jnp.concatenate([c[:, 4 * BLOCK : 5 * BLOCK] for c in couplings], axis=0)
+    inverse = jnp.concatenate([c[:, units:] for c in couplings], axis=0)
+    weight = -dot32(mine, inverse, ((0,), (0,)))
+    for s in range(STEPS):
+        weight = jnp.where(column == s, couplings[s][:, units:], weight)
+    parts = split(weight)
     outs = []
     for step in range(count):
         if step == 0:
-            head, block, parts = home_ref[0:HEAD, :], home_ref[HEAD:, :], home_weights
+            head, block = home_ref[0:HEAD, :], home_ref[HEAD:, :]
         else:
-            got = got_refs[step - 1]
-            head = jnp.concatenate([got[0:HALF, :], mate_refs[step - 1][0:HALF, :]], axis=0)
-            block, parts = got[HALF:, :], other_weights
+            got, mate = got_refs[step - 1], mate_refs[step - 1]
+            first, last = got[0:HALF, :], mate[0:HALF, :]
+            head = jnp.where(
+                second,
+                jnp.concatenate([last, first], axis=0),
+                jnp.concatenate([first, last], axis=0),
+            )
+            block = got[HALF:, :]
         head_high, head_low = split(head)
         results[step] = jnp.where(follows, block, 0.0) + dot3(*parts, head_high, head_low)
         source = lax.rem(chip + count - step, count)
@@ -379,15 +381,16 @@
         (shape((HEAD + BLOCK, CHIP), F32),) + (shape((HALF + BLOCK, CHIP), F32),) * (count - 1),
         (core, chip, lead, other, applied), (), [SMEM] * 2 + [VMEM] * 3,
     )
+    piece = (OWN // 128) * HEAD // planes
+    everyone = planes * CORES
+    gram = exchange(gram.reshape(planes, piece, 128), plane)
+    gram, home, *sent = lax.optimization_barrier((gram, home, *sent))
+    gram = call(sum_kernel, "sum_plane", shape((depth, piece, 128), F32), (gram,))
     got = [
         lax.ppermute(value, "x", [(i, (i + step + 1) % count) for i in range(count)])
         for step, value in enumerate(sent)
     ]
     theirs = [lax.ppermute(value, "core", [(0, 1), (1, 0)]) for value in got]
-    piece = (OWN // 128) * HEAD // planes
-    everyone = planes * CORES
-    gram = exchange(gram.reshape(planes, piece, 128), plane)
-    gram = call(sum_kernel, "sum_plane", shape((depth, piece, 128), F32), (gram,))
     gram = exchange(gram, "z")
     gram = call(sum_kernel, "sum_depth", shape((everyone, piece, 128), F32), (gram,))
     gram = exchange(gram, (*plane, "core"))

time: 109 us -> 109 us (level)
  blocking collectives: 21 us -> 10.7 us
  waiting for transfers between devices: 18.4 us -> 26.6 us
  starting transfers between devices: 49.6 us -> 52.5 us
    all_to_all x2 -> x1, blocking collectives: 21 us -> 10.7 us  [exchange(): return lax.all_to_all(value, axes, split_axis=0, concat_axis=0, tiled=True)]
    all_to_all x2 -> x3, waiting for transfers between devices: 5.59 us -> 13.3 us  [exchange(): return lax.all_to_all(value, axes, split_axis=0, concat_axis=0, tiled=True)]
    all_to_all x2 -> x3, starting transfers between devices: 18.9 us -> 21.7 us  [exchange(): return lax.all_to_all(value, axes, split_axis=0, concat_axis=0, tiled=True)]
  transfers between devices with their start and end apart: 11 -> 12, of which waited for: 6 -> 7; matrix products, arithmetic and copies ran while one was open for 0% -> 0% of each run, Pallas kernels for 3% -> 2%
where the time goes in v11:
time: 109 us; the launch traced here: 108 us
  starting transfers between devices  52.5 us (48%)
  waiting for transfers between devices  26.6 us (24%)
  Pallas kernels  18.2 us (17%)
  blocking collectives  10.7 us (10%)
    all_to_all x3, starting transfers between devices, exchange(): return lax.all_to_all(value, axes, split_axis=0, concat_axis=0, tiled=True)  21.7 us
    pallas_call x8, Pallas kernels, call(): pl.pallas_call(kernel, out_shape=out_shape, in_specs=specs or [VMEM] * le...  18.2 us
    all_to_all x3, waiting for transfers between devices, exchange(): return lax.all_to_all(value, axes, split_axis=0, concat_axis=0, tiled=True)  13.3 us
    ppermute x2, starting transfers between devices, shift(): lax.ppermute(value, chips, [(i, (i + step) % chip_count) for i in range(c...  12.3 us
    ppermute x2, waiting for transfers between devices, shift(): lax.ppermute(value, chips, [(i, (i + step) % chip_count) for i in range(c...  10.9 us
    all_to_all x1, blocking collectives, exchange(): return lax.all_to_all(value, axes, split_axis=0, concat_axis=0, tiled=True)  10.7 us
    ppermute x3, starting transfers between devices, on_device(): lax.ppermute(value, 'x', [(i, (i + step + 1) % count) for i in range(coun...  8.87 us
    ppermute x3, starting transfers between devices, on_device(): theirs = [lax.ppermute(value, 'core', [(0, 1), (1, 0)]) for value in got]  6.47 us
  transfers between devices with their start and end apart: 12, of which 7 were waited for; matrix products, arithmetic and copies ran while one was open for 0% of the time, Pallas kernels for 2%

profile of v11, /device:TPU:1, one launch (start us, length us, event | category | flops | bytes accessed | tf_op | source)
XLA Modules:
  0.0 108.2 jit_solution(13633718414655952426)
XLA Ops:
  0.0 1.2 %pack.1 = f32[2,296,256]{2,1,0:T(8,128)S(1)} custom-call(f32[512,256]{1,0:T(8,128)} %vectors_ref.1, f32[16,256]{1,0:T(8,128)} %cosines_ref.1, f32[16,256]{1,0:T(8,128)} %distances_ref.1, s32[16,256]{1,0:T(8,128)} %offsets_ref.1, s32[1,256]{1,0:T(1,128)} %bitcast.6, s32[2,256]{1,0:T(2,128)} %labels_ref.1), custom_call_target="tpu_custom_call" | custom-call | tf_op jit(solution)/shard_map/pack/pallas_call | solution.py:329
  1.2 10.7 %all_to_all.20.slab_ref.own_ref = f32[2,296,256]{2,1,0:T(8,128)S(1)} all-to-all(f32[2,296,256]{2,1,0:T(8,128)S(1)} %pack.1), channel_id=1, replica_groups=mesh['y'=4,'z'=16,'x'=4,'core'=2] {'core'}, dimensions={0} | all-to-all | bytes 1212416 | tf_op jit(solution)/shard_map/all_to_all | solution.py:315
  11.9 1.9 %collective-permute-start = (f32[2,296,256]{2,1,0:T(8,128)S(1)}, f32[2,296,256]{2,1,0:T(8,128)S(1)}, u32[]{:S(2)}, u32[]{:S(2)}) collective-permute-start(f32[2,296,256]{2,1,0:T(8,128)S(1)} %all_to_all.20.slab_ref.own_ref), channel_id=1, source_target_pairs={{0,2},{2,4},{4,6},{6,8},{8,10},{10,12},{12,14},{14,16},{16,18},{18... | collective-permute-start | bytes 1818632 | tf_op jit(solution)/shard_map/ppermute | solution.py:349
  13.9 10.4 %collective-permute-start.1 = (f32[2,296,256]{2,1,0:T(8,128)S(1)}, f32[2,296,256]{2,1,0:T(8,128)S(1)}, u32[]{:S(2)}, u32[]{:S(2)}) collective-permute-start(f32[2,296,256]{2,1,0:T(8,128)S(1)} %all_to_all.20.slab_ref.own_ref), channel_id=1, source_target_pairs={{0,510},{2,0},{4,2},{6,4},{8,6},{10,8},{12,10},{14,12},{16,14},{18... | collective-permute-start | bytes 1818632 | tf_op jit(solution)/shard_map/ppermute | solution.py:349
  24.3 1.8 %own_matrix.1 = (bf16[768,256]{1,0:T(8,128)(2,1)S(1)}, bf16[768,256]{1,0:T(8,128)(2,1)S(1)}, bf16[768,256]{1,0:T(8,128)(2,1)S(1)}, bf16[768,256]{1,0:T(8,128)(2,1)S(1)}) custom-call(f32[2,296,256]{2,1,0:T(8,128)S(1)} %all_to_all.20.slab_ref.own_ref), custom_call_target="tpu_custom_call" | custom-call | tf_op jit(solution)/shard_map/own_matrix/pallas_call | solution.py:329
  26.1 10.0 %collective-permute-done.left_ref = f32[2,296,256]{2,1,0:T(8,128)S(1)} collective-permute-done((f32[2,296,256]{2,1,0:T(8,128)S(1)}, f32[2,296,256]{2,1,0:T(8,128)S(1)}, u32[]{:S(2)}, u32[]{:S(2)}) %collective-permute-start) | collective-permute-done | bytes 606240 | tf_op jit(solution)/shard_map/ppermute | solution.py:349
  36.1 0.9 collective-permute-done.1.right_ref
  36.9 3.8 %apply_twice.1 = (f32[256,512]{1,0:T(8,128)S(1)}, f32[128,512]{1,0:T(8,128)S(1)}) custom-call(f32[2,296,256]{2,1,0:T(8,128)S(1)} %collective-permute-done.left_ref, f32[2,296,256]{2,1,0:T(8,128)S(1)} %all_to_all.20.slab_ref.own_ref, f32[2,296,256]{2,1,0:T(8,128)S(1)} %collective-permute-done.1.right_ref, ...), custom_call_target="tpu_custom_call" | custom-call | tf_op jit(solution)/shard_map/apply_twice/pallas_call | solution.py:329
  40.7 3.1 %collective-permute-start.2 = (f32[128,512]{1,0:T(8,128)S(1)}, f32[128,512]{1,0:T(8,128)S(1)}, u32[]{:S(2)}, u32[]{:S(2)}) collective-permute-start(f32[128,512]{1,0:T(8,128)S(1)} %get-tuple-element.24.lead_ref), channel_id=1, source_target_pairs={{0,1},{1,0},{2,3},{3,2},{4,5},{5,4},{6,7},{7,6},{8,9},{9,8},{10,11... | collective-permute-start | bytes 786440 | tf_op jit(solution)/shard_map/ppermute | solution.py:372
  43.8 1.1 %collective-permute-done.2.other_ref = f32[128,512]{1,0:T(8,128)S(1)} collective-permute-done((f32[128,512]{1,0:T(8,128)S(1)}, f32[128,512]{1,0:T(8,128)S(1)}, u32[]{:S(2)}, u32[]{:S(2)}) %collective-permute-start.2) | collective-permute-done | bytes 262176 | tf_op jit(solution)/shard_map/ppermute | solution.py:372
  45.0 1.4 %gram.1 = f32[2,192,128]{2,1,0:T(8,128)} custom-call(s32[1]{0:T(128)} %bitcast.core_ref.refs_0_, f32[128,512]{1,0:T(8,128)S(1)} %get-tuple-element.24.lead_ref, f32[128,512]{1,0:T(8,128)S(1)} %collective-permute-done.2.other_ref, f32[256,512]{1,0:T(8,128)S(1)} %get-tuple-element.25.applied_ref), custom_call_target="tpu_custom_call" | custom-call | tf_op jit(solution)/shard_map/gram/pallas_call | solution.py:329
  46.4 3.5 %all-to-all-start.1 = ((f32[16,24,128]{2,1,0:T(8,128)}), f32[16,24,128]{2,1,0:T(8,128)S(1)}, u32[]{:S(2)}, u32[]{:S(2)}) async-start(f32[16,24,128]{2,1,0:T(8,128)} %bitcast.3), calls=%async_computation.1 | async-start | bytes 393216 | tf_op jit(solution)/shard_map/all_to_all | solution.py:315
  49.9 0.1 share.1
  50.0 7.6 %all-to-all-done.1.pieces_ref = f32[16,24,128]{2,1,0:T(8,128)S(1)} async-done(((f32[16,24,128]{2,1,0:T(8,128)}), f32[16,24,128]{2,1,0:T(8,128)S(1)}, u32[]{:S(2)}, u32[]{:S(2)}) %all-to-all-start.1) | async-done | bytes 196640 | tf_op jit(solution)/shard_map/all_to_all | solution.py:315
  57.6 0.7 sum_plane.1
  58.3 9.2 %all-to-all-start.2 = ((f32[16,24,128]{2,1,0:T(8,128)}), f32[16,24,128]{2,1,0:T(8,128)S(1)}, u32[]{:S(2)}, u32[]{:S(2)}) async-start(f32[16,24,128]{2,1,0:T(8,128)} %sum_plane.1), calls=%async_computation.2 | async-start | bytes 393216 | tf_op jit(solution)/shard_map/all_to_all | solution.py:315
  67.5 2.5 %collective-permute-start.3 = (f32[160,512]{1,0:T(8,128)S(1)}, f32[160,512]{1,0:T(8,128)S(1)}, u32[]{:S(2)}, u32[]{:S(2)}) collective-permute-start(f32[160,512]{1,0:T(8,128)S(1)} %get-tuple-element.32), channel_id=1, source_target_pairs={{0,2},{2,4},{4,6},{6,0},{1,3},{3,5},{5,7},{7,1},{8,10},{10,12},{12... | collective-permute-start | bytes 983048 | tf_op jit(solution)/shard_map/ppermute | solution.py:390
  70.0 3.2 %collective-permute-start.4 = (f32[160,512]{1,0:T(8,128)S(1)}, f32[160,512]{1,0:T(8,128)S(1)}, u32[]{:S(2)}, u32[]{:S(2)}) collective-permute-start(f32[160,512]{1,0:T(8,128)S(1)} %get-tuple-element.33), channel_id=1, source_target_pairs={{0,4},{2,6},{4,0},{6,2},{1,5},{3,7},{5,1},{7,3},{8,12},{10,14},{12... | collective-permute-start | bytes 983048 | tf_op jit(solution)/shard_map/ppermute | solution.py:390
  73.2 3.2 %collective-permute-start.5 = (f32[160,512]{1,0:T(8,128)S(1)}, f32[160,512]{1,0:T(8,128)S(1)}, u32[]{:S(2)}, u32[]{:S(2)}) collective-permute-start(f32[160,512]{1,0:T(8,128)S(1)} %get-tuple-element.34), channel_id=1, source_target_pairs={{0,6},{2,0},{4,2},{6,4},{1,7},{3,1},{5,3},{7,5},{8,14},{10,8},{12,... | collective-permute-start | bytes 983048 | tf_op jit(solution)/shard_map/ppermute | solution.py:390
  76.4 3.4 %all-to-all-done.2.pieces_ref = f32[16,24,128]{2,1,0:T(8,128)S(1)} async-done(((f32[16,24,128]{2,1,0:T(8,128)}), f32[16,24,128]{2,1,0:T(8,128)S(1)}, u32[]{:S(2)}, u32[]{:S(2)}) %all-to-all-start.2) | async-done | bytes 196640 | tf_op jit(solution)/shard_map/all_to_all | solution.py:315
  79.9 0.8 sum_depth.1
  80.7 9.0 %all-to-all-start.3 = ((f32[32,24,128]{2,1,0:T(8,128)}), f32[32,24,128]{2,1,0:T(8,128)S(1)}, u32[]{:S(2)}, u32[]{:S(2)}) async-start(f32[32,24,128]{2,1,0:T(8,128)} %sum_depth.1), calls=%async_computation.3 | async-start | bytes 786432 | tf_op jit(solution)/shard_map/all_to_all | solution.py:315
  89.6 0.0 collective-permute-done.3.refs_4_
  89.6 2.1 %collective-permute-start.6 = (f32[160,512]{1,0:T(8,128)S(1)}, f32[160,512]{1,0:T(8,128)S(1)}, u32[]{:S(2)}, u32[]{:S(2)}) collective-permute-start(f32[160,512]{1,0:T(8,128)S(1)} %collective-permute-done.3.refs_4_), channel_id=1, source_target_pairs={{0,1},{1,0},{2,3},{3,2},{4,5},{5,4},{6,7},{7,6},{8,9},{9,8},{10,11... | collective-permute-start | bytes 983048 | tf_op jit(solution)/shard_map/ppermute | solution.py:393
  91.8 0.0 collective-permute-done.4.refs_5_
  91.8 2.2 %collective-permute-start.7 = (f32[160,512]{1,0:T(8,128)S(1)}, f32[160,512]{1,0:T(8,128)S(1)}, u32[]{:S(2)}, u32[]{:S(2)}) collective-permute-start(f32[160,512]{1,0:T(8,128)S(1)} %collective-permute-done.4.refs_5_), channel_id=1, source_target_pairs={{0,1},{1,0},{2,3},{3,2},{4,5},{5,4},{6,7},{7,6},{8,9},{9,8},{10,11... | collective-permute-start | bytes 983048 | tf_op jit(solution)/shard_map/ppermute | solution.py:393
  94.0 0.0 collective-permute-done.5.refs_6_
  94.0 2.1 %collective-permute-start.8 = (f32[160,512]{1,0:T(8,128)S(1)}, f32[160,512]{1,0:T(8,128)S(1)}, u32[]{:S(2)}, u32[]{:S(2)}) collective-permute-start(f32[160,512]{1,0:T(8,128)S(1)} %collective-permute-done.5.refs_6_), channel_id=1, source_target_pairs={{0,1},{1,0},{2,3},{3,2},{4,5},{5,4},{6,7},{7,6},{8,9},{9,8},{10,11... | collective-permute-start | bytes 983048 | tf_op jit(solution)/shard_map/ppermute | solution.py:393
  96.2 0.0 collective-permute-done.6.refs_7_
  96.2 0.0 collective-permute-done.7.refs_8_
  96.2 1.3 %collective-permute-done.8.refs_9_ = f32[160,512]{1,0:T(8,128)S(1)} collective-permute-done((f32[160,512]{1,0:T(8,128)S(1)}, f32[160,512]{1,0:T(8,128)S(1)}, u32[]{:S(2)}, u32[]{:S(2)}) %collective-permute-start.8) | collective-permute-done | bytes 327712 | tf_op jit(solution)/shard_map/ppermute | solution.py:393
  97.5 2.3 %all-to-all-done.3 = f32[32,24,128]{2,1,0:T(8,128)S(1)} async-done(((f32[32,24,128]{2,1,0:T(8,128)}), f32[32,24,128]{2,1,0:T(8,128)S(1)}, u32[]{:S(2)}, u32[]{:S(2)}) %all-to-all-start.3) | async-done | bytes 393248 | tf_op jit(solution)/shard_map/all_to_all | solution.py:315
  99.8 8.4 %finish.1 = f32[64,2048]{1,0:T(8,128)} custom-call(s32[1]{0:T(128)} %bitcast.core_ref.refs_0_, s32[1]{0:T(128)} %bitcast.1.chip_ref.refs_1_, f32[16,2,24,128]{3,2,1,0:T(8,128)S(1)} %bitcast.5, f32[256,512]{1,0:T(8,128)S(1)} %get-tuple-element.31.refs_3_, f32[160,512]{1,0:T(8,128)S(1)} %collective-permute-done.3.refs_4_, ...), custom_call_target="tpu_custom_call" | custom-call | tf_op jit(solution)/shard_map/finish/pallas_call | solution.py:329
Async XLA Ops:
  11.9 24.1 %collective-permute-start = (f32[2,296,256]{2,1,0:T(8,128)S(1)}, f32[2,296,256]{2,1,0:T(8,128)S(1)}, u32[]{:S(2)}, u32[]{:S(2)}) collective-permute-start(f32[2,296,256]{2,1,0:T(8,128)S(1)} %all_to_all.20.slab_ref.own_ref), channel_id=1, source_target_pairs={{0,2},{2,4},{4,6},{6,8},{8,10},{10,12},{12,14},{14,16},{16,18},{18... | collective-permute-start | bytes 1818632 | tf_op jit(solution)/shard_map/ppermute | solution.py:349
  13.9 23.1 %collective-permute-start.1 = (f32[2,296,256]{2,1,0:T(8,128)S(1)}, f32[2,296,256]{2,1,0:T(8,128)S(1)}, u32[]{:S(2)}, u32[]{:S(2)}) collective-permute-start(f32[2,296,256]{2,1,0:T(8,128)S(1)} %all_to_all.20.slab_ref.own_ref), channel_id=1, source_target_pairs={{0,510},{2,0},{4,2},{6,4},{8,6},{10,8},{12,10},{14,12},{16,14},{18... | collective-permute-start | bytes 1818632 | tf_op jit(solution)/shard_map/ppermute | solution.py:349
  40.7 4.3 %collective-permute-start.2 = (f32[128,512]{1,0:T(8,128)S(1)}, f32[128,512]{1,0:T(8,128)S(1)}, u32[]{:S(2)}, u32[]{:S(2)}) collective-permute-start(f32[128,512]{1,0:T(8,128)S(1)} %get-tuple-element.24.lead_ref), channel_id=1, source_target_pairs={{0,1},{1,0},{2,3},{3,2},{4,5},{5,4},{6,7},{7,6},{8,9},{9,8},{10,11... | collective-permute-start | bytes 786440 | tf_op jit(solution)/shard_map/ppermute | solution.py:372
  46.4 11.2 %all-to-all-start.1 = ((f32[16,24,128]{2,1,0:T(8,128)}), f32[16,24,128]{2,1,0:T(8,128)S(1)}, u32[]{:S(2)}, u32[]{:S(2)}) async-start(f32[16,24,128]{2,1,0:T(8,128)} %bitcast.3), calls=%async_computation.1 | async-start | bytes 393216 | tf_op jit(solution)/shard_map/all_to_all | solution.py:315
  58.3 21.6 %all-to-all-start.2 = ((f32[16,24,128]{2,1,0:T(8,128)}), f32[16,24,128]{2,1,0:T(8,128)S(1)}, u32[]{:S(2)}, u32[]{:S(2)}) async-start(f32[16,24,128]{2,1,0:T(8,128)} %sum_plane.1), calls=%async_computation.2 | async-start | bytes 393216 | tf_op jit(solution)/shard_map/all_to_all | solution.py:315
  67.5 22.1 %collective-permute-start.3 = (f32[160,512]{1,0:T(8,128)S(1)}, f32[160,512]{1,0:T(8,128)S(1)}, u32[]{:S(2)}, u32[]{:S(2)}) collective-permute-start(f32[160,512]{1,0:T(8,128)S(1)} %get-tuple-element.32), channel_id=1, source_target_pairs={{0,2},{2,4},{4,6},{6,0},{1,3},{3,5},{5,7},{7,1},{8,10},{10,12},{12... | collective-permute-start | bytes 983048 | tf_op jit(solution)/shard_map/ppermute | solution.py:390
  70.0 21.8 %collective-permute-start.4 = (f32[160,512]{1,0:T(8,128)S(1)}, f32[160,512]{1,0:T(8,128)S(1)}, u32[]{:S(2)}, u32[]{:S(2)}) collective-permute-start(f32[160,512]{1,0:T(8,128)S(1)} %get-tuple-element.33), channel_id=1, source_target_pairs={{0,4},{2,6},{4,0},{6,2},{1,5},{3,7},{5,1},{7,3},{8,12},{10,14},{12... | collective-permute-start | bytes 983048 | tf_op jit(solution)/shard_map/ppermute | solution.py:390
  73.2 20.8 %collective-permute-start.5 = (f32[160,512]{1,0:T(8,128)S(1)}, f32[160,512]{1,0:T(8,128)S(1)}, u32[]{:S(2)}, u32[]{:S(2)}) collective-permute-start(f32[160,512]{1,0:T(8,128)S(1)} %get-tuple-element.34), channel_id=1, source_target_pairs={{0,6},{2,0},{4,2},{6,4},{1,7},{3,1},{5,3},{7,5},{8,14},{10,8},{12,... | collective-permute-start | bytes 983048 | tf_op jit(solution)/shard_map/ppermute | solution.py:390
  80.7 19.1 %all-to-all-start.3 = ((f32[32,24,128]{2,1,0:T(8,128)}), f32[32,24,128]{2,1,0:T(8,128)S(1)}, u32[]{:S(2)}, u32[]{:S(2)}) async-start(f32[32,24,128]{2,1,0:T(8,128)} %sum_depth.1), calls=%async_computation.3 | async-start | bytes 786432 | tf_op jit(solution)/shard_map/all_to_all | solution.py:315
  89.6 6.5 %collective-permute-start.6 = (f32[160,512]{1,0:T(8,128)S(1)}, f32[160,512]{1,0:T(8,128)S(1)}, u32[]{:S(2)}, u32[]{:S(2)}) collective-permute-start(f32[160,512]{1,0:T(8,128)S(1)} %collective-permute-done.3.refs_4_), channel_id=1, source_target_pairs={{0,1},{1,0},{2,3},{3,2},{4,5},{5,4},{6,7},{7,6},{8,9},{9,8},{10,11... | collective-permute-start | bytes 983048 | tf_op jit(solution)/shard_map/ppermute | solution.py:393
  91.8 4.4 %collective-permute-start.7 = (f32[160,512]{1,0:T(8,128)S(1)}, f32[160,512]{1,0:T(8,128)S(1)}, u32[]{:S(2)}, u32[]{:S(2)}) collective-permute-start(f32[160,512]{1,0:T(8,128)S(1)} %collective-permute-done.4.refs_5_), channel_id=1, source_target_pairs={{0,1},{1,0},{2,3},{3,2},{4,5},{5,4},{6,7},{7,6},{8,9},{9,8},{10,11... | collective-permute-start | bytes 983048 | tf_op jit(solution)/shard_map/ppermute | solution.py:393
  94.0 3.5 %collective-permute-start.8 = (f32[160,512]{1,0:T(8,128)S(1)}, f32[160,512]{1,0:T(8,128)S(1)}, u32[]{:S(2)}, u32[]{:S(2)}) collective-permute-start(f32[160,512]{1,0:T(8,128)S(1)} %collective-permute-done.5.refs_6_), channel_id=1, source_target_pairs={{0,1},{1,0},{2,3},{3,2},{4,5},{5,4},{6,7},{7,6},{8,9},{9,8},{10,11... | collective-permute-start | bytes 983048 | tf_op jit(solution)/shard_map/ppermute | solution.py:393

commit v12 on v11

--- a/solution.py
+++ b/solution.py
@@ -185,24 +185,27 @@
         gram_ref[part] = gram[:, 128 * part : 128 * part + 128]
 
 
-def share_kernel(core_ref, chip_ref, lead_ref, other_ref, applied_ref, home_ref, *sent_refs):
+def share_kernel(core_ref, chip_ref, lead_ref, other_ref, applied_ref, *sent_refs):
     count = 1 + len(sent_refs)
     second = core_ref[0] == 1
     head = [head_block(s, core_ref, lead_ref, other_ref) for s in range(STEPS)]
-    for s in range(STEPS):
-        home_ref[BLOCK * s : BLOCK * s + BLOCK, :] = head[s]
     middle = HALF - BLOCK
-    half = (
-        jnp.where(second, head[1][middle:], head[0][0 : BLOCK - middle]),
-        jnp.where(second, head[2][0:BLOCK], jnp.concatenate(
-            [head[0][BLOCK - middle :], head[1][0:middle]], axis=0)),
-    )
-    for ref in sent_refs:
-        ref[0 : BLOCK - middle, :] = half[0]
-        ref[BLOCK - middle : HALF, :] = half[1]
-    for step, ref in enumerate((home_ref, *sent_refs)):
-        start = pl.multiple_of(lax.rem(chip_ref[0] + step, count) * BLOCK, BLOCK)
-        ref[ref.shape[0] - BLOCK :, :] = applied_ref[pl.ds(start, BLOCK), :]
+    rest = BLOCK - middle
+    top = jnp.where(second, head[1][middle:], head[0][0:rest])
+    bottom = jnp.where(
+        second, head[2], jnp.concatenate([head[0][rest:], head[1][0:middle]], axis=0)
+    )
+    for step, ref in enumerate(sent_refs):
+        ref[0:rest, :] = top
+        ref[rest:HALF, :] = bottom
+        start = pl.multiple_of(lax.rem(chip_ref[0] + step + 1, count) * BLOCK, BLOCK)
+        ref[HALF:, :] = applied_ref[pl.ds(start, BLOCK), :]
+
+
+def stack_kernel(*refs):
+    *got_refs, out_ref = refs
+    for step, ref in enumerate(got_refs):
+        out_ref[HALF * step : HALF * step + HALF, :] = ref[0:HALF, :]
 
 
 def spread(value):
@@ -240,9 +243,8 @@
 
 
 def finish_kernel(scale, core_ref, chip_ref, gram_ref, *refs):
-    home_ref, *others, basis_ref, results, sems = refs
-    count = 1 + len(others) // 2
-    got_refs, mate_refs = others[: count - 1], others[count - 1 :]
+    lead_ref, other_ref, applied_ref, mate_ref, *got_refs, basis_ref, results, sems = refs
+    count = 1 + len(got_refs)
     chip, core = chip_ref[0], core_ref[0]
     second = core == 1
     column = CORES * chip + core
@@ -290,10 +292,13 @@
     outs = []
     for step in range(count):
         if step == 0:
-            head, block = home_ref[0:HEAD, :], home_ref[HEAD:, :]
+            head = jnp.concatenate(
+                [head_block(s, core_ref, lead_ref, other_ref) for s in range(STEPS)], axis=0
+            )
+            block = applied_ref[pl.ds(pl.multiple_of(chip * BLOCK, BLOCK), BLOCK), :]
         else:
-            got, mate = got_refs[step - 1], mate_refs[step - 1]
-            first, last = got[0:HALF, :], mate[0:HALF, :]
+            got = got_refs[step - 1]
+            first, last = got[0:HALF, :], mate_ref[HALF * (step - 1) : HALF * step, :]
             head = jnp.where(
                 second,
                 jnp.concatenate([last, first], axis=0),
@@ -376,21 +381,20 @@
         gram_kernel, "gram", shape((OWN // 128, HEAD, 128), F32),
         (core, lead, other, applied), (), [SMEM] + [VMEM] * 3,
     )
-    home, *sent = call(
-        share_kernel, "share",
-        (shape((HEAD + BLOCK, CHIP), F32),) + (shape((HALF + BLOCK, CHIP), F32),) * (count - 1),
+    sent = call(
+        share_kernel, "share", (shape((HALF + BLOCK, CHIP), F32),) * (count - 1),
         (core, chip, lead, other, applied), (), [SMEM] * 2 + [VMEM] * 3,
     )
     piece = (OWN // 128) * HEAD // planes
     everyone = planes * CORES
     gram = exchange(gram.reshape(planes, piece, 128), plane)
-    gram, home, *sent = lax.optimization_barrier((gram, home, *sent))
     gram = call(sum_kernel, "sum_plane", shape((depth, piece, 128), F32), (gram,))
     got = [
         lax.ppermute(value, "x", [(i, (i + step + 1) % count) for i in range(count)])
         for step, value in enumerate(sent)
     ]
-    theirs = [lax.ppermute(value, "core", [(0, 1), (1, 0)]) for value in got]
+    stacked = call(stack_kernel, "stack", shape((HALF * (count - 1), CHIP), F32), got)
+    theirs = lax.ppermute(stacked, "core", [(0, 1), (1, 0)])
     gram = exchange(gram, "z")
     gram = call(sum_kernel, "sum_depth", shape((everyone, piece, 128), F32), (gram,))
     gram = exchange(gram, (*plane, "core"))
@@ -399,9 +403,9 @@
     slab_width = CHIP * count
     return call(
         lambda *refs: finish_kernel(scale, *refs), "finish", shape((BLOCK, slab_width), F32),
-        (core, chip, gram, home, *got, *theirs),
+        (core, chip, gram, lead, other, applied, theirs, *got),
         [pltpu.VMEM((count, BLOCK, CHIP), F32), pltpu.SemaphoreType.DMA((count,))],
-        [SMEM] * 2 + [VMEM] * (2 * count), RAW,
+        [SMEM] * 2 + [VMEM] * (4 + count), RAW,
     )
 
 

time: 109 us -> 117 us (1.073)
  blocking collectives: 10.7 us -> 21 us
  starting transfers between devices: 52.5 us -> 42.9 us
  waiting for transfers between devices: 26.6 us -> 34.1 us
    ppermute x3, waiting for transfers between devices: 0.01 us -> 12 us  [on_device(): lax.ppermute(value, 'x', [(i, (i + step + 1) % count) for i in range(coun...]
    all_to_all x1 -> x2, blocking collectives: 10.7 us -> 21 us  [exchange(): return lax.all_to_all(value, axes, split_axis=0, concat_axis=0, tiled=True)]
    all_to_all x3 -> x2, starting transfers between devices: 21.7 us -> 14.7 us  [exchange(): return lax.all_to_all(value, axes, split_axis=0, concat_axis=0, tiled=True)]
    all_to_all x3 -> x2, waiting for transfers between devices: 13.3 us -> 10.2 us  [exchange(): return lax.all_to_all(value, axes, split_axis=0, concat_axis=0, tiled=True)]
    ppermute x3 -> x1, starting transfers between devices: 6.47 us -> 3.84 us  [on_device(): theirs = lax.ppermute(stacked, 'core', [(0, 1), (1, 0)])]
    ppermute x3 -> x1, waiting for transfers between devices: 1.35 us -> 0.01 us  [on_device(): theirs = lax.ppermute(stacked, 'core', [(0, 1), (1, 0)])]
    pallas_call x8 -> x9, Pallas kernels: 18.2 us -> 18.6 us  [call(): pl.pallas_call(kernel, out_shape=out_shape, in_specs=specs or [VMEM] * le...]
  transfers between devices with their start and end apart: 12 -> 9, of which waited for: 7 -> 7; matrix products, arithmetic and copies ran while one was open for 0% -> 0% of each run, Pallas kernels for 2% -> 2%
where the time goes in v12:
time: 117 us
  starting transfers between devices  42.9 us (37%)
  waiting for transfers between devices  34.1 us (29%)
  blocking collectives  21 us (18%)
  Pallas kernels  18.6 us (16%)
    all_to_all x2, blocking collectives, exchange(): return lax.all_to_all(value, axes, split_axis=0, concat_axis=0, tiled=True)  21 us
    pallas_call x9, Pallas kernels, call(): pl.pallas_call(kernel, out_shape=out_shape, in_specs=specs or [VMEM] * le...  18.6 us
    all_to_all x2, starting transfers between devices, exchange(): return lax.all_to_all(value, axes, split_axis=0, concat_axis=0, tiled=True)  14.7 us
    ppermute x2, starting transfers between devices, shift(): lax.ppermute(value, chips, [(i, (i + step) % chip_count) for i in range(c...  12.3 us
    ppermute x3, waiting for transfers between devices, on_device(): lax.ppermute(value, 'x', [(i, (i + step + 1) % count) for i in range(coun...  12 us
    ppermute x2, waiting for transfers between devices, shift(): lax.ppermute(value, chips, [(i, (i + step) % chip_count) for i in range(c...  10.9 us
    all_to_all x2, waiting for transfers between devices, exchange(): return lax.all_to_all(value, axes, split_axis=0, concat_axis=0, tiled=True)  10.2 us
    ppermute x3, starting transfers between devices, on_device(): lax.ppermute(value, 'x', [(i, (i + step + 1) % count) for i in range(coun...  8.87 us
  transfers between devices with their start and end apart: 9, of which 7 were waited for; matrix products, arithmetic and copies ran while one was open for 0% of the time, Pallas kernels for 2%

profile of v12, /device:TPU:1, one launch (start us, length us, event | category | flops | bytes accessed | tf_op | source)
XLA Modules:
  0.0 116.7 jit_solution(10757382758267213488)
XLA Ops:
  0.0 1.2 %pack.1 = f32[2,296,256]{2,1,0:T(8,128)S(1)} custom-call(f32[512,256]{1,0:T(8,128)} %vectors_ref.1, f32[16,256]{1,0:T(8,128)} %cosines_ref.1, f32[16,256]{1,0:T(8,128)} %distances_ref.1, s32[16,256]{1,0:T(8,128)} %offsets_ref.1, s32[1,256]{1,0:T(1,128)} %bitcast.7, s32[2,256]{1,0:T(2,128)} %labels_ref.1), custom_call_target="tpu_custom_call" | custom-call | tf_op jit(solution)/shard_map/pack/pallas_call | solution.py:334
  1.2 10.7 %all_to_all.20.slab_ref.own_ref = f32[2,296,256]{2,1,0:T(8,128)S(1)} all-to-all(f32[2,296,256]{2,1,0:T(8,128)S(1)} %pack.1), channel_id=1, replica_groups=mesh['y'=4,'z'=16,'x'=4,'core'=2] {'core'}, dimensions={0} | all-to-all | bytes 1212416 | tf_op jit(solution)/shard_map/all_to_all | solution.py:320
  11.9 1.9 %collective-permute-start = (f32[2,296,256]{2,1,0:T(8,128)S(1)}, f32[2,296,256]{2,1,0:T(8,128)S(1)}, u32[]{:S(2)}, u32[]{:S(2)}) collective-permute-start(f32[2,296,256]{2,1,0:T(8,128)S(1)} %all_to_all.20.slab_ref.own_ref), channel_id=1, source_target_pairs={{0,2},{2,4},{4,6},{6,8},{8,10},{10,12},{12,14},{14,16},{16,18},{18... | collective-permute-start | bytes 1818632 | tf_op jit(solution)/shard_map/ppermute | solution.py:354
  13.9 10.4 %collective-permute-start.1 = (f32[2,296,256]{2,1,0:T(8,128)S(1)}, f32[2,296,256]{2,1,0:T(8,128)S(1)}, u32[]{:S(2)}, u32[]{:S(2)}) collective-permute-start(f32[2,296,256]{2,1,0:T(8,128)S(1)} %all_to_all.20.slab_ref.own_ref), channel_id=1, source_target_pairs={{0,510},{2,0},{4,2},{6,4},{8,6},{10,8},{12,10},{14,12},{16,14},{18... | collective-permute-start | bytes 1818632 | tf_op jit(solution)/shard_map/ppermute | solution.py:354
  24.3 1.8 %own_matrix.1 = (bf16[768,256]{1,0:T(8,128)(2,1)S(1)}, bf16[768,256]{1,0:T(8,128)(2,1)S(1)}, bf16[768,256]{1,0:T(8,128)(2,1)S(1)}, bf16[768,256]{1,0:T(8,128)(2,1)S(1)}) custom-call(f32[2,296,256]{2,1,0:T(8,128)S(1)} %all_to_all.20.slab_ref.own_ref), custom_call_target="tpu_custom_call" | custom-call | tf_op jit(solution)/shard_map/own_matrix/pallas_call | solution.py:334
  26.1 10.0 %collective-permute-done.left_ref = f32[2,296,256]{2,1,0:T(8,128)S(1)} collective-permute-done((f32[2,296,256]{2,1,0:T(8,128)S(1)}, f32[2,296,256]{2,1,0:T(8,128)S(1)}, u32[]{:S(2)}, u32[]{:S(2)}) %collective-permute-start) | collective-permute-done | bytes 606240 | tf_op jit(solution)/shard_map/ppermute | solution.py:354
  36.1 0.9 collective-permute-done.1.right_ref
  36.9 3.8 %apply_twice.1 = (f32[256,512]{1,0:T(8,128)S(1)}, f32[128,512]{1,0:T(8,128)S(1)}) custom-call(f32[2,296,256]{2,1,0:T(8,128)S(1)} %collective-permute-done.left_ref, f32[2,296,256]{2,1,0:T(8,128)S(1)} %all_to_all.20.slab_ref.own_ref, f32[2,296,256]{2,1,0:T(8,128)S(1)} %collective-permute-done.1.right_ref, ...), custom_call_target="tpu_custom_call" | custom-call | tf_op jit(solution)/shard_map/apply_twice/pallas_call | solution.py:334
  40.7 3.1 %collective-permute-start.2 = (f32[128,512]{1,0:T(8,128)S(1)}, f32[128,512]{1,0:T(8,128)S(1)}, u32[]{:S(2)}, u32[]{:S(2)}) collective-permute-start(f32[128,512]{1,0:T(8,128)S(1)} %get-tuple-element.18.lead_ref.refs_3_), channel_id=1, source_target_pairs={{0,1},{1,0},{2,3},{3,2},{4,5},{5,4},{6,7},{7,6},{8,9},{9,8},{10,11... | collective-permute-start | bytes 786440 | tf_op jit(solution)/shard_map/ppermute | solution.py:377
  43.8 1.1 collective-permute-done.2.other_ref.refs_4_
  45.0 0.7 gram.1
  45.7 10.3 %all_to_all.21.pieces_ref = f32[16,24,128]{2,1,0:T(8,128)S(1)} all-to-all(f32[16,24,128]{2,1,0:T(8,128)S(1)} %bitcast.6), channel_id=1, replica_groups=mesh['y'=4,'z'=16,'x'=4,'core'=2] {'y','x'}, dimensions={0} | all-to-all | bytes 393216 | tf_op jit(solution)/shard_map/all_to_all | solution.py:320
  56.0 0.7 sum_plane.1
  56.7 9.9 %all-to-all-start.2 = ((f32[16,24,128]{2,1,0:T(8,128)}), f32[16,24,128]{2,1,0:T(8,128)S(1)}, u32[]{:S(2)}, u32[]{:S(2)}) async-start(f32[16,24,128]{2,1,0:T(8,128)} %sum_plane.1), calls=%async_computation.2 | async-start | bytes 393216 | tf_op jit(solution)/shard_map/all_to_all | solution.py:320
  66.7 0.1 share.1
  66.7 2.5 %collective-permute-start.3 = (f32[160,512]{1,0:T(8,128)S(1)}, f32[160,512]{1,0:T(8,128)S(1)}, u32[]{:S(2)}, u32[]{:S(2)}) collective-permute-start(f32[160,512]{1,0:T(8,128)S(1)} %get-tuple-element.20), channel_id=1, source_target_pairs={{0,2},{2,4},{4,6},{6,0},{1,3},{3,5},{5,7},{7,1},{8,10},{10,12},{12... | collective-permute-start | bytes 983048 | tf_op jit(solution)/shard_map/ppermute | solution.py:393
  69.2 3.2 %collective-permute-start.4 = (f32[160,512]{1,0:T(8,128)S(1)}, f32[160,512]{1,0:T(8,128)S(1)}, u32[]{:S(2)}, u32[]{:S(2)}) collective-permute-start(f32[160,512]{1,0:T(8,128)S(1)} %get-tuple-element.21), channel_id=1, source_target_pairs={{0,4},{2,6},{4,0},{6,2},{1,5},{3,7},{5,1},{7,3},{8,12},{10,14},{12... | collective-permute-start | bytes 983048 | tf_op jit(solution)/shard_map/ppermute | solution.py:393
  72.4 3.2 %collective-permute-start.5 = (f32[160,512]{1,0:T(8,128)S(1)}, f32[160,512]{1,0:T(8,128)S(1)}, u32[]{:S(2)}, u32[]{:S(2)}) collective-permute-start(f32[160,512]{1,0:T(8,128)S(1)} %get-tuple-element.22), channel_id=1, source_target_pairs={{0,6},{2,0},{4,2},{6,4},{1,7},{3,1},{5,3},{7,5},{8,14},{10,8},{12,... | collective-permute-start | bytes 983048 | tf_op jit(solution)/shard_map/ppermute | solution.py:393
  75.6 2.0 %collective-permute-done.3.refs_0_.refs_7_ = f32[160,512]{1,0:T(8,128)S(1)} collective-permute-done((f32[160,512]{1,0:T(8,128)S(1)}, f32[160,512]{1,0:T(8,128)S(1)}, u32[]{:S(2)}, u32[]{:S(2)}) %collective-permute-start.3) | collective-permute-done | bytes 327712 | tf_op jit(solution)/shard_map/ppermute | solution.py:393
  77.7 5.6 %collective-permute-done.4.refs_1_.refs_8_ = f32[160,512]{1,0:T(8,128)S(1)} collective-permute-done((f32[160,512]{1,0:T(8,128)S(1)}, f32[160,512]{1,0:T(8,128)S(1)}, u32[]{:S(2)}, u32[]{:S(2)}) %collective-permute-start.4) | collective-permute-done | bytes 327712 | tf_op jit(solution)/shard_map/ppermute | solution.py:393
  83.3 4.3 %collective-permute-done.5.refs_2_.refs_9_ = f32[160,512]{1,0:T(8,128)S(1)} collective-permute-done((f32[160,512]{1,0:T(8,128)S(1)}, f32[160,512]{1,0:T(8,128)S(1)}, u32[]{:S(2)}, u32[]{:S(2)}) %collective-permute-start.5) | collective-permute-done | bytes 327712 | tf_op jit(solution)/shard_map/ppermute | solution.py:393
  87.6 3.8 %collective-permute-start.6 = (f32[288,512]{1,0:T(8,128)S(1)}, f32[288,512]{1,0:T(8,128)}, u32[]{:S(2)}, u32[]{:S(2)}) collective-permute-start(f32[288,512]{1,0:T(8,128)S(1)} %stack.1), channel_id=1, source_target_pairs={{0,1},{1,0},{2,3},{3,2},{4,5},{5,4},{6,7},{7,6},{8,9},{9,8},{10,11... | collective-permute-start | bytes 1769480 | tf_op jit(solution)/shard_map/ppermute | solution.py:397
  91.5 0.0 all-to-all-done.2.pieces_ref
  91.5 0.8 sum_depth.1
  92.3 4.8 %all-to-all-start.3 = ((f32[32,24,128]{2,1,0:T(8,128)}), f32[32,24,128]{2,1,0:T(8,128)S(1)}, u32[]{:S(2)}, u32[]{:S(2)}) async-start(f32[32,24,128]{2,1,0:T(8,128)} %sum_depth.1), calls=%async_computation.3 | async-start | bytes 786432 | tf_op jit(solution)/shard_map/all_to_all | solution.py:320
  97.1 0.0 collective-permute-done.6.refs_6_
  97.1 10.2 %all-to-all-done.3 = f32[32,24,128]{2,1,0:T(8,128)S(1)} async-done(((f32[32,24,128]{2,1,0:T(8,128)}), f32[32,24,128]{2,1,0:T(8,128)S(1)}, u32[]{:S(2)}, u32[]{:S(2)}) %all-to-all-start.3) | async-done | bytes 393248 | tf_op jit(solution)/shard_map/all_to_all | solution.py:320
  107.3 9.4 %finish.1 = f32[64,2048]{1,0:T(8,128)} custom-call(s32[1]{0:T(128)} %bitcast.core_ref.refs_0_, s32[1]{0:T(128)} %bitcast.1.chip_ref.refs_1_, f32[16,2,24,128]{3,2,1,0:T(8,128)S(1)} %bitcast.5, f32[128,512]{1,0:T(8,128)S(1)} %get-tuple-element.18.lead_ref.refs_3_, f32[128,512]{1,0:T(8,128)S(1)} %collective-permute-done.2.other_ref.refs_4_, ...), custom_call_target="tpu_custom_call" | custom-call | tf_op jit(solution)/shard_map/finish/pallas_call | solution.py:334
  (1 shorter events, 0.0 us)
Async XLA Ops:
  11.9 24.1 %collective-permute-start = (f32[2,296,256]{2,1,0:T(8,128)S(1)}, f32[2,296,256]{2,1,0:T(8,128)S(1)}, u32[]{:S(2)}, u32[]{:S(2)}) collective-permute-start(f32[2,296,256]{2,1,0:T(8,128)S(1)} %all_to_all.20.slab_ref.own_ref), channel_id=1, source_target_pairs={{0,2},{2,4},{4,6},{6,8},{8,10},{10,12},{12,14},{14,16},{16,18},{18... | collective-permute-start | bytes 1818632 | tf_op jit(solution)/shard_map/ppermute | solution.py:354
  13.9 23.1 %collective-permute-start.1 = (f32[2,296,256]{2,1,0:T(8,128)S(1)}, f32[2,296,256]{2,1,0:T(8,128)S(1)}, u32[]{:S(2)}, u32[]{:S(2)}) collective-permute-start(f32[2,296,256]{2,1,0:T(8,128)S(1)} %all_to_all.20.slab_ref.own_ref), channel_id=1, source_target_pairs={{0,510},{2,0},{4,2},{6,4},{8,6},{10,8},{12,10},{14,12},{16,14},{18... | collective-permute-start | bytes 1818632 | tf_op jit(solution)/shard_map/ppermute | solution.py:354
  40.7 4.3 %collective-permute-start.2 = (f32[128,512]{1,0:T(8,128)S(1)}, f32[128,512]{1,0:T(8,128)S(1)}, u32[]{:S(2)}, u32[]{:S(2)}) collective-permute-start(f32[128,512]{1,0:T(8,128)S(1)} %get-tuple-element.18.lead_ref.refs_3_), channel_id=1, source_target_pairs={{0,1},{1,0},{2,3},{3,2},{4,5},{5,4},{6,7},{7,6},{8,9},{9,8},{10,11... | collective-permute-start | bytes 786440 | tf_op jit(solution)/shard_map/ppermute | solution.py:377
  56.7 34.8 %all-to-all-start.2 = ((f32[16,24,128]{2,1,0:T(8,128)}), f32[16,24,128]{2,1,0:T(8,128)S(1)}, u32[]{:S(2)}, u32[]{:S(2)}) async-start(f32[16,24,128]{2,1,0:T(8,128)} %sum_plane.1), calls=%async_computation.2 | async-start | bytes 393216 | tf_op jit(solution)/shard_map/all_to_all | solution.py:320
  66.7 10.9 %collective-permute-start.3 = (f32[160,512]{1,0:T(8,128)S(1)}, f32[160,512]{1,0:T(8,128)S(1)}, u32[]{:S(2)}, u32[]{:S(2)}) collective-permute-start(f32[160,512]{1,0:T(8,128)S(1)} %get-tuple-element.20), channel_id=1, source_target_pairs={{0,2},{2,4},{4,6},{6,0},{1,3},{3,5},{5,7},{7,1},{8,10},{10,12},{12... | collective-permute-start | bytes 983048 | tf_op jit(solution)/shard_map/ppermute | solution.py:393
  69.2 14.1 %collective-permute-start.4 = (f32[160,512]{1,0:T(8,128)S(1)}, f32[160,512]{1,0:T(8,128)S(1)}, u32[]{:S(2)}, u32[]{:S(2)}) collective-permute-start(f32[160,512]{1,0:T(8,128)S(1)} %get-tuple-element.21), channel_id=1, source_target_pairs={{0,4},{2,6},{4,0},{6,2},{1,5},{3,7},{5,1},{7,3},{8,12},{10,14},{12... | collective-permute-start | bytes 983048 | tf_op jit(solution)/shard_map/ppermute | solution.py:393
  72.4 15.2 %collective-permute-start.5 = (f32[160,512]{1,0:T(8,128)S(1)}, f32[160,512]{1,0:T(8,128)S(1)}, u32[]{:S(2)}, u32[]{:S(2)}) collective-permute-start(f32[160,512]{1,0:T(8,128)S(1)} %get-tuple-element.22), channel_id=1, source_target_pairs={{0,6},{2,0},{4,2},{6,4},{1,7},{3,1},{5,3},{7,5},{8,14},{10,8},{12,... | collective-permute-start | bytes 983048 | tf_op jit(solution)/shard_map/ppermute | solution.py:393
  87.6 9.5 %collective-permute-start.6 = (f32[288,512]{1,0:T(8,128)S(1)}, f32[288,512]{1,0:T(8,128)}, u32[]{:S(2)}, u32[]{:S(2)}) collective-permute-start(f32[288,512]{1,0:T(8,128)S(1)} %stack.1), channel_id=1, source_target_pairs={{0,1},{1,0},{2,3},{3,2},{4,5},{5,4},{6,7},{7,6},{8,9},{9,8},{10,11... | collective-permute-start | bytes 1769480 | tf_op jit(solution)/shard_map/ppermute | solution.py:397
  92.3 15.0 %all-to-all-start.3 = ((f32[32,24,128]{2,1,0:T(8,128)}), f32[32,24,128]{2,1,0:T(8,128)S(1)}, u32[]{:S(2)}, u32[]{:S(2)}) async-start(f32[32,24,128]{2,1,0:T(8,128)} %sum_depth.1), calls=%async_computation.3 | async-start | bytes 786432 | tf_op jit(solution)/shard_map/all_to_all | solution.py:320

commit v13 on v11

--- a/solution.py
+++ b/solution.py
@@ -205,6 +205,14 @@
         ref[ref.shape[0] - BLOCK :, :] = applied_ref[pl.ds(start, BLOCK), :]
 
 
+def stack_kernel(one_ref, two_ref, three_ref, first_ref, last_ref):
+    middle = HALF // 2
+    first_ref[0:HALF, :] = one_ref[0:HALF, :]
+    first_ref[HALF:, :] = two_ref[0:middle, :]
+    last_ref[0:middle, :] = two_ref[middle:HALF, :]
+    last_ref[middle:, :] = three_ref[0:HALF, :]
+
+
 def spread(value):
     return jnp.broadcast_to(value, (8, 128))
 
@@ -240,9 +248,14 @@
 
 
 def finish_kernel(scale, core_ref, chip_ref, gram_ref, *refs):
-    home_ref, *others, basis_ref, results, sems = refs
-    count = 1 + len(others) // 2
-    got_refs, mate_refs = others[: count - 1], others[count - 1 :]
+    home_ref, mate_ref, mate_last_ref, *got_refs, basis_ref, results, sems = refs
+    count = 1 + len(got_refs)
+    middle = HALF // 2
+    mates = (
+        lambda: mate_ref[0:HALF, :],
+        lambda: jnp.concatenate([mate_ref[HALF:, :], mate_last_ref[0:middle, :]], axis=0),
+        lambda: mate_last_ref[middle:, :],
+    )
     chip, core = chip_ref[0], core_ref[0]
     second = core == 1
     column = CORES * chip + core
@@ -292,8 +305,8 @@
         if step == 0:
             head, block = home_ref[0:HEAD, :], home_ref[HEAD:, :]
         else:
-            got, mate = got_refs[step - 1], mate_refs[step - 1]
-            first, last = got[0:HALF, :], mate[0:HALF, :]
+            got = got_refs[step - 1]
+            first, last = got[0:HALF, :], mates[step - 1]()
             head = jnp.where(
                 second,
                 jnp.concatenate([last, first], axis=0),
@@ -384,24 +397,27 @@
     piece = (OWN // 128) * HEAD // planes
     everyone = planes * CORES
     gram = exchange(gram.reshape(planes, piece, 128), plane)
-    gram, home, *sent = lax.optimization_barrier((gram, home, *sent))
     gram = call(sum_kernel, "sum_plane", shape((depth, piece, 128), F32), (gram,))
     got = [
         lax.ppermute(value, "x", [(i, (i + step + 1) % count) for i in range(count)])
         for step, value in enumerate(sent)
     ]
-    theirs = [lax.ppermute(value, "core", [(0, 1), (1, 0)]) for value in got]
     gram = exchange(gram, "z")
     gram = call(sum_kernel, "sum_depth", shape((everyone, piece, 128), F32), (gram,))
+    _, *ready = lax.optimization_barrier((gram, *got))
+    stacked = call(
+        stack_kernel, "stack", (shape((HALF * (count - 1) // 2, CHIP), F32),) * 2, ready
+    )
+    theirs = [lax.ppermute(value, "core", [(0, 1), (1, 0)]) for value in stacked]
     gram = exchange(gram, (*plane, "core"))
     gram = gram.reshape(planes, CORES, piece, 128)
     scale = 1.0 / (CHIP * chip_count)
     slab_width = CHIP * count
     return call(
         lambda *refs: finish_kernel(scale, *refs), "finish", shape((BLOCK, slab_width), F32),
-        (core, chip, gram, home, *got, *theirs),
+        (core, chip, gram, home, *theirs, *got),
         [pltpu.VMEM((count, BLOCK, CHIP), F32), pltpu.SemaphoreType.DMA((count,))],
-        [SMEM] * 2 + [VMEM] * (2 * count), RAW,
+        [SMEM] * 2 + [VMEM] * (3 + count), RAW,
     )
 
 

time: 109 us -> 108 us (level)
  blocking collectives: 10.7 us -> 21 us
  waiting for transfers between devices: 26.6 us -> 20.8 us
  starting transfers between devices: 52.5 us -> 47.8 us
    all_to_all x1 -> x2, blocking collectives: 10.7 us -> 21 us  [exchange(): return lax.all_to_all(value, axes, split_axis=0, concat_axis=0, tiled=True)]
    all_to_all x3 -> x2, waiting for transfers between devices: 13.3 us -> 7.23 us  [exchange(): return lax.all_to_all(value, axes, split_axis=0, concat_axis=0, tiled=True)]
    all_to_all x3 -> x2, starting transfers between devices: 21.7 us -> 18.9 us  [exchange(): return lax.all_to_all(value, axes, split_axis=0, concat_axis=0, tiled=True)]
    ppermute x3 -> x2, starting transfers between devices: 6.47 us -> 4.61 us  [on_device(): lax.ppermute(value, 'core', [(0, 1), (1, 0)])]
    pallas_call x8 -> x9, Pallas kernels: 18.2 us -> 17.5 us  [call(): pl.pallas_call(kernel, out_shape=out_shape, in_specs=specs or [VMEM] * le...]
  transfers between devices with their start and end apart: 12 -> 10, of which waited for: 7 -> 6; matrix products, arithmetic and copies ran while one was open for 0% -> 0% of each run, Pallas kernels for 2% -> 3%
where the time goes in v13:
time: 108 us; the launch traced here: 107 us
  starting transfers between devices  47.8 us (44%)
  blocking collectives  21 us (19%)
  waiting for transfers between devices  20.8 us (19%)
  Pallas kernels  17.5 us (16%)
    all_to_all x2, blocking collectives, exchange(): return lax.all_to_all(value, axes, split_axis=0, concat_axis=0, tiled=True)  21 us
    all_to_all x2, starting transfers between devices, exchange(): return lax.all_to_all(value, axes, split_axis=0, concat_axis=0, tiled=True)  18.9 us
    pallas_call x9, Pallas kernels, call(): pl.pallas_call(kernel, out_shape=out_shape, in_specs=specs or [VMEM] * le...  17.5 us
    ppermute x2, starting transfers between devices, shift(): lax.ppermute(value, chips, [(i, (i + step) % chip_count) for i in range(c...  12.3 us
    ppermute x2, waiting for transfers between devices, shift(): lax.ppermute(value, chips, [(i, (i + step) % chip_count) for i in range(c...  10.9 us
    ppermute x3, starting transfers between devices, on_device(): lax.ppermute(value, 'x', [(i, (i + step + 1) % count) for i in range(coun...  8.87 us
    all_to_all x2, waiting for transfers between devices, exchange(): return lax.all_to_all(value, axes, split_axis=0, concat_axis=0, tiled=True)  7.23 us
    ppermute x2, starting transfers between devices, on_device(): lax.ppermute(value, 'core', [(0, 1), (1, 0)])  4.61 us
  transfers between devices with their start and end apart: 10, of which 6 were waited for; matrix products, arithmetic and copies ran while one was open for 0% of the time, Pallas kernels for 3%

profile of v13, /device:TPU:1, one launch (start us, length us, event | category | flops | bytes accessed | tf_op | source)
XLA Modules:
  0.0 107.3 jit_solution(7376267009243830623)
XLA Ops:
  0.0 1.2 %pack.1 = f32[2,296,256]{2,1,0:T(8,128)S(1)} custom-call(f32[512,256]{1,0:T(8,128)} %vectors_ref.1, f32[16,256]{1,0:T(8,128)} %cosines_ref.1, f32[16,256]{1,0:T(8,128)} %distances_ref.1, s32[16,256]{1,0:T(8,128)} %offsets_ref.1, s32[1,256]{1,0:T(1,128)} %bitcast.7, s32[2,256]{1,0:T(2,128)} %labels_ref.1), custom_call_target="tpu_custom_call" | custom-call | tf_op jit(solution)/shard_map/pack/pallas_call | solution.py:342
  1.2 10.7 %all_to_all.20.slab_ref.own_ref = f32[2,296,256]{2,1,0:T(8,128)S(1)} all-to-all(f32[2,296,256]{2,1,0:T(8,128)S(1)} %pack.1), channel_id=1, replica_groups=mesh['y'=4,'z'=16,'x'=4,'core'=2] {'core'}, dimensions={0} | all-to-all | bytes 1212416 | tf_op jit(solution)/shard_map/all_to_all | solution.py:328
  11.9 1.9 %collective-permute-start = (f32[2,296,256]{2,1,0:T(8,128)S(1)}, f32[2,296,256]{2,1,0:T(8,128)S(1)}, u32[]{:S(2)}, u32[]{:S(2)}) collective-permute-start(f32[2,296,256]{2,1,0:T(8,128)S(1)} %all_to_all.20.slab_ref.own_ref), channel_id=1, source_target_pairs={{0,2},{2,4},{4,6},{6,8},{8,10},{10,12},{12,14},{14,16},{16,18},{18... | collective-permute-start | bytes 1818632 | tf_op jit(solution)/shard_map/ppermute | solution.py:362
  13.9 10.4 %collective-permute-start.1 = (f32[2,296,256]{2,1,0:T(8,128)S(1)}, f32[2,296,256]{2,1,0:T(8,128)S(1)}, u32[]{:S(2)}, u32[]{:S(2)}) collective-permute-start(f32[2,296,256]{2,1,0:T(8,128)S(1)} %all_to_all.20.slab_ref.own_ref), channel_id=1, source_target_pairs={{0,510},{2,0},{4,2},{6,4},{8,6},{10,8},{12,10},{14,12},{16,14},{18... | collective-permute-start | bytes 1818632 | tf_op jit(solution)/shard_map/ppermute | solution.py:362
  24.3 1.8 %own_matrix.1 = (bf16[768,256]{1,0:T(8,128)(2,1)S(1)}, bf16[768,256]{1,0:T(8,128)(2,1)S(1)}, bf16[768,256]{1,0:T(8,128)(2,1)S(1)}, bf16[768,256]{1,0:T(8,128)(2,1)S(1)}) custom-call(f32[2,296,256]{2,1,0:T(8,128)S(1)} %all_to_all.20.slab_ref.own_ref), custom_call_target="tpu_custom_call" | custom-call | tf_op jit(solution)/shard_map/own_matrix/pallas_call | solution.py:342
  26.1 10.0 %collective-permute-done.left_ref = f32[2,296,256]{2,1,0:T(8,128)S(1)} collective-permute-done((f32[2,296,256]{2,1,0:T(8,128)S(1)}, f32[2,296,256]{2,1,0:T(8,128)S(1)}, u32[]{:S(2)}, u32[]{:S(2)}) %collective-permute-start) | collective-permute-done | bytes 606240 | tf_op jit(solution)/shard_map/ppermute | solution.py:362
  36.1 0.9 collective-permute-done.1.right_ref
  36.9 3.8 %apply_twice.1 = (f32[256,512]{1,0:T(8,128)S(1)}, f32[128,512]{1,0:T(8,128)S(1)}) custom-call(f32[2,296,256]{2,1,0:T(8,128)S(1)} %collective-permute-done.left_ref, f32[2,296,256]{2,1,0:T(8,128)S(1)} %all_to_all.20.slab_ref.own_ref, f32[2,296,256]{2,1,0:T(8,128)S(1)} %collective-permute-done.1.right_ref, ...), custom_call_target="tpu_custom_call" | custom-call | tf_op jit(solution)/shard_map/apply_twice/pallas_call | solution.py:342
  40.7 3.1 %collective-permute-start.2 = (f32[128,512]{1,0:T(8,128)S(1)}, f32[128,512]{1,0:T(8,128)S(1)}, u32[]{:S(2)}, u32[]{:S(2)}) collective-permute-start(f32[128,512]{1,0:T(8,128)S(1)} %get-tuple-element.24.lead_ref), channel_id=1, source_target_pairs={{0,1},{1,0},{2,3},{3,2},{4,5},{5,4},{6,7},{7,6},{8,9},{9,8},{10,11... | collective-permute-start | bytes 786440 | tf_op jit(solution)/shard_map/ppermute | solution.py:385
  43.8 1.1 %collective-permute-done.2.other_ref = f32[128,512]{1,0:T(8,128)S(1)} collective-permute-done((f32[128,512]{1,0:T(8,128)S(1)}, f32[128,512]{1,0:T(8,128)S(1)}, u32[]{:S(2)}, u32[]{:S(2)}) %collective-permute-start.2) | collective-permute-done | bytes 262176 | tf_op jit(solution)/shard_map/ppermute | solution.py:385
  45.0 0.7 gram.1
  45.7 10.3 %all_to_all.21.pieces_ref = f32[16,24,128]{2,1,0:T(8,128)S(1)} all-to-all(f32[16,24,128]{2,1,0:T(8,128)S(1)} %bitcast.6), channel_id=1, replica_groups=mesh['y'=4,'z'=16,'x'=4,'core'=2] {'y','x'}, dimensions={0} | all-to-all | bytes 393216 | tf_op jit(solution)/shard_map/all_to_all | solution.py:328
  56.0 0.7 sum_plane.1
  56.7 9.9 %all-to-all-start.2 = ((f32[16,24,128]{2,1,0:T(8,128)}), f32[16,24,128]{2,1,0:T(8,128)S(1)}, u32[]{:S(2)}, u32[]{:S(2)}) async-start(f32[16,24,128]{2,1,0:T(8,128)} %sum_plane.1), calls=%async_computation.2 | async-start | bytes 393216 | tf_op jit(solution)/shard_map/all_to_all | solution.py:328
  66.7 0.1 share.1
  66.8 2.5 %collective-permute-start.3 = (f32[160,512]{1,0:T(8,128)S(1)}, f32[160,512]{1,0:T(8,128)S(1)}, u32[]{:S(2)}, u32[]{:S(2)}) collective-permute-start(f32[160,512]{1,0:T(8,128)S(1)} %get-tuple-element.27), channel_id=1, source_target_pairs={{0,2},{2,4},{4,6},{6,0},{1,3},{3,5},{5,7},{7,1},{8,10},{10,12},{12... | collective-permute-start | bytes 983048 | tf_op jit(solution)/shard_map/ppermute | solution.py:402
  69.3 3.2 %collective-permute-start.4 = (f32[160,512]{1,0:T(8,128)S(1)}, f32[160,512]{1,0:T(8,128)S(1)}, u32[]{:S(2)}, u32[]{:S(2)}) collective-permute-start(f32[160,512]{1,0:T(8,128)S(1)} %get-tuple-element.28), channel_id=1, source_target_pairs={{0,4},{2,6},{4,0},{6,2},{1,5},{3,7},{5,1},{7,3},{8,12},{10,14},{12... | collective-permute-start | bytes 983048 | tf_op jit(solution)/shard_map/ppermute | solution.py:402
  72.5 3.2 %collective-permute-start.5 = (f32[160,512]{1,0:T(8,128)S(1)}, f32[160,512]{1,0:T(8,128)S(1)}, u32[]{:S(2)}, u32[]{:S(2)}) collective-permute-start(f32[160,512]{1,0:T(8,128)S(1)} %get-tuple-element.29), channel_id=1, source_target_pairs={{0,6},{2,0},{4,2},{6,4},{1,7},{3,1},{5,3},{7,5},{8,14},{10,8},{12,... | collective-permute-start | bytes 983048 | tf_op jit(solution)/shard_map/ppermute | solution.py:402
  75.7 3.3 %all-to-all-done.2.pieces_ref = f32[16,24,128]{2,1,0:T(8,128)S(1)} async-done(((f32[16,24,128]{2,1,0:T(8,128)}), f32[16,24,128]{2,1,0:T(8,128)S(1)}, u32[]{:S(2)}, u32[]{:S(2)}) %all-to-all-start.2) | async-done | bytes 196640 | tf_op jit(solution)/shard_map/all_to_all | solution.py:328
  79.0 0.8 sum_depth.1
  79.8 9.0 %all-to-all-start.3 = ((f32[32,24,128]{2,1,0:T(8,128)}), f32[32,24,128]{2,1,0:T(8,128)S(1)}, u32[]{:S(2)}, u32[]{:S(2)}) async-start(f32[32,24,128]{2,1,0:T(8,128)} %sum_depth.1), calls=%async_computation.3 | async-start | bytes 786432 | tf_op jit(solution)/shard_map/all_to_all | solution.py:328
  88.7 0.0 collective-permute-done.3.one_ref.refs_6_
  88.7 0.0 collective-permute-done.4.two_ref.refs_7_
  88.8 0.0 collective-permute-done.5.three_ref.refs_8_
  88.8 2.7 %collective-permute-start.6 = (f32[144,512]{1,0:T(8,128)S(1)}, f32[144,512]{1,0:T(8,128)S(1)}, u32[]{:S(2)}, u32[]{:S(2)}) collective-permute-start(f32[144,512]{1,0:T(8,128)S(1)} %get-tuple-element.33), channel_id=1, source_target_pairs={{0,1},{1,0},{2,3},{3,2},{4,5},{5,4},{6,7},{7,6},{8,9},{9,8},{10,11... | collective-permute-start | bytes 884744 | tf_op jit(solution)/shard_map/ppermute | solution.py:411
  91.5 1.9 %collective-permute-start.7 = (f32[144,512]{1,0:T(8,128)S(1)}, f32[144,512]{1,0:T(8,128)S(1)}, u32[]{:S(2)}, u32[]{:S(2)}) collective-permute-start(f32[144,512]{1,0:T(8,128)S(1)} %get-tuple-element.34), channel_id=1, source_target_pairs={{0,1},{1,0},{2,3},{3,2},{4,5},{5,4},{6,7},{7,6},{8,9},{9,8},{10,11... | collective-permute-start | bytes 884744 | tf_op jit(solution)/shard_map/ppermute | solution.py:411
  93.4 0.0 collective-permute-done.6.refs_4_
  93.5 1.5 %collective-permute-done.7.refs_5_ = f32[144,512]{1,0:T(8,128)S(1)} collective-permute-done((f32[144,512]{1,0:T(8,128)S(1)}, f32[144,512]{1,0:T(8,128)S(1)}, u32[]{:S(2)}, u32[]{:S(2)}) %collective-permute-start.7) | collective-permute-done | bytes 294944 | tf_op jit(solution)/shard_map/ppermute | solution.py:411
  95.0 3.9 %all-to-all-done.3 = f32[32,24,128]{2,1,0:T(8,128)S(1)} async-done(((f32[32,24,128]{2,1,0:T(8,128)}), f32[32,24,128]{2,1,0:T(8,128)S(1)}, u32[]{:S(2)}, u32[]{:S(2)}) %all-to-all-start.3) | async-done | bytes 393248 | tf_op jit(solution)/shard_map/all_to_all | solution.py:328
  98.9 8.4 %finish.1 = f32[64,2048]{1,0:T(8,128)} custom-call(s32[1]{0:T(128)} %bitcast.core_ref.refs_0_, s32[1]{0:T(128)} %bitcast.1.chip_ref.refs_1_, f32[16,2,24,128]{3,2,1,0:T(8,128)S(1)} %bitcast.5, f32[256,512]{1,0:T(8,128)S(1)} %get-tuple-element.26.refs_3_, f32[144,512]{1,0:T(8,128)S(1)} %collective-permute-done.6.refs_4_, ...), custom_call_target="tpu_custom_call" | custom-call | tf_op jit(solution)/shard_map/finish/pallas_call | solution.py:342
  (1 shorter events, 0.0 us)
Async XLA Ops:
  11.9 24.1 %collective-permute-start = (f32[2,296,256]{2,1,0:T(8,128)S(1)}, f32[2,296,256]{2,1,0:T(8,128)S(1)}, u32[]{:S(2)}, u32[]{:S(2)}) collective-permute-start(f32[2,296,256]{2,1,0:T(8,128)S(1)} %all_to_all.20.slab_ref.own_ref), channel_id=1, source_target_pairs={{0,2},{2,4},{4,6},{6,8},{8,10},{10,12},{12,14},{14,16},{16,18},{18... | collective-permute-start | bytes 1818632 | tf_op jit(solution)/shard_map/ppermute | solution.py:362
  13.9 23.1 %collective-permute-start.1 = (f32[2,296,256]{2,1,0:T(8,128)S(1)}, f32[2,296,256]{2,1,0:T(8,128)S(1)}, u32[]{:S(2)}, u32[]{:S(2)}) collective-permute-start(f32[2,296,256]{2,1,0:T(8,128)S(1)} %all_to_all.20.slab_ref.own_ref), channel_id=1, source_target_pairs={{0,510},{2,0},{4,2},{6,4},{8,6},{10,8},{12,10},{14,12},{16,14},{18... | collective-permute-start | bytes 1818632 | tf_op jit(solution)/shard_map/ppermute | solution.py:362
  40.7 4.3 %collective-permute-start.2 = (f32[128,512]{1,0:T(8,128)S(1)}, f32[128,512]{1,0:T(8,128)S(1)}, u32[]{:S(2)}, u32[]{:S(2)}) collective-permute-start(f32[128,512]{1,0:T(8,128)S(1)} %get-tuple-element.24.lead_ref), channel_id=1, source_target_pairs={{0,1},{1,0},{2,3},{3,2},{4,5},{5,4},{6,7},{7,6},{8,9},{9,8},{10,11... | collective-permute-start | bytes 786440 | tf_op jit(solution)/shard_map/ppermute | solution.py:385
  56.7 22.3 %all-to-all-start.2 = ((f32[16,24,128]{2,1,0:T(8,128)}), f32[16,24,128]{2,1,0:T(8,128)S(1)}, u32[]{:S(2)}, u32[]{:S(2)}) async-start(f32[16,24,128]{2,1,0:T(8,128)} %sum_plane.1), calls=%async_computation.2 | async-start | bytes 393216 | tf_op jit(solution)/shard_map/all_to_all | solution.py:328
  66.8 22.0 %collective-permute-start.3 = (f32[160,512]{1,0:T(8,128)S(1)}, f32[160,512]{1,0:T(8,128)S(1)}, u32[]{:S(2)}, u32[]{:S(2)}) collective-permute-start(f32[160,512]{1,0:T(8,128)S(1)} %get-tuple-element.27), channel_id=1, source_target_pairs={{0,2},{2,4},{4,6},{6,0},{1,3},{3,5},{5,7},{7,1},{8,10},{10,12},{12... | collective-permute-start | bytes 983048 | tf_op jit(solution)/shard_map/ppermute | solution.py:402
  69.3 19.5 %collective-permute-start.4 = (f32[160,512]{1,0:T(8,128)S(1)}, f32[160,512]{1,0:T(8,128)S(1)}, u32[]{:S(2)}, u32[]{:S(2)}) collective-permute-start(f32[160,512]{1,0:T(8,128)S(1)} %get-tuple-element.28), channel_id=1, source_target_pairs={{0,4},{2,6},{4,0},{6,2},{1,5},{3,7},{5,1},{7,3},{8,12},{10,14},{12... | collective-permute-start | bytes 983048 | tf_op jit(solution)/shard_map/ppermute | solution.py:402
  72.5 16.3 %collective-permute-start.5 = (f32[160,512]{1,0:T(8,128)S(1)}, f32[160,512]{1,0:T(8,128)S(1)}, u32[]{:S(2)}, u32[]{:S(2)}) collective-permute-start(f32[160,512]{1,0:T(8,128)S(1)} %get-tuple-element.29), channel_id=1, source_target_pairs={{0,6},{2,0},{4,2},{6,4},{1,7},{3,1},{5,3},{7,5},{8,14},{10,8},{12,... | collective-permute-start | bytes 983048 | tf_op jit(solution)/shard_map/ppermute | solution.py:402
  79.8 19.1 %all-to-all-start.3 = ((f32[32,24,128]{2,1,0:T(8,128)}), f32[32,24,128]{2,1,0:T(8,128)S(1)}, u32[]{:S(2)}, u32[]{:S(2)}) async-start(f32[32,24,128]{2,1,0:T(8,128)} %sum_depth.1), calls=%async_computation.3 | async-start | bytes 786432 | tf_op jit(solution)/shard_map/all_to_all | solution.py:328
  88.8 4.6 %collective-permute-start.6 = (f32[144,512]{1,0:T(8,128)S(1)}, f32[144,512]{1,0:T(8,128)S(1)}, u32[]{:S(2)}, u32[]{:S(2)}) collective-permute-start(f32[144,512]{1,0:T(8,128)S(1)} %get-tuple-element.33), channel_id=1, source_target_pairs={{0,1},{1,0},{2,3},{3,2},{4,5},{5,4},{6,7},{7,6},{8,9},{9,8},{10,11... | collective-permute-start | bytes 884744 | tf_op jit(solution)/shard_map/ppermute | solution.py:411
  91.5 3.5 %collective-permute-start.7 = (f32[144,512]{1,0:T(8,128)S(1)}, f32[144,512]{1,0:T(8,128)S(1)}, u32[]{:S(2)}, u32[]{:S(2)}) collective-permute-start(f32[144,512]{1,0:T(8,128)S(1)} %get-tuple-element.34), channel_id=1, source_target_pairs={{0,1},{1,0},{2,3},{3,2},{4,5},{5,4},{6,7},{7,6},{8,9},{9,8},{10,11... | collective-permute-start | bytes 884744 | tf_op jit(solution)/shard_map/ppermute | solution.py:411

commit v14 on v13

--- a/solution.py
+++ b/solution.py
@@ -35,8 +35,8 @@
 
 
 def pack_kernel(
-    vectors_ref, cosines_ref, distances_ref, offsets_ref, counts_ref, labels_ref, out_ref,
-    cosines, distances, offsets, counts, labels, table_sems, block_sems,
+    core_ref, vectors_ref, cosines_ref, distances_ref, offsets_ref, counts_ref, labels_ref,
+    own_ref, send_ref, cosines, distances, offsets, counts, labels, table_sems, block_sems,
 ):
     tables = (
         (cosines_ref, cosines), (distances_ref, distances), (offsets_ref, offsets),
@@ -46,15 +46,17 @@
         pltpu.make_async_copy(source, target, table_sems.at[i])
         for i, (source, target) in enumerate(tables)
     ]
-    block_copies = [
-        pltpu.make_async_copy(
-            vectors_ref.at[pl.ds(BLOCK * (core + CORES * p), BLOCK)],
-            out_ref.at[core, pl.ds(BLOCK * p, BLOCK)],
-            block_sems.at[core + CORES * p],
-        )
-        for core in range(CORES)
-        for p in range(OWN // BLOCK)
-    ]
+    block_copies = []
+    for owner, ref in ((core_ref[0], own_ref), (1 - core_ref[0], send_ref)):
+        for p in range(OWN // BLOCK):
+            start = pl.multiple_of((owner + CORES * p) * BLOCK, BLOCK)
+            block_copies.append(
+                pltpu.make_async_copy(
+                    vectors_ref.at[pl.ds(start, BLOCK)],
+                    ref.at[pl.ds(BLOCK * p, BLOCK)],
+                    block_sems.at[len(block_copies)],
+                )
+            )
     for copy in table_copies + block_copies:
         copy.start()
     for copy in table_copies:
@@ -70,12 +72,17 @@
         merged = merged + jnp.where(steps == steps[k : k + 1], hopping[k : k + 1], 0.0)
     sides = labels[...].astype(F32)
     onsite = SITE_MASS * (2.0 * sides[0:1] - 1.0) + LAYER_BIAS * (2.0 * sides[1:2] - 1.0)
-    for core in range(CORES):
-        out_ref[core, OWN : OWN + 16, :] = merged
-        out_ref[core, OWN + 16 : OWN + 32, :] = steps
-        out_ref[core, OWN + 32 : OWN + 40, :] = jnp.broadcast_to(onsite, (8, LOCAL))
+    for ref in (own_ref, send_ref):
+        ref[OWN : OWN + 16, :] = merged
+        ref[OWN + 16 : OWN + 32, :] = steps
+        ref[OWN + 32 : OWN + 40, :] = jnp.broadcast_to(onsite, (8, LOCAL))
     for copy in block_copies:
         copy.wait()
+
+
+def merge_kernel(core_ref, own_ref, mate_ref, slab_ref):
+    slab_ref[core_ref[0]] = own_ref[...]
+    slab_ref[1 - core_ref[0]] = mate_ref[...]
 
 
 def sum_kernel(pieces_ref, out_ref):
@@ -363,13 +370,19 @@
 
     shape = jax.ShapeDtypeStruct
     tables = (cosines, distances, offsets, counts.reshape(1, LOCAL), labels)
-    slab = call(
-        pack_kernel, "pack", shape((CORES, OWN + TABLE, LOCAL), F32), (vectors, *tables),
+    core = lax.axis_index("core").reshape(1)
+    part = shape((OWN + TABLE, LOCAL), F32)
+    own, send = call(
+        pack_kernel, "pack", (part, part), (core, vectors, *tables),
         [pltpu.VMEM(t.shape, t.dtype) for t in tables]
         + [pltpu.SemaphoreType.DMA((len(tables),)), pltpu.SemaphoreType.DMA((NV // BLOCK,))],
-        [RAW] * 6,
-    )
-    slab = exchange(slab, "core")
+        [SMEM] + [RAW] * 6,
+    )
+    mate = lax.ppermute(send, "core", [(0, 1), (1, 0)])
+    slab = call(
+        merge_kernel, "merge", shape((CORES, OWN + TABLE, LOCAL), F32), (core, own, mate), (),
+        [SMEM, VMEM, VMEM],
+    )
     left = shift(slab, 1)
     right = shift(slab, -1)
     matrix = shape((WIDE, LOCAL), BF16)
@@ -383,7 +396,6 @@
         [pltpu.VMEM((OWN, 3 * CHIP), BF16)] * 2 + [pltpu.VMEM((OWN, 2 * CHIP), BF16)] * 2 + [wide] * 4,
     )
     other = lax.ppermute(lead, "core", [(0, 1), (1, 0)])
-    core = lax.axis_index("core").reshape(1)
     chip = lax.axis_index("x").reshape(1)
     gram = call(
         gram_kernel, "gram", shape((OWN // 128, HEAD, 128), F32),

time: 108 us -> 108 us (level)
  blocking collectives: 21 us -> 10.3 us
  waiting for transfers between devices: 20.8 us -> 29.4 us
  starting transfers between devices: 47.8 us -> 50 us
    all_to_all x2 -> x1, blocking collectives: 21 us -> 10.3 us  [exchange(): return lax.all_to_all(value, axes, split_axis=0, concat_axis=0, tiled=True)]
    ppermute x0 -> x1, starting transfers between devices: none -> 8.79 us  [on_device(): mate = lax.ppermute(send, 'core', [(0, 1), (1, 0)])]
    ppermute x2, waiting for transfers between devices: 10.9 us -> 18.1 us  [shift(): lax.ppermute(value, chips, [(i, (i + step) % chip_count) for i in range(c...]
    all_to_all x2, starting transfers between devices: 18.9 us -> 12.1 us  [exchange(): return lax.all_to_all(value, axes, split_axis=0, concat_axis=0, tiled=True)]
    ppermute x0 -> x1, waiting for transfers between devices: none -> 1.2 us  [on_device(): mate = lax.ppermute(send, 'core', [(0, 1), (1, 0)])]
    pallas_call x9 -> x10, Pallas kernels: 17.5 us -> 17.6 us  [call(): pl.pallas_call(kernel, out_shape=out_shape, in_specs=specs or [VMEM] * le...]
  transfers between devices with their start and end apart: 10 -> 11, of which waited for: 6 -> 7; matrix products, arithmetic and copies ran while one was open for 0% -> 0% of each run, Pallas kernels for 3% -> 3%
where the time goes in v14:
time: 108 us
  starting transfers between devices  50 us (46%)
  waiting for transfers between devices  29.4 us (27%)
  Pallas kernels  17.6 us (16%)
  blocking collectives  10.3 us (10%)
    ppermute x2, waiting for transfers between devices, shift(): lax.ppermute(value, chips, [(i, (i + step) % chip_count) for i in range(c...  18.1 us
    pallas_call x10, Pallas kernels, call(): pl.pallas_call(kernel, out_shape=out_shape, in_specs=specs or [VMEM] * le...  17.6 us
    ppermute x2, starting transfers between devices, shift(): lax.ppermute(value, chips, [(i, (i + step) % chip_count) for i in range(c...  12.3 us
    all_to_all x2, starting transfers between devices, exchange(): return lax.all_to_all(value, axes, split_axis=0, concat_axis=0, tiled=True)  12.1 us
    all_to_all x1, blocking collectives, exchange(): return lax.all_to_all(value, axes, split_axis=0, concat_axis=0, tiled=True)  10.3 us
    ppermute x1, starting transfers between devices, on_device(): mate = lax.ppermute(send, 'core', [(0, 1), (1, 0)])  8.79 us
    ppermute x3, starting transfers between devices, on_device(): lax.ppermute(value, 'x', [(i, (i + step + 1) % count) for i in range(coun...  8.42 us
    all_to_all x2, waiting for transfers between devices, exchange(): return lax.all_to_all(value, axes, split_axis=0, concat_axis=0, tiled=True)  7.4 us
  transfers between devices with their start and end apart: 11, of which 7 were waited for; matrix products, arithmetic and copies ran while one was open for 0% of the time, Pallas kernels for 3%

profile of v14, /device:TPU:1, one launch (start us, length us, event | category | flops | bytes accessed | tf_op | source)
XLA Modules:
  0.0 107.6 jit_solution(9815376871151685448)
XLA Ops:
  0.0 1.2 %pack.1 = (f32[296,256]{1,0:T(8,128)S(1)}, f32[296,256]{1,0:T(8,128)S(1)}) custom-call(s32[1]{0:T(128)} %bitcast.core_ref.refs_0_, f32[512,256]{1,0:T(8,128)} %vectors_ref.1, f32[16,256]{1,0:T(8,128)} %cosines_ref.1, f32[16,256]{1,0:T(8,128)} %distances_ref.1, s32[16,256]{1,0:T(8,128)} %offsets_ref.1, s32[1,256]{1,0:T(1,128)} %bitcast.7, s32[2,256]{1,0:T(2,128)} %labels_ref.1), custom_call_target="tpu_custom_call" | custom-call | tf_op jit(solution)/shard_map/pack/pallas_call | solution.py:349
  1.2 8.8 %collective-permute-start = (f32[296,256]{1,0:T(8,128)S(1)}, f32[296,256]{1,0:T(8,128)S(1)}, u32[]{:S(2)}, u32[]{:S(2)}) collective-permute-start(f32[296,256]{1,0:T(8,128)S(1)} %get-tuple-element.23), channel_id=1, source_target_pairs={{0,1},{1,0},{2,3},{3,2},{4,5},{5,4},{6,7},{7,6},{8,9},{9,8},{10,11... | collective-permute-start | bytes 909320 | tf_op jit(solution)/shard_map/ppermute | solution.py:381
  10.0 1.2 %collective-permute-done.mate_ref = f32[296,256]{1,0:T(8,128)S(1)} collective-permute-done((f32[296,256]{1,0:T(8,128)S(1)}, f32[296,256]{1,0:T(8,128)S(1)}, u32[]{:S(2)}, u32[]{:S(2)}) %collective-permute-start) | collective-permute-done | bytes 303136 | tf_op jit(solution)/shard_map/ppermute | solution.py:381
  11.3 10.4 %collective-permute-start.2 = (f32[2,296,256]{2,1,0:T(8,128)S(1)}, f32[2,296,256]{2,1,0:T(8,128)S(1)}, u32[]{:S(2)}, u32[]{:S(2)}) collective-permute-start(f32[2,296,256]{2,1,0:T(8,128)S(1)} %merge.1.slab_ref.own_ref), channel_id=1, source_target_pairs={{0,510},{2,0},{4,2},{6,4},{8,6},{10,8},{12,10},{14,12},{16,14},{18... | collective-permute-start | bytes 1818632 | tf_op jit(solution)/shard_map/ppermute | solution.py:369
  21.7 1.9 %collective-permute-start.1 = (f32[2,296,256]{2,1,0:T(8,128)S(1)}, f32[2,296,256]{2,1,0:T(8,128)S(1)}, u32[]{:S(2)}, u32[]{:S(2)}) collective-permute-start(f32[2,296,256]{2,1,0:T(8,128)S(1)} %merge.1.slab_ref.own_ref), channel_id=1, source_target_pairs={{0,2},{2,4},{4,6},{6,8},{8,10},{10,12},{12,14},{14,16},{16,18},{18... | collective-permute-start | bytes 1818632 | tf_op jit(solution)/shard_map/ppermute | solution.py:369
  23.6 1.8 %own_matrix.1 = (bf16[768,256]{1,0:T(8,128)(2,1)S(1)}, bf16[768,256]{1,0:T(8,128)(2,1)S(1)}, bf16[768,256]{1,0:T(8,128)(2,1)S(1)}, bf16[768,256]{1,0:T(8,128)(2,1)S(1)}) custom-call(f32[2,296,256]{2,1,0:T(8,128)S(1)} %merge.1.slab_ref.own_ref), custom_call_target="tpu_custom_call" | custom-call | tf_op jit(solution)/shard_map/own_matrix/pallas_call | solution.py:349
  25.4 8.9 %collective-permute-done.2.right_ref = f32[2,296,256]{2,1,0:T(8,128)S(1)} collective-permute-done((f32[2,296,256]{2,1,0:T(8,128)S(1)}, f32[2,296,256]{2,1,0:T(8,128)S(1)}, u32[]{:S(2)}, u32[]{:S(2)}) %collective-permute-start.2) | collective-permute-done | bytes 606240 | tf_op jit(solution)/shard_map/ppermute | solution.py:369
  34.3 9.2 %collective-permute-done.1.left_ref = f32[2,296,256]{2,1,0:T(8,128)S(1)} collective-permute-done((f32[2,296,256]{2,1,0:T(8,128)S(1)}, f32[2,296,256]{2,1,0:T(8,128)S(1)}, u32[]{:S(2)}, u32[]{:S(2)}) %collective-permute-start.1) | collective-permute-done | bytes 606240 | tf_op jit(solution)/shard_map/ppermute | solution.py:369
  43.6 3.8 %apply_twice.1 = (f32[256,512]{1,0:T(8,128)S(1)}, f32[128,512]{1,0:T(8,128)S(1)}) custom-call(f32[2,296,256]{2,1,0:T(8,128)S(1)} %collective-permute-done.1.left_ref, f32[2,296,256]{2,1,0:T(8,128)S(1)} %merge.1.slab_ref.own_ref, f32[2,296,256]{2,1,0:T(8,128)S(1)} %collective-permute-done.2.right_ref, bf16[768,256]{1,0:T(8,128)(2,1)S(1)} %get-tuple-element.24.first_high_ref, ...), custom_call_target="tpu_custom_call" | custom-call | tf_op jit(solution)/shard_map/apply_twice/pallas_call | solution.py:349
  47.4 3.4 %collective-permute-start.3 = (f32[128,512]{1,0:T(8,128)S(1)}, f32[128,512]{1,0:T(8,128)S(1)}, u32[]{:S(2)}, u32[]{:S(2)}) collective-permute-start(f32[128,512]{1,0:T(8,128)S(1)} %get-tuple-element.28.lead_ref), channel_id=1, source_target_pairs={{0,1},{1,0},{2,3},{3,2},{4,5},{5,4},{6,7},{7,6},{8,9},{9,8},{10,11... | collective-permute-start | bytes 786440 | tf_op jit(solution)/shard_map/ppermute | solution.py:398
  50.8 1.1 %collective-permute-done.3.other_ref = f32[128,512]{1,0:T(8,128)S(1)} collective-permute-done((f32[128,512]{1,0:T(8,128)S(1)}, f32[128,512]{1,0:T(8,128)S(1)}, u32[]{:S(2)}, u32[]{:S(2)}) %collective-permute-start.3) | collective-permute-done | bytes 262176 | tf_op jit(solution)/shard_map/ppermute | solution.py:398
  51.9 0.7 gram.1
  52.7 10.3 %all_to_all.15.pieces_ref = f32[16,24,128]{2,1,0:T(8,128)S(1)} all-to-all(f32[16,24,128]{2,1,0:T(8,128)S(1)} %bitcast.6), channel_id=1, replica_groups=mesh['y'=4,'z'=16,'x'=4,'core'=2] {'y','x'}, dimensions={0} | all-to-all | bytes 393216 | tf_op jit(solution)/shard_map/all_to_all | solution.py:335
  63.0 0.7 sum_plane.1
  63.7 3.5 %all-to-all-start.1 = ((f32[16,24,128]{2,1,0:T(8,128)}), f32[16,24,128]{2,1,0:T(8,128)S(1)}, u32[]{:S(2)}, u32[]{:S(2)}) async-start(f32[16,24,128]{2,1,0:T(8,128)} %sum_plane.1), calls=%async_computation.1 | async-start | bytes 393216 | tf_op jit(solution)/shard_map/all_to_all | solution.py:335
  67.2 0.1 share.1
  67.3 2.2 %collective-permute-start.4 = (f32[160,512]{1,0:T(8,128)S(1)}, f32[160,512]{1,0:T(8,128)S(1)}, u32[]{:S(2)}, u32[]{:S(2)}) collective-permute-start(f32[160,512]{1,0:T(8,128)S(1)} %get-tuple-element.31), channel_id=1, source_target_pairs={{0,2},{2,4},{4,6},{6,0},{1,3},{3,5},{5,7},{7,1},{8,10},{10,12},{12... | collective-permute-start | bytes 983048 | tf_op jit(solution)/shard_map/ppermute | solution.py:414
  69.5 2.9 %collective-permute-start.5 = (f32[160,512]{1,0:T(8,128)S(1)}, f32[160,512]{1,0:T(8,128)S(1)}, u32[]{:S(2)}, u32[]{:S(2)}) collective-permute-start(f32[160,512]{1,0:T(8,128)S(1)} %get-tuple-element.32), channel_id=1, source_target_pairs={{0,4},{2,6},{4,0},{6,2},{1,5},{3,7},{5,1},{7,3},{8,12},{10,14},{12... | collective-permute-start | bytes 983048 | tf_op jit(solution)/shard_map/ppermute | solution.py:414
  72.4 3.3 %collective-permute-start.6 = (f32[160,512]{1,0:T(8,128)S(1)}, f32[160,512]{1,0:T(8,128)S(1)}, u32[]{:S(2)}, u32[]{:S(2)}) collective-permute-start(f32[160,512]{1,0:T(8,128)S(1)} %get-tuple-element.33), channel_id=1, source_target_pairs={{0,6},{2,0},{4,2},{6,4},{1,7},{3,1},{5,3},{7,5},{8,14},{10,8},{12,... | collective-permute-start | bytes 983048 | tf_op jit(solution)/shard_map/ppermute | solution.py:414
  75.8 3.8 %all-to-all-done.1.pieces_ref = f32[16,24,128]{2,1,0:T(8,128)S(1)} async-done(((f32[16,24,128]{2,1,0:T(8,128)}), f32[16,24,128]{2,1,0:T(8,128)S(1)}, u32[]{:S(2)}, u32[]{:S(2)}) %all-to-all-start.1) | async-done | bytes 196640 | tf_op jit(solution)/shard_map/all_to_all | solution.py:335
  79.6 0.8 sum_depth.1
  80.3 8.6 %all-to-all-start.2 = ((f32[32,24,128]{2,1,0:T(8,128)}), f32[32,24,128]{2,1,0:T(8,128)S(1)}, u32[]{:S(2)}, u32[]{:S(2)}) async-start(f32[32,24,128]{2,1,0:T(8,128)} %sum_depth.1), calls=%async_computation.2 | async-start | bytes 786432 | tf_op jit(solution)/shard_map/all_to_all | solution.py:335
  88.9 0.0 collective-permute-done.4.one_ref.refs_6_
  88.9 0.0 collective-permute-done.5.two_ref.refs_7_
  88.9 0.0 collective-permute-done.6.three_ref.refs_8_
  89.0 3.1 %collective-permute-start.7 = (f32[144,512]{1,0:T(8,128)S(1)}, f32[144,512]{1,0:T(8,128)S(1)}, u32[]{:S(2)}, u32[]{:S(2)}) collective-permute-start(f32[144,512]{1,0:T(8,128)S(1)} %get-tuple-element.37), channel_id=1, source_target_pairs={{0,1},{1,0},{2,3},{3,2},{4,5},{5,4},{6,7},{7,6},{8,9},{9,8},{10,11... | collective-permute-start | bytes 884744 | tf_op jit(solution)/shard_map/ppermute | solution.py:423
  92.1 1.9 %collective-permute-start.8 = (f32[144,512]{1,0:T(8,128)S(1)}, f32[144,512]{1,0:T(8,128)S(1)}, u32[]{:S(2)}, u32[]{:S(2)}) collective-permute-start(f32[144,512]{1,0:T(8,128)S(1)} %get-tuple-element.38), channel_id=1, source_target_pairs={{0,1},{1,0},{2,3},{3,2},{4,5},{5,4},{6,7},{7,6},{8,9},{9,8},{10,11... | collective-permute-start | bytes 884744 | tf_op jit(solution)/shard_map/ppermute | solution.py:423
  94.0 0.0 collective-permute-done.7.refs_4_
  94.0 1.5 %collective-permute-done.8.refs_5_ = f32[144,512]{1,0:T(8,128)S(1)} collective-permute-done((f32[144,512]{1,0:T(8,128)S(1)}, f32[144,512]{1,0:T(8,128)S(1)}, u32[]{:S(2)}, u32[]{:S(2)}) %collective-permute-start.8) | collective-permute-done | bytes 294944 | tf_op jit(solution)/shard_map/ppermute | solution.py:423
  95.6 3.6 %all-to-all-done.2 = f32[32,24,128]{2,1,0:T(8,128)S(1)} async-done(((f32[32,24,128]{2,1,0:T(8,128)}), f32[32,24,128]{2,1,0:T(8,128)S(1)}, u32[]{:S(2)}, u32[]{:S(2)}) %all-to-all-start.2) | async-done | bytes 393248 | tf_op jit(solution)/shard_map/all_to_all | solution.py:335
  99.2 8.4 %finish.1 = f32[64,2048]{1,0:T(8,128)} custom-call(s32[1]{0:T(128)} %bitcast.core_ref.refs_0_, s32[1]{0:T(128)} %bitcast.1.chip_ref.refs_1_, f32[16,2,24,128]{3,2,1,0:T(8,128)S(1)} %bitcast.5, f32[256,512]{1,0:T(8,128)S(1)} %get-tuple-element.30.refs_3_, f32[144,512]{1,0:T(8,128)S(1)} %collective-permute-done.7.refs_4_, ...), custom_call_target="tpu_custom_call" | custom-call | tf_op jit(solution)/shard_map/finish/pallas_call | solution.py:349
  (2 shorter events, 0.1 us)
Async XLA Ops:
  1.2 10.0 %collective-permute-start = (f32[296,256]{1,0:T(8,128)S(1)}, f32[296,256]{1,0:T(8,128)S(1)}, u32[]{:S(2)}, u32[]{:S(2)}) collective-permute-start(f32[296,256]{1,0:T(8,128)S(1)} %get-tuple-element.23), channel_id=1, source_target_pairs={{0,1},{1,0},{2,3},{3,2},{4,5},{5,4},{6,7},{7,6},{8,9},{9,8},{10,11... | collective-permute-start | bytes 909320 | tf_op jit(solution)/shard_map/ppermute | solution.py:381
  11.3 23.1 %collective-permute-start.2 = (f32[2,296,256]{2,1,0:T(8,128)S(1)}, f32[2,296,256]{2,1,0:T(8,128)S(1)}, u32[]{:S(2)}, u32[]{:S(2)}) collective-permute-start(f32[2,296,256]{2,1,0:T(8,128)S(1)} %merge.1.slab_ref.own_ref), channel_id=1, source_target_pairs={{0,510},{2,0},{4,2},{6,4},{8,6},{10,8},{12,10},{14,12},{16,14},{18... | collective-permute-start | bytes 1818632 | tf_op jit(solution)/shard_map/ppermute | solution.py:369
  21.7 21.9 %collective-permute-start.1 = (f32[2,296,256]{2,1,0:T(8,128)S(1)}, f32[2,296,256]{2,1,0:T(8,128)S(1)}, u32[]{:S(2)}, u32[]{:S(2)}) collective-permute-start(f32[2,296,256]{2,1,0:T(8,128)S(1)} %merge.1.slab_ref.own_ref), channel_id=1, source_target_pairs={{0,2},{2,4},{4,6},{6,8},{8,10},{10,12},{12,14},{14,16},{16,18},{18... | collective-permute-start | bytes 1818632 | tf_op jit(solution)/shard_map/ppermute | solution.py:369
  47.4 4.6 %collective-permute-start.3 = (f32[128,512]{1,0:T(8,128)S(1)}, f32[128,512]{1,0:T(8,128)S(1)}, u32[]{:S(2)}, u32[]{:S(2)}) collective-permute-start(f32[128,512]{1,0:T(8,128)S(1)} %get-tuple-element.28.lead_ref), channel_id=1, source_target_pairs={{0,1},{1,0},{2,3},{3,2},{4,5},{5,4},{6,7},{7,6},{8,9},{9,8},{10,11... | collective-permute-start | bytes 786440 | tf_op jit(solution)/shard_map/ppermute | solution.py:398
  63.7 15.9 %all-to-all-start.1 = ((f32[16,24,128]{2,1,0:T(8,128)}), f32[16,24,128]{2,1,0:T(8,128)S(1)}, u32[]{:S(2)}, u32[]{:S(2)}) async-start(f32[16,24,128]{2,1,0:T(8,128)} %sum_plane.1), calls=%async_computation.1 | async-start | bytes 393216 | tf_op jit(solution)/shard_map/all_to_all | solution.py:335
  67.3 21.6 %collective-permute-start.4 = (f32[160,512]{1,0:T(8,128)S(1)}, f32[160,512]{1,0:T(8,128)S(1)}, u32[]{:S(2)}, u32[]{:S(2)}) collective-permute-start(f32[160,512]{1,0:T(8,128)S(1)} %get-tuple-element.31), channel_id=1, source_target_pairs={{0,2},{2,4},{4,6},{6,0},{1,3},{3,5},{5,7},{7,1},{8,10},{10,12},{12... | collective-permute-start | bytes 983048 | tf_op jit(solution)/shard_map/ppermute | solution.py:414
  69.5 19.4 %collective-permute-start.5 = (f32[160,512]{1,0:T(8,128)S(1)}, f32[160,512]{1,0:T(8,128)S(1)}, u32[]{:S(2)}, u32[]{:S(2)}) collective-permute-start(f32[160,512]{1,0:T(8,128)S(1)} %get-tuple-element.32), channel_id=1, source_target_pairs={{0,4},{2,6},{4,0},{6,2},{1,5},{3,7},{5,1},{7,3},{8,12},{10,14},{12... | collective-permute-start | bytes 983048 | tf_op jit(solution)/shard_map/ppermute | solution.py:414
  72.4 16.5 %collective-permute-start.6 = (f32[160,512]{1,0:T(8,128)S(1)}, f32[160,512]{1,0:T(8,128)S(1)}, u32[]{:S(2)}, u32[]{:S(2)}) collective-permute-start(f32[160,512]{1,0:T(8,128)S(1)} %get-tuple-element.33), channel_id=1, source_target_pairs={{0,6},{2,0},{4,2},{6,4},{1,7},{3,1},{5,3},{7,5},{8,14},{10,8},{12,... | collective-permute-start | bytes 983048 | tf_op jit(solution)/shard_map/ppermute | solution.py:414
  80.3 18.8 %all-to-all-start.2 = ((f32[32,24,128]{2,1,0:T(8,128)}), f32[32,24,128]{2,1,0:T(8,128)S(1)}, u32[]{:S(2)}, u32[]{:S(2)}) async-start(f32[32,24,128]{2,1,0:T(8,128)} %sum_depth.1), calls=%async_computation.2 | async-start | bytes 786432 | tf_op jit(solution)/shard_map/all_to_all | solution.py:335
  89.0 5.0 %collective-permute-start.7 = (f32[144,512]{1,0:T(8,128)S(1)}, f32[144,512]{1,0:T(8,128)S(1)}, u32[]{:S(2)}, u32[]{:S(2)}) collective-permute-start(f32[144,512]{1,0:T(8,128)S(1)} %get-tuple-element.37), channel_id=1, source_target_pairs={{0,1},{1,0},{2,3},{3,2},{4,5},{5,4},{6,7},{7,6},{8,9},{9,8},{10,11... | collective-permute-start | bytes 884744 | tf_op jit(solution)/shard_map/ppermute | solution.py:423
  92.1 3.5 %collective-permute-start.8 = (f32[144,512]{1,0:T(8,128)S(1)}, f32[144,512]{1,0:T(8,128)S(1)}, u32[]{:S(2)}, u32[]{:S(2)}) collective-permute-start(f32[144,512]{1,0:T(8,128)S(1)} %get-tuple-element.38), channel_id=1, source_target_pairs={{0,1},{1,0},{2,3},{3,2},{4,5},{5,4},{6,7},{7,6},{8,9},{9,8},{10,11... | collective-permute-start | bytes 884744 | tf_op jit(solution)/shard_map/ppermute | solution.py:423

commit v15 on v14

--- a/solution.py
+++ b/solution.py
@@ -389,10 +389,10 @@
     matrices = call(own_matrix_kernel, "own_matrix", (matrix,) * 4, (slab,))
     wide = pltpu.VMEM((WIDE, LOCAL), BF16)
     applied, lead = call(
-        apply_kernel,
+        lambda right, own, left, *rest: apply_kernel(left, own, right, *rest),
         "apply_twice",
         (shape((OWN, CHIP), F32), shape((2 * BLOCK, CHIP), F32)),
-        (left, slab, right, *matrices),
+        (right, slab, left, *matrices),
         [pltpu.VMEM((OWN, 3 * CHIP), BF16)] * 2 + [pltpu.VMEM((OWN, 2 * CHIP), BF16)] * 2 + [wide] * 4,
     )
     other = lax.ppermute(lead, "core", [(0, 1), (1, 0)])

time: 108 us -> 107 us (level)
  waiting for transfers between devices: 29.4 us -> 22 us
  starting transfers between devices: 50 us -> 56.6 us
    ppermute x2, waiting for transfers between devices: 18.1 us -> 10.9 us  [shift(): lax.ppermute(value, chips, [(i, (i + step) % chip_count) for i in range(c...]
    all_to_all x2, starting transfers between devices: 12.1 us -> 18.9 us  [exchange(): return lax.all_to_all(value, axes, split_axis=0, concat_axis=0, tiled=True)]
where the time goes in v15:
time: 107 us
  starting transfers between devices  56.6 us (53%)
  waiting for transfers between devices  22 us (21%)
  Pallas kernels  17.6 us (16%)
  blocking collectives  10.3 us (10%)
    all_to_all x2, starting transfers between devices, exchange(): return lax.all_to_all(value, axes, split_axis=0, concat_axis=0, tiled=True)  18.9 us
    pallas_call x10, Pallas kernels, call(): pl.pallas_call(kernel, out_shape=out_shape, in_specs=specs or [VMEM] * le...  17.6 us
    ppermute x2, starting transfers between devices, shift(): lax.ppermute(value, chips, [(i, (i + step) % chip_count) for i in range(c...  12.3 us
    ppermute x2, waiting for transfers between devices, shift(): lax.ppermute(value, chips, [(i, (i + step) % chip_count) for i in range(c...  10.9 us
    all_to_all x1, blocking collectives, exchange(): return lax.all_to_all(value, axes, split_axis=0, concat_axis=0, tiled=True)  10.3 us
    ppermute x3, starting transfers between devices, on_device(): lax.ppermute(value, 'x', [(i, (i + step + 1) % count) for i in range(coun...  8.88 us
    ppermute x1, starting transfers between devices, on_device(): mate = lax.ppermute(send, 'core', [(0, 1), (1, 0)])  8.79 us
    all_to_all x2, waiting for transfers between devices, exchange(): return lax.all_to_all(value, axes, split_axis=0, concat_axis=0, tiled=True)  7.23 us
  transfers between devices with their start and end apart: 11, of which 7 were waited for; matrix products, arithmetic and copies ran while one was open for 0% of the time, Pallas kernels for 3%

profile of v15, /device:TPU:1, one launch (start us, length us, event | category | flops | bytes accessed | tf_op | source)
XLA Modules:
  0.0 106.6 jit_solution(5821229985158732950)
XLA Ops:
  0.0 1.2 %pack.1 = (f32[296,256]{1,0:T(8,128)S(1)}, f32[296,256]{1,0:T(8,128)S(1)}) custom-call(s32[1]{0:T(128)} %bitcast.core_ref.refs_0_, f32[512,256]{1,0:T(8,128)} %vectors_ref.1, f32[16,256]{1,0:T(8,128)} %cosines_ref.1, f32[16,256]{1,0:T(8,128)} %distances_ref.1, s32[16,256]{1,0:T(8,128)} %offsets_ref.1, s32[1,256]{1,0:T(1,128)} %bitcast.7, s32[2,256]{1,0:T(2,128)} %labels_ref.1), custom_call_target="tpu_custom_call" | custom-call | tf_op jit(solution)/shard_map/pack/pallas_call | solution.py:349
  1.2 8.8 %collective-permute-start = (f32[296,256]{1,0:T(8,128)S(1)}, f32[296,256]{1,0:T(8,128)S(1)}, u32[]{:S(2)}, u32[]{:S(2)}) collective-permute-start(f32[296,256]{1,0:T(8,128)S(1)} %get-tuple-element.23), channel_id=1, source_target_pairs={{0,1},{1,0},{2,3},{3,2},{4,5},{5,4},{6,7},{7,6},{8,9},{9,8},{10,11... | collective-permute-start | bytes 909320 | tf_op jit(solution)/shard_map/ppermute | solution.py:381
  10.0 1.2 %collective-permute-done.mate_ref = f32[296,256]{1,0:T(8,128)S(1)} collective-permute-done((f32[296,256]{1,0:T(8,128)S(1)}, f32[296,256]{1,0:T(8,128)S(1)}, u32[]{:S(2)}, u32[]{:S(2)}) %collective-permute-start) | collective-permute-done | bytes 303136 | tf_op jit(solution)/shard_map/ppermute | solution.py:381
  11.3 1.9 %collective-permute-start.2 = (f32[2,296,256]{2,1,0:T(8,128)S(1)}, f32[2,296,256]{2,1,0:T(8,128)S(1)}, u32[]{:S(2)}, u32[]{:S(2)}) collective-permute-start(f32[2,296,256]{2,1,0:T(8,128)S(1)} %merge.1.slab_ref.own), channel_id=1, source_target_pairs={{0,2},{2,4},{4,6},{6,8},{8,10},{10,12},{12,14},{14,16},{16,18},{18... | collective-permute-start | bytes 1818632 | tf_op jit(solution)/shard_map/ppermute | solution.py:369
  13.2 10.4 %collective-permute-start.1 = (f32[2,296,256]{2,1,0:T(8,128)S(1)}, f32[2,296,256]{2,1,0:T(8,128)S(1)}, u32[]{:S(2)}, u32[]{:S(2)}) collective-permute-start(f32[2,296,256]{2,1,0:T(8,128)S(1)} %merge.1.slab_ref.own), channel_id=1, source_target_pairs={{0,510},{2,0},{4,2},{6,4},{8,6},{10,8},{12,10},{14,12},{16,14},{18... | collective-permute-start | bytes 1818632 | tf_op jit(solution)/shard_map/ppermute | solution.py:369
  23.6 1.8 %own_matrix.1 = (bf16[768,256]{1,0:T(8,128)(2,1)S(1)}, bf16[768,256]{1,0:T(8,128)(2,1)S(1)}, bf16[768,256]{1,0:T(8,128)(2,1)S(1)}, bf16[768,256]{1,0:T(8,128)(2,1)S(1)}) custom-call(f32[2,296,256]{2,1,0:T(8,128)S(1)} %merge.1.slab_ref.own), custom_call_target="tpu_custom_call" | custom-call | tf_op jit(solution)/shard_map/own_matrix/pallas_call | solution.py:349
  25.4 10.0 %collective-permute-done.2.left = f32[2,296,256]{2,1,0:T(8,128)S(1)} collective-permute-done((f32[2,296,256]{2,1,0:T(8,128)S(1)}, f32[2,296,256]{2,1,0:T(8,128)S(1)}, u32[]{:S(2)}, u32[]{:S(2)}) %collective-permute-start.2) | collective-permute-done | bytes 606240 | tf_op jit(solution)/shard_map/ppermute | solution.py:369
  35.4 0.9 collective-permute-done.1.right
  36.3 3.8 %apply_twice.1 = (f32[256,512]{1,0:T(8,128)S(1)}, f32[128,512]{1,0:T(8,128)S(1)}) custom-call(f32[2,296,256]{2,1,0:T(8,128)S(1)} %collective-permute-done.1.right, f32[2,296,256]{2,1,0:T(8,128)S(1)} %merge.1.slab_ref.own, f32[2,296,256]{2,1,0:T(8,128)S(1)} %collective-permute-done.2.left, bf16[768,256]{1,0:T(8,128)(2,1)S(1)} %get-tuple-element.24.rest_0_, ...), custom_call_target="tpu_custom_call" | custom-call | tf_op jit(solution)/shard_map/apply_twice/pallas_call | solution.py:349
  40.1 3.1 %collective-permute-start.3 = (f32[128,512]{1,0:T(8,128)S(1)}, f32[128,512]{1,0:T(8,128)S(1)}, u32[]{:S(2)}, u32[]{:S(2)}) collective-permute-start(f32[128,512]{1,0:T(8,128)S(1)} %get-tuple-element.28.lead_ref), channel_id=1, source_target_pairs={{0,1},{1,0},{2,3},{3,2},{4,5},{5,4},{6,7},{7,6},{8,9},{9,8},{10,11... | collective-permute-start | bytes 786440 | tf_op jit(solution)/shard_map/ppermute | solution.py:398
  43.2 1.1 %collective-permute-done.3.other_ref = f32[128,512]{1,0:T(8,128)S(1)} collective-permute-done((f32[128,512]{1,0:T(8,128)S(1)}, f32[128,512]{1,0:T(8,128)S(1)}, u32[]{:S(2)}, u32[]{:S(2)}) %collective-permute-start.3) | collective-permute-done | bytes 262176 | tf_op jit(solution)/shard_map/ppermute | solution.py:398
  44.3 0.7 gram.1
  45.0 10.3 %all_to_all.15.pieces_ref = f32[16,24,128]{2,1,0:T(8,128)S(1)} all-to-all(f32[16,24,128]{2,1,0:T(8,128)S(1)} %bitcast.6), channel_id=1, replica_groups=mesh['y'=4,'z'=16,'x'=4,'core'=2] {'y','x'}, dimensions={0} | all-to-all | bytes 393216 | tf_op jit(solution)/shard_map/all_to_all | solution.py:335
  55.4 0.7 sum_plane.1
  56.1 9.9 %all-to-all-start.1 = ((f32[16,24,128]{2,1,0:T(8,128)}), f32[16,24,128]{2,1,0:T(8,128)S(1)}, u32[]{:S(2)}, u32[]{:S(2)}) async-start(f32[16,24,128]{2,1,0:T(8,128)} %sum_plane.1), calls=%async_computation.1 | async-start | bytes 393216 | tf_op jit(solution)/shard_map/all_to_all | solution.py:335
  66.0 0.1 share.1
  66.1 2.5 %collective-permute-start.4 = (f32[160,512]{1,0:T(8,128)S(1)}, f32[160,512]{1,0:T(8,128)S(1)}, u32[]{:S(2)}, u32[]{:S(2)}) collective-permute-start(f32[160,512]{1,0:T(8,128)S(1)} %get-tuple-element.31), channel_id=1, source_target_pairs={{0,2},{2,4},{4,6},{6,0},{1,3},{3,5},{5,7},{7,1},{8,10},{10,12},{12... | collective-permute-start | bytes 983048 | tf_op jit(solution)/shard_map/ppermute | solution.py:414
  68.6 3.2 %collective-permute-start.5 = (f32[160,512]{1,0:T(8,128)S(1)}, f32[160,512]{1,0:T(8,128)S(1)}, u32[]{:S(2)}, u32[]{:S(2)}) collective-permute-start(f32[160,512]{1,0:T(8,128)S(1)} %get-tuple-element.32), channel_id=1, source_target_pairs={{0,4},{2,6},{4,0},{6,2},{1,5},{3,7},{5,1},{7,3},{8,12},{10,14},{12... | collective-permute-start | bytes 983048 | tf_op jit(solution)/shard_map/ppermute | solution.py:414
  71.8 3.2 %collective-permute-start.6 = (f32[160,512]{1,0:T(8,128)S(1)}, f32[160,512]{1,0:T(8,128)S(1)}, u32[]{:S(2)}, u32[]{:S(2)}) collective-permute-start(f32[160,512]{1,0:T(8,128)S(1)} %get-tuple-element.33), channel_id=1, source_target_pairs={{0,6},{2,0},{4,2},{6,4},{1,7},{3,1},{5,3},{7,5},{8,14},{10,8},{12,... | collective-permute-start | bytes 983048 | tf_op jit(solution)/shard_map/ppermute | solution.py:414
  75.0 3.3 %all-to-all-done.1.pieces_ref = f32[16,24,128]{2,1,0:T(8,128)S(1)} async-done(((f32[16,24,128]{2,1,0:T(8,128)}), f32[16,24,128]{2,1,0:T(8,128)S(1)}, u32[]{:S(2)}, u32[]{:S(2)}) %all-to-all-start.1) | async-done | bytes 196640 | tf_op jit(solution)/shard_map/all_to_all | solution.py:335
  78.3 0.8 sum_depth.1
  79.1 9.0 %all-to-all-start.2 = ((f32[32,24,128]{2,1,0:T(8,128)}), f32[32,24,128]{2,1,0:T(8,128)S(1)}, u32[]{:S(2)}, u32[]{:S(2)}) async-start(f32[32,24,128]{2,1,0:T(8,128)} %sum_depth.1), calls=%async_computation.2 | async-start | bytes 786432 | tf_op jit(solution)/shard_map/all_to_all | solution.py:335
  88.1 0.0 collective-permute-done.4.one_ref.refs_6_
  88.1 0.0 collective-permute-done.5.two_ref.refs_7_
  88.1 0.0 collective-permute-done.6.three_ref.refs_8_
  88.2 2.7 %collective-permute-start.7 = (f32[144,512]{1,0:T(8,128)S(1)}, f32[144,512]{1,0:T(8,128)S(1)}, u32[]{:S(2)}, u32[]{:S(2)}) collective-permute-start(f32[144,512]{1,0:T(8,128)S(1)} %get-tuple-element.37), channel_id=1, source_target_pairs={{0,1},{1,0},{2,3},{3,2},{4,5},{5,4},{6,7},{7,6},{8,9},{9,8},{10,11... | collective-permute-start | bytes 884744 | tf_op jit(solution)/shard_map/ppermute | solution.py:423
  90.9 1.9 %collective-permute-start.8 = (f32[144,512]{1,0:T(8,128)S(1)}, f32[144,512]{1,0:T(8,128)S(1)}, u32[]{:S(2)}, u32[]{:S(2)}) collective-permute-start(f32[144,512]{1,0:T(8,128)S(1)} %get-tuple-element.38), channel_id=1, source_target_pairs={{0,1},{1,0},{2,3},{3,2},{4,5},{5,4},{6,7},{7,6},{8,9},{9,8},{10,11... | collective-permute-start | bytes 884744 | tf_op jit(solution)/shard_map/ppermute | solution.py:423
  92.8 0.0 collective-permute-done.7.refs_4_
  92.8 1.5 %collective-permute-done.8.refs_5_ = f32[144,512]{1,0:T(8,128)S(1)} collective-permute-done((f32[144,512]{1,0:T(8,128)S(1)}, f32[144,512]{1,0:T(8,128)S(1)}, u32[]{:S(2)}, u32[]{:S(2)}) %collective-permute-start.8) | collective-permute-done | bytes 294944 | tf_op jit(solution)/shard_map/ppermute | solution.py:423
  94.3 3.9 %all-to-all-done.2 = f32[32,24,128]{2,1,0:T(8,128)S(1)} async-done(((f32[32,24,128]{2,1,0:T(8,128)}), f32[32,24,128]{2,1,0:T(8,128)S(1)}, u32[]{:S(2)}, u32[]{:S(2)}) %all-to-all-start.2) | async-done | bytes 393248 | tf_op jit(solution)/shard_map/all_to_all | solution.py:335
  98.3 8.4 %finish.1 = f32[64,2048]{1,0:T(8,128)} custom-call(s32[1]{0:T(128)} %bitcast.core_ref.refs_0_, s32[1]{0:T(128)} %bitcast.1.chip_ref.refs_1_, f32[16,2,24,128]{3,2,1,0:T(8,128)S(1)} %bitcast.5, f32[256,512]{1,0:T(8,128)S(1)} %get-tuple-element.30.refs_3_, f32[144,512]{1,0:T(8,128)S(1)} %collective-permute-done.7.refs_4_, ...), custom_call_target="tpu_custom_call" | custom-call | tf_op jit(solution)/shard_map/finish/pallas_call | solution.py:349
  (2 shorter events, 0.1 us)
Async XLA Ops:
  1.2 10.0 %collective-permute-start = (f32[296,256]{1,0:T(8,128)S(1)}, f32[296,256]{1,0:T(8,128)S(1)}, u32[]{:S(2)}, u32[]{:S(2)}) collective-permute-start(f32[296,256]{1,0:T(8,128)S(1)} %get-tuple-element.23), channel_id=1, source_target_pairs={{0,1},{1,0},{2,3},{3,2},{4,5},{5,4},{6,7},{7,6},{8,9},{9,8},{10,11... | collective-permute-start | bytes 909320 | tf_op jit(solution)/shard_map/ppermute | solution.py:381
  11.3 24.1 %collective-permute-start.2 = (f32[2,296,256]{2,1,0:T(8,128)S(1)}, f32[2,296,256]{2,1,0:T(8,128)S(1)}, u32[]{:S(2)}, u32[]{:S(2)}) collective-permute-start(f32[2,296,256]{2,1,0:T(8,128)S(1)} %merge.1.slab_ref.own), channel_id=1, source_target_pairs={{0,2},{2,4},{4,6},{6,8},{8,10},{10,12},{12,14},{14,16},{16,18},{18... | collective-permute-start | bytes 1818632 | tf_op jit(solution)/shard_map/ppermute | solution.py:369
  13.2 23.1 %collective-permute-start.1 = (f32[2,296,256]{2,1,0:T(8,128)S(1)}, f32[2,296,256]{2,1,0:T(8,128)S(1)}, u32[]{:S(2)}, u32[]{:S(2)}) collective-permute-start(f32[2,296,256]{2,1,0:T(8,128)S(1)} %merge.1.slab_ref.own), channel_id=1, source_target_pairs={{0,510},{2,0},{4,2},{6,4},{8,6},{10,8},{12,10},{14,12},{16,14},{18... | collective-permute-start | bytes 1818632 | tf_op jit(solution)/shard_map/ppermute | solution.py:369
  40.1 4.3 %collective-permute-start.3 = (f32[128,512]{1,0:T(8,128)S(1)}, f32[128,512]{1,0:T(8,128)S(1)}, u32[]{:S(2)}, u32[]{:S(2)}) collective-permute-start(f32[128,512]{1,0:T(8,128)S(1)} %get-tuple-element.28.lead_ref), channel_id=1, source_target_pairs={{0,1},{1,0},{2,3},{3,2},{4,5},{5,4},{6,7},{7,6},{8,9},{9,8},{10,11... | collective-permute-start | bytes 786440 | tf_op jit(solution)/shard_map/ppermute | solution.py:398
  56.1 22.3 %all-to-all-start.1 = ((f32[16,24,128]{2,1,0:T(8,128)}), f32[16,24,128]{2,1,0:T(8,128)S(1)}, u32[]{:S(2)}, u32[]{:S(2)}) async-start(f32[16,24,128]{2,1,0:T(8,128)} %sum_plane.1), calls=%async_computation.1 | async-start | bytes 393216 | tf_op jit(solution)/shard_map/all_to_all | solution.py:335
  66.1 22.0 %collective-permute-start.4 = (f32[160,512]{1,0:T(8,128)S(1)}, f32[160,512]{1,0:T(8,128)S(1)}, u32[]{:S(2)}, u32[]{:S(2)}) collective-permute-start(f32[160,512]{1,0:T(8,128)S(1)} %get-tuple-element.31), channel_id=1, source_target_pairs={{0,2},{2,4},{4,6},{6,0},{1,3},{3,5},{5,7},{7,1},{8,10},{10,12},{12... | collective-permute-start | bytes 983048 | tf_op jit(solution)/shard_map/ppermute | solution.py:414
  68.6 19.5 %collective-permute-start.5 = (f32[160,512]{1,0:T(8,128)S(1)}, f32[160,512]{1,0:T(8,128)S(1)}, u32[]{:S(2)}, u32[]{:S(2)}) collective-permute-start(f32[160,512]{1,0:T(8,128)S(1)} %get-tuple-element.32), channel_id=1, source_target_pairs={{0,4},{2,6},{4,0},{6,2},{1,5},{3,7},{5,1},{7,3},{8,12},{10,14},{12... | collective-permute-start | bytes 983048 | tf_op jit(solution)/shard_map/ppermute | solution.py:414
  71.8 16.3 %collective-permute-start.6 = (f32[160,512]{1,0:T(8,128)S(1)}, f32[160,512]{1,0:T(8,128)S(1)}, u32[]{:S(2)}, u32[]{:S(2)}) collective-permute-start(f32[160,512]{1,0:T(8,128)S(1)} %get-tuple-element.33), channel_id=1, source_target_pairs={{0,6},{2,0},{4,2},{6,4},{1,7},{3,1},{5,3},{7,5},{8,14},{10,8},{12,... | collective-permute-start | bytes 983048 | tf_op jit(solution)/shard_map/ppermute | solution.py:414
  79.1 19.1 %all-to-all-start.2 = ((f32[32,24,128]{2,1,0:T(8,128)}), f32[32,24,128]{2,1,0:T(8,128)S(1)}, u32[]{:S(2)}, u32[]{:S(2)}) async-start(f32[32,24,128]{2,1,0:T(8,128)} %sum_depth.1), calls=%async_computation.2 | async-start | bytes 786432 | tf_op jit(solution)/shard_map/all_to_all | solution.py:335
  88.2 4.6 %collective-permute-start.7 = (f32[144,512]{1,0:T(8,128)S(1)}, f32[144,512]{1,0:T(8,128)S(1)}, u32[]{:S(2)}, u32[]{:S(2)}) collective-permute-start(f32[144,512]{1,0:T(8,128)S(1)} %get-tuple-element.37), channel_id=1, source_target_pairs={{0,1},{1,0},{2,3},{3,2},{4,5},{5,4},{6,7},{7,6},{8,9},{9,8},{10,11... | collective-permute-start | bytes 884744 | tf_op jit(solution)/shard_map/ppermute | solution.py:423
  90.9 3.5 %collective-permute-start.8 = (f32[144,512]{1,0:T(8,128)S(1)}, f32[144,512]{1,0:T(8,128)S(1)}, u32[]{:S(2)}, u32[]{:S(2)}) collective-permute-start(f32[144,512]{1,0:T(8,128)S(1)} %get-tuple-element.38), channel_id=1, source_target_pairs={{0,1},{1,0},{2,3},{3,2},{4,5},{5,4},{6,7},{7,6},{8,9},{9,8},{10,11... | collective-permute-start | bytes 884744 | tf_op jit(solution)/shard_map/ppermute | solution.py:423

commit v16 on v15

--- a/solution.py
+++ b/solution.py
@@ -192,32 +192,37 @@
         gram_ref[part] = gram[:, 128 * part : 128 * part + 128]
 
 
-def share_kernel(core_ref, chip_ref, lead_ref, other_ref, applied_ref, home_ref, *sent_refs):
+def share_kernel(core_ref, chip_ref, lead_ref, other_ref, applied_ref, *sent_refs):
     count = 1 + len(sent_refs)
     second = core_ref[0] == 1
     head = [head_block(s, core_ref, lead_ref, other_ref) for s in range(STEPS)]
-    for s in range(STEPS):
-        home_ref[BLOCK * s : BLOCK * s + BLOCK, :] = head[s]
     middle = HALF - BLOCK
-    half = (
-        jnp.where(second, head[1][middle:], head[0][0 : BLOCK - middle]),
-        jnp.where(second, head[2][0:BLOCK], jnp.concatenate(
-            [head[0][BLOCK - middle :], head[1][0:middle]], axis=0)),
-    )
-    for ref in sent_refs:
-        ref[0 : BLOCK - middle, :] = half[0]
-        ref[BLOCK - middle : HALF, :] = half[1]
-    for step, ref in enumerate((home_ref, *sent_refs)):
-        start = pl.multiple_of(lax.rem(chip_ref[0] + step, count) * BLOCK, BLOCK)
-        ref[ref.shape[0] - BLOCK :, :] = applied_ref[pl.ds(start, BLOCK), :]
-
-
-def stack_kernel(one_ref, two_ref, three_ref, first_ref, last_ref):
+    rest = BLOCK - middle
+    top = jnp.where(second, head[1][middle:], head[0][0:rest])
+    bottom = jnp.where(
+        second, head[2], jnp.concatenate([head[0][rest:], head[1][0:middle]], axis=0)
+    )
+    for step, ref in enumerate(sent_refs):
+        ref[0:rest, :] = top
+        ref[rest:HALF, :] = bottom
+        start = pl.multiple_of(lax.rem(chip_ref[0] + step + 1, count) * BLOCK, BLOCK)
+        ref[HALF:, :] = applied_ref[pl.ds(start, BLOCK), :]
+
+
+def stack_kernel(
+    core_ref, chip_ref, lead_ref, other_ref, applied_ref, one_ref, two_ref, three_ref,
+    first_ref, last_ref, home_ref,
+):
     middle = HALF // 2
     first_ref[0:HALF, :] = one_ref[0:HALF, :]
     first_ref[HALF:, :] = two_ref[0:middle, :]
     last_ref[0:middle, :] = two_ref[middle:HALF, :]
     last_ref[middle:, :] = three_ref[0:HALF, :]
+    for s in range(STEPS):
+        block = head_block(s, core_ref, lead_ref, other_ref)
+        home_ref[BLOCK * s : BLOCK * s + BLOCK, :] = block
+    start = pl.multiple_of(chip_ref[0] * BLOCK, BLOCK)
+    home_ref[HEAD:, :] = applied_ref[pl.ds(start, BLOCK), :]
 
 
 def spread(value):
@@ -401,9 +406,8 @@
         gram_kernel, "gram", shape((OWN // 128, HEAD, 128), F32),
         (core, lead, other, applied), (), [SMEM] + [VMEM] * 3,
     )
-    home, *sent = call(
-        share_kernel, "share",
-        (shape((HEAD + BLOCK, CHIP), F32),) + (shape((HALF + BLOCK, CHIP), F32),) * (count - 1),
+    sent = call(
+        share_kernel, "share", (shape((HALF + BLOCK, CHIP), F32),) * (count - 1),
         (core, chip, lead, other, applied), (), [SMEM] * 2 + [VMEM] * 3,
     )
     piece = (OWN // 128) * HEAD // planes
@@ -417,8 +421,10 @@
     gram = exchange(gram, "z")
     gram = call(sum_kernel, "sum_depth", shape((everyone, piece, 128), F32), (gram,))
     _, *ready = lax.optimization_barrier((gram, *got))
-    stacked = call(
-        stack_kernel, "stack", (shape((HALF * (count - 1) // 2, CHIP), F32),) * 2, ready
+    *stacked, home = call(
+        stack_kernel, "stack",
+        (shape((HALF * (count - 1) // 2, CHIP), F32),) * 2 + (shape((HEAD + BLOCK, CHIP), F32),),
+        (core, chip, lead, other, applied, *ready), (), [SMEM] * 2 + [VMEM] * (2 + count),
     )
     theirs = [lax.ppermute(value, "core", [(0, 1), (1, 0)]) for value in stacked]
     gram = exchange(gram, (*plane, "core"))

time: 107 us -> 107 us (level)
  no operation moved by 1% of the time
where the time goes in v16:
time: 107 us
  starting transfers between devices  56.5 us (53%)
  waiting for transfers between devices  22 us (21%)
  Pallas kernels  17.6 us (16%)
  blocking collectives  10.3 us (10%)
    all_to_all x2, starting transfers between devices, exchange(): return lax.all_to_all(value, axes, split_axis=0, concat_axis=0, tiled=True)  18.9 us
    pallas_call x10, Pallas kernels, call(): pl.pallas_call(kernel, out_shape=out_shape, in_specs=specs or [VMEM] * le...  17.6 us
    ppermute x2, starting transfers between devices, shift(): lax.ppermute(value, chips, [(i, (i + step) % chip_count) for i in range(c...  12.3 us
    ppermute x2, waiting for transfers between devices, shift(): lax.ppermute(value, chips, [(i, (i + step) % chip_count) for i in range(c...  10.9 us
    all_to_all x1, blocking collectives, exchange(): return lax.all_to_all(value, axes, split_axis=0, concat_axis=0, tiled=True)  10.3 us
    ppermute x3, starting transfers between devices, on_device(): lax.ppermute(value, 'x', [(i, (i + step + 1) % count) for i in range(coun...  8.88 us
    ppermute x1, starting transfers between devices, on_device(): mate = lax.ppermute(send, 'core', [(0, 1), (1, 0)])  8.79 us
    all_to_all x2, waiting for transfers between devices, exchange(): return lax.all_to_all(value, axes, split_axis=0, concat_axis=0, tiled=True)  7.26 us
  transfers between devices with their start and end apart: 11, of which 7 were waited for; matrix products, arithmetic and copies ran while one was open for 0% of the time, Pallas kernels for 3%

profile of v16, /device:TPU:1, one launch (start us, length us, event | category | flops | bytes accessed | tf_op | source)
XLA Modules:
  0.0 106.6 jit_solution(129977814755021813)
XLA Ops:
  0.0 1.2 %pack.1 = (f32[296,256]{1,0:T(8,128)S(1)}, f32[296,256]{1,0:T(8,128)S(1)}) custom-call(s32[1]{0:T(128)} %bitcast.core_ref.refs_0_, f32[512,256]{1,0:T(8,128)} %vectors_ref.1, f32[16,256]{1,0:T(8,128)} %cosines_ref.1, f32[16,256]{1,0:T(8,128)} %distances_ref.1, s32[16,256]{1,0:T(8,128)} %offsets_ref.1, s32[1,256]{1,0:T(1,128)} %bitcast.7, s32[2,256]{1,0:T(2,128)} %labels_ref.1), custom_call_target="tpu_custom_call" | custom-call | tf_op jit(solution)/shard_map/pack/pallas_call | solution.py:354
  1.2 8.8 %collective-permute-start = (f32[296,256]{1,0:T(8,128)S(1)}, f32[296,256]{1,0:T(8,128)S(1)}, u32[]{:S(2)}, u32[]{:S(2)}) collective-permute-start(f32[296,256]{1,0:T(8,128)S(1)} %get-tuple-element.23), channel_id=1, source_target_pairs={{0,1},{1,0},{2,3},{3,2},{4,5},{5,4},{6,7},{7,6},{8,9},{9,8},{10,11... | collective-permute-start | bytes 909320 | tf_op jit(solution)/shard_map/ppermute | solution.py:386
  10.0 1.2 %collective-permute-done.mate_ref = f32[296,256]{1,0:T(8,128)S(1)} collective-permute-done((f32[296,256]{1,0:T(8,128)S(1)}, f32[296,256]{1,0:T(8,128)S(1)}, u32[]{:S(2)}, u32[]{:S(2)}) %collective-permute-start) | collective-permute-done | bytes 303136 | tf_op jit(solution)/shard_map/ppermute | solution.py:386
  11.3 1.9 %collective-permute-start.2 = (f32[2,296,256]{2,1,0:T(8,128)S(1)}, f32[2,296,256]{2,1,0:T(8,128)S(1)}, u32[]{:S(2)}, u32[]{:S(2)}) collective-permute-start(f32[2,296,256]{2,1,0:T(8,128)S(1)} %merge.1.slab_ref.own), channel_id=1, source_target_pairs={{0,2},{2,4},{4,6},{6,8},{8,10},{10,12},{12,14},{14,16},{16,18},{18... | collective-permute-start | bytes 1818632 | tf_op jit(solution)/shard_map/ppermute | solution.py:374
  13.2 10.4 %collective-permute-start.1 = (f32[2,296,256]{2,1,0:T(8,128)S(1)}, f32[2,296,256]{2,1,0:T(8,128)S(1)}, u32[]{:S(2)}, u32[]{:S(2)}) collective-permute-start(f32[2,296,256]{2,1,0:T(8,128)S(1)} %merge.1.slab_ref.own), channel_id=1, source_target_pairs={{0,510},{2,0},{4,2},{6,4},{8,6},{10,8},{12,10},{14,12},{16,14},{18... | collective-permute-start | bytes 1818632 | tf_op jit(solution)/shard_map/ppermute | solution.py:374
  23.6 1.8 %own_matrix.1 = (bf16[768,256]{1,0:T(8,128)(2,1)S(1)}, bf16[768,256]{1,0:T(8,128)(2,1)S(1)}, bf16[768,256]{1,0:T(8,128)(2,1)S(1)}, bf16[768,256]{1,0:T(8,128)(2,1)S(1)}) custom-call(f32[2,296,256]{2,1,0:T(8,128)S(1)} %merge.1.slab_ref.own), custom_call_target="tpu_custom_call" | custom-call | tf_op jit(solution)/shard_map/own_matrix/pallas_call | solution.py:354
  25.4 10.0 %collective-permute-done.2.left = f32[2,296,256]{2,1,0:T(8,128)S(1)} collective-permute-done((f32[2,296,256]{2,1,0:T(8,128)S(1)}, f32[2,296,256]{2,1,0:T(8,128)S(1)}, u32[]{:S(2)}, u32[]{:S(2)}) %collective-permute-start.2) | collective-permute-done | bytes 606240 | tf_op jit(solution)/shard_map/ppermute | solution.py:374
  35.4 0.9 collective-permute-done.1.right
  36.3 3.8 %apply_twice.1 = (f32[256,512]{1,0:T(8,128)S(1)}, f32[128,512]{1,0:T(8,128)S(1)}) custom-call(f32[2,296,256]{2,1,0:T(8,128)S(1)} %collective-permute-done.1.right, f32[2,296,256]{2,1,0:T(8,128)S(1)} %merge.1.slab_ref.own, f32[2,296,256]{2,1,0:T(8,128)S(1)} %collective-permute-done.2.left, bf16[768,256]{1,0:T(8,128)(2,1)S(1)} %get-tuple-element.24.rest_0_, ...), custom_call_target="tpu_custom_call" | custom-call | tf_op jit(solution)/shard_map/apply_twice/pallas_call | solution.py:354
  40.1 3.1 %collective-permute-start.3 = (f32[128,512]{1,0:T(8,128)S(1)}, f32[128,512]{1,0:T(8,128)S(1)}, u32[]{:S(2)}, u32[]{:S(2)}) collective-permute-start(f32[128,512]{1,0:T(8,128)S(1)} %get-tuple-element.28.lead_ref), channel_id=1, source_target_pairs={{0,1},{1,0},{2,3},{3,2},{4,5},{5,4},{6,7},{7,6},{8,9},{9,8},{10,11... | collective-permute-start | bytes 786440 | tf_op jit(solution)/shard_map/ppermute | solution.py:403
  43.2 1.1 %collective-permute-done.3.other_ref = f32[128,512]{1,0:T(8,128)S(1)} collective-permute-done((f32[128,512]{1,0:T(8,128)S(1)}, f32[128,512]{1,0:T(8,128)S(1)}, u32[]{:S(2)}, u32[]{:S(2)}) %collective-permute-start.3) | collective-permute-done | bytes 262176 | tf_op jit(solution)/shard_map/ppermute | solution.py:403
  44.3 0.7 gram.1
  45.0 10.3 %all_to_all.15.pieces_ref = f32[16,24,128]{2,1,0:T(8,128)S(1)} all-to-all(f32[16,24,128]{2,1,0:T(8,128)S(1)} %bitcast.6), channel_id=1, replica_groups=mesh['y'=4,'z'=16,'x'=4,'core'=2] {'y','x'}, dimensions={0} | all-to-all | bytes 393216 | tf_op jit(solution)/shard_map/all_to_all | solution.py:340
  55.4 0.7 sum_plane.1
  56.1 9.9 %all-to-all-start.1 = ((f32[16,24,128]{2,1,0:T(8,128)}), f32[16,24,128]{2,1,0:T(8,128)S(1)}, u32[]{:S(2)}, u32[]{:S(2)}) async-start(f32[16,24,128]{2,1,0:T(8,128)} %sum_plane.1), calls=%async_computation.1 | async-start | bytes 393216 | tf_op jit(solution)/shard_map/all_to_all | solution.py:340
  66.0 0.1 share.1
  66.1 2.5 %collective-permute-start.4 = (f32[160,512]{1,0:T(8,128)S(1)}, f32[160,512]{1,0:T(8,128)S(1)}, u32[]{:S(2)}, u32[]{:S(2)}) collective-permute-start(f32[160,512]{1,0:T(8,128)S(1)} %get-tuple-element.30), channel_id=1, source_target_pairs={{0,2},{2,4},{4,6},{6,0},{1,3},{3,5},{5,7},{7,1},{8,10},{10,12},{12... | collective-permute-start | bytes 983048 | tf_op jit(solution)/shard_map/ppermute | solution.py:418
  68.6 3.2 %collective-permute-start.5 = (f32[160,512]{1,0:T(8,128)S(1)}, f32[160,512]{1,0:T(8,128)S(1)}, u32[]{:S(2)}, u32[]{:S(2)}) collective-permute-start(f32[160,512]{1,0:T(8,128)S(1)} %get-tuple-element.31), channel_id=1, source_target_pairs={{0,4},{2,6},{4,0},{6,2},{1,5},{3,7},{5,1},{7,3},{8,12},{10,14},{12... | collective-permute-start | bytes 983048 | tf_op jit(solution)/shard_map/ppermute | solution.py:418
  71.8 3.2 %collective-permute-start.6 = (f32[160,512]{1,0:T(8,128)S(1)}, f32[160,512]{1,0:T(8,128)S(1)}, u32[]{:S(2)}, u32[]{:S(2)}) collective-permute-start(f32[160,512]{1,0:T(8,128)S(1)} %get-tuple-element.32), channel_id=1, source_target_pairs={{0,6},{2,0},{4,2},{6,4},{1,7},{3,1},{5,3},{7,5},{8,14},{10,8},{12,... | collective-permute-start | bytes 983048 | tf_op jit(solution)/shard_map/ppermute | solution.py:418
  75.0 3.3 %all-to-all-done.1.pieces_ref = f32[16,24,128]{2,1,0:T(8,128)S(1)} async-done(((f32[16,24,128]{2,1,0:T(8,128)}), f32[16,24,128]{2,1,0:T(8,128)S(1)}, u32[]{:S(2)}, u32[]{:S(2)}) %all-to-all-start.1) | async-done | bytes 196640 | tf_op jit(solution)/shard_map/all_to_all | solution.py:340
  78.3 0.8 sum_depth.1
  79.1 9.0 %all-to-all-start.2 = ((f32[32,24,128]{2,1,0:T(8,128)}), f32[32,24,128]{2,1,0:T(8,128)S(1)}, u32[]{:S(2)}, u32[]{:S(2)}) async-start(f32[32,24,128]{2,1,0:T(8,128)} %sum_depth.1), calls=%async_computation.2 | async-start | bytes 786432 | tf_op jit(solution)/shard_map/all_to_all | solution.py:340
  88.1 0.0 collective-permute-done.4.one_ref.refs_6_
  88.1 0.0 collective-permute-done.5.two_ref.refs_7_
  88.1 0.0 collective-permute-done.6.three_ref.refs_8_
  88.1 0.1 stack.1
  88.2 2.7 %collective-permute-start.7 = (f32[144,512]{1,0:T(8,128)S(1)}, f32[144,512]{1,0:T(8,128)S(1)}, u32[]{:S(2)}, u32[]{:S(2)}) collective-permute-start(f32[144,512]{1,0:T(8,128)S(1)} %get-tuple-element.37), channel_id=1, source_target_pairs={{0,1},{1,0},{2,3},{3,2},{4,5},{5,4},{6,7},{7,6},{8,9},{9,8},{10,11... | collective-permute-start | bytes 884744 | tf_op jit(solution)/shard_map/ppermute | solution.py:429
  90.9 1.9 %collective-permute-start.8 = (f32[144,512]{1,0:T(8,128)S(1)}, f32[144,512]{1,0:T(8,128)S(1)}, u32[]{:S(2)}, u32[]{:S(2)}) collective-permute-start(f32[144,512]{1,0:T(8,128)S(1)} %get-tuple-element.38), channel_id=1, source_target_pairs={{0,1},{1,0},{2,3},{3,2},{4,5},{5,4},{6,7},{7,6},{8,9},{9,8},{10,11... | collective-permute-start | bytes 884744 | tf_op jit(solution)/shard_map/ppermute | solution.py:429
  92.8 0.0 collective-permute-done.7.refs_4_
  92.8 1.5 %collective-permute-done.8.refs_5_ = f32[144,512]{1,0:T(8,128)S(1)} collective-permute-done((f32[144,512]{1,0:T(8,128)S(1)}, f32[144,512]{1,0:T(8,128)S(1)}, u32[]{:S(2)}, u32[]{:S(2)}) %collective-permute-start.8) | collective-permute-done | bytes 294944 | tf_op jit(solution)/shard_map/ppermute | solution.py:429
  94.3 3.9 %all-to-all-done.2 = f32[32,24,128]{2,1,0:T(8,128)S(1)} async-done(((f32[32,24,128]{2,1,0:T(8,128)}), f32[32,24,128]{2,1,0:T(8,128)S(1)}, u32[]{:S(2)}, u32[]{:S(2)}) %all-to-all-start.2) | async-done | bytes 393248 | tf_op jit(solution)/shard_map/all_to_all | solution.py:340
  98.3 8.4 %finish.1 = f32[64,2048]{1,0:T(8,128)} custom-call(s32[1]{0:T(128)} %bitcast.core_ref.refs_0_, s32[1]{0:T(128)} %bitcast.1.chip_ref.refs_1_, f32[16,2,24,128]{3,2,1,0:T(8,128)S(1)} %bitcast.5, f32[256,512]{1,0:T(8,128)S(1)} %get-tuple-element.36.refs_3_, f32[144,512]{1,0:T(8,128)S(1)} %collective-permute-done.7.refs_4_, ...), custom_call_target="tpu_custom_call" | custom-call | tf_op jit(solution)/shard_map/finish/pallas_call | solution.py:354
  (1 shorter events, 0.0 us)
Async XLA Ops:
  1.2 10.0 %collective-permute-start = (f32[296,256]{1,0:T(8,128)S(1)}, f32[296,256]{1,0:T(8,128)S(1)}, u32[]{:S(2)}, u32[]{:S(2)}) collective-permute-start(f32[296,256]{1,0:T(8,128)S(1)} %get-tuple-element.23), channel_id=1, source_target_pairs={{0,1},{1,0},{2,3},{3,2},{4,5},{5,4},{6,7},{7,6},{8,9},{9,8},{10,11... | collective-permute-start | bytes 909320 | tf_op jit(solution)/shard_map/ppermute | solution.py:386
  11.3 24.1 %collective-permute-start.2 = (f32[2,296,256]{2,1,0:T(8,128)S(1)}, f32[2,296,256]{2,1,0:T(8,128)S(1)}, u32[]{:S(2)}, u32[]{:S(2)}) collective-permute-start(f32[2,296,256]{2,1,0:T(8,128)S(1)} %merge.1.slab_ref.own), channel_id=1, source_target_pairs={{0,2},{2,4},{4,6},{6,8},{8,10},{10,12},{12,14},{14,16},{16,18},{18... | collective-permute-start | bytes 1818632 | tf_op jit(solution)/shard_map/ppermute | solution.py:374
  13.2 23.1 %collective-permute-start.1 = (f32[2,296,256]{2,1,0:T(8,128)S(1)}, f32[2,296,256]{2,1,0:T(8,128)S(1)}, u32[]{:S(2)}, u32[]{:S(2)}) collective-permute-start(f32[2,296,256]{2,1,0:T(8,128)S(1)} %merge.1.slab_ref.own), channel_id=1, source_target_pairs={{0,510},{2,0},{4,2},{6,4},{8,6},{10,8},{12,10},{14,12},{16,14},{18... | collective-permute-start | bytes 1818632 | tf_op jit(solution)/shard_map/ppermute | solution.py:374
  40.1 4.3 %collective-permute-start.3 = (f32[128,512]{1,0:T(8,128)S(1)}, f32[128,512]{1,0:T(8,128)S(1)}, u32[]{:S(2)}, u32[]{:S(2)}) collective-permute-start(f32[128,512]{1,0:T(8,128)S(1)} %get-tuple-element.28.lead_ref), channel_id=1, source_target_pairs={{0,1},{1,0},{2,3},{3,2},{4,5},{5,4},{6,7},{7,6},{8,9},{9,8},{10,11... | collective-permute-start | bytes 786440 | tf_op jit(solution)/shard_map/ppermute | solution.py:403
  56.1 22.3 %all-to-all-start.1 = ((f32[16,24,128]{2,1,0:T(8,128)}), f32[16,24,128]{2,1,0:T(8,128)S(1)}, u32[]{:S(2)}, u32[]{:S(2)}) async-start(f32[16,24,128]{2,1,0:T(8,128)} %sum_plane.1), calls=%async_computation.1 | async-start | bytes 393216 | tf_op jit(solution)/shard_map/all_to_all | solution.py:340
  66.1 22.0 %collective-permute-start.4 = (f32[160,512]{1,0:T(8,128)S(1)}, f32[160,512]{1,0:T(8,128)S(1)}, u32[]{:S(2)}, u32[]{:S(2)}) collective-permute-start(f32[160,512]{1,0:T(8,128)S(1)} %get-tuple-element.30), channel_id=1, source_target_pairs={{0,2},{2,4},{4,6},{6,0},{1,3},{3,5},{5,7},{7,1},{8,10},{10,12},{12... | collective-permute-start | bytes 983048 | tf_op jit(solution)/shard_map/ppermute | solution.py:418
  68.6 19.5 %collective-permute-start.5 = (f32[160,512]{1,0:T(8,128)S(1)}, f32[160,512]{1,0:T(8,128)S(1)}, u32[]{:S(2)}, u32[]{:S(2)}) collective-permute-start(f32[160,512]{1,0:T(8,128)S(1)} %get-tuple-element.31), channel_id=1, source_target_pairs={{0,4},{2,6},{4,0},{6,2},{1,5},{3,7},{5,1},{7,3},{8,12},{10,14},{12... | collective-permute-start | bytes 983048 | tf_op jit(solution)/shard_map/ppermute | solution.py:418
  71.8 16.3 %collective-permute-start.6 = (f32[160,512]{1,0:T(8,128)S(1)}, f32[160,512]{1,0:T(8,128)S(1)}, u32[]{:S(2)}, u32[]{:S(2)}) collective-permute-start(f32[160,512]{1,0:T(8,128)S(1)} %get-tuple-element.32), channel_id=1, source_target_pairs={{0,6},{2,0},{4,2},{6,4},{1,7},{3,1},{5,3},{7,5},{8,14},{10,8},{12,... | collective-permute-start | bytes 983048 | tf_op jit(solution)/shard_map/ppermute | solution.py:418
  79.1 19.1 %all-to-all-start.2 = ((f32[32,24,128]{2,1,0:T(8,128)}), f32[32,24,128]{2,1,0:T(8,128)S(1)}, u32[]{:S(2)}, u32[]{:S(2)}) async-start(f32[32,24,128]{2,1,0:T(8,128)} %sum_depth.1), calls=%async_computation.2 | async-start | bytes 786432 | tf_op jit(solution)/shard_map/all_to_all | solution.py:340
  88.2 4.6 %collective-permute-start.7 = (f32[144,512]{1,0:T(8,128)S(1)}, f32[144,512]{1,0:T(8,128)S(1)}, u32[]{:S(2)}, u32[]{:S(2)}) collective-permute-start(f32[144,512]{1,0:T(8,128)S(1)} %get-tuple-element.37), channel_id=1, source_target_pairs={{0,1},{1,0},{2,3},{3,2},{4,5},{5,4},{6,7},{7,6},{8,9},{9,8},{10,11... | collective-permute-start | bytes 884744 | tf_op jit(solution)/shard_map/ppermute | solution.py:429
  90.9 3.5 %collective-permute-start.8 = (f32[144,512]{1,0:T(8,128)S(1)}, f32[144,512]{1,0:T(8,128)S(1)}, u32[]{:S(2)}, u32[]{:S(2)}) collective-permute-start(f32[144,512]{1,0:T(8,128)S(1)} %get-tuple-element.38), channel_id=1, source_target_pairs={{0,1},{1,0},{2,3},{3,2},{4,5},{5,4},{6,7},{7,6},{8,9},{9,8},{10,11... | collective-permute-start | bytes 884744 | tf_op jit(solution)/shard_map/ppermute | solution.py:429
